TPU v7x, 32 devices: a whole 2x2x4 slice. The times are simulated.
32 devices in a mesh: row: 8 (over z, y), rep: 4 (over x, core).
Axes of the slice: x: 2, y: 2, z: 4, core: 2. Of those that a mesh axis runs over, the one named last changes fastest.
Arguments:
- features: bfloat16 [4096, 256], P(('row', 'rep')), may hold values from -6 to 6
- w_self: bfloat16 [256, 256], replicated, may hold values from -0.375 to 0.375
- w_neigh: bfloat16 [256, 256], replicated, may hold values from -0.75 to 0.75
- bias: float32 [256], replicated, may hold values from -3 to 3
- d_out: bfloat16 [4096, 256], P(('row', 'rep')), may hold values from -6 to 6
- tile_row: int32 [8192], P(('row', 'rep')), may hold values from 0 to 3
- tile_col: int32 [8192], P(('row', 'rep')), may hold values from 0 to 7
- tile_count: int32 [8192], P(('row', 'rep')), may hold values from 64 to 256, as said below
- edge_src: int32 [8192, 256], P(('row', 'rep')), may hold values from 0 to 127
- edge_dst: int32 [8192, 256], P(('row', 'rep')), may hold values from 0 to 127
Outputs:
- out: bfloat16 [4096, 256], P(('row', 'rep'))
- d_features: float32 [4096, 256], P(('row', 'rep'))
- grad_self: float32 [256, 256], replicated
- grad_neigh: float32 [256, 256], replicated
- grad_bias: float32 [256], replicated
Inputs may be any that keep to these rules, and one draw needn't show every extreme that they name: `tile_count`: every device has a tile with exactly 256 live edges in every draw; each device's live counts lie between a lower bound of its own and 256.
All inputs are finite; a program needn't handle non-finite values.
Results may differ from a plain program's by a relative error of at most 0.014.
Values may be sent and summed in bfloat16 or wider, within the bound.
No kernel may reach another device: no remote copies, remote signals or barrier semaphores. Data moves between devices by JAX's collectives and lax.ppermute only.
A program may use at most 128 MiB of HBM per device.

v0:
```python
import jax
import jax.numpy as jnp
from jax import lax
from jax.sharding import PartitionSpec as P

BLK = 128


def smooth_gate(value):
    return jax.nn.gelu(value, approximate=True)


def on_device(
    features, w_self, w_neigh, bias, d_out, tile_row, tile_col, tile_count, edge_src, edge_dst
):
    rows, width = features.shape
    row_count = lax.axis_size("row")
    rep_count = lax.axis_size("rep")
    group_blocks = rep_count * rows // BLK
    class_blocks = row_count * rows // BLK
    slots = edge_src.shape[1]
    lanes = jnp.arange(BLK, dtype=jnp.int32)
    live = jnp.arange(slots, dtype=jnp.int32)[None, :] < tile_count[:, None]
    dst_hot = ((edge_dst[:, :, None] == lanes) & live[:, :, None]).astype(jnp.bfloat16)
    src_hot = (edge_src[:, :, None] == lanes).astype(jnp.bfloat16)
    adjacency = jnp.einsum(
        "teb,tec->tbc", dst_hot, src_hot, preferred_element_type=jnp.float32
    ).astype(jnp.bfloat16)
    row_hot = (tile_row[:, None] == jnp.arange(group_blocks, dtype=jnp.int32)).astype(jnp.float32)
    col_hot = (tile_col[:, None] == jnp.arange(class_blocks, dtype=jnp.int32)).astype(jnp.float32)
    in_degree = jnp.sum(adjacency.astype(jnp.float32), axis=2)
    group_degree = jnp.einsum("tg,tb->gb", row_hot, in_degree).reshape(group_blocks * BLK)
    own_degree = lax.psum_scatter(group_degree, "rep", scatter_dimension=0, tiled=True)
    gathered = lax.all_gather(features, "row", axis=0, tiled=True)
    col_blocks = gathered.reshape(class_blocks, BLK, width)[tile_col]
    contrib = jnp.einsum("tbc,tcf->tbf", adjacency, col_blocks, preferred_element_type=jnp.float32)
    group_agg = jnp.einsum("tg,tbf->gbf", row_hot, contrib).reshape(group_blocks * BLK, width)
    own_agg = lax.psum_scatter(
        group_agg.astype(jnp.bfloat16), "rep", scatter_dimension=0, tiled=True
    ).astype(jnp.float32)
    inverse = 1.0 / jnp.maximum(own_degree, 1.0)
    agg = (own_agg * inverse[:, None]).astype(jnp.bfloat16)
    pre = (
        jnp.dot(features, w_self, preferred_element_type=jnp.float32)
        + jnp.dot(agg, w_neigh, preferred_element_type=jnp.float32)
        + bias
    )
    out_full, pullback = jax.vjp(smooth_gate, pre)
    out = out_full.astype(jnp.bfloat16)
    d_pre = pullback(d_out.astype(jnp.float32))[0].astype(jnp.bfloat16)
    self_term = jnp.einsum("nf,ng->fg", features, d_pre, preferred_element_type=jnp.float32)
    neigh_term = jnp.einsum("nf,ng->fg", agg, d_pre, preferred_element_type=jnp.float32)
    bias_term = jnp.sum(d_pre.astype(jnp.float32), axis=0)
    grad_self, grad_neigh, grad_bias = lax.psum((self_term, neigh_term, bias_term), ("row", "rep"))
    g_own = (
        jnp.einsum("ng,fg->nf", d_pre, w_neigh, preferred_element_type=jnp.float32)
        * inverse[:, None]
    ).astype(jnp.bfloat16)
    g_group = lax.all_gather(g_own, "rep", axis=0, tiled=True)
    row_blocks = g_group.reshape(group_blocks, BLK, width)[tile_row]
    back = jnp.einsum("tbc,tbf->tcf", adjacency, row_blocks, preferred_element_type=jnp.float32)
    scattered = lax.psum_scatter(
        jnp.einsum("tk,tcf->kcf", col_hot, back).reshape(rows * lax.axis_size("row"), width),
        "row",
        scatter_dimension=0,
        tiled=True,
    )
    d_features = (
        jnp.einsum("ng,fg->nf", d_pre, w_self, preferred_element_type=jnp.float32) + scattered
    )
    return (out, d_features, grad_self, grad_neigh, grad_bias)


def solution(mesh):
    return jax.shard_map(
        on_device,
        mesh=mesh,
        in_specs=(
            P(("row", "rep"), None),
            P(),
            P(),
            P(),
            P(("row", "rep"), None),
            P(("row", "rep")),
            P(("row", "rep")),
            P(("row", "rep")),
            P(("row", "rep"), None),
            P(("row", "rep"), None),
        ),
        out_specs=(P(("row", "rep"), None), P(("row", "rep"), None), P(), P(), P()),
        check_vma=False,
    )
```

profile of v0, /device:TPU:0, one launch (start us, length us, event | category | flops | bytes accessed | tf_op | source)
XLA Modules:
  0.0 380.2 jit_solution(10193224078478357397)
XLA Ops:
  7.2 0.0 copy-start
  7.2 0.0 reduce-scatter.3.cloned.1.call-start
  7.2 0.8 iota_compare_fusion.5
  8.0 9.3 %iota_compare_fusion.4.clone.5 = pred[256,256,128]{1,2,0:T(32,128)(4,1)} fusion(s32[256,256]{1,0:T(8,128)} %param.18), kind=kLoop, calls=%fused_computation.6.clone.clone.clone.clone.clone.clone.2 | loop fusion | flops 8388608 | bytes 8650752 | tf_op jit(solution)/shard_map/reduce_sum | solution.py:31
  17.3 33.2 %all_gather.6 = bf16[1024,256]{1,0:T(8,128)(2,1)S(1)} all-gather(bf16[128,256]{1,0:T(8,128)(2,1)} %param.10), channel_id=1, replica_groups=mesh['row'=8,'rep'=4] {'row'}, dimensions={0}, use_global_device_ids=true | all-gather | bytes 589824 | tf_op jit(solution)/shard_map/all_gather | solution.py:34
  50.5 0.7 compare_select_fusion.1
  51.2 0.0 copy-start.7
  51.2 9.6 %gather_fusion = bf16[256,128,256]{2,1,0:T(8,128)(2,1)} fusion(bf16[8,128,256]{2,1,0:T(8,128)(2,1)S(1)} %bitcast.32, s32[1024]{0:T(1024)S(1)} %pad_clamp_fusion.1), kind=kCustom, calls=%fused_computation | custom fusion | bytes 33555456 | tf_op jit(solution)/shard_map/gather | solution.py:35
  60.9 0.0 copy-done.7
  60.9 26.6 %convert_reduce_fusion = (bf16[256,128]{1,0:T(8,128)(2,1)S(1)}, bf16[256,128,128]{1,2,0:T(8,128)(2,1)S(1)}) fusion(s32[256,256]{1,0:T(8,128)S(1)} %copy-done.7, pred[256,256]{1,0:T(8,128)(4,1)S(1)} %iota_compare_fusion.5, pred[256,256,128]{1,2,0:T(32,128)(4,1)} %iota_compare_fusion.4.clone.5), kind=kOutput, calls=%fused_computation.10 | convolution fusion | flops 2176811008 | bytes 17170432 | tf_op jit(solution)/shard_map/teb,tec->tbc/dot_general | solution.py:26
  87.5 0.0 copy-start.1
  87.5 0.0 copy-start.5
  87.5 17.8 %fusion.39 = bf16[256,128,256]{2,1,0:T(8,128)(2,1)} fusion(bf16[256,128,128]{1,2,0:T(8,128)(2,1)S(1)} %get-tuple-element.26, bf16[256,128,256]{2,1,0:T(8,128)(2,1)} %gather_fusion), kind=kOutput, calls=%fused_computation.56 | convolution fusion | flops 2147483648 | bytes 41943040 | tf_op jit(solution)/shard_map/tbc,tcf->tbf/dot_general | solution.py:36
  105.3 0.0 copy-done.1
  105.3 0.0 copy-done.5
  105.3 0.0 copy-start.10
  105.3 0.0 copy-start.2
  105.4 0.0 copy-start.3
  105.4 0.0 copy-start.8
  105.4 0.0 copy-start.9
  105.4 14.7 %fusion.13 = bf16[4,128,256]{2,0,1:T(4,128)(2,1)S(1)} fusion(bf16[256,128,256]{2,1,0:T(8,128)(2,1)} %fusion.39, s32[256]{0:T(256)S(1)} %copy-done.5), kind=kOutput, calls=%fused_computation.15 | convolution fusion | flops 67109888 | bytes 17040384 | tf_op jit(solution)/shard_map/tg,tbf->gbf/dot_general | solution.py:37
  120.1 0.7 copy.22
  120.8 0.0 reduce-scatter.3.cloned.1.call-update
  120.8 0.0 all-reduce.4.cloned.1.call-start
  120.9 0.1 convolution_bitcast_fusion.1
  121.0 5.6 %all-reduce = f32[512]{0:T(512)S(1)} all-reduce(f32[512]{0:T(512)S(1)} %convolution_bitcast_fusion.1), channel_id=3, replica_groups=mesh['row'=8,'rep'=4] {'rep'}, use_global_device_ids=true, to_apply=%region_2.0.clone | all-reduce | flops 512 | bytes 4096
  126.6 0.0 copy-done.10
  126.6 0.6 dynamic-slice
  127.9 0.1 fusion.36
  128.0 0.0 copy-done.2
  128.0 0.0 copy-done.3
  128.0 0.2 fusion.38
  128.2 14.0 %reduce-scatter.3.cloned.1.call-done = bf16[128,256]{1,0:T(8,128)(2,1)} async-done(((bf16[512,256]{1,0:T(8,128)(2,1)}), bf16[128,256]{1,0:T(8,128)(2,1)}) %reduce-scatter.3.cloned.1.call-update) | async-done | bytes 65552 | tf_op jit(solution)/shard_map/reduce_scatter | solution.py:38
  142.1 0.0 copy-done
  142.1 0.0 copy-done.8
  142.1 0.0 copy-done.9
  142.1 1.8 convert_reduce_fusion.1
  143.9 0.2 fusion.17
  144.1 0.9 convolution_bitcast_fusion
  145.0 5.8 %all_gather.7 = bf16[512,256]{1,0:T(8,128)(2,1)S(1)} all-gather(bf16[128,256]{1,0:T(8,128)(2,1)S(1)} %fusion.17), channel_id=1, replica_groups=mesh['row'=8,'rep'=4] {'rep'}, dimensions={0}, use_global_device_ids=true | all-gather | bytes 327680 | tf_op jit(solution)/shard_map/all_gather | solution.py:59
  150.8 9.7 %gather_fusion.1 = bf16[256,128,256]{2,1,0:T(8,128)(2,1)} fusion(bf16[4,128,256]{2,1,0:T(8,128)(2,1)S(1)} %bitcast.31, s32[1024]{0:T(1024)S(1)} %pad_clamp_fusion), kind=kCustom, calls=%fused_computation.1 | custom fusion | bytes 33555456 | tf_op jit(solution)/shard_map/gather | solution.py:60
  160.5 0.0 copy-start.4
  160.5 0.0 copy-start.6
  160.5 14.4 %fusion.40 = bf16[256,128,256]{2,1,0:T(8,128)(2,1)} fusion(bf16[256,128,128]{1,2,0:T(8,128)(2,1)} %copy-done.1, bf16[256,128,256]{2,1,0:T(8,128)(2,1)} %gather_fusion.1), kind=kOutput, calls=%fused_computation.57 | convolution fusion | flops 2147483648 | bytes 41943040 | tf_op jit(solution)/shard_map/tbc,tbf->tcf/dot_general | solution.py:61
  175.0 0.0 copy-done.4
  175.0 1.0 fusion.28
  175.9 0.0 all-reduce.4.cloned.1.call-update
  176.0 0.0 reduce-scatter.5.cloned.1.call-start
  176.0 0.0 copy-done.6
  176.0 16.6 %fusion = f32[8,128,256]{2,0,1:T(8,128)S(1)} fusion(bf16[256,128,256]{2,1,0:T(8,128)(2,1)} %fusion.40, s32[256]{0:T(256)S(1)} %copy-done.6), kind=kOutput, calls=%fused_computation.2 | convolution fusion | flops 134219776 | bytes 17826816 | tf_op jit(solution)/shard_map/tk,tcf->kcf/dot_general | solution.py:63
  192.6 1.3 copy.24
  193.9 0.0 reduce-scatter.5.cloned.1.call-update
  193.9 39.5 %psum.23 = f32[256]{0:T(256)} all-reduce(f32[256]{0:T(256)S(1)} %get-tuple-element.22), channel_id=1, replica_groups=mesh['row'=8,'rep'=4] {'row','rep'}, use_global_device_ids=true, to_apply=%region_7.0 | all-reduce | flops 256 | bytes 2048 | tf_op jit(solution)/shard_map/psum | solution.py:54
  233.4 71.0 %all-reduce.4.cloned.1.call-done = (f32[256,256]{0,1:T(8,128)}, f32[256,256]{1,0:T(8,128)}) async-done(((f32[256,256]{0,1:T(8,128)}, f32[256,256]{1,0:T(8,128)}), (f32[256,256]{0,1:T(8,128)}, f32[256,256]{1,0:T(8,128)})) %all-reduce.4.cloned.1.call-update) | async-done | bytes 524304 | tf_op jit(solution)/shard_map/psum | solution.py:54
  304.4 1.8 copy.25
  306.2 64.0 %reduce-scatter.5.cloned.1.call-done = f32[128,256]{1,0:T(8,128)} async-done(((f32[1024,256]{1,0:T(8,128)}), f32[128,256]{1,0:T(8,128)}) %reduce-scatter.5.cloned.1.call-update) | async-done | bytes 131088 | tf_op jit(solution)/shard_map/reduce_scatter | solution.py:62
  370.2 1.8 convolution_add_fusion
  372.0 1.7 copy.37
  (3 shorter events, 0.0 us)
Async XLA Ops:
  7.2 135.0 %copy-start = (bf16[256,256]{1,0:T(8,128)(2,1)S(1)}, bf16[256,256]{1,0:T(8,128)(2,1)}, u32[]{:S(2)}) copy-start(bf16[256,256]{1,0:T(8,128)(2,1)} %param.12) | copy-start | bytes 393220
  7.2 135.0 %reduce-scatter.3.cloned.1.call-start = ((), (), s32[]{:S(2)}) async-start(), calls=%async_computation.2 | async-start | bytes 327680 | tf_op jit(solution)/shard_map/reduce_scatter | solution.py:38
  51.2 9.6 %copy-start.7 = (s32[256,256]{1,0:T(8,128)S(1)}, s32[256,256]{1,0:T(8,128)}, u32[]{:S(2)}) copy-start(s32[256,256]{1,0:T(8,128)} %param.19) | copy-start | bytes 786436
  87.5 17.9 %copy-start.1 = (bf16[256,128,128]{1,2,0:T(8,128)(2,1)}, bf16[256,128,128]{1,2,0:T(8,128)(2,1)S(1)}, u32[]{:S(2)}) copy-start(bf16[256,128,128]{1,2,0:T(8,128)(2,1)S(1)} %get-tuple-element.26) | copy-start | bytes 25165828
  87.5 17.9 %copy-start.5 = (s32[256]{0:T(256)S(1)}, s32[256]{0:T(256)}, u32[]{:S(2)}) copy-start(s32[256]{0:T(256)} %param.15) | copy-start | bytes 3076
  105.3 21.3 %copy-start.10 = (u32[32]{0:T(128)S(1)}, u32[32]{0:T(128)}, u32[]{:S(2)}) copy-start(u32[32]{0:T(128)} %constant.23) | copy-start | bytes 388
  105.3 22.6 %copy-start.2 = (bf16[128,256]{1,0:T(8,128)(2,1)S(1)}, bf16[128,256]{1,0:T(8,128)(2,1)}, u32[]{:S(2)}) copy-start(bf16[128,256]{1,0:T(8,128)(2,1)} %param.10) | copy-start | bytes 196612
  105.4 22.6 %copy-start.3 = (bf16[256,256]{1,0:T(8,128)(2,1)S(1)}, bf16[256,256]{1,0:T(8,128)(2,1)}, u32[]{:S(2)}) copy-start(bf16[256,256]{1,0:T(8,128)(2,1)} %param.11) | copy-start | bytes 393220
  105.4 36.8 %copy-start.8 = (bf16[128,256]{1,0:T(8,128)(2,1)S(1)}, bf16[128,256]{1,0:T(8,128)(2,1)}, u32[]{:S(2)}) copy-start(bf16[128,256]{1,0:T(8,128)(2,1)} %param.14) | copy-start | bytes 196612
  105.4 36.8 %copy-start.9 = (f32[256]{0:T(256)S(1)}, f32[256]{0:T(256)}, u32[]{:S(2)}) copy-start(f32[256]{0:T(256)} %param.13) | copy-start | bytes 3076
  120.8 183.6 %all-reduce.4.cloned.1.call-start = ((), (), s32[]{:S(2)}) async-start(), calls=%async_computation.4 | async-start | bytes 1048576 | tf_op jit(solution)/shard_map/psum | solution.py:54
  160.5 14.4 %copy-start.4 = (bf16[128,256]{1,0:T(8,128)(2,1)S(1)}, bf16[128,256]{1,0:T(8,128)(2,1)}, u32[]{:S(2)}) copy-start(bf16[128,256]{1,0:T(8,128)(2,1)} %reduce-scatter.3.cloned.1.call-done) | copy-start | bytes 196612
  160.5 15.5 %copy-start.6 = (s32[256]{0:T(256)S(1)}, s32[256]{0:T(256)}, u32[]{:S(2)}) copy-start(s32[256]{0:T(256)} %param.16) | copy-start | bytes 3076
  176.0 194.2 %reduce-scatter.5.cloned.1.call-start = ((), (), s32[]{:S(2)}) async-start(), calls=%async_computation.3 | async-start | bytes 1179648 | tf_op jit(solution)/shard_map/reduce_scatter | solution.py:62
Sparse Core Ops, SparseCore 0:
  120.9 21.1 reduce-scatter.2
  176.1 128.2 all-reduce.3
  307.8 62.3 reduce-scatter.4
where the time goes:
time: 381 us; the launch traced here: 380 us
  waiting for transfers between devices  149 us (39%)
  matrix products  96 us (25%)
  blocking collectives  84.1 us (22%)
  local copies, waits for them, and re-layouts  25.5 us (7%)
  between operations  14.5 us (4%)
  other arithmetic  10.9 us (3%)
    psum x1, waiting for transfers between devices, on_device(): lax.psum((self_term, neigh_term, bias_term), ('row', 'rep'))  71 us
    reduce_scatter x1, waiting for transfers between devices, on_device(): lax.psum_scatter(jnp.einsum('tk,tcf->kcf', col_hot, back).reshape(rows *...  64 us
    psum x1, blocking collectives, on_device(): lax.psum((self_term, neigh_term, bias_term), ('row', 'rep'))  39.5 us
    all_gather x1, blocking collectives, on_device(): gathered = lax.all_gather(features, 'row', axis=0, tiled=True)  33.2 us
    dot_general x1, matrix products, on_device(): jnp.einsum('teb,tec->tbc', dst_hot, src_hot, preferred_element_type=jnp.f...  26.6 us
    dot_general x1, matrix products, on_device(): jnp.einsum('tbc,tcf->tbf', adjacency, col_blocks, preferred_element_type=...  17.8 us
    dot_general x1, matrix products, on_device(): jnp.einsum('tk,tcf->kcf', col_hot, back)  16.6 us
    dot_general x1, matrix products, on_device(): jnp.einsum('tg,tbf->gbf', row_hot, contrib)  14.7 us
  transfers between devices with their start and end apart: 3, of which 3 were waited for; matrix products, arithmetic and copies ran while one was open for 5% of the time, Pallas kernels for 0%

commit v1 on v0

v1 whole, which is shorter than its diff:
```python
import jax
import jax.numpy as jnp
from jax import lax
from jax.experimental import pallas as pl
from jax.experimental.pallas import tpu as pltpu
from jax.sharding import PartitionSpec as P

BLK = 128
PAD = 16
BF16 = jnp.bfloat16
F32 = jnp.float32
UNROLL = 8
VMEM = pl.BlockSpec(memory_space=pltpu.VMEM)
SMEM = pl.BlockSpec(memory_space=pltpu.SMEM)


def params():
    return pltpu.CompilerParams(vmem_limit_bytes=56 * 1024 * 1024)


def row_place(block):
    away = block ^ lax.axis_index("rep")
    return ((away & 1) << 1) | (away >> 1)


def col_place(block, row_count):
    me = lax.axis_index("row")
    half = row_count // 2
    return 2 * lax.rem((me >> 1) - (block >> 1) + half, half) + ((block ^ me) & 1)


def col_block(place, row_count):
    me = lax.axis_index("row")
    half = row_count // 2
    return 2 * lax.rem((me >> 1) - place // 2 + half, half) + ((me & 1) ^ (place & 1))


def split(value):
    high = value.astype(BF16).astype(F32)
    line = lax.broadcasted_iota(jnp.int32, (PAD, value.shape[1]), 0)
    return jnp.where(line == 0, high, jnp.where(line == 1, value - high, 0.0)).astype(BF16)


def joined(rows):
    rows = rows.astype(F32)
    return rows[0:1] + rows[1:2]


def build_kernel(row_ref, col_ref, count_ref, src_ref, dst_ref, adj_ref, acc_ref):
    tiles, slots = src_ref.shape
    row_blocks, col_blocks = acc_ref.shape[:2]
    acc_ref[...] = jnp.zeros_like(acc_ref)
    line = lax.broadcasted_iota(jnp.int32, (BLK, slots), 0).astype(BF16)
    slot = lax.broadcasted_iota(jnp.int32, (1, slots), 1)
    one, zero = jnp.ones((), BF16), jnp.zeros((), BF16)

    def step(i, carry):
        base = pl.multiple_of(i * UNROLL, UNROLL)
        dst, src = dst_ref[pl.ds(base, UNROLL), :], src_ref[pl.ds(base, UNROLL), :]
        for u in range(UNROLL):
            tile = base + u
            live = jnp.where(slot < count_ref[tile], dst[u : u + 1], -1)
            dst_hot = jnp.where(line == live.astype(BF16), one, zero)
            src_hot = jnp.where(line == src[u : u + 1].astype(BF16), one, zero)
            part = lax.dot_general(
                dst_hot, src_hot, (((1,), (1,)), ((), ())), preferred_element_type=F32
            )
            acc_ref[row_place(row_ref[tile]), col_place(col_ref[tile], col_blocks)] += part
        return carry

    lax.fori_loop(0, tiles // UNROLL, step, 0)
    for g in range(row_blocks):
        for c in range(col_blocks):
            adj_ref[g * BLK : (g + 1) * BLK, c * BLK : (c + 1) * BLK] = acc_ref[g, c].astype(BF16)


def gather_kernel(adj_ref, *refs):
    *feature_refs, keep_ref, send_ref = refs
    half = keep_ref.shape[0] - PAD
    total, at = None, 0
    for ref in feature_refs:
        size = ref.shape[0]
        part = jnp.dot(adj_ref[:, at : at + size], ref[...], preferred_element_type=F32)
        total = part if total is None else total + part
        at += size
    ones = jnp.ones((PAD, adj_ref.shape[1]), BF16)
    degree = lax.dot_general(
        ones, adj_ref[...], (((1,), (1,)), ((), ())), preferred_element_type=F32
    )
    keep_ref[:half] = total[:half]
    keep_ref[half:] = degree[:, :half]
    send_ref[:half] = total[half:].astype(BF16)
    send_ref[half:] = split(degree[:1, half:])


def pair_kernel(keep_ref, got_ref, pair_ref):
    half = keep_ref.shape[0] - PAD
    pair_ref[:half] = (keep_ref[:half] + got_ref[:half].astype(F32)).astype(BF16)
    pair_ref[half:] = split(keep_ref[half : half + 1] + joined(got_ref[half:]))


def node_kernel(
    pair_ref, got_ref, own_ref, near_ref, w_self_ref, w_neigh_ref, bias_ref,
    out_ref, self_ref, keep_ref, send_ref,
):
    rows, width = out_ref.shape
    half = 2 * rows
    swapped = jnp.concatenate([got_ref[rows:half], got_ref[:rows]], axis=0).astype(F32)
    sums = pair_ref[:half].astype(F32) + swapped
    far = joined(got_ref[half:])
    degree = joined(pair_ref[half:]) + jnp.concatenate([far[:, rows:], far[:, :rows]], axis=1)
    inverse_row = 1.0 / jnp.maximum(degree, 1.0)
    diagonal = lax.broadcasted_iota(jnp.int32, (half, half), 0) == lax.broadcasted_iota(
        jnp.int32, (half, half), 1
    )
    inverse = jnp.sum(jnp.where(diagonal, inverse_row, 0.0), axis=1, keepdims=True)
    agg = (sums * inverse).astype(BF16)
    features = jnp.concatenate([own_ref[:rows], near_ref[:rows]], axis=0)
    d_out = jnp.concatenate([own_ref[rows:], near_ref[rows:]], axis=0).astype(F32)
    pre = (
        jnp.dot(features, w_self_ref[...], preferred_element_type=F32)
        + jnp.dot(agg, w_neigh_ref[...], preferred_element_type=F32)
        + bias_ref[...]
    )
    square = pre * pre
    bend = jnp.tanh(0.7978845608 * pre * (1.0 + 0.044715 * square))
    out_ref[...] = (0.5 * pre[:rows] * (1.0 + bend[:rows])).astype(BF16)
    slope = 0.5 * (1.0 + bend) + 0.5 * pre * (1.0 - bend * bend) * (
        0.7978845608 * (1.0 + 3.0 * 0.044715 * square)
    )
    d_pre = (d_out * slope).astype(BF16)
    transposed = (((1,), (1,)), ((), ()))
    self_ref[...] = lax.dot_general(
        d_pre[:rows], w_self_ref[...], transposed, preferred_element_type=F32
    )
    back = lax.dot_general(d_pre, w_neigh_ref[...], transposed, preferred_element_type=F32)
    send_ref[:half] = (back * inverse).astype(BF16)
    me = lax.axis_index("rep")
    terms = jnp.where(me >> 1 == 0, features, agg)
    grads = lax.dot_general(terms, d_pre, (((0,), (0,)), ((), ())), preferred_element_type=F32)
    middle = width // 2
    low = me & 1 == 0
    bias_term = jnp.sum(d_pre.astype(F32), axis=0, keepdims=True)
    keep_ref[:middle] = jnp.where(low, grads[:middle], grads[middle:])
    keep_ref[middle:] = jnp.broadcast_to(bias_term, (PAD, width))
    send_ref[half : half + middle] = jnp.where(low, grads[middle:], grads[:middle]).astype(BF16)
    send_ref[half + middle :] = split(bias_term)


def spread_kernel(adj_ref, sent_ref, got_ref, keep_ref, msg_ref):
    row_count = msg_ref.shape[0]
    half = adj_ref.shape[0] // 2
    middle = keep_ref.shape[0] - PAD
    share = middle // row_count
    g = jnp.concatenate([sent_ref[:half], got_ref[:half]], axis=0)
    grads = keep_ref[:middle] + got_ref[half : half + middle].astype(F32)
    bias_rows = split(keep_ref[middle : middle + 1] + joined(got_ref[half + middle :]))
    for place in range(row_count):
        block = lax.dot_general(
            adj_ref[:, place * BLK : (place + 1) * BLK],
            g,
            (((0,), (0,)), ((), ())),
            preferred_element_type=F32,
        )
        msg_ref[col_block(place, row_count), :BLK] = block.astype(BF16)
    for k in range(row_count):
        msg_ref[k, BLK : BLK + share] = grads[k * share : (k + 1) * share].astype(BF16)
        if share < PAD:
            msg_ref[k, BLK + share : BLK + PAD] = jnp.zeros((PAD - share, grads.shape[1]), BF16)
        msg_ref[k, BLK + PAD :] = bias_rows


def finish_kernel(msg_ref, self_ref, d_features_ref, share_ref, bias_ref):
    row_count = msg_ref.shape[0]
    total = msg_ref[0].astype(F32)
    for k in range(1, row_count):
        total = total + msg_ref[k].astype(F32)
    d_features_ref[...] = self_ref[...] + total[:BLK]
    share_ref[...] = total[BLK : BLK + PAD].astype(BF16)
    bias_ref[...] = total[BLK + PAD : BLK + PAD + 1] + total[BLK + PAD + 1 : BLK + PAD + 2]


def call(kernel, out_shape, specs, scratch=()):
    many = isinstance(out_shape, (list, tuple))
    return pl.pallas_call(
        kernel,
        out_shape=out_shape,
        in_specs=specs,
        out_specs=[VMEM] * len(out_shape) if many else VMEM,
        scratch_shapes=list(scratch),
        compiler_params=params(),
    )


def on_device(
    features, w_self, w_neigh, bias, d_out, tile_row, tile_col, tile_count, edge_src, edge_dst
):
    rows, width = features.shape
    row_count, rep_count = lax.axis_size("row"), lax.axis_size("rep")
    group, columns = rep_count * rows, row_count * rows
    half, middle = group // 2, width // 2
    shape = jax.ShapeDtypeStruct

    def swap(value, axis, bit):
        return lax.ppermute(value, axis, [(i, i ^ bit) for i in range(lax.axis_size(axis))])

    pair = jnp.concatenate([features, swap(features, "row", 1)], axis=0)
    pieces = [pair] + [
        lax.ppermute(pair, "row", [(i, (i + 2 * s) % row_count) for i in range(row_count)])
        for s in range(1, row_count // 2)
    ]
    own = jnp.concatenate([features, d_out], axis=0)
    near = swap(own, "rep", 2)
    adjacency = call(
        build_kernel,
        shape((group, columns), BF16),
        [SMEM, SMEM, SMEM, VMEM, VMEM],
        [pltpu.VMEM((rep_count, row_count, BLK, BLK), F32)],
    )(tile_row, tile_col, tile_count, edge_src, edge_dst)
    keep, send = call(
        gather_kernel,
        (shape((half + PAD, width), F32), shape((half + PAD, width), BF16)),
        [VMEM] * (1 + len(pieces)),
    )(adjacency, *pieces)
    pair_sum = call(pair_kernel, shape((half + PAD, width), BF16), [VMEM] * 2)(
        keep, swap(send, "rep", 1)
    )
    out, self_term, keep, send = call(
        node_kernel,
        (
            shape((rows, width), BF16),
            shape((rows, width), F32),
            shape((middle + PAD, width), F32),
            shape((half + middle + PAD, width), BF16),
        ),
        [VMEM] * 7,
    )(pair_sum, swap(pair_sum, "rep", 2), own, near, w_self, w_neigh, bias[None, :])
    message = call(
        spread_kernel, shape((row_count, BLK + 2 * PAD, width), BF16), [VMEM] * 4
    )(adjacency, send, swap(send, "rep", 1), keep)
    message = lax.all_to_all(message, "row", 0, 0, tiled=True)
    d_features, share, grad_bias = call(
        finish_kernel,
        (shape((rows, width), F32), shape((PAD, width), BF16), shape((1, width), F32)),
        [VMEM] * 2,
    )(message, self_term)
    share = share[: middle // row_count]
    quarter = lax.all_to_all(
        jnp.broadcast_to(share[None], (row_count,) + share.shape), "row", 0, 0, tiled=True
    ).reshape(middle, width)
    grads = lax.all_gather(quarter, "rep", axis=0, tiled=True).astype(F32)
    return (out, d_features, grads[:width], grads[width:], grad_bias[0])


def solution(mesh):
    return jax.shard_map(
        on_device,
        mesh=mesh,
        in_specs=(
            P(("row", "rep"), None),
            P(),
            P(),
            P(),
            P(("row", "rep"), None),
            P(("row", "rep")),
            P(("row", "rep")),
            P(("row", "rep")),
            P(("row", "rep"), None),
            P(("row", "rep"), None),
        ),
        out_specs=(P(("row", "rep"), None), P(("row", "rep"), None), P(), P(), P()),
        check_vma=False,
    )
```

time: 381 us -> 91.6 us (0.24)
  waiting for transfers between devices: 149 us -> 11.4 us
  matrix products: 96 us -> 0 us
  blocking collectives: 84.1 us -> 38.9 us
  Pallas kernels: 0 us -> 24.1 us
  local copies, waits for them, and re-layouts: 25.5 us -> 5.8 us
  between operations: 14.5 us -> 0.7 us
  other arithmetic: 10.9 us -> 0 us
  starting transfers between devices: 0.12 us -> 10.3 us
    dot_general x12 -> x0, matrix products: 96 us -> none  [the longest x1 26.6 us: on_device(): jnp.einsum('teb,tec->tbc', dst_hot, src_hot, preferred_element_type=jnp.f...]
    reduce_scatter x2 -> x0, waiting for transfers between devices: 78 us -> none  [the longest x1 64 us: on_device(): lax.psum_scatter(jnp.einsum('tk,tcf->kcf', col_hot, back).reshape(rows *...]
    psum x1 -> x0, waiting for transfers between devices: 71 us -> none  [on_device(): lax.psum((self_term, neigh_term, bias_term), ('row', 'rep'))]
    psum x1 -> x0, blocking collectives: 39.5 us -> none  [on_device(): lax.psum((self_term, neigh_term, bias_term), ('row', 'rep'))]
    all_gather x2 -> x1, blocking collectives: 39 us -> 5.77 us  [on_device(): grads = lax.all_gather(quarter, 'rep', axis=0, tiled=True).astype(F32)]
    all_to_all x0 -> x2, blocking collectives: none -> 33.1 us  [the longest x1 23.1 us: on_device(): message = lax.all_to_all(message, 'row', 0, 0, tiled=True)]
    pallas_call x0 -> x6, Pallas kernels: none -> 24.1 us  [the longest x1 12.4 us: on_device(): call(build_kernel, shape((group, columns), BF16), [SMEM, SMEM, SMEM, VMEM...]
    gather x2 -> x0, local copies, waits for them, and re-layouts: 19.4 us -> none  [the longest x1 9.72 us: on_device(): row_blocks = g_group.reshape(group_blocks, BLK, width)[tile_row]]
  transfers between devices with their start and end apart: 3 -> 8, of which waited for: 3 -> 4; matrix products, arithmetic and copies ran while one was open for 5% -> 1% of each run, Pallas kernels for 0% -> 14%
where the time goes in v1:
time: 91.6 us; the launch traced here: 91.1 us
  blocking collectives  38.9 us (42%)
  Pallas kernels  24.1 us (26%)
  waiting for transfers between devices  11.4 us (12%)
  starting transfers between devices  10.3 us (11%)
  local copies, waits for them, and re-layouts  5.8 us (6%)
    all_to_all x1, blocking collectives, on_device(): message = lax.all_to_all(message, 'row', 0, 0, tiled=True)  23.1 us
    pallas_call x1, Pallas kernels, on_device(): call(build_kernel, shape((group, columns), BF16), [SMEM, SMEM, SMEM, VMEM...  12.4 us
    ppermute x5, waiting for transfers between devices, swap(): lax.ppermute(value, axis, [(i, i ^ bit) for i in range(lax.axis_size(axis...  11.4 us
    all_to_all x1, blocking collectives, on_device(): lax.all_to_all(jnp.broadcast_to(share[None], (row_count,) + share.shape),...  9.95 us
    all_gather x1, blocking collectives, on_device(): grads = lax.all_gather(quarter, 'rep', axis=0, tiled=True).astype(F32)  5.77 us
    ppermute x3, starting transfers between devices, on_device(): lax.ppermute(pair, 'row', [(i, (i + 2 * s) % row_count) for i in range(ro...  5.17 us
    ppermute x5, starting transfers between devices, swap(): lax.ppermute(value, axis, [(i, i ^ bit) for i in range(lax.axis_size(axis...  5.13 us
    unnamed x22, local copies, waits for them, and re-layouts  4.26 us
  transfers between devices with their start and end apart: 8, of which 4 were waited for; matrix products, arithmetic and copies ran while one was open for 1% of the time, Pallas kernels for 14%

profile of v1, /device:TPU:0, one launch (start us, length us, event | category | flops | bytes accessed | tf_op | source)
XLA Modules:
  0.0 91.1 jit_solution(13289899983205558038)
XLA Ops:
  0.6 3.0 %collective-permute-start = (bf16[128,256]{1,0:T(8,128)(2,1)}, bf16[128,256]{1,0:T(8,128)(2,1)S(1)}, u32[]{:S(2)}, u32[]{:S(2)}) collective-permute-start(bf16[128,256]{1,0:T(8,128)(2,1)} %param.10), channel_id=1, source_target_pairs={{0,4},{4,0},{8,12},{12,8},{16,20},{20,16},{24,28},{28,24},{1,5},{5... | collective-permute-start | bytes 196616 | tf_op jit(solution)/shard_map/ppermute | solution.py:205
  3.7 0.9 constant_dynamic-update-slice_fusion.1
  4.6 1.6 %collective-permute-done = bf16[128,256]{1,0:T(8,128)(2,1)S(1)} collective-permute-done((bf16[128,256]{1,0:T(8,128)(2,1)}, bf16[128,256]{1,0:T(8,128)(2,1)S(1)}, u32[]{:S(2)}, u32[]{:S(2)}) %collective-permute-start) | collective-permute-done | bytes 65568 | tf_op jit(solution)/shard_map/ppermute | solution.py:205
  6.1 0.0 copy-start
  6.1 4.2 %collective-permute-start.3 = (bf16[256,256]{1,0:T(8,128)(2,1)S(1)}, bf16[256,256]{1,0:T(8,128)(2,1)S(1)}, u32[]{:S(2)}, u32[]{:S(2)}) collective-permute-start(bf16[256,256]{1,0:T(8,128)(2,1)S(1)} %constant_dynamic-update-slice_fusion.refs_0_), channel_id=1, source_target_pairs={{0,24},{4,28},{8,0},{12,4},{16,8},{20,12},{24,16},{28,20},{1,25},{... | collective-permute-start | bytes 393224 | tf_op jit(solution)/shard_map/ppermute | solution.py:209
  10.3 0.0 collective-permute-start.2
  10.3 1.0 %collective-permute-start.1 = (bf16[256,256]{1,0:T(8,128)(2,1)S(1)}, bf16[256,256]{1,0:T(8,128)(2,1)S(1)}, u32[]{:S(2)}, u32[]{:S(2)}) collective-permute-start(bf16[256,256]{1,0:T(8,128)(2,1)S(1)} %constant_dynamic-update-slice_fusion.refs_0_), channel_id=1, source_target_pairs={{0,8},{4,12},{8,16},{12,20},{16,24},{20,28},{24,0},{28,4},{1,9},{5... | collective-permute-start | bytes 393224 | tf_op jit(solution)/shard_map/ppermute | solution.py:209
  11.3 12.4 %shard_map.137.adj_ref = bf16[512,1024]{1,0:T(8,128)(2,1)} custom-call(s32[256]{0:T(256)} %row_ref.1, s32[256]{0:T(256)} %col_ref.1, s32[256]{0:T(256)} %count_ref.1, s32[256,256]{1,0:T(8,128)} %src_ref.1, s32[256,256]{1,0:T(8,128)} %dst_ref.1), custom_call_target="tpu_custom_call" | custom-call | tf_op jit(solution)/shard_map/pallas_call | solution.py:214
  23.7 0.0 copy-done
  23.7 0.0 collective-permute-done.3.refs_3_
  23.7 0.0 copy-start.5
  23.7 0.0 collective-permute-done.2.refs_2_
  23.7 0.0 copy-start.6
  23.7 0.0 collective-permute-done.1.refs_1_
  23.7 0.6 copy-done.5
  24.3 0.1 copy-done.6
  24.4 0.0 copy-start.7
  24.4 0.7 copy-done.7
  25.1 2.8 %shard_map.138 = (f32[272,256]{1,0:T(8,128)}, bf16[272,256]{1,0:T(8,128)(2,1)}) custom-call(bf16[512,1024]{1,0:T(8,128)(2,1)} %shard_map.137.adj_ref, bf16[256,256]{1,0:T(8,128)(2,1)} %copy-done, bf16[256,256]{1,0:T(8,128)(2,1)} %copy-done.7, bf16[256,256]{1,0:T(8,128)(2,1)} %copy-done.6, bf16[256,256]{1,0:T(8,128)(2,1)} %copy-done.5), custom_call_target="tpu_custom_call" | custom-call | tf_op jit(solution)/shard_map/pallas_call | solution.py:220
  27.8 0.0 collective-permute-start.4
  27.8 1.6 %collective-permute-done.4.got_ref = bf16[272,256]{1,0:T(8,128)(2,1)S(1)} collective-permute-done((bf16[272,256]{1,0:T(8,128)(2,1)}, bf16[272,256]{1,0:T(8,128)(2,1)S(1)}, u32[]{:S(2)}, u32[]{:S(2)}) %collective-permute-start.4) | collective-permute-done | bytes 139296 | tf_op jit(solution)/shard_map/ppermute | solution.py:205
  29.4 0.0 copy-start.4
  29.4 0.7 copy-done.4
  30.0 0.0 copy-start.9
  30.0 1.7 %shard_map.139.pair_ref = bf16[272,256]{1,0:T(8,128)(2,1)} custom-call(f32[272,256]{1,0:T(8,128)} %get-tuple-element.14.keep_ref, bf16[272,256]{1,0:T(8,128)(2,1)} %copy-done.4), custom_call_target="tpu_custom_call" | custom-call | tf_op jit(solution)/shard_map/pallas_call | solution.py:225
  31.8 1.5 %collective-permute-start.5 = (bf16[272,256]{1,0:T(8,128)(2,1)}, bf16[272,256]{1,0:T(8,128)(2,1)S(1)}, u32[]{:S(2)}, u32[]{:S(2)}) collective-permute-start(bf16[272,256]{1,0:T(8,128)(2,1)} %shard_map.139.pair_ref), channel_id=1, source_target_pairs={{0,2},{1,3},{2,0},{3,1},{4,6},{5,7},{6,4},{7,5},{8,10},{9,11},{10,... | collective-permute-start | bytes 417800 | tf_op jit(solution)/shard_map/ppermute | solution.py:205
  33.3 0.0 copy-done.9
  33.3 0.0 copy-start.1
  33.3 0.6 collective-permute-start.6
  33.9 6.6 %collective-permute-done.6.near_ref = bf16[256,256]{1,0:T(8,128)(2,1)S(1)} collective-permute-done((bf16[256,256]{1,0:T(8,128)(2,1)S(1)}, bf16[256,256]{1,0:T(8,128)(2,1)S(1)}, u32[]{:S(2)}, u32[]{:S(2)}) %collective-permute-start.6) | collective-permute-done | bytes 131104 | tf_op jit(solution)/shard_map/ppermute | solution.py:205
  40.5 0.0 copy-start.8
  40.5 0.0 collective-permute-done.5.got_ref
  40.5 0.0 copy-start.3
  40.5 0.0 copy-done.1
  40.5 0.6 copy-done.8
  41.2 0.1 copy-done.3
  41.2 2.6 %shard_map.140 = (bf16[128,256]{1,0:T(8,128)(2,1)}, f32[128,256]{1,0:T(8,128)}, f32[144,256]{1,0:T(8,128)}, bf16[400,256]{1,0:T(8,128)(2,1)}) custom-call(bf16[272,256]{1,0:T(8,128)(2,1)} %shard_map.139.pair_ref, bf16[272,256]{1,0:T(8,128)(2,1)} %copy-done.3, bf16[256,256]{1,0:T(8,128)(2,1)} %copy-done.1, bf16[256,256]{1,0:T(8,128)(2,1)} %copy-done.8, ...), custom_call_target="tpu_custom_call" | custom-call | tf_op jit(solution)/shard_map/pallas_call | solution.py:228
  43.8 0.0 collective-permute-start.7
  43.8 1.7 %collective-permute-done.7.got_ref = bf16[400,256]{1,0:T(8,128)(2,1)S(1)} collective-permute-done((bf16[400,256]{1,0:T(8,128)(2,1)}, bf16[400,256]{1,0:T(8,128)(2,1)S(1)}, u32[]{:S(2)}, u32[]{:S(2)}) %collective-permute-start.7) | collective-permute-done | bytes 204832 | tf_op jit(solution)/shard_map/ppermute | solution.py:205
  45.5 0.0 copy-start.2
  45.5 0.7 copy-done.2
  46.2 2.8 %shard_map.141 = bf16[8,160,256]{2,1,0:T(8,128)(2,1)} custom-call(bf16[512,1024]{1,0:T(8,128)(2,1)} %shard_map.137.adj_ref, bf16[400,256]{1,0:T(8,128)(2,1)} %get-tuple-element.17.sent_ref, bf16[400,256]{1,0:T(8,128)(2,1)} %copy-done.2, f32[144,256]{1,0:T(8,128)} %get-tuple-element.18.keep_ref), custom_call_target="tpu_custom_call" | custom-call | tf_op jit(solution)/shard_map/pallas_call | solution.py:238
  48.9 23.1 %all_to_all.10.msg_ref = bf16[8,160,256]{2,1,0:T(8,128)(2,1)} all-to-all(bf16[8,160,256]{2,1,0:T(8,128)(2,1)} %shard_map.141), channel_id=1, replica_groups=mesh['row'=8,'rep'=4] {'row'}, dimensions={0} | all-to-all | bytes 1310720 | tf_op jit(solution)/shard_map/all_to_all | solution.py:241
  72.0 1.8 %shard_map.142 = (f32[128,256]{1,0:T(8,128)}, bf16[16,256]{1,0:T(8,128)(2,1)}, f32[1,256]{1,0:T(1,128)}) custom-call(bf16[8,160,256]{2,1,0:T(8,128)(2,1)} %all_to_all.10.msg_ref, f32[128,256]{1,0:T(8,128)} %get-tuple-element.19.self_ref), custom_call_target="tpu_custom_call" | custom-call | tf_op jit(solution)/shard_map/pallas_call | solution.py:242
  73.9 0.7 broadcast_in_dim.10
  74.6 10.0 %all_to_all.11 = bf16[8,16,256]{2,1,0:T(8,128)(2,1)S(1)} all-to-all(bf16[8,16,256]{2,1,0:T(8,128)(2,1)S(1)} %broadcast_in_dim.10), channel_id=1, replica_groups=mesh['row'=8,'rep'=4] {'row'}, dimensions={0} | all-to-all | bytes 131072 | tf_op jit(solution)/shard_map/all_to_all | solution.py:248
  84.5 5.8 %all_gather.3 = bf16[512,256]{1,0:T(8,128)(2,1)S(1)} all-gather(bf16[128,256]{1,0:T(8,128)(2,1)S(1)} %bitcast.3), channel_id=1, replica_groups=mesh['row'=8,'rep'=4] {'rep'}, dimensions={0}, use_global_device_ids=true | all-gather | bytes 327680 | tf_op jit(solution)/shard_map/all_gather | solution.py:251
  90.3 0.8 fusion
  (3 shorter events, 0.0 us)
Async XLA Ops:
  0.6 5.5 %collective-permute-start = (bf16[128,256]{1,0:T(8,128)(2,1)}, bf16[128,256]{1,0:T(8,128)(2,1)S(1)}, u32[]{:S(2)}, u32[]{:S(2)}) collective-permute-start(bf16[128,256]{1,0:T(8,128)(2,1)} %param.10), channel_id=1, source_target_pairs={{0,4},{4,0},{8,12},{12,8},{16,20},{20,16},{24,28},{28,24},{1,5},{5... | collective-permute-start | bytes 196616 | tf_op jit(solution)/shard_map/ppermute | solution.py:205
  6.1 17.6 %copy-start = (bf16[256,256]{1,0:T(8,128)(2,1)}, bf16[256,256]{1,0:T(8,128)(2,1)S(1)}, u32[]{:S(2)}) copy-start(bf16[256,256]{1,0:T(8,128)(2,1)S(1)} %constant_dynamic-update-slice_fusion.refs_0_) | copy-start | bytes 393220
  6.1 17.6 %collective-permute-start.3 = (bf16[256,256]{1,0:T(8,128)(2,1)S(1)}, bf16[256,256]{1,0:T(8,128)(2,1)S(1)}, u32[]{:S(2)}, u32[]{:S(2)}) collective-permute-start(bf16[256,256]{1,0:T(8,128)(2,1)S(1)} %constant_dynamic-update-slice_fusion.refs_0_), channel_id=1, source_target_pairs={{0,24},{4,28},{8,0},{12,4},{16,8},{20,12},{24,16},{28,20},{1,25},{... | collective-permute-start | bytes 393224 | tf_op jit(solution)/shard_map/ppermute | solution.py:209
  10.3 13.4 %collective-permute-start.2 = (bf16[256,256]{1,0:T(8,128)(2,1)S(1)}, bf16[256,256]{1,0:T(8,128)(2,1)S(1)}, u32[]{:S(2)}, u32[]{:S(2)}) collective-permute-start(bf16[256,256]{1,0:T(8,128)(2,1)S(1)} %constant_dynamic-update-slice_fusion.refs_0_), channel_id=1, source_target_pairs={{0,16},{4,20},{8,24},{12,28},{16,0},{20,4},{24,8},{28,12},{1,17},{... | collective-permute-start | bytes 393224 | tf_op jit(solution)/shard_map/ppermute | solution.py:209
  10.3 13.4 %collective-permute-start.1 = (bf16[256,256]{1,0:T(8,128)(2,1)S(1)}, bf16[256,256]{1,0:T(8,128)(2,1)S(1)}, u32[]{:S(2)}, u32[]{:S(2)}) collective-permute-start(bf16[256,256]{1,0:T(8,128)(2,1)S(1)} %constant_dynamic-update-slice_fusion.refs_0_), channel_id=1, source_target_pairs={{0,8},{4,12},{8,16},{12,20},{16,24},{20,28},{24,0},{28,4},{1,9},{5... | collective-permute-start | bytes 393224 | tf_op jit(solution)/shard_map/ppermute | solution.py:209
  23.7 0.6 copy-start.5
  23.7 0.7 copy-start.6
  24.4 0.7 copy-start.7
  27.8 1.6 %collective-permute-start.4 = (bf16[272,256]{1,0:T(8,128)(2,1)}, bf16[272,256]{1,0:T(8,128)(2,1)S(1)}, u32[]{:S(2)}, u32[]{:S(2)}) collective-permute-start(bf16[272,256]{1,0:T(8,128)(2,1)} %get-tuple-element.15), channel_id=1, source_target_pairs={{0,1},{1,0},{2,3},{3,2},{4,5},{5,4},{6,7},{7,6},{8,9},{9,8},{10,11... | collective-permute-start | bytes 417800 | tf_op jit(solution)/shard_map/ppermute | solution.py:205
  29.4 0.7 copy-start.4
  30.0 3.2 %copy-start.9 = (bf16[128,256]{1,0:T(8,128)(2,1)S(1)}, bf16[128,256]{1,0:T(8,128)(2,1)}, u32[]{:S(2)}) copy-start(bf16[128,256]{1,0:T(8,128)(2,1)} %param.14) | copy-start | bytes 196612
  31.8 8.7 %collective-permute-start.5 = (bf16[272,256]{1,0:T(8,128)(2,1)}, bf16[272,256]{1,0:T(8,128)(2,1)S(1)}, u32[]{:S(2)}, u32[]{:S(2)}) collective-permute-start(bf16[272,256]{1,0:T(8,128)(2,1)} %shard_map.139.pair_ref), channel_id=1, source_target_pairs={{0,2},{1,3},{2,0},{3,1},{4,6},{5,7},{6,4},{7,5},{8,10},{9,11},{10,... | collective-permute-start | bytes 417800 | tf_op jit(solution)/shard_map/ppermute | solution.py:205
  33.3 7.3 %copy-start.1 = (bf16[256,256]{1,0:T(8,128)(2,1)}, bf16[256,256]{1,0:T(8,128)(2,1)S(1)}, u32[]{:S(2)}) copy-start(bf16[256,256]{1,0:T(8,128)(2,1)S(1)} %constant_dynamic-update-slice_fusion.2.own_ref) | copy-start | bytes 393220
  33.3 7.2 %collective-permute-start.6 = (bf16[256,256]{1,0:T(8,128)(2,1)S(1)}, bf16[256,256]{1,0:T(8,128)(2,1)S(1)}, u32[]{:S(2)}, u32[]{:S(2)}) collective-permute-start(bf16[256,256]{1,0:T(8,128)(2,1)S(1)} %constant_dynamic-update-slice_fusion.2.own_ref), channel_id=1, source_target_pairs={{0,2},{1,3},{2,0},{3,1},{4,6},{5,7},{6,4},{7,5},{8,10},{9,11},{10,... | collective-permute-start | bytes 393224 | tf_op jit(solution)/shard_map/ppermute | solution.py:205
  40.5 0.7 copy-start.8
  40.5 0.7 copy-start.3
  43.8 1.7 %collective-permute-start.7 = (bf16[400,256]{1,0:T(8,128)(2,1)}, bf16[400,256]{1,0:T(8,128)(2,1)S(1)}, u32[]{:S(2)}, u32[]{:S(2)}) collective-permute-start(bf16[400,256]{1,0:T(8,128)(2,1)} %get-tuple-element.17.sent_ref), channel_id=1, source_target_pairs={{0,1},{1,0},{2,3},{3,2},{4,5},{5,4},{6,7},{7,6},{8,9},{9,8},{10,11... | collective-permute-start | bytes 614408 | tf_op jit(solution)/shard_map/ppermute | solution.py:205
  45.5 0.7 copy-start.2

commit v2 on v1

--- a/solution.py
+++ b/solution.py
@@ -1,3 +1,5 @@
+import math
+
 import jax
 import jax.numpy as jnp
 from jax import lax
@@ -9,13 +11,13 @@
 PAD = 16
 BF16 = jnp.bfloat16
 F32 = jnp.float32
-UNROLL = 8
+UNROLL = 32
 VMEM = pl.BlockSpec(memory_space=pltpu.VMEM)
 SMEM = pl.BlockSpec(memory_space=pltpu.SMEM)
 
 
-def params():
-    return pltpu.CompilerParams(vmem_limit_bytes=56 * 1024 * 1024)
+def size_of(value):
+    return math.prod(value.shape) * jnp.dtype(value.dtype).itemsize
 
 
 def row_place(block):
@@ -180,16 +182,17 @@
     bias_ref[...] = total[BLK + PAD : BLK + PAD + 1] + total[BLK + PAD + 1 : BLK + PAD + 2]
 
 
-def call(kernel, out_shape, specs, scratch=()):
-    many = isinstance(out_shape, (list, tuple))
+def call(kernel, out_shape, specs, args, scratch=()):
+    outs = out_shape if isinstance(out_shape, (list, tuple)) else [out_shape]
+    held = sum(size_of(v) for v in [*args, *outs, *scratch])
     return pl.pallas_call(
         kernel,
         out_shape=out_shape,
         in_specs=specs,
-        out_specs=[VMEM] * len(out_shape) if many else VMEM,
+        out_specs=[VMEM] * len(outs) if outs is out_shape else VMEM,
         scratch_shapes=list(scratch),
-        compiler_params=params(),
-    )
+        compiler_params=pltpu.CompilerParams(vmem_limit_bytes=2 * held + 4 * 1024 * 1024),
+    )(*args)
 
 
 def on_device(
@@ -215,15 +218,21 @@
         build_kernel,
         shape((group, columns), BF16),
         [SMEM, SMEM, SMEM, VMEM, VMEM],
+        (tile_row, tile_col, tile_count, edge_src, edge_dst),
         [pltpu.VMEM((rep_count, row_count, BLK, BLK), F32)],
-    )(tile_row, tile_col, tile_count, edge_src, edge_dst)
+    )
+    adjacency, near, pieces = lax.optimization_barrier((adjacency, near, pieces))
     keep, send = call(
         gather_kernel,
         (shape((half + PAD, width), F32), shape((half + PAD, width), BF16)),
         [VMEM] * (1 + len(pieces)),
-    )(adjacency, *pieces)
-    pair_sum = call(pair_kernel, shape((half + PAD, width), BF16), [VMEM] * 2)(
-        keep, swap(send, "rep", 1)
+        (adjacency, *pieces),
+    )
+    pair_sum = call(
+        pair_kernel,
+        shape((half + PAD, width), BF16),
+        [VMEM] * 2,
+        (keep, swap(send, "rep", 1)),
     )
     out, self_term, keep, send = call(
         node_kernel,
@@ -234,16 +243,21 @@
             shape((half + middle + PAD, width), BF16),
         ),
         [VMEM] * 7,
-    )(pair_sum, swap(pair_sum, "rep", 2), own, near, w_self, w_neigh, bias[None, :])
+        (pair_sum, swap(pair_sum, "rep", 2), own, near, w_self, w_neigh, bias[None, :]),
+    )
     message = call(
-        spread_kernel, shape((row_count, BLK + 2 * PAD, width), BF16), [VMEM] * 4
-    )(adjacency, send, swap(send, "rep", 1), keep)
+        spread_kernel,
+        shape((row_count, BLK + 2 * PAD, width), BF16),
+        [VMEM] * 4,
+        (adjacency, send, swap(send, "rep", 1), keep),
+    )
     message = lax.all_to_all(message, "row", 0, 0, tiled=True)
     d_features, share, grad_bias = call(
         finish_kernel,
         (shape((rows, width), F32), shape((PAD, width), BF16), shape((1, width), F32)),
         [VMEM] * 2,
-    )(message, self_term)
+        (message, self_term),
+    )
     share = share[: middle // row_count]
     quarter = lax.all_to_all(
         jnp.broadcast_to(share[None], (row_count,) + share.shape), "row", 0, 0, tiled=True

time: 91.6 us -> 71.4 us (0.78)
  Pallas kernels: 24.1 us -> 9.7 us
  local copies, waits for them, and re-layouts: 5.8 us -> 1.8 us
  waiting for transfers between devices: 11.4 us -> 10.1 us
  blocking collectives: 38.9 us -> 37.6 us
    pallas_call x6, Pallas kernels: 24.1 us -> 9.7 us  [call(): pl.pallas_call(kernel, out_shape=out_shape, in_specs=specs, out_specs=[VM...]
    ppermute x5, waiting for transfers between devices: 11.4 us -> 7.04 us  [swap(): lax.ppermute(value, axis, [(i, i ^ bit) for i in range(lax.axis_size(axis...]
    unnamed x22 -> x20, local copies, waits for them, and re-layouts: 4.26 us -> 0.96 us
    ppermute x3, waiting for transfers between devices: 0.01 us -> 3.01 us  [on_device(): lax.ppermute(pair, 'row', [(i, (i + 2 * s) % row_count) for i in range(ro...]
    all_to_all x1, blocking collectives: 23.1 us -> 21.9 us  [on_device(): message = lax.all_to_all(message, 'row', 0, 0, tiled=True)]
    ppermute x5, starting transfers between devices: 5.13 us -> 6.22 us  [swap(): lax.ppermute(value, axis, [(i, i ^ bit) for i in range(lax.axis_size(axis...]
  transfers between devices with their start and end apart: 8 -> 8, of which waited for: 4 -> 4; matrix products, arithmetic and copies ran while one was open for 1% -> 1% of each run, Pallas kernels for 14% -> 9%
where the time goes in v2:
time: 71.4 us; the launch traced here: 71.2 us
  blocking collectives  37.6 us (53%)
  starting transfers between devices  11.2 us (16%)
  waiting for transfers between devices  10.1 us (14%)
  Pallas kernels  9.7 us (14%)
  local copies, waits for them, and re-layouts  1.8 us (3%)
  between operations  0.76 us (1%)
    all_to_all x1, blocking collectives, on_device(): message = lax.all_to_all(message, 'row', 0, 0, tiled=True)  21.9 us
    all_to_all x1, blocking collectives, on_device(): lax.all_to_all(jnp.broadcast_to(share[None], (row_count,) + share.shape),...  9.95 us
    pallas_call x6, Pallas kernels, call(): pl.pallas_call(kernel, out_shape=out_shape, in_specs=specs, out_specs=[VM...  9.7 us
    ppermute x5, waiting for transfers between devices, swap(): lax.ppermute(value, axis, [(i, i ^ bit) for i in range(lax.axis_size(axis...  7.04 us
    ppermute x5, starting transfers between devices, swap(): lax.ppermute(value, axis, [(i, i ^ bit) for i in range(lax.axis_size(axis...  6.22 us
    all_gather x1, blocking collectives, on_device(): grads = lax.all_gather(quarter, 'rep', axis=0, tiled=True).astype(F32)  5.77 us
    ppermute x3, starting transfers between devices, on_device(): lax.ppermute(pair, 'row', [(i, (i + 2 * s) % row_count) for i in range(ro...  5.02 us
    ppermute x3, waiting for transfers between devices, on_device(): lax.ppermute(pair, 'row', [(i, (i + 2 * s) % row_count) for i in range(ro...  3.01 us
  transfers between devices with their start and end apart: 8, of which 4 were waited for; matrix products, arithmetic and copies ran while one was open for 1% of the time, Pallas kernels for 9%

profile of v2, /device:TPU:0, one launch (start us, length us, event | category | flops | bytes accessed | tf_op | source)
XLA Modules:
  0.0 71.2 jit_solution(11011016669198630733)
XLA Ops:
  0.6 3.0 %collective-permute-start.1 = (bf16[128,256]{1,0:T(8,128)(2,1)}, bf16[128,256]{1,0:T(8,128)(2,1)S(1)}, u32[]{:S(2)}, u32[]{:S(2)}) collective-permute-start(bf16[128,256]{1,0:T(8,128)(2,1)} %param.10), channel_id=1, source_target_pairs={{0,4},{4,0},{8,12},{12,8},{16,20},{20,16},{24,28},{28,24},{1,5},{5... | collective-permute-start | bytes 196616 | tf_op jit(solution)/shard_map/ppermute | solution.py:208
  3.7 0.0 copy-start.8
  3.7 0.0 copy-start.1
  3.7 0.9 %constant_dynamic-update-slice_fusion.1 = bf16[256,256]{1,0:T(8,128)(2,1)S(1)} fusion(bf16[128,256]{1,0:T(8,128)(2,1)} %param.10), kind=kLoop, calls=%fused_computation.1 | loop fusion | bytes 131072
  4.6 0.0 copy-start
  4.6 0.0 copy-done.8
  4.6 0.0 copy-start.5
  4.6 0.0 copy-start.6
  4.6 0.0 copy-start.7
  4.7 1.6 %collective-permute-start = (bf16[256,256]{1,0:T(8,128)(2,1)S(1)}, bf16[256,256]{1,0:T(8,128)(2,1)S(1)}, u32[]{:S(2)}, u32[]{:S(2)}) collective-permute-start(bf16[256,256]{1,0:T(8,128)(2,1)S(1)} %constant_dynamic-update-slice_fusion.own_ref), channel_id=1, source_target_pairs={{0,2},{1,3},{2,0},{3,1},{4,6},{5,7},{6,4},{7,5},{8,10},{9,11},{10,... | collective-permute-start | bytes 393224 | tf_op jit(solution)/shard_map/ppermute | solution.py:208
  6.2 0.0 collective-permute-done.1
  6.2 4.0 %collective-permute-start.4 = (bf16[256,256]{1,0:T(8,128)(2,1)S(1)}, bf16[256,256]{1,0:T(8,128)(2,1)S(1)}, u32[]{:S(2)}, u32[]{:S(2)}) collective-permute-start(bf16[256,256]{1,0:T(8,128)(2,1)S(1)} %constant_dynamic-update-slice_fusion.2.refs_0_), channel_id=1, source_target_pairs={{0,24},{4,28},{8,0},{12,4},{16,8},{20,12},{24,16},{28,20},{1,25},{... | collective-permute-start | bytes 393224 | tf_op jit(solution)/shard_map/ppermute | solution.py:212
  10.2 0.0 collective-permute-start.3
  10.2 1.0 %collective-permute-start.2 = (bf16[256,256]{1,0:T(8,128)(2,1)S(1)}, bf16[256,256]{1,0:T(8,128)(2,1)S(1)}, u32[]{:S(2)}, u32[]{:S(2)}) collective-permute-start(bf16[256,256]{1,0:T(8,128)(2,1)S(1)} %constant_dynamic-update-slice_fusion.2.refs_0_), channel_id=1, source_target_pairs={{0,8},{4,12},{8,16},{12,20},{16,24},{20,28},{24,0},{28,4},{1,9},{5... | collective-permute-start | bytes 393224 | tf_op jit(solution)/shard_map/ppermute | solution.py:212
  11.2 0.0 copy-done.1
  11.2 0.0 copy-done
  11.2 0.0 copy-done.5
  11.3 0.0 copy-done.6
  11.3 0.0 copy-done.7
  11.3 6.7 %shard_map.137.adj_ref = bf16[512,1024]{1,0:T(8,128)(2,1)S(1)} custom-call(s32[256]{0:T(256)S(1)} %copy-done.5, s32[256]{0:T(256)S(1)} %copy-done.6, s32[256]{0:T(256)S(1)} %copy-done.7, s32[256,256]{1,0:T(8,128)S(1)} %copy-done, s32[256,256]{1,0:T(8,128)S(1)} %copy-done.1), custom_call_target="tpu_custom_call" | custom-call | tf_op jit(solution)/shard_map/pallas_call | solution.py:188
  18.0 0.0 collective-permute-done.near_ref
  18.0 0.0 collective-permute-done.4.refs_3_
  18.0 3.0 %collective-permute-done.3.refs_2_ = bf16[256,256]{1,0:T(8,128)(2,1)S(1)} collective-permute-done((bf16[256,256]{1,0:T(8,128)(2,1)S(1)}, bf16[256,256]{1,0:T(8,128)(2,1)S(1)}, u32[]{:S(2)}, u32[]{:S(2)}) %collective-permute-start.3) | collective-permute-done | bytes 131104 | tf_op jit(solution)/shard_map/ppermute | solution.py:212
  21.0 0.0 collective-permute-done.2.refs_1_
  21.0 0.7 shard_map.138
  21.7 0.1 collective-permute-start.5
  21.8 1.3 %collective-permute-done.5.got_ref = bf16[272,256]{1,0:T(8,128)(2,1)S(1)} collective-permute-done((bf16[272,256]{1,0:T(8,128)(2,1)S(1)}, bf16[272,256]{1,0:T(8,128)(2,1)S(1)}, u32[]{:S(2)}, u32[]{:S(2)}) %collective-permute-start.5) | collective-permute-done | bytes 139296 | tf_op jit(solution)/shard_map/ppermute | solution.py:208
  23.2 0.0 copy-start.2
  23.2 0.0 copy-start.3
  23.2 0.0 copy-start.4
  23.2 1.6 %collective-permute-start.6 = (bf16[272,256]{1,0:T(8,128)(2,1)S(1)}, bf16[272,256]{1,0:T(8,128)(2,1)S(1)}, u32[]{:S(2)}, u32[]{:S(2)}) collective-permute-start(bf16[272,256]{1,0:T(8,128)(2,1)S(1)} %shard_map.139.pair_ref), channel_id=1, source_target_pairs={{0,2},{1,3},{2,0},{3,1},{4,6},{5,7},{6,4},{7,5},{8,10},{9,11},{10,... | collective-permute-start | bytes 417800 | tf_op jit(solution)/shard_map/ppermute | solution.py:208
  24.8 4.2 %collective-permute-done.6.got_ref = bf16[272,256]{1,0:T(8,128)(2,1)S(1)} collective-permute-done((bf16[272,256]{1,0:T(8,128)(2,1)S(1)}, bf16[272,256]{1,0:T(8,128)(2,1)S(1)}, u32[]{:S(2)}, u32[]{:S(2)}) %collective-permute-start.6) | collective-permute-done | bytes 139296 | tf_op jit(solution)/shard_map/ppermute | solution.py:208
  29.0 0.0 copy-done.2
  29.0 0.0 copy-done.3
  29.0 0.0 copy-done.4
  29.0 1.0 %shard_map.140 = (bf16[128,256]{1,0:T(8,128)(2,1)}, f32[128,256]{1,0:T(8,128)S(1)}, f32[144,256]{1,0:T(8,128)S(1)}, bf16[400,256]{1,0:T(8,128)(2,1)S(1)}) custom-call(bf16[272,256]{1,0:T(8,128)(2,1)S(1)} %shard_map.139.pair_ref, bf16[272,256]{1,0:T(8,128)(2,1)S(1)} %collective-permute-done.6.got_ref, ...), custom_call_target="tpu_custom_call" | custom-call | tf_op jit(solution)/shard_map/pallas_call | solution.py:188
  30.0 0.0 collective-permute-start.7
  30.0 1.5 %collective-permute-done.7.got_ref = bf16[400,256]{1,0:T(8,128)(2,1)S(1)} collective-permute-done((bf16[400,256]{1,0:T(8,128)(2,1)S(1)}, bf16[400,256]{1,0:T(8,128)(2,1)S(1)}, u32[]{:S(2)}, u32[]{:S(2)}) %collective-permute-start.7) | collective-permute-done | bytes 204832 | tf_op jit(solution)/shard_map/ppermute | solution.py:208
  31.5 0.5 shard_map.141
  32.0 21.9 %all_to_all.10.msg_ref = bf16[8,160,256]{2,1,0:T(8,128)(2,1)S(1)} all-to-all(bf16[8,160,256]{2,1,0:T(8,128)(2,1)S(1)} %shard_map.141), channel_id=1, replica_groups=mesh['row'=8,'rep'=4] {'row'}, dimensions={0} | all-to-all | bytes 1310720 | tf_op jit(solution)/shard_map/all_to_all | solution.py:254
  53.9 0.7 %shard_map.142 = (f32[128,256]{1,0:T(8,128)}, bf16[16,256]{1,0:T(8,128)(2,1)S(1)}, f32[1,256]{1,0:T(1,128)}) custom-call(bf16[8,160,256]{2,1,0:T(8,128)(2,1)S(1)} %all_to_all.10.msg_ref, f32[128,256]{1,0:T(8,128)S(1)} %get-tuple-element.31.self_ref), custom_call_target="tpu_custom_call" | custom-call | tf_op jit(solution)/shard_map/pallas_call | solution.py:188
  54.6 10.0 %all_to_all.11 = bf16[8,16,256]{2,1,0:T(8,128)(2,1)S(1)} all-to-all(bf16[8,16,256]{2,1,0:T(8,128)(2,1)S(1)} %broadcast_in_dim.10), channel_id=1, replica_groups=mesh['row'=8,'rep'=4] {'row'}, dimensions={0} | all-to-all | bytes 131072 | tf_op jit(solution)/shard_map/all_to_all | solution.py:262
  64.6 5.8 %all_gather.3 = bf16[512,256]{1,0:T(8,128)(2,1)S(1)} all-gather(bf16[128,256]{1,0:T(8,128)(2,1)S(1)} %bitcast.4), channel_id=1, replica_groups=mesh['row'=8,'rep'=4] {'rep'}, dimensions={0}, use_global_device_ids=true | all-gather | bytes 327680 | tf_op jit(solution)/shard_map/all_gather | solution.py:265
  70.4 0.8 %fusion = (f32[256,256]{1,0:T(8,128)}, f32[256,256]{1,0:T(8,128)}) fusion(bf16[512,256]{1,0:T(8,128)(2,1)S(1)} %all_gather.3), kind=kLoop, calls=%fused_computation.4 | loop fusion | bytes 1048576 | tf_op jit(solution)/shard_map/slice | solution.py:266
  (5 shorter events, 0.1 us)
Async XLA Ops:
  0.6 5.6 %collective-permute-start.1 = (bf16[128,256]{1,0:T(8,128)(2,1)}, bf16[128,256]{1,0:T(8,128)(2,1)S(1)}, u32[]{:S(2)}, u32[]{:S(2)}) collective-permute-start(bf16[128,256]{1,0:T(8,128)(2,1)} %param.10), channel_id=1, source_target_pairs={{0,4},{4,0},{8,12},{12,8},{16,20},{20,16},{24,28},{28,24},{1,5},{5... | collective-permute-start | bytes 196616 | tf_op jit(solution)/shard_map/ppermute | solution.py:208
  3.7 0.9 %copy-start.8 = (bf16[128,256]{1,0:T(8,128)(2,1)S(1)}, bf16[128,256]{1,0:T(8,128)(2,1)}, u32[]{:S(2)}) copy-start(bf16[128,256]{1,0:T(8,128)(2,1)} %param.14) | copy-start | bytes 196612
  3.7 7.6 %copy-start.1 = (s32[256,256]{1,0:T(8,128)S(1)}, s32[256,256]{1,0:T(8,128)}, u32[]{:S(2)}) copy-start(s32[256,256]{1,0:T(8,128)} %dst_ref.1) | copy-start | bytes 786436
  4.6 6.7 %copy-start = (s32[256,256]{1,0:T(8,128)S(1)}, s32[256,256]{1,0:T(8,128)}, u32[]{:S(2)}) copy-start(s32[256,256]{1,0:T(8,128)} %src_ref.1) | copy-start | bytes 786436
  4.6 6.6 %copy-start.5 = (s32[256]{0:T(256)S(1)}, s32[256]{0:T(256)}, u32[]{:S(2)}) copy-start(s32[256]{0:T(256)} %row_ref.1) | copy-start | bytes 3076
  4.6 6.6 %copy-start.6 = (s32[256]{0:T(256)S(1)}, s32[256]{0:T(256)}, u32[]{:S(2)}) copy-start(s32[256]{0:T(256)} %col_ref.1) | copy-start | bytes 3076
  4.6 6.6 %copy-start.7 = (s32[256]{0:T(256)S(1)}, s32[256]{0:T(256)}, u32[]{:S(2)}) copy-start(s32[256]{0:T(256)} %count_ref.1) | copy-start | bytes 3076
  4.7 13.3 %collective-permute-start = (bf16[256,256]{1,0:T(8,128)(2,1)S(1)}, bf16[256,256]{1,0:T(8,128)(2,1)S(1)}, u32[]{:S(2)}, u32[]{:S(2)}) collective-permute-start(bf16[256,256]{1,0:T(8,128)(2,1)S(1)} %constant_dynamic-update-slice_fusion.own_ref), channel_id=1, source_target_pairs={{0,2},{1,3},{2,0},{3,1},{4,6},{5,7},{6,4},{7,5},{8,10},{9,11},{10,... | collective-permute-start | bytes 393224 | tf_op jit(solution)/shard_map/ppermute | solution.py:208
  6.2 11.8 %collective-permute-start.4 = (bf16[256,256]{1,0:T(8,128)(2,1)S(1)}, bf16[256,256]{1,0:T(8,128)(2,1)S(1)}, u32[]{:S(2)}, u32[]{:S(2)}) collective-permute-start(bf16[256,256]{1,0:T(8,128)(2,1)S(1)} %constant_dynamic-update-slice_fusion.2.refs_0_), channel_id=1, source_target_pairs={{0,24},{4,28},{8,0},{12,4},{16,8},{20,12},{24,16},{28,20},{1,25},{... | collective-permute-start | bytes 393224 | tf_op jit(solution)/shard_map/ppermute | solution.py:212
  10.2 10.8 %collective-permute-start.3 = (bf16[256,256]{1,0:T(8,128)(2,1)S(1)}, bf16[256,256]{1,0:T(8,128)(2,1)S(1)}, u32[]{:S(2)}, u32[]{:S(2)}) collective-permute-start(bf16[256,256]{1,0:T(8,128)(2,1)S(1)} %constant_dynamic-update-slice_fusion.2.refs_0_), channel_id=1, source_target_pairs={{0,16},{4,20},{8,24},{12,28},{16,0},{20,4},{24,8},{28,12},{1,17},{... | collective-permute-start | bytes 393224 | tf_op jit(solution)/shard_map/ppermute | solution.py:212
  10.2 10.8 %collective-permute-start.2 = (bf16[256,256]{1,0:T(8,128)(2,1)S(1)}, bf16[256,256]{1,0:T(8,128)(2,1)S(1)}, u32[]{:S(2)}, u32[]{:S(2)}) collective-permute-start(bf16[256,256]{1,0:T(8,128)(2,1)S(1)} %constant_dynamic-update-slice_fusion.2.refs_0_), channel_id=1, source_target_pairs={{0,8},{4,12},{8,16},{12,20},{16,24},{20,28},{24,0},{28,4},{1,9},{5... | collective-permute-start | bytes 393224 | tf_op jit(solution)/shard_map/ppermute | solution.py:212
  21.7 1.4 %collective-permute-start.5 = (bf16[272,256]{1,0:T(8,128)(2,1)S(1)}, bf16[272,256]{1,0:T(8,128)(2,1)S(1)}, u32[]{:S(2)}, u32[]{:S(2)}) collective-permute-start(bf16[272,256]{1,0:T(8,128)(2,1)S(1)} %get-tuple-element.26), channel_id=1, source_target_pairs={{0,1},{1,0},{2,3},{3,2},{4,5},{5,4},{6,7},{7,6},{8,9},{9,8},{10,11... | collective-permute-start | bytes 417800 | tf_op jit(solution)/shard_map/ppermute | solution.py:208
  23.2 5.8 %copy-start.2 = (bf16[256,256]{1,0:T(8,128)(2,1)S(1)}, bf16[256,256]{1,0:T(8,128)(2,1)}, u32[]{:S(2)}) copy-start(bf16[256,256]{1,0:T(8,128)(2,1)} %w_self_ref.1) | copy-start | bytes 393220
  23.2 5.8 %copy-start.3 = (bf16[256,256]{1,0:T(8,128)(2,1)S(1)}, bf16[256,256]{1,0:T(8,128)(2,1)}, u32[]{:S(2)}) copy-start(bf16[256,256]{1,0:T(8,128)(2,1)} %w_neigh_ref.1) | copy-start | bytes 393220
  23.2 5.8 %copy-start.4 = (f32[256]{0:T(256)S(1)}, f32[256]{0:T(256)}, u32[]{:S(2)}) copy-start(f32[256]{0:T(256)} %param.13) | copy-start | bytes 3076
  23.2 5.8 %collective-permute-start.6 = (bf16[272,256]{1,0:T(8,128)(2,1)S(1)}, bf16[272,256]{1,0:T(8,128)(2,1)S(1)}, u32[]{:S(2)}, u32[]{:S(2)}) collective-permute-start(bf16[272,256]{1,0:T(8,128)(2,1)S(1)} %shard_map.139.pair_ref), channel_id=1, source_target_pairs={{0,2},{1,3},{2,0},{3,1},{4,6},{5,7},{6,4},{7,5},{8,10},{9,11},{10,... | collective-permute-start | bytes 417800 | tf_op jit(solution)/shard_map/ppermute | solution.py:208
  30.0 1.5 %collective-permute-start.7 = (bf16[400,256]{1,0:T(8,128)(2,1)S(1)}, bf16[400,256]{1,0:T(8,128)(2,1)S(1)}, u32[]{:S(2)}, u32[]{:S(2)}) collective-permute-start(bf16[400,256]{1,0:T(8,128)(2,1)S(1)} %get-tuple-element.29.sent_ref), channel_id=1, source_target_pairs={{0,1},{1,0},{2,3},{3,2},{4,5},{5,4},{6,7},{7,6},{8,9},{9,8},{10,11... | collective-permute-start | bytes 614408 | tf_op jit(solution)/shard_map/ppermute | solution.py:208

commit v3 on v2

--- a/solution.py
+++ b/solution.py
@@ -26,15 +26,14 @@
 
 
 def col_place(block, row_count):
-    me = lax.axis_index("row")
-    half = row_count // 2
-    return 2 * lax.rem((me >> 1) - (block >> 1) + half, half) + ((block ^ me) & 1)
-
-
-def col_block(place, row_count):
-    me = lax.axis_index("row")
-    half = row_count // 2
-    return 2 * lax.rem((me >> 1) - place // 2 + half, half) + ((me & 1) ^ (place & 1))
+    away = block ^ lax.axis_index("row")
+    return (away & 3) * (row_count // 4) + (away >> 2)
+
+
+def tree(values):
+    while len(values) > 1:
+        values = [values[i] + values[i + 1] for i in range(0, len(values), 2)]
+    return values[0]
 
 
 def split(value):
@@ -48,16 +47,15 @@
     return rows[0:1] + rows[1:2]
 
 
-def build_kernel(row_ref, col_ref, count_ref, src_ref, dst_ref, adj_ref, acc_ref):
-    tiles, slots = src_ref.shape
-    row_blocks, col_blocks = acc_ref.shape[:2]
-    acc_ref[...] = jnp.zeros_like(acc_ref)
+def add_tiles(first, last, row_ref, col_ref, count_ref, src_ref, dst_ref, acc_ref):
+    slots = src_ref.shape[1]
+    col_blocks = acc_ref.shape[1]
     line = lax.broadcasted_iota(jnp.int32, (BLK, slots), 0).astype(BF16)
     slot = lax.broadcasted_iota(jnp.int32, (1, slots), 1)
     one, zero = jnp.ones((), BF16), jnp.zeros((), BF16)
 
     def step(i, carry):
-        base = pl.multiple_of(i * UNROLL, UNROLL)
+        base = pl.multiple_of(first + i * UNROLL, UNROLL)
         dst, src = dst_ref[pl.ds(base, UNROLL), :], src_ref[pl.ds(base, UNROLL), :]
         for u in range(UNROLL):
             tile = base + u
@@ -70,7 +68,20 @@
             acc_ref[row_place(row_ref[tile]), col_place(col_ref[tile], col_blocks)] += part
         return carry
 
-    lax.fori_loop(0, tiles // UNROLL, step, 0)
+    lax.fori_loop(0, (last - first) // UNROLL, step, 0)
+
+
+def first_build_kernel(row_ref, col_ref, count_ref, src_ref, dst_ref, acc_ref):
+    acc_ref[...] = jnp.zeros_like(acc_ref)
+    tiles = src_ref.shape[0]
+    add_tiles(0, tiles // 2, row_ref, col_ref, count_ref, src_ref, dst_ref, acc_ref)
+
+
+def last_build_kernel(row_ref, col_ref, count_ref, src_ref, dst_ref, half_ref, adj_ref, acc_ref):
+    acc_ref[...] = half_ref[...]
+    tiles = src_ref.shape[0]
+    add_tiles(tiles // 2, tiles, row_ref, col_ref, count_ref, src_ref, dst_ref, acc_ref)
+    row_blocks, col_blocks = acc_ref.shape[:2]
     for g in range(row_blocks):
         for c in range(col_blocks):
             adj_ref[g * BLK : (g + 1) * BLK, c * BLK : (c + 1) * BLK] = acc_ref[g, c].astype(BF16)
@@ -142,44 +153,56 @@
     grads = lax.dot_general(terms, d_pre, (((0,), (0,)), ((), ())), preferred_element_type=F32)
     middle = width // 2
     low = me & 1 == 0
-    bias_term = jnp.sum(d_pre.astype(F32), axis=0, keepdims=True)
+    bias_term = jnp.sum(d_pre[:rows].astype(F32), axis=0, keepdims=True) + jnp.sum(
+        d_pre[rows:].astype(F32), axis=0, keepdims=True
+    )
     keep_ref[:middle] = jnp.where(low, grads[:middle], grads[middle:])
-    keep_ref[middle:] = jnp.broadcast_to(bias_term, (PAD, width))
+    keep_ref[middle:] = split(bias_term).astype(F32)
     send_ref[half : half + middle] = jnp.where(low, grads[middle:], grads[:middle]).astype(BF16)
     send_ref[half + middle :] = split(bias_term)
 
 
-def spread_kernel(adj_ref, sent_ref, got_ref, keep_ref, msg_ref):
-    row_count = msg_ref.shape[0]
+def spread_kernel(adj_ref, sent_ref, got_ref, terms_ref, keep_ref, *msg_refs):
     half = adj_ref.shape[0] // 2
-    middle = keep_ref.shape[0] - PAD
-    share = middle // row_count
+    middle = terms_ref.shape[0] - PAD
+    size = adj_ref.shape[1] // 4
     g = jnp.concatenate([sent_ref[:half], got_ref[:half]], axis=0)
-    grads = keep_ref[:middle] + got_ref[half : half + middle].astype(F32)
-    bias_rows = split(keep_ref[middle : middle + 1] + joined(got_ref[half + middle :]))
-    for place in range(row_count):
-        block = lax.dot_general(
-            adj_ref[:, place * BLK : (place + 1) * BLK],
+    grads = (terms_ref[:middle] + got_ref[half : half + middle].astype(F32)).astype(BF16)
+    bias_rows = split(joined(terms_ref[middle:]) + joined(got_ref[half + middle :]))
+    for m, ref in enumerate([keep_ref, *msg_refs]):
+        blocks = lax.dot_general(
+            adj_ref[:, m * size : (m + 1) * size],
             g,
             (((0,), (0,)), ((), ())),
             preferred_element_type=F32,
         )
-        msg_ref[col_block(place, row_count), :BLK] = block.astype(BF16)
-    for k in range(row_count):
-        msg_ref[k, BLK : BLK + share] = grads[k * share : (k + 1) * share].astype(BF16)
-        if share < PAD:
-            msg_ref[k, BLK + share : BLK + PAD] = jnp.zeros((PAD - share, grads.shape[1]), BF16)
-        msg_ref[k, BLK + PAD :] = bias_rows
-
-
-def finish_kernel(msg_ref, self_ref, d_features_ref, share_ref, bias_ref):
-    row_count = msg_ref.shape[0]
-    total = msg_ref[0].astype(F32)
-    for k in range(1, row_count):
-        total = total + msg_ref[k].astype(F32)
-    d_features_ref[...] = self_ref[...] + total[:BLK]
-    share_ref[...] = total[BLK : BLK + PAD].astype(BF16)
-    bias_ref[...] = total[BLK + PAD : BLK + PAD + 1] + total[BLK + PAD + 1 : BLK + PAD + 2]
+        ref[:size] = blocks.astype(ref.dtype)
+        ref[size : size + middle] = grads.astype(ref.dtype)
+        ref[size + middle :] = bias_rows.astype(ref.dtype)
+
+
+def near_sum_kernel(keep_ref, *refs):
+    *got_refs, own_ref = refs[:4]
+    msg_refs = refs[4:]
+    size = (1 + len(msg_refs)) * BLK
+    middle = keep_ref.shape[0] - size - PAD
+    terms = [keep_ref, *got_refs]
+    blocks = tree([ref[:size].astype(F32) for ref in terms])
+    grads = tree([ref[size : size + middle].astype(F32) for ref in terms]).astype(BF16)
+    bias_rows = split(tree([joined(ref[size + middle :]) for ref in terms]))
+    for h, ref in enumerate([own_ref, *msg_refs]):
+        ref[:BLK] = blocks[h * BLK : (h + 1) * BLK].astype(ref.dtype)
+        ref[BLK : BLK + middle] = grads.astype(ref.dtype)
+        ref[BLK + middle :] = bias_rows.astype(ref.dtype)
+
+
+def finish_kernel(self_ref, own_ref, *refs):
+    *got_refs, d_features_ref, quarter_ref, bias_ref = refs
+    middle = own_ref.shape[0] - BLK - PAD
+    terms = [own_ref, *got_refs]
+    d_features_ref[...] = self_ref[...] + tree([ref[:BLK].astype(F32) for ref in terms])
+    quarter_ref[...] = tree([ref[BLK : BLK + middle].astype(F32) for ref in terms]).astype(BF16)
+    bias_ref[...] = tree([joined(ref[BLK + middle :]) for ref in terms])
 
 
 def call(kernel, out_shape, specs, args, scratch=()):
@@ -202,24 +225,28 @@
     row_count, rep_count = lax.axis_size("row"), lax.axis_size("rep")
     group, columns = rep_count * rows, row_count * rows
     half, middle = group // 2, width // 2
+    far = row_count // 4
     shape = jax.ShapeDtypeStruct
 
-    def swap(value, axis, bit):
-        return lax.ppermute(value, axis, [(i, i ^ bit) for i in range(lax.axis_size(axis))])
-
-    pair = jnp.concatenate([features, swap(features, "row", 1)], axis=0)
-    pieces = [pair] + [
-        lax.ppermute(pair, "row", [(i, (i + 2 * s) % row_count) for i in range(row_count)])
-        for s in range(1, row_count // 2)
-    ]
+    def swap(value, axis, bits):
+        return lax.ppermute(value, axis, [(i, i ^ bits) for i in range(lax.axis_size(axis))])
+
+    far_pieces = [swap(features, "row", 4 * h) for h in range(1, far)]
     own = jnp.concatenate([features, d_out], axis=0)
     near = swap(own, "rep", 2)
+    tiles = (tile_row, tile_col, tile_count, edge_src, edge_dst)
+    tile_specs = [SMEM, SMEM, SMEM, VMEM, VMEM]
+    acc_shape = (rep_count, row_count, BLK, BLK)
+    acc = call(first_build_kernel, shape(acc_shape, F32), tile_specs, tiles)
+    acc, far_pieces = lax.optimization_barrier((acc, far_pieces))
+    line = jnp.concatenate([features, *far_pieces], axis=0)
+    pieces = [line] + [swap(line, "row", m) for m in range(1, 4)]
     adjacency = call(
-        build_kernel,
+        last_build_kernel,
         shape((group, columns), BF16),
-        [SMEM, SMEM, SMEM, VMEM, VMEM],
-        (tile_row, tile_col, tile_count, edge_src, edge_dst),
-        [pltpu.VMEM((rep_count, row_count, BLK, BLK), F32)],
+        tile_specs + [VMEM],
+        (*tiles, acc),
+        [pltpu.VMEM(acc_shape, F32)],
     )
     adjacency, near, pieces = lax.optimization_barrier((adjacency, near, pieces))
     keep, send = call(
@@ -245,23 +272,27 @@
         [VMEM] * 7,
         (pair_sum, swap(pair_sum, "rep", 2), own, near, w_self, w_neigh, bias[None, :]),
     )
-    message = call(
+    terms = middle + PAD
+    keep, *near_msgs = call(
         spread_kernel,
-        shape((row_count, BLK + 2 * PAD, width), BF16),
+        (shape((far * BLK + terms, width), F32),) + (shape((far * BLK + terms, width), BF16),) * 3,
         [VMEM] * 4,
         (adjacency, send, swap(send, "rep", 1), keep),
     )
-    message = lax.all_to_all(message, "row", 0, 0, tiled=True)
-    d_features, share, grad_bias = call(
+    got = [swap(msg, "row", m + 1) for m, msg in enumerate(near_msgs)]
+    keep, *far_msgs = call(
+        near_sum_kernel,
+        (shape((BLK + terms, width), F32),) + (shape((BLK + terms, width), BF16),) * (far - 1),
+        [VMEM] * 4,
+        (keep, *got),
+    )
+    got = [swap(msg, "row", 4 * (h + 1)) for h, msg in enumerate(far_msgs)]
+    d_features, quarter, grad_bias = call(
         finish_kernel,
-        (shape((rows, width), F32), shape((PAD, width), BF16), shape((1, width), F32)),
-        [VMEM] * 2,
-        (message, self_term),
-    )
-    share = share[: middle // row_count]
-    quarter = lax.all_to_all(
-        jnp.broadcast_to(share[None], (row_count,) + share.shape), "row", 0, 0, tiled=True
-    ).reshape(middle, width)
+        (shape((rows, width), F32), shape((middle, width), BF16), shape((1, width), F32)),
+        [VMEM] * (2 + len(got)),
+        (self_term, keep, *got),
+    )
     grads = lax.all_gather(quarter, "rep", axis=0, tiled=True).astype(F32)
     return (out, d_features, grads[:width], grads[width:], grad_bias[0])
 

time: 71.4 us -> 64.9 us (0.909)
  blocking collectives: 37.6 us -> 5.77 us
  waiting for transfers between devices: 10.1 us -> 27.2 us
  local copies, waits for them, and re-layouts: 1.8 us -> 6.54 us
  starting transfers between devices: 11.2 us -> 13.8 us
  Pallas kernels: 9.7 us -> 10.5 us
    all_to_all x2 -> x0, blocking collectives: 31.9 us -> none  [the longest x1 21.9 us: on_device(): message = lax.all_to_all(message, 'row', 0, 0, tiled=True)]
    ppermute x8 -> x12, waiting for transfers between devices: 10.1 us -> 27.2 us  [swap(): lax.ppermute(value, axis, [(i, i ^ bits) for i in range(lax.axis_size(axi...]
    unnamed x20 -> x26, local copies, waits for them, and re-layouts: 0.96 us -> 4.87 us
    ppermute x8 -> x12, starting transfers between devices: 11.2 us -> 13.8 us  [swap(): lax.ppermute(value, axis, [(i, i ^ bits) for i in range(lax.axis_size(axi...]
    concatenate x1, local copies, waits for them, and re-layouts: 0.01 us -> 0.85 us  [on_device(): own = jnp.concatenate([features, d_out], axis=0)]
    pallas_call x6 -> x8, Pallas kernels: 9.7 us -> 10.5 us  [call(): pl.pallas_call(kernel, out_shape=out_shape, in_specs=specs, out_specs=[VM...]
  transfers between devices with their start and end apart: 8 -> 12, of which waited for: 4 -> 8; matrix products, arithmetic and copies ran while one was open for 1% -> 3% of each run, Pallas kernels for 9% -> 12%
where the time goes in v3:
time: 64.9 us; the launch traced here: 64.5 us
  waiting for transfers between devices  27.2 us (42%)
  starting transfers between devices  13.8 us (21%)
  Pallas kernels  10.5 us (16%)
  local copies, waits for them, and re-layouts  6.54 us (10%)
  blocking collectives  5.77 us (9%)
  between operations  0.8 us (1%)
    ppermute x12, waiting for transfers between devices, swap(): lax.ppermute(value, axis, [(i, i ^ bits) for i in range(lax.axis_size(axi...  27.2 us
    ppermute x12, starting transfers between devices, swap(): lax.ppermute(value, axis, [(i, i ^ bits) for i in range(lax.axis_size(axi...  13.8 us
    pallas_call x8, Pallas kernels, call(): pl.pallas_call(kernel, out_shape=out_shape, in_specs=specs, out_specs=[VM...  10.5 us
    all_gather x1, blocking collectives, on_device(): grads = lax.all_gather(quarter, 'rep', axis=0, tiled=True).astype(F32)  5.77 us
    unnamed x26, local copies, waits for them, and re-layouts  4.87 us
  transfers between devices with their start and end apart: 12, of which 8 were waited for; matrix products, arithmetic and copies ran while one was open for 3% of the time, Pallas kernels for 12%

profile of v3, /device:TPU:0, one launch (start us, length us, event | category | flops | bytes accessed | tf_op | source)
XLA Modules:
  0.0 64.5 jit_solution(9986644203719945724)
XLA Ops:
  0.6 0.0 copy-start.6
  0.6 0.0 copy-start.8
  0.7 0.0 copy-start.10
  0.7 0.0 copy-start.1
  0.7 4.1 %collective-permute-start = (bf16[128,256]{1,0:T(8,128)(2,1)}, bf16[128,256]{1,0:T(8,128)(2,1)S(1)}, u32[]{:S(2)}, u32[]{:S(2)}) collective-permute-start(bf16[128,256]{1,0:T(8,128)(2,1)} %param.10), channel_id=1, source_target_pairs={{0,16},{4,20},{8,24},{12,28},{16,0},{20,4},{24,8},{28,12},{1,17},{... | collective-permute-start | bytes 196616 | tf_op jit(solution)/shard_map/ppermute | solution.py:232
  4.8 0.9 %constant_dynamic-update-slice_fusion.1 = bf16[256,256]{1,0:T(8,128)(2,1)S(1)} fusion(bf16[128,256]{1,0:T(8,128)(2,1)} %param.10), kind=kLoop, calls=%fused_computation.1 | loop fusion | bytes 131072
  5.7 0.8 %constant_dynamic-update-slice_fusion.own_ref = bf16[256,256]{1,0:T(8,128)(2,1)S(1)} fusion(bf16[256,256]{1,0:T(8,128)(2,1)S(1)} %constant_dynamic-update-slice_fusion.1, bf16[128,256]{1,0:T(8,128)(2,1)} %param.14), kind=kLoop, calls=%fused_computation | loop fusion | bytes 131072 | tf_op jit(solution)/shard_map/concatenate | solution.py:235
  6.5 1.5 %collective-permute-start.1 = (bf16[256,256]{1,0:T(8,128)(2,1)S(1)}, bf16[256,256]{1,0:T(8,128)(2,1)S(1)}, u32[]{:S(2)}, u32[]{:S(2)}) collective-permute-start(bf16[256,256]{1,0:T(8,128)(2,1)S(1)} %constant_dynamic-update-slice_fusion.own_ref), channel_id=1, source_target_pairs={{0,2},{1,3},{2,0},{3,1},{4,6},{5,7},{6,4},{7,5},{8,10},{9,11},{10,... | collective-permute-start | bytes 393224 | tf_op jit(solution)/shard_map/ppermute | solution.py:232
  8.0 0.0 copy-start
  8.0 0.9 %copy-done = s32[256,256]{1,0:T(8,128)S(1)} copy-done((s32[256,256]{1,0:T(8,128)S(1)}, s32[256,256]{1,0:T(8,128)}, u32[]{:S(2)}) %copy-start) | copy-done | bytes 262168
  9.0 0.0 copy-start.2
  9.0 0.9 %copy-done.2 = s32[256,256]{1,0:T(8,128)S(1)} copy-done((s32[256,256]{1,0:T(8,128)S(1)}, s32[256,256]{1,0:T(8,128)}, u32[]{:S(2)}) %copy-start.2) | copy-done | bytes 262168
  9.9 0.0 copy-start.5
  9.9 0.7 %copy-done.5 = s32[256]{0:T(256)S(1)} copy-done((s32[256]{0:T(256)S(1)}, s32[256]{0:T(256)}, u32[]{:S(2)}) %copy-start.5) | copy-done | bytes 1048
  10.6 0.0 copy-start.7
  10.6 0.7 %copy-done.7 = s32[256]{0:T(256)S(1)} copy-done((s32[256]{0:T(256)S(1)}, s32[256]{0:T(256)}, u32[]{:S(2)}) %copy-start.7) | copy-done | bytes 1048
  11.3 0.0 copy-start.9
  11.3 0.7 %copy-done.9 = s32[256]{0:T(256)S(1)} copy-done((s32[256]{0:T(256)S(1)}, s32[256]{0:T(256)}, u32[]{:S(2)}) %copy-start.9) | copy-done | bytes 1048
  11.9 3.6 %shard_map.137.half_ref = f32[4,8,128,128]{3,2,1,0:T(8,128)S(1)} custom-call(s32[256]{0:T(256)S(1)} %copy-done.5, s32[256]{0:T(256)S(1)} %copy-done.7, s32[256]{0:T(256)S(1)} %copy-done.9, s32[256,256]{1,0:T(8,128)S(1)} %copy-done, s32[256,256]{1,0:T(8,128)S(1)} %copy-done.2), custom_call_target="tpu_custom_call" | custom-call | tf_op jit(solution)/shard_map/pallas_call | solution.py:211
  15.6 0.0 collective-permute-done
  15.6 0.0 copy-start.3
  15.6 0.0 copy-start.4
  15.6 0.0 copy-start.11
  15.6 1.6 %collective-permute-start.2 = (bf16[256,256]{1,0:T(8,128)(2,1)S(1)}, bf16[256,256]{1,0:T(8,128)(2,1)S(1)}, u32[]{:S(2)}, u32[]{:S(2)}) collective-permute-start(bf16[256,256]{1,0:T(8,128)(2,1)S(1)} %constant_dynamic-update-slice_fusion.2.refs_0_), channel_id=1, source_target_pairs={{0,4},{4,0},{8,12},{12,8},{16,20},{20,16},{24,28},{28,24},{1,5},{5... | collective-permute-start | bytes 393224 | tf_op jit(solution)/shard_map/ppermute | solution.py:232
  17.2 1.6 %collective-permute-start.3 = (bf16[256,256]{1,0:T(8,128)(2,1)S(1)}, bf16[256,256]{1,0:T(8,128)(2,1)S(1)}, u32[]{:S(2)}, u32[]{:S(2)}) collective-permute-start(bf16[256,256]{1,0:T(8,128)(2,1)S(1)} %constant_dynamic-update-slice_fusion.2.refs_0_), channel_id=1, source_target_pairs={{0,8},{4,12},{8,0},{12,4},{16,24},{20,28},{24,16},{28,20},{1,9},{5... | collective-permute-start | bytes 393224 | tf_op jit(solution)/shard_map/ppermute | solution.py:232
  18.8 0.4 collective-permute-start.4
  19.2 0.0 copy-done.6
  19.2 0.0 copy-done.8
  19.2 0.0 copy-done.10
  19.2 0.0 copy-done.1
  19.2 3.8 %shard_map.138.adj_ref = bf16[512,1024]{1,0:T(8,128)(2,1)S(1)} custom-call(s32[256]{0:T(256)S(1)} %copy-done.6, s32[256]{0:T(256)S(1)} %copy-done.8, s32[256]{0:T(256)S(1)} %copy-done.10, s32[256,256]{1,0:T(8,128)S(1)} %copy-done.1, s32[256,256]{1,0:T(8,128)S(1)} %copy-done.2, f32[4,8,128,128]{3,2,1,0:T(8,128)S(1)} %shard_map.137.half_ref), custom_call_target="tpu_custom_call" | custom-call | tf_op jit(solution)/shard_map/pallas_call | solution.py:211
  23.0 0.0 collective-permute-done.1.near_ref
  23.0 0.0 collective-permute-done.2.refs_1_
  23.0 0.0 collective-permute-done.3.refs_2_
  23.1 1.9 %collective-permute-done.4.refs_3_ = bf16[256,256]{1,0:T(8,128)(2,1)S(1)} collective-permute-done((bf16[256,256]{1,0:T(8,128)(2,1)S(1)}, bf16[256,256]{1,0:T(8,128)(2,1)S(1)}, u32[]{:S(2)}, u32[]{:S(2)}) %collective-permute-start.4) | collective-permute-done | bytes 131104 | tf_op jit(solution)/shard_map/ppermute | solution.py:232
  24.9 0.7 %shard_map.139 = (f32[272,256]{1,0:T(8,128)S(1)}, bf16[272,256]{1,0:T(8,128)(2,1)S(1)}) custom-call(bf16[512,1024]{1,0:T(8,128)(2,1)S(1)} %shard_map.138.adj_ref, bf16[256,256]{1,0:T(8,128)(2,1)S(1)} %constant_dynamic-update-slice_fusion.2.refs_0_, bf16[256,256]{1,0:T(8,128)(2,1)S(1)} %collective-permute-done.2.refs_1_, ...), custom_call_target="tpu_custom_call" | custom-call | tf_op jit(solution)/shard_map/pallas_call | solution.py:211
  25.6 0.1 collective-permute-start.5
  25.7 1.3 %collective-permute-done.5.got_ref = bf16[272,256]{1,0:T(8,128)(2,1)S(1)} collective-permute-done((bf16[272,256]{1,0:T(8,128)(2,1)S(1)}, bf16[272,256]{1,0:T(8,128)(2,1)S(1)}, u32[]{:S(2)}, u32[]{:S(2)}) %collective-permute-start.5) | collective-permute-done | bytes 139296 | tf_op jit(solution)/shard_map/ppermute | solution.py:232
  27.1 0.6 collective-permute-start.6
  27.7 5.2 %collective-permute-done.6.got_ref = bf16[272,256]{1,0:T(8,128)(2,1)S(1)} collective-permute-done((bf16[272,256]{1,0:T(8,128)(2,1)S(1)}, bf16[272,256]{1,0:T(8,128)(2,1)S(1)}, u32[]{:S(2)}, u32[]{:S(2)}) %collective-permute-start.6) | collective-permute-done | bytes 139296 | tf_op jit(solution)/shard_map/ppermute | solution.py:232
  32.9 0.0 copy-done.3
  32.9 0.0 copy-done.4
  32.9 0.0 copy-done.11
  32.9 1.0 %shard_map.141 = (bf16[128,256]{1,0:T(8,128)(2,1)}, f32[128,256]{1,0:T(8,128)S(1)}, f32[144,256]{1,0:T(8,128)S(1)}, bf16[400,256]{1,0:T(8,128)(2,1)S(1)}) custom-call(bf16[272,256]{1,0:T(8,128)(2,1)S(1)} %shard_map.140.pair_ref, bf16[272,256]{1,0:T(8,128)(2,1)S(1)} %collective-permute-done.6.got_ref, ...), custom_call_target="tpu_custom_call" | custom-call | tf_op jit(solution)/shard_map/pallas_call | solution.py:211
  33.9 0.0 collective-permute-start.7
  33.9 1.5 %collective-permute-done.7.got_ref = bf16[400,256]{1,0:T(8,128)(2,1)S(1)} collective-permute-done((bf16[400,256]{1,0:T(8,128)(2,1)S(1)}, bf16[400,256]{1,0:T(8,128)(2,1)S(1)}, u32[]{:S(2)}, u32[]{:S(2)}) %collective-permute-start.7) | collective-permute-done | bytes 204832 | tf_op jit(solution)/shard_map/ppermute | solution.py:232
  35.4 0.5 shard_map.142
  35.9 1.0 %collective-permute-start.8 = (bf16[400,256]{1,0:T(8,128)(2,1)S(1)}, bf16[400,256]{1,0:T(8,128)(2,1)S(1)}, u32[]{:S(2)}, u32[]{:S(2)}) collective-permute-start(bf16[400,256]{1,0:T(8,128)(2,1)S(1)} %get-tuple-element.43), channel_id=1, source_target_pairs={{0,4},{4,0},{8,12},{12,8},{16,20},{20,16},{24,28},{28,24},{1,5},{5... | collective-permute-start | bytes 614408 | tf_op jit(solution)/shard_map/ppermute | solution.py:232
  36.9 1.6 %collective-permute-start.9 = (bf16[400,256]{1,0:T(8,128)(2,1)S(1)}, bf16[400,256]{1,0:T(8,128)(2,1)S(1)}, u32[]{:S(2)}, u32[]{:S(2)}) collective-permute-start(bf16[400,256]{1,0:T(8,128)(2,1)S(1)} %get-tuple-element.44), channel_id=1, source_target_pairs={{0,8},{4,12},{8,0},{12,4},{16,24},{20,28},{24,16},{28,20},{1,9},{5... | collective-permute-start | bytes 614408 | tf_op jit(solution)/shard_map/ppermute | solution.py:232
  38.5 1.0 %collective-permute-start.10 = (bf16[400,256]{1,0:T(8,128)(2,1)S(1)}, bf16[400,256]{1,0:T(8,128)(2,1)S(1)}, u32[]{:S(2)}, u32[]{:S(2)}) collective-permute-start(bf16[400,256]{1,0:T(8,128)(2,1)S(1)} %get-tuple-element.45), channel_id=1, source_target_pairs={{0,12},{4,8},{8,4},{12,0},{16,28},{20,24},{24,20},{28,16},{1,13},{... | collective-permute-start | bytes 614408 | tf_op jit(solution)/shard_map/ppermute | solution.py:232
  39.4 3.6 %collective-permute-done.8.refs_0_ = bf16[400,256]{1,0:T(8,128)(2,1)S(1)} collective-permute-done((bf16[400,256]{1,0:T(8,128)(2,1)S(1)}, bf16[400,256]{1,0:T(8,128)(2,1)S(1)}, u32[]{:S(2)}, u32[]{:S(2)}) %collective-permute-start.8) | collective-permute-done | bytes 204832 | tf_op jit(solution)/shard_map/ppermute | solution.py:232
  43.1 1.8 %collective-permute-done.9.refs_1_ = bf16[400,256]{1,0:T(8,128)(2,1)S(1)} collective-permute-done((bf16[400,256]{1,0:T(8,128)(2,1)S(1)}, bf16[400,256]{1,0:T(8,128)(2,1)S(1)}, u32[]{:S(2)}, u32[]{:S(2)}) %collective-permute-start.9) | collective-permute-done | bytes 204832 | tf_op jit(solution)/shard_map/ppermute | solution.py:232
  44.9 3.8 %collective-permute-done.10.refs_2_ = bf16[400,256]{1,0:T(8,128)(2,1)S(1)} collective-permute-done((bf16[400,256]{1,0:T(8,128)(2,1)S(1)}, bf16[400,256]{1,0:T(8,128)(2,1)S(1)}, u32[]{:S(2)}, u32[]{:S(2)}) %collective-permute-start.10) | collective-permute-done | bytes 204832 | tf_op jit(solution)/shard_map/ppermute | solution.py:232
  48.6 0.1 shard_map.143
  48.7 0.4 collective-permute-start.11
  49.2 8.1 %collective-permute-done.11.refs_0_ = bf16[272,256]{1,0:T(8,128)(2,1)S(1)} collective-permute-done((bf16[272,256]{1,0:T(8,128)(2,1)S(1)}, bf16[272,256]{1,0:T(8,128)(2,1)S(1)}, u32[]{:S(2)}, u32[]{:S(2)}) %collective-permute-start.11) | collective-permute-done | bytes 139296 | tf_op jit(solution)/shard_map/ppermute | solution.py:232
  57.3 0.7 %shard_map.144 = (f32[128,256]{1,0:T(8,128)}, bf16[128,256]{1,0:T(8,128)(2,1)S(1)}, f32[1,256]{1,0:T(1,128)}) custom-call(f32[128,256]{1,0:T(8,128)S(1)} %get-tuple-element.39.self_ref, f32[272,256]{1,0:T(8,128)S(1)} %get-tuple-element.46.own_ref, bf16[272,256]{1,0:T(8,128)(2,1)S(1)} %collective-permute-done.11.refs_0_), custom_call_target="tpu_custom_call" | custom-call | tf_op jit(solution)/shard_map/pallas_call | solution.py:211
  58.0 5.8 %all_gather.3 = bf16[512,256]{1,0:T(8,128)(2,1)S(1)} all-gather(bf16[128,256]{1,0:T(8,128)(2,1)S(1)} %get-tuple-element.49), channel_id=1, replica_groups=mesh['row'=8,'rep'=4] {'rep'}, dimensions={0}, use_global_device_ids=true | all-gather | bytes 327680 | tf_op jit(solution)/shard_map/all_gather | solution.py:296
  63.7 0.8 %fusion = (f32[256,256]{1,0:T(8,128)}, f32[256,256]{1,0:T(8,128)}) fusion(bf16[512,256]{1,0:T(8,128)(2,1)S(1)} %all_gather.3), kind=kLoop, calls=%fused_computation.4 | loop fusion | bytes 1048576 | tf_op jit(solution)/shard_map/slice | solution.py:297
  (3 shorter events, 0.1 us)
Async XLA Ops:
  0.6 18.5 %copy-start.6 = (s32[256]{0:T(256)S(1)}, s32[256]{0:T(256)}, u32[]{:S(2)}) copy-start(s32[256]{0:T(256)} %row_ref.3) | copy-start | bytes 3076
  0.6 18.5 %copy-start.8 = (s32[256]{0:T(256)S(1)}, s32[256]{0:T(256)}, u32[]{:S(2)}) copy-start(s32[256]{0:T(256)} %col_ref.3) | copy-start | bytes 3076
  0.7 18.5 %copy-start.10 = (s32[256]{0:T(256)S(1)}, s32[256]{0:T(256)}, u32[]{:S(2)}) copy-start(s32[256]{0:T(256)} %count_ref.3) | copy-start | bytes 3076
  0.7 18.5 %copy-start.1 = (s32[256,256]{1,0:T(8,128)S(1)}, s32[256,256]{1,0:T(8,128)}, u32[]{:S(2)}) copy-start(s32[256,256]{1,0:T(8,128)} %src_ref.3) | copy-start | bytes 786436
  0.7 14.9 %collective-permute-start = (bf16[128,256]{1,0:T(8,128)(2,1)}, bf16[128,256]{1,0:T(8,128)(2,1)S(1)}, u32[]{:S(2)}, u32[]{:S(2)}) collective-permute-start(bf16[128,256]{1,0:T(8,128)(2,1)} %param.10), channel_id=1, source_target_pairs={{0,16},{4,20},{8,24},{12,28},{16,0},{20,4},{24,8},{28,12},{1,17},{... | collective-permute-start | bytes 196616 | tf_op jit(solution)/shard_map/ppermute | solution.py:232
  6.5 16.5 %collective-permute-start.1 = (bf16[256,256]{1,0:T(8,128)(2,1)S(1)}, bf16[256,256]{1,0:T(8,128)(2,1)S(1)}, u32[]{:S(2)}, u32[]{:S(2)}) collective-permute-start(bf16[256,256]{1,0:T(8,128)(2,1)S(1)} %constant_dynamic-update-slice_fusion.own_ref), channel_id=1, source_target_pairs={{0,2},{1,3},{2,0},{3,1},{4,6},{5,7},{6,4},{7,5},{8,10},{9,11},{10,... | collective-permute-start | bytes 393224 | tf_op jit(solution)/shard_map/ppermute | solution.py:232
  8.0 0.9 %copy-start = (s32[256,256]{1,0:T(8,128)S(1)}, s32[256,256]{1,0:T(8,128)}, u32[]{:S(2)}) copy-start(s32[256,256]{1,0:T(8,128)} %src_ref.3) | copy-start | bytes 786436
  9.0 0.9 %copy-start.2 = (s32[256,256]{1,0:T(8,128)S(1)}, s32[256,256]{1,0:T(8,128)}, u32[]{:S(2)}) copy-start(s32[256,256]{1,0:T(8,128)} %dst_ref.3) | copy-start | bytes 786436
  9.9 0.7 %copy-start.5 = (s32[256]{0:T(256)S(1)}, s32[256]{0:T(256)}, u32[]{:S(2)}) copy-start(s32[256]{0:T(256)} %row_ref.3) | copy-start | bytes 3076
  10.6 0.7 %copy-start.7 = (s32[256]{0:T(256)S(1)}, s32[256]{0:T(256)}, u32[]{:S(2)}) copy-start(s32[256]{0:T(256)} %col_ref.3) | copy-start | bytes 3076
  11.3 0.7 %copy-start.9 = (s32[256]{0:T(256)S(1)}, s32[256]{0:T(256)}, u32[]{:S(2)}) copy-start(s32[256]{0:T(256)} %count_ref.3) | copy-start | bytes 3076
  15.6 17.3 %copy-start.3 = (bf16[256,256]{1,0:T(8,128)(2,1)S(1)}, bf16[256,256]{1,0:T(8,128)(2,1)}, u32[]{:S(2)}) copy-start(bf16[256,256]{1,0:T(8,128)(2,1)} %w_self_ref.1) | copy-start | bytes 393220
  15.6 17.3 %copy-start.4 = (bf16[256,256]{1,0:T(8,128)(2,1)S(1)}, bf16[256,256]{1,0:T(8,128)(2,1)}, u32[]{:S(2)}) copy-start(bf16[256,256]{1,0:T(8,128)(2,1)} %w_neigh_ref.1) | copy-start | bytes 393220
  15.6 17.3 %copy-start.11 = (f32[256]{0:T(256)S(1)}, f32[256]{0:T(256)}, u32[]{:S(2)}) copy-start(f32[256]{0:T(256)} %param.13) | copy-start | bytes 3076
  15.6 7.4 %collective-permute-start.2 = (bf16[256,256]{1,0:T(8,128)(2,1)S(1)}, bf16[256,256]{1,0:T(8,128)(2,1)S(1)}, u32[]{:S(2)}, u32[]{:S(2)}) collective-permute-start(bf16[256,256]{1,0:T(8,128)(2,1)S(1)} %constant_dynamic-update-slice_fusion.2.refs_0_), channel_id=1, source_target_pairs={{0,4},{4,0},{8,12},{12,8},{16,20},{20,16},{24,28},{28,24},{1,5},{5... | collective-permute-start | bytes 393224 | tf_op jit(solution)/shard_map/ppermute | solution.py:232
  17.2 5.8 %collective-permute-start.3 = (bf16[256,256]{1,0:T(8,128)(2,1)S(1)}, bf16[256,256]{1,0:T(8,128)(2,1)S(1)}, u32[]{:S(2)}, u32[]{:S(2)}) collective-permute-start(bf16[256,256]{1,0:T(8,128)(2,1)S(1)} %constant_dynamic-update-slice_fusion.2.refs_0_), channel_id=1, source_target_pairs={{0,8},{4,12},{8,0},{12,4},{16,24},{20,28},{24,16},{28,20},{1,9},{5... | collective-permute-start | bytes 393224 | tf_op jit(solution)/shard_map/ppermute | solution.py:232
  18.8 6.1 %collective-permute-start.4 = (bf16[256,256]{1,0:T(8,128)(2,1)S(1)}, bf16[256,256]{1,0:T(8,128)(2,1)S(1)}, u32[]{:S(2)}, u32[]{:S(2)}) collective-permute-start(bf16[256,256]{1,0:T(8,128)(2,1)S(1)} %constant_dynamic-update-slice_fusion.2.refs_0_), channel_id=1, source_target_pairs={{0,12},{4,8},{8,4},{12,0},{16,28},{20,24},{24,20},{28,16},{1,13},{... | collective-permute-start | bytes 393224 | tf_op jit(solution)/shard_map/ppermute | solution.py:232
  25.6 1.4 %collective-permute-start.5 = (bf16[272,256]{1,0:T(8,128)(2,1)S(1)}, bf16[272,256]{1,0:T(8,128)(2,1)S(1)}, u32[]{:S(2)}, u32[]{:S(2)}) collective-permute-start(bf16[272,256]{1,0:T(8,128)(2,1)S(1)} %get-tuple-element.36), channel_id=1, source_target_pairs={{0,1},{1,0},{2,3},{3,2},{4,5},{5,4},{6,7},{7,6},{8,9},{9,8},{10,11... | collective-permute-start | bytes 417800 | tf_op jit(solution)/shard_map/ppermute | solution.py:232
  27.1 5.8 %collective-permute-start.6 = (bf16[272,256]{1,0:T(8,128)(2,1)S(1)}, bf16[272,256]{1,0:T(8,128)(2,1)S(1)}, u32[]{:S(2)}, u32[]{:S(2)}) collective-permute-start(bf16[272,256]{1,0:T(8,128)(2,1)S(1)} %shard_map.140.pair_ref), channel_id=1, source_target_pairs={{0,2},{1,3},{2,0},{3,1},{4,6},{5,7},{6,4},{7,5},{8,10},{9,11},{10,... | collective-permute-start | bytes 417800 | tf_op jit(solution)/shard_map/ppermute | solution.py:232
  33.9 1.5 %collective-permute-start.7 = (bf16[400,256]{1,0:T(8,128)(2,1)S(1)}, bf16[400,256]{1,0:T(8,128)(2,1)S(1)}, u32[]{:S(2)}, u32[]{:S(2)}) collective-permute-start(bf16[400,256]{1,0:T(8,128)(2,1)S(1)} %get-tuple-element.40.sent_ref), channel_id=1, source_target_pairs={{0,1},{1,0},{2,3},{3,2},{4,5},{5,4},{6,7},{7,6},{8,9},{9,8},{10,11... | collective-permute-start | bytes 614408 | tf_op jit(solution)/shard_map/ppermute | solution.py:232
  35.9 7.2 %collective-permute-start.8 = (bf16[400,256]{1,0:T(8,128)(2,1)S(1)}, bf16[400,256]{1,0:T(8,128)(2,1)S(1)}, u32[]{:S(2)}, u32[]{:S(2)}) collective-permute-start(bf16[400,256]{1,0:T(8,128)(2,1)S(1)} %get-tuple-element.43), channel_id=1, source_target_pairs={{0,4},{4,0},{8,12},{12,8},{16,20},{20,16},{24,28},{28,24},{1,5},{5... | collective-permute-start | bytes 614408 | tf_op jit(solution)/shard_map/ppermute | solution.py:232
  36.9 8.0 %collective-permute-start.9 = (bf16[400,256]{1,0:T(8,128)(2,1)S(1)}, bf16[400,256]{1,0:T(8,128)(2,1)S(1)}, u32[]{:S(2)}, u32[]{:S(2)}) collective-permute-start(bf16[400,256]{1,0:T(8,128)(2,1)S(1)} %get-tuple-element.44), channel_id=1, source_target_pairs={{0,8},{4,12},{8,0},{12,4},{16,24},{20,28},{24,16},{28,20},{1,9},{5... | collective-permute-start | bytes 614408 | tf_op jit(solution)/shard_map/ppermute | solution.py:232
  38.5 10.2 %collective-permute-start.10 = (bf16[400,256]{1,0:T(8,128)(2,1)S(1)}, bf16[400,256]{1,0:T(8,128)(2,1)S(1)}, u32[]{:S(2)}, u32[]{:S(2)}) collective-permute-start(bf16[400,256]{1,0:T(8,128)(2,1)S(1)} %get-tuple-element.45), channel_id=1, source_target_pairs={{0,12},{4,8},{8,4},{12,0},{16,28},{20,24},{24,20},{28,16},{1,13},{... | collective-permute-start | bytes 614408 | tf_op jit(solution)/shard_map/ppermute | solution.py:232
  48.7 8.5 %collective-permute-start.11 = (bf16[272,256]{1,0:T(8,128)(2,1)S(1)}, bf16[272,256]{1,0:T(8,128)(2,1)S(1)}, u32[]{:S(2)}, u32[]{:S(2)}) collective-permute-start(bf16[272,256]{1,0:T(8,128)(2,1)S(1)} %get-tuple-element.47), channel_id=1, source_target_pairs={{0,16},{4,20},{8,24},{12,28},{16,0},{20,4},{24,8},{28,12},{1,17},{... | collective-permute-start | bytes 417800 | tf_op jit(solution)/shard_map/ppermute | solution.py:232

commit v4 on v3

--- a/solution.py
+++ b/solution.py
@@ -11,9 +11,9 @@
 PAD = 16
 BF16 = jnp.bfloat16
 F32 = jnp.float32
-UNROLL = 32
+UNROLL = 64
 VMEM = pl.BlockSpec(memory_space=pltpu.VMEM)
-SMEM = pl.BlockSpec(memory_space=pltpu.SMEM)
+HBM = pl.BlockSpec(memory_space=pltpu.HBM)
 
 
 def size_of(value):
@@ -47,18 +47,20 @@
     return rows[0:1] + rows[1:2]
 
 
-def add_tiles(first, last, row_ref, col_ref, count_ref, src_ref, dst_ref, acc_ref):
-    slots = src_ref.shape[1]
+def add_tiles(first, scalars, src_ref, dst_ref, acc_ref, ready):
+    row_ref, col_ref, count_ref = scalars
+    tiles, slots = src_ref.shape
     col_blocks = acc_ref.shape[1]
     line = lax.broadcasted_iota(jnp.int32, (BLK, slots), 0).astype(BF16)
     slot = lax.broadcasted_iota(jnp.int32, (1, slots), 1)
     one, zero = jnp.ones((), BF16), jnp.zeros((), BF16)
 
     def step(i, carry):
-        base = pl.multiple_of(first + i * UNROLL, UNROLL)
+        base = pl.multiple_of(i * UNROLL, UNROLL)
+        ready(i, pl.ds(base, UNROLL))
         dst, src = dst_ref[pl.ds(base, UNROLL), :], src_ref[pl.ds(base, UNROLL), :]
         for u in range(UNROLL):
-            tile = base + u
+            tile = first + base + u
             live = jnp.where(slot < count_ref[tile], dst[u : u + 1], -1)
             dst_hot = jnp.where(line == live.astype(BF16), one, zero)
             src_hot = jnp.where(line == src[u : u + 1].astype(BF16), one, zero)
@@ -68,19 +70,69 @@
             acc_ref[row_place(row_ref[tile]), col_place(col_ref[tile], col_blocks)] += part
         return carry
 
-    lax.fori_loop(0, (last - first) // UNROLL, step, 0)
-
-
-def first_build_kernel(row_ref, col_ref, count_ref, src_ref, dst_ref, acc_ref):
+    lax.fori_loop(0, tiles // UNROLL, step, 0)
+
+
+def first_build_kernel(
+    row_ref, col_ref, count_ref, src_ref, dst_ref, features_ref, d_out_ref,
+    acc_ref, own_ref, line_ref, late_src_ref, late_dst_ref,
+    row_buf, col_buf, count_buf, src_buf, dst_buf, sems, src_sems, dst_sems,
+):
+    half, rows = src_buf.shape[0], features_ref.shape[0]
+    scalars = [row_buf, col_buf, count_buf]
+    copies = [
+        pltpu.make_async_copy(ref, buf, sems.at[i])
+        for i, (ref, buf) in enumerate(zip([row_ref, col_ref, count_ref], scalars))
+    ]
+
+    def edges(i, at):
+        return (
+            pltpu.make_async_copy(src_ref.at[at], src_buf.at[at], src_sems.at[i]),
+            pltpu.make_async_copy(dst_ref.at[at], dst_buf.at[at], dst_sems.at[i]),
+        )
+
+    late = [
+        pltpu.make_async_copy(src_ref.at[pl.ds(half, half)], late_src_ref, sems.at[3]),
+        pltpu.make_async_copy(dst_ref.at[pl.ds(half, half)], late_dst_ref, sems.at[4]),
+        pltpu.make_async_copy(features_ref, own_ref.at[pl.ds(0, rows)], sems.at[5]),
+        pltpu.make_async_copy(d_out_ref, own_ref.at[pl.ds(rows, rows)], sems.at[6]),
+        pltpu.make_async_copy(features_ref, line_ref.at[pl.ds(0, rows)], sems.at[7]),
+    ]
+    for copy in copies:
+        copy.start()
+    for i in range(half // UNROLL):
+        for copy in edges(i, pl.ds(i * UNROLL, UNROLL)):
+            copy.start()
+    for copy in late:
+        copy.start()
     acc_ref[...] = jnp.zeros_like(acc_ref)
-    tiles = src_ref.shape[0]
-    add_tiles(0, tiles // 2, row_ref, col_ref, count_ref, src_ref, dst_ref, acc_ref)
-
-
-def last_build_kernel(row_ref, col_ref, count_ref, src_ref, dst_ref, half_ref, adj_ref, acc_ref):
+    for copy in copies:
+        copy.wait()
+
+    def ready(i, at):
+        for copy in edges(i, at):
+            copy.wait()
+
+    add_tiles(0, scalars, src_buf, dst_buf, acc_ref, ready)
+    for copy in late:
+        copy.wait()
+
+
+def last_build_kernel(
+    row_ref, col_ref, count_ref, src_ref, dst_ref, half_ref, adj_ref,
+    acc_ref, row_buf, col_buf, count_buf, sems,
+):
+    scalars = [row_buf, col_buf, count_buf]
+    copies = [
+        pltpu.make_async_copy(ref, buf, sems.at[i])
+        for i, (ref, buf) in enumerate(zip([row_ref, col_ref, count_ref], scalars))
+    ]
+    for copy in copies:
+        copy.start()
     acc_ref[...] = half_ref[...]
-    tiles = src_ref.shape[0]
-    add_tiles(tiles // 2, tiles, row_ref, col_ref, count_ref, src_ref, dst_ref, acc_ref)
+    for copy in copies:
+        copy.wait()
+    add_tiles(src_ref.shape[0], scalars, src_ref, dst_ref, acc_ref, lambda i, at: None)
     row_blocks, col_blocks = acc_ref.shape[:2]
     for g in range(row_blocks):
         for c in range(col_blocks):
@@ -207,7 +259,8 @@
 
 def call(kernel, out_shape, specs, args, scratch=()):
     outs = out_shape if isinstance(out_shape, (list, tuple)) else [out_shape]
-    held = sum(size_of(v) for v in [*args, *outs, *scratch])
+    held = sum(size_of(v) for v in [*args, *outs])
+    held += sum(math.prod(v.shape) * 4 for v in scratch)
     return pl.pallas_call(
         kernel,
         out_shape=out_shape,
@@ -232,21 +285,43 @@
         return lax.ppermute(value, axis, [(i, i ^ bits) for i in range(lax.axis_size(axis))])
 
     far_pieces = [swap(features, "row", 4 * h) for h in range(1, far)]
-    own = jnp.concatenate([features, d_out], axis=0)
+    tiles, slots = edge_src.shape
+    early = tiles // 2
+    tile_row, tile_col, tile_count, edge_src, edge_dst, held_features, d_out = (
+        pltpu.with_memory_space_constraint(v, pltpu.HBM)
+        for v in (tile_row, tile_col, tile_count, edge_src, edge_dst, features, d_out)
+    )
+    scalars = (tile_row, tile_col, tile_count)
+    buffers = [pltpu.SMEM((tiles,), jnp.int32)] * 3
+    acc_shape = (rep_count, row_count, BLK, BLK)
+    chunk_sems = [pltpu.SemaphoreType.DMA((early // UNROLL,))] * 2
+    acc, own, line, late_src, late_dst = call(
+        first_build_kernel,
+        (
+            shape(acc_shape, F32),
+            shape((2 * rows, width), BF16),
+            shape((far * rows, width), BF16),
+            shape((early, slots), jnp.int32),
+            shape((early, slots), jnp.int32),
+        ),
+        [HBM] * 7,
+        (*scalars, edge_src, edge_dst, held_features, d_out),
+        buffers
+        + [pltpu.VMEM((early, slots), jnp.int32)] * 2
+        + [pltpu.SemaphoreType.DMA((8,))]
+        + chunk_sems,
+    )
+    acc, line, far_pieces = lax.optimization_barrier((acc, line, far_pieces))
+    for h, piece in enumerate(far_pieces):
+        line = lax.dynamic_update_slice(line, piece, ((h + 1) * rows, 0))
     near = swap(own, "rep", 2)
-    tiles = (tile_row, tile_col, tile_count, edge_src, edge_dst)
-    tile_specs = [SMEM, SMEM, SMEM, VMEM, VMEM]
-    acc_shape = (rep_count, row_count, BLK, BLK)
-    acc = call(first_build_kernel, shape(acc_shape, F32), tile_specs, tiles)
-    acc, far_pieces = lax.optimization_barrier((acc, far_pieces))
-    line = jnp.concatenate([features, *far_pieces], axis=0)
     pieces = [line] + [swap(line, "row", m) for m in range(1, 4)]
     adjacency = call(
         last_build_kernel,
         shape((group, columns), BF16),
-        tile_specs + [VMEM],
-        (*tiles, acc),
-        [pltpu.VMEM(acc_shape, F32)],
+        [HBM] * 3 + [VMEM] * 3,
+        (*scalars, late_src, late_dst, acc),
+        [pltpu.VMEM(acc_shape, F32)] + buffers + [pltpu.SemaphoreType.DMA((3,))],
     )
     adjacency, near, pieces = lax.optimization_barrier((adjacency, near, pieces))
     keep, send = call(

time: 64.9 us -> 58.4 us (0.90)
  local copies, waits for them, and re-layouts: 6.54 us -> 0.84 us
  waiting for transfers between devices: 27.2 us -> 25.9 us
  starting transfers between devices: 13.8 us -> 14.6 us
    unnamed x26 -> x6, local copies, waits for them, and re-layouts: 4.87 us -> 0.01 us
    ppermute x12, waiting for transfers between devices: 27.2 us -> 25.9 us  [swap(): lax.ppermute(value, axis, [(i, i ^ bits) for i in range(lax.axis_size(axi...]
    concatenate x2 -> x0, local copies, waits for them, and re-layouts: 0.85 us -> none  [the longest x1 0.85 us: on_device(): own = jnp.concatenate([features, d_out], axis=0)]
    ppermute x12, starting transfers between devices: 13.8 us -> 14.6 us  [swap(): lax.ppermute(value, axis, [(i, i ^ bits) for i in range(lax.axis_size(axi...]
  transfers between devices with their start and end apart: 12 -> 12, of which waited for: 8 -> 9; matrix products, arithmetic and copies ran while one was open for 3% -> 0% of each run, Pallas kernels for 12% -> 13%
where the time goes in v4:
time: 58.4 us; the launch traced here: 58.2 us
  waiting for transfers between devices  25.9 us (44%)
  starting transfers between devices  14.6 us (25%)
  Pallas kernels  10.4 us (18%)
  blocking collectives  5.77 us (10%)
  local copies, waits for them, and re-layouts  0.84 us (1%)
  between operations  0.71 us (1%)
    ppermute x12, waiting for transfers between devices, swap(): lax.ppermute(value, axis, [(i, i ^ bits) for i in range(lax.axis_size(axi...  25.9 us
    ppermute x12, starting transfers between devices, swap(): lax.ppermute(value, axis, [(i, i ^ bits) for i in range(lax.axis_size(axi...  14.6 us
    pallas_call x8, Pallas kernels, call(): pl.pallas_call(kernel, out_shape=out_shape, in_specs=specs, out_specs=[VM...  10.4 us
    all_gather x1, blocking collectives, on_device(): grads = lax.all_gather(quarter, 'rep', axis=0, tiled=True).astype(F32)  5.77 us
  transfers between devices with their start and end apart: 12, of which 9 were waited for; matrix products, arithmetic and copies ran while one was open for 0% of the time, Pallas kernels for 13%

profile of v4, /device:TPU:0, one launch (start us, length us, event | category | flops | bytes accessed | tf_op | source)
XLA Modules:
  0.0 58.2 jit_solution(6812334478076095867)
XLA Ops:
  0.6 4.1 %collective-permute-start = (bf16[128,256]{1,0:T(8,128)(2,1)}, bf16[128,256]{1,0:T(8,128)(2,1)S(1)}, u32[]{:S(2)}, u32[]{:S(2)}) collective-permute-start(bf16[128,256]{1,0:T(8,128)(2,1)} %features_ref.1), channel_id=1, source_target_pairs={{0,16},{4,20},{8,24},{12,28},{16,0},{20,4},{24,8},{28,12},{1,17},{... | collective-permute-start | bytes 196616 | tf_op jit(solution)/shard_map/ppermute | solution.py:285
  4.7 3.7 %shard_map.137 = (f32[4,8,128,128]{3,2,1,0:T(8,128)S(1)}, bf16[256,256]{1,0:T(8,128)(2,1)S(1)}, bf16[256,256]{1,0:T(8,128)(2,1)S(1)}, s32[128,256]{1,0:T(8,128)S(1)}, s32[128,256]{1,0:T(8,128)S(1)}) custom-call(s32[256]{0:T(256)} %row_ref.3, s32[256]{0:T(256)} %col_ref.3, s32[256]{0:T(256)} %count_ref.3, s32[256,256]{1,0:T(8,128)} %src_ref.1, ...), custom_call_target="tpu_custom_call" | custom-call | tf_op jit(solution)/shard_map/pallas_call | solution.py:264
  8.4 1.6 %collective-permute-start.1 = (bf16[256,256]{1,0:T(8,128)(2,1)S(1)}, bf16[256,256]{1,0:T(8,128)(2,1)S(1)}, u32[]{:S(2)}, u32[]{:S(2)}) collective-permute-start(bf16[256,256]{1,0:T(8,128)(2,1)S(1)} %get-tuple-element.39.own_ref), channel_id=1, source_target_pairs={{0,2},{1,3},{2,0},{3,1},{4,6},{5,7},{6,4},{7,5},{8,10},{9,11},{10,... | collective-permute-start | bytes 393224 | tf_op jit(solution)/shard_map/ppermute | solution.py:285
  10.0 0.0 collective-permute-done
  10.0 2.6 %collective-permute-start.4 = (bf16[256,256]{1,0:T(8,128)(2,1)S(1)}, bf16[256,256]{1,0:T(8,128)(2,1)S(1)}, u32[]{:S(2)}, u32[]{:S(2)}) collective-permute-start(bf16[256,256]{1,0:T(8,128)(2,1)S(1)} %constant_dynamic-update-slice_fusion.refs_0_), channel_id=1, source_target_pairs={{0,12},{4,8},{8,4},{12,0},{16,28},{20,24},{24,20},{28,16},{1,13},{... | collective-permute-start | bytes 393224 | tf_op jit(solution)/shard_map/ppermute | solution.py:285
  12.6 0.4 collective-permute-start.3
  13.0 0.5 collective-permute-start.2
  13.6 0.0 copy-start
  13.6 0.0 copy-start.1
  13.6 0.0 copy-start.2
  13.6 3.6 %shard_map.138.adj_ref = bf16[512,1024]{1,0:T(8,128)(2,1)S(1)} custom-call(s32[256]{0:T(256)} %row_ref.3, s32[256]{0:T(256)} %col_ref.3, s32[256]{0:T(256)} %count_ref.3, s32[128,256]{1,0:T(8,128)S(1)} %get-tuple-element.34.src_ref, s32[128,256]{1,0:T(8,128)S(1)} %get-tuple-element.35.dst_ref, f32[4,8,128,128]{3,2,1,0:T(8,128)S(1)} %get-tuple-element.38.half_ref), custom_call_target="tpu_custom_call" | custom-call | tf_op jit(solution)/shard_map/pallas_call | solution.py:264
  17.2 0.0 collective-permute-done.1.near_ref
  17.2 0.0 collective-permute-done.4.refs_3_
  17.2 1.3 %collective-permute-done.3.refs_2_ = bf16[256,256]{1,0:T(8,128)(2,1)S(1)} collective-permute-done((bf16[256,256]{1,0:T(8,128)(2,1)S(1)}, bf16[256,256]{1,0:T(8,128)(2,1)S(1)}, u32[]{:S(2)}, u32[]{:S(2)}) %collective-permute-start.3) | collective-permute-done | bytes 131104 | tf_op jit(solution)/shard_map/ppermute | solution.py:285
  18.5 0.1 collective-permute-done.2.refs_1_
  18.6 0.7 %shard_map.139 = (f32[272,256]{1,0:T(8,128)S(1)}, bf16[272,256]{1,0:T(8,128)(2,1)S(1)}) custom-call(bf16[512,1024]{1,0:T(8,128)(2,1)S(1)} %shard_map.138.adj_ref, bf16[256,256]{1,0:T(8,128)(2,1)S(1)} %constant_dynamic-update-slice_fusion.refs_0_, bf16[256,256]{1,0:T(8,128)(2,1)S(1)} %collective-permute-done.2.refs_1_, ...), custom_call_target="tpu_custom_call" | custom-call | tf_op jit(solution)/shard_map/pallas_call | solution.py:264
  19.3 0.1 collective-permute-start.5
  19.3 1.3 %collective-permute-done.5.got_ref = bf16[272,256]{1,0:T(8,128)(2,1)S(1)} collective-permute-done((bf16[272,256]{1,0:T(8,128)(2,1)S(1)}, bf16[272,256]{1,0:T(8,128)(2,1)S(1)}, u32[]{:S(2)}, u32[]{:S(2)}) %collective-permute-start.5) | collective-permute-done | bytes 139296 | tf_op jit(solution)/shard_map/ppermute | solution.py:285
  20.7 0.6 %collective-permute-start.6 = (bf16[272,256]{1,0:T(8,128)(2,1)S(1)}, bf16[272,256]{1,0:T(8,128)(2,1)S(1)}, u32[]{:S(2)}, u32[]{:S(2)}) collective-permute-start(bf16[272,256]{1,0:T(8,128)(2,1)S(1)} %shard_map.140.pair_ref), channel_id=1, source_target_pairs={{0,2},{1,3},{2,0},{3,1},{4,6},{5,7},{6,4},{7,5},{8,10},{9,11},{10,... | collective-permute-start | bytes 417800 | tf_op jit(solution)/shard_map/ppermute | solution.py:285
  21.3 5.2 %collective-permute-done.6.got_ref = bf16[272,256]{1,0:T(8,128)(2,1)S(1)} collective-permute-done((bf16[272,256]{1,0:T(8,128)(2,1)S(1)}, bf16[272,256]{1,0:T(8,128)(2,1)S(1)}, u32[]{:S(2)}, u32[]{:S(2)}) %collective-permute-start.6) | collective-permute-done | bytes 139296 | tf_op jit(solution)/shard_map/ppermute | solution.py:285
  26.5 0.0 copy-done
  26.5 0.0 copy-done.1
  26.5 0.0 copy-done.2
  26.5 1.0 %shard_map.141 = (bf16[128,256]{1,0:T(8,128)(2,1)}, f32[128,256]{1,0:T(8,128)S(1)}, f32[144,256]{1,0:T(8,128)S(1)}, bf16[400,256]{1,0:T(8,128)(2,1)S(1)}) custom-call(bf16[272,256]{1,0:T(8,128)(2,1)S(1)} %shard_map.140.pair_ref, bf16[272,256]{1,0:T(8,128)(2,1)S(1)} %collective-permute-done.6.got_ref, bf16[256,256]{1,0:T(8,128)(2,1)S(1)} %get-tuple-element.39.own_ref, ...), custom_call_target="tpu_custom_call" | custom-call | tf_op jit(solution)/shard_map/pallas_call | solution.py:264
  27.5 0.0 collective-permute-start.7
  27.5 1.5 %collective-permute-done.7.got_ref = bf16[400,256]{1,0:T(8,128)(2,1)S(1)} collective-permute-done((bf16[400,256]{1,0:T(8,128)(2,1)S(1)}, bf16[400,256]{1,0:T(8,128)(2,1)S(1)}, u32[]{:S(2)}, u32[]{:S(2)}) %collective-permute-start.7) | collective-permute-done | bytes 204832 | tf_op jit(solution)/shard_map/ppermute | solution.py:285
  29.0 0.5 shard_map.142
  29.5 1.5 %collective-permute-start.8 = (bf16[400,256]{1,0:T(8,128)(2,1)S(1)}, bf16[400,256]{1,0:T(8,128)(2,1)S(1)}, u32[]{:S(2)}, u32[]{:S(2)}) collective-permute-start(bf16[400,256]{1,0:T(8,128)(2,1)S(1)} %get-tuple-element.55), channel_id=1, source_target_pairs={{0,4},{4,0},{8,12},{12,8},{16,20},{20,16},{24,28},{28,24},{1,5},{5... | collective-permute-start | bytes 614408 | tf_op jit(solution)/shard_map/ppermute | solution.py:285
  31.0 1.6 %collective-permute-start.9 = (bf16[400,256]{1,0:T(8,128)(2,1)S(1)}, bf16[400,256]{1,0:T(8,128)(2,1)S(1)}, u32[]{:S(2)}, u32[]{:S(2)}) collective-permute-start(bf16[400,256]{1,0:T(8,128)(2,1)S(1)} %get-tuple-element.56), channel_id=1, source_target_pairs={{0,8},{4,12},{8,0},{12,4},{16,24},{20,28},{24,16},{28,20},{1,9},{5... | collective-permute-start | bytes 614408 | tf_op jit(solution)/shard_map/ppermute | solution.py:285
  32.6 0.5 collective-permute-start.10
  33.1 3.6 %collective-permute-done.8.refs_0_ = bf16[400,256]{1,0:T(8,128)(2,1)S(1)} collective-permute-done((bf16[400,256]{1,0:T(8,128)(2,1)S(1)}, bf16[400,256]{1,0:T(8,128)(2,1)S(1)}, u32[]{:S(2)}, u32[]{:S(2)}) %collective-permute-start.8) | collective-permute-done | bytes 204832 | tf_op jit(solution)/shard_map/ppermute | solution.py:285
  36.7 2.2 %collective-permute-done.9.refs_1_ = bf16[400,256]{1,0:T(8,128)(2,1)S(1)} collective-permute-done((bf16[400,256]{1,0:T(8,128)(2,1)S(1)}, bf16[400,256]{1,0:T(8,128)(2,1)S(1)}, u32[]{:S(2)}, u32[]{:S(2)}) %collective-permute-start.9) | collective-permute-done | bytes 204832 | tf_op jit(solution)/shard_map/ppermute | solution.py:285
  38.9 3.3 %collective-permute-done.10.refs_2_ = bf16[400,256]{1,0:T(8,128)(2,1)S(1)} collective-permute-done((bf16[400,256]{1,0:T(8,128)(2,1)S(1)}, bf16[400,256]{1,0:T(8,128)(2,1)S(1)}, u32[]{:S(2)}, u32[]{:S(2)}) %collective-permute-start.10) | collective-permute-done | bytes 204832 | tf_op jit(solution)/shard_map/ppermute | solution.py:285
  42.3 0.1 shard_map.143
  42.4 1.1 %collective-permute-start.11 = (bf16[272,256]{1,0:T(8,128)(2,1)S(1)}, bf16[272,256]{1,0:T(8,128)(2,1)S(1)}, u32[]{:S(2)}, u32[]{:S(2)}) collective-permute-start(bf16[272,256]{1,0:T(8,128)(2,1)S(1)} %get-tuple-element.59), channel_id=1, source_target_pairs={{0,16},{4,20},{8,24},{12,28},{16,0},{20,4},{24,8},{28,12},{1,17},{... | collective-permute-start | bytes 417800 | tf_op jit(solution)/shard_map/ppermute | solution.py:285
  43.5 7.4 %collective-permute-done.11.refs_0_ = bf16[272,256]{1,0:T(8,128)(2,1)S(1)} collective-permute-done((bf16[272,256]{1,0:T(8,128)(2,1)S(1)}, bf16[272,256]{1,0:T(8,128)(2,1)S(1)}, u32[]{:S(2)}, u32[]{:S(2)}) %collective-permute-start.11) | collective-permute-done | bytes 139296 | tf_op jit(solution)/shard_map/ppermute | solution.py:285
  50.9 0.7 %shard_map.144 = (f32[128,256]{1,0:T(8,128)}, bf16[128,256]{1,0:T(8,128)(2,1)S(1)}, f32[1,256]{1,0:T(1,128)}) custom-call(f32[128,256]{1,0:T(8,128)S(1)} %get-tuple-element.51.self_ref, f32[272,256]{1,0:T(8,128)S(1)} %get-tuple-element.58.own_ref, bf16[272,256]{1,0:T(8,128)(2,1)S(1)} %collective-permute-done.11.refs_0_), custom_call_target="tpu_custom_call" | custom-call | tf_op jit(solution)/shard_map/pallas_call | solution.py:264
  51.6 5.8 %all_gather.3 = bf16[512,256]{1,0:T(8,128)(2,1)S(1)} all-gather(bf16[128,256]{1,0:T(8,128)(2,1)S(1)} %get-tuple-element.61), channel_id=1, replica_groups=mesh['row'=8,'rep'=4] {'rep'}, dimensions={0}, use_global_device_ids=true | all-gather | bytes 327680 | tf_op jit(solution)/shard_map/all_gather | solution.py:371
  57.4 0.8 %fusion = (f32[256,256]{1,0:T(8,128)}, f32[256,256]{1,0:T(8,128)}) fusion(bf16[512,256]{1,0:T(8,128)(2,1)S(1)} %all_gather.3), kind=kLoop, calls=%fused_computation.1 | loop fusion | bytes 1048576 | tf_op jit(solution)/shard_map/slice | solution.py:372
  (2 shorter events, 0.0 us)
Async XLA Ops:
  0.6 9.4 %collective-permute-start = (bf16[128,256]{1,0:T(8,128)(2,1)}, bf16[128,256]{1,0:T(8,128)(2,1)S(1)}, u32[]{:S(2)}, u32[]{:S(2)}) collective-permute-start(bf16[128,256]{1,0:T(8,128)(2,1)} %features_ref.1), channel_id=1, source_target_pairs={{0,16},{4,20},{8,24},{12,28},{16,0},{20,4},{24,8},{28,12},{1,17},{... | collective-permute-start | bytes 196616 | tf_op jit(solution)/shard_map/ppermute | solution.py:285
  8.4 8.8 %collective-permute-start.1 = (bf16[256,256]{1,0:T(8,128)(2,1)S(1)}, bf16[256,256]{1,0:T(8,128)(2,1)S(1)}, u32[]{:S(2)}, u32[]{:S(2)}) collective-permute-start(bf16[256,256]{1,0:T(8,128)(2,1)S(1)} %get-tuple-element.39.own_ref), channel_id=1, source_target_pairs={{0,2},{1,3},{2,0},{3,1},{4,6},{5,7},{6,4},{7,5},{8,10},{9,11},{10,... | collective-permute-start | bytes 393224 | tf_op jit(solution)/shard_map/ppermute | solution.py:285
  10.0 7.2 %collective-permute-start.4 = (bf16[256,256]{1,0:T(8,128)(2,1)S(1)}, bf16[256,256]{1,0:T(8,128)(2,1)S(1)}, u32[]{:S(2)}, u32[]{:S(2)}) collective-permute-start(bf16[256,256]{1,0:T(8,128)(2,1)S(1)} %constant_dynamic-update-slice_fusion.refs_0_), channel_id=1, source_target_pairs={{0,12},{4,8},{8,4},{12,0},{16,28},{20,24},{24,20},{28,16},{1,13},{... | collective-permute-start | bytes 393224 | tf_op jit(solution)/shard_map/ppermute | solution.py:285
  12.6 5.9 %collective-permute-start.3 = (bf16[256,256]{1,0:T(8,128)(2,1)S(1)}, bf16[256,256]{1,0:T(8,128)(2,1)S(1)}, u32[]{:S(2)}, u32[]{:S(2)}) collective-permute-start(bf16[256,256]{1,0:T(8,128)(2,1)S(1)} %constant_dynamic-update-slice_fusion.refs_0_), channel_id=1, source_target_pairs={{0,8},{4,12},{8,0},{12,4},{16,24},{20,28},{24,16},{28,20},{1,9},{5... | collective-permute-start | bytes 393224 | tf_op jit(solution)/shard_map/ppermute | solution.py:285
  13.0 5.5 %collective-permute-start.2 = (bf16[256,256]{1,0:T(8,128)(2,1)S(1)}, bf16[256,256]{1,0:T(8,128)(2,1)S(1)}, u32[]{:S(2)}, u32[]{:S(2)}) collective-permute-start(bf16[256,256]{1,0:T(8,128)(2,1)S(1)} %constant_dynamic-update-slice_fusion.refs_0_), channel_id=1, source_target_pairs={{0,4},{4,0},{8,12},{12,8},{16,20},{20,16},{24,28},{28,24},{1,5},{5... | collective-permute-start | bytes 393224 | tf_op jit(solution)/shard_map/ppermute | solution.py:285
  13.6 13.0 %copy-start = (bf16[256,256]{1,0:T(8,128)(2,1)S(1)}, bf16[256,256]{1,0:T(8,128)(2,1)}, u32[]{:S(2)}) copy-start(bf16[256,256]{1,0:T(8,128)(2,1)} %w_self_ref.1) | copy-start | bytes 393220
  13.6 13.0 %copy-start.1 = (bf16[256,256]{1,0:T(8,128)(2,1)S(1)}, bf16[256,256]{1,0:T(8,128)(2,1)}, u32[]{:S(2)}) copy-start(bf16[256,256]{1,0:T(8,128)(2,1)} %w_neigh_ref.1) | copy-start | bytes 393220
  13.6 13.0 %copy-start.2 = (f32[256]{0:T(256)S(1)}, f32[256]{0:T(256)}, u32[]{:S(2)}) copy-start(f32[256]{0:T(256)} %param.13) | copy-start | bytes 3076
  19.3 1.4 %collective-permute-start.5 = (bf16[272,256]{1,0:T(8,128)(2,1)S(1)}, bf16[272,256]{1,0:T(8,128)(2,1)S(1)}, u32[]{:S(2)}, u32[]{:S(2)}) collective-permute-start(bf16[272,256]{1,0:T(8,128)(2,1)S(1)} %get-tuple-element.48), channel_id=1, source_target_pairs={{0,1},{1,0},{2,3},{3,2},{4,5},{5,4},{6,7},{7,6},{8,9},{9,8},{10,11... | collective-permute-start | bytes 417800 | tf_op jit(solution)/shard_map/ppermute | solution.py:285
  20.7 5.8 %collective-permute-start.6 = (bf16[272,256]{1,0:T(8,128)(2,1)S(1)}, bf16[272,256]{1,0:T(8,128)(2,1)S(1)}, u32[]{:S(2)}, u32[]{:S(2)}) collective-permute-start(bf16[272,256]{1,0:T(8,128)(2,1)S(1)} %shard_map.140.pair_ref), channel_id=1, source_target_pairs={{0,2},{1,3},{2,0},{3,1},{4,6},{5,7},{6,4},{7,5},{8,10},{9,11},{10,... | collective-permute-start | bytes 417800 | tf_op jit(solution)/shard_map/ppermute | solution.py:285
  27.5 1.5 %collective-permute-start.7 = (bf16[400,256]{1,0:T(8,128)(2,1)S(1)}, bf16[400,256]{1,0:T(8,128)(2,1)S(1)}, u32[]{:S(2)}, u32[]{:S(2)}) collective-permute-start(bf16[400,256]{1,0:T(8,128)(2,1)S(1)} %get-tuple-element.52.sent_ref), channel_id=1, source_target_pairs={{0,1},{1,0},{2,3},{3,2},{4,5},{5,4},{6,7},{7,6},{8,9},{9,8},{10,11... | collective-permute-start | bytes 614408 | tf_op jit(solution)/shard_map/ppermute | solution.py:285
  29.5 7.2 %collective-permute-start.8 = (bf16[400,256]{1,0:T(8,128)(2,1)S(1)}, bf16[400,256]{1,0:T(8,128)(2,1)S(1)}, u32[]{:S(2)}, u32[]{:S(2)}) collective-permute-start(bf16[400,256]{1,0:T(8,128)(2,1)S(1)} %get-tuple-element.55), channel_id=1, source_target_pairs={{0,4},{4,0},{8,12},{12,8},{16,20},{20,16},{24,28},{28,24},{1,5},{5... | collective-permute-start | bytes 614408 | tf_op jit(solution)/shard_map/ppermute | solution.py:285
  31.0 8.0 %collective-permute-start.9 = (bf16[400,256]{1,0:T(8,128)(2,1)S(1)}, bf16[400,256]{1,0:T(8,128)(2,1)S(1)}, u32[]{:S(2)}, u32[]{:S(2)}) collective-permute-start(bf16[400,256]{1,0:T(8,128)(2,1)S(1)} %get-tuple-element.56), channel_id=1, source_target_pairs={{0,8},{4,12},{8,0},{12,4},{16,24},{20,28},{24,16},{28,20},{1,9},{5... | collective-permute-start | bytes 614408 | tf_op jit(solution)/shard_map/ppermute | solution.py:285
  32.6 9.7 %collective-permute-start.10 = (bf16[400,256]{1,0:T(8,128)(2,1)S(1)}, bf16[400,256]{1,0:T(8,128)(2,1)S(1)}, u32[]{:S(2)}, u32[]{:S(2)}) collective-permute-start(bf16[400,256]{1,0:T(8,128)(2,1)S(1)} %get-tuple-element.57), channel_id=1, source_target_pairs={{0,12},{4,8},{8,4},{12,0},{16,28},{20,24},{24,20},{28,16},{1,13},{... | collective-permute-start | bytes 614408 | tf_op jit(solution)/shard_map/ppermute | solution.py:285
  42.4 8.5 %collective-permute-start.11 = (bf16[272,256]{1,0:T(8,128)(2,1)S(1)}, bf16[272,256]{1,0:T(8,128)(2,1)S(1)}, u32[]{:S(2)}, u32[]{:S(2)}) collective-permute-start(bf16[272,256]{1,0:T(8,128)(2,1)S(1)} %get-tuple-element.59), channel_id=1, source_target_pairs={{0,16},{4,20},{8,24},{12,28},{16,0},{20,4},{24,8},{28,12},{1,17},{... | collective-permute-start | bytes 417800 | tf_op jit(solution)/shard_map/ppermute | solution.py:285

commit v5 on v4

--- a/solution.py
+++ b/solution.py
@@ -214,13 +214,10 @@
     send_ref[half + middle :] = split(bias_term)
 
 
-def spread_kernel(adj_ref, sent_ref, got_ref, terms_ref, keep_ref, *msg_refs):
+def spread_kernel(adj_ref, sent_ref, got_ref, keep_ref, *msg_refs):
     half = adj_ref.shape[0] // 2
-    middle = terms_ref.shape[0] - PAD
     size = adj_ref.shape[1] // 4
     g = jnp.concatenate([sent_ref[:half], got_ref[:half]], axis=0)
-    grads = (terms_ref[:middle] + got_ref[half : half + middle].astype(F32)).astype(BF16)
-    bias_rows = split(joined(terms_ref[middle:]) + joined(got_ref[half + middle :]))
     for m, ref in enumerate([keep_ref, *msg_refs]):
         blocks = lax.dot_general(
             adj_ref[:, m * size : (m + 1) * size],
@@ -228,33 +225,45 @@
             (((0,), (0,)), ((), ())),
             preferred_element_type=F32,
         )
-        ref[:size] = blocks.astype(ref.dtype)
-        ref[size : size + middle] = grads.astype(ref.dtype)
-        ref[size + middle :] = bias_rows.astype(ref.dtype)
+        ref[...] = blocks.astype(ref.dtype)
 
 
 def near_sum_kernel(keep_ref, *refs):
-    *got_refs, own_ref = refs[:4]
-    msg_refs = refs[4:]
-    size = (1 + len(msg_refs)) * BLK
-    middle = keep_ref.shape[0] - size - PAD
-    terms = [keep_ref, *got_refs]
-    blocks = tree([ref[:size].astype(F32) for ref in terms])
-    grads = tree([ref[size : size + middle].astype(F32) for ref in terms]).astype(BF16)
-    bias_rows = split(tree([joined(ref[size + middle :]) for ref in terms]))
-    for h, ref in enumerate([own_ref, *msg_refs]):
-        ref[:BLK] = blocks[h * BLK : (h + 1) * BLK].astype(ref.dtype)
-        ref[BLK : BLK + middle] = grads.astype(ref.dtype)
-        ref[BLK + middle :] = bias_rows.astype(ref.dtype)
-
-
-def finish_kernel(self_ref, own_ref, *refs):
-    *got_refs, d_features_ref, quarter_ref, bias_ref = refs
-    middle = own_ref.shape[0] - BLK - PAD
-    terms = [own_ref, *got_refs]
-    d_features_ref[...] = self_ref[...] + tree([ref[:BLK].astype(F32) for ref in terms])
-    quarter_ref[...] = tree([ref[BLK : BLK + middle].astype(F32) for ref in terms]).astype(BF16)
-    bias_ref[...] = tree([joined(ref[BLK + middle :]) for ref in terms])
+    blocks = tree([ref[...].astype(F32) for ref in (keep_ref, *refs[:3])])
+    for h, ref in enumerate(refs[3:]):
+        ref[...] = blocks[h * BLK : (h + 1) * BLK].astype(ref.dtype)
+
+
+def finish_kernel(self_ref, *refs):
+    *terms, d_features_ref = refs
+    d_features_ref[...] = self_ref[...] + tree([ref[...].astype(F32) for ref in terms])
+
+
+def core_terms_kernel(keep_ref, got_ref, terms_ref):
+    middle = keep_ref.shape[0] - PAD
+    at = got_ref.shape[0] - PAD
+    grads = keep_ref[:middle] + got_ref[at - middle : at].astype(F32)
+    terms_ref[:middle] = grads.astype(BF16)
+    terms_ref[middle:] = split(joined(keep_ref[middle:]) + joined(got_ref[at:]))
+
+
+def add_terms(refs):
+    middle = refs[0].shape[0] - PAD
+    grads = tree([ref[:middle].astype(F32) for ref in refs]).astype(BF16)
+    return grads, tree([joined(ref[middle:]) for ref in refs])
+
+
+def far_terms_kernel(*refs):
+    *terms, sum_ref = refs
+    middle = sum_ref.shape[0] - PAD
+    grads, bias_term = add_terms(terms)
+    sum_ref[:middle] = grads
+    sum_ref[middle:] = split(bias_term)
+
+
+def near_terms_kernel(*refs):
+    *terms, quarter_ref, bias_ref = refs
+    quarter_ref[...], bias_ref[...] = add_terms(terms)
 
 
 def call(kernel, out_shape, specs, args, scratch=()):
@@ -347,26 +356,37 @@
         [VMEM] * 7,
         (pair_sum, swap(pair_sum, "rep", 2), own, near, w_self, w_neigh, bias[None, :]),
     )
-    terms = middle + PAD
-    keep, *near_msgs = call(
+    back = swap(send, "rep", 1)
+    keep_blocks, *near_msgs = call(
         spread_kernel,
-        (shape((far * BLK + terms, width), F32),) + (shape((far * BLK + terms, width), BF16),) * 3,
+        (shape((far * BLK, width), F32),) + (shape((far * BLK, width), BF16),) * 3,
+        [VMEM] * 3,
+        (adjacency, send, back),
+    )
+    got = [swap(msg, "row", m + 1) for m, msg in enumerate(near_msgs)]
+    terms_shape = shape((middle + PAD, width), BF16)
+    terms = call(core_terms_kernel, terms_shape, [VMEM] * 2, (keep, back))
+    far_terms = [terms] + [swap(terms, "row", 4 * h) for h in range(1, far)]
+    terms = call(far_terms_kernel, terms_shape, [VMEM] * far, far_terms)
+    near_terms = [terms] + [swap(terms, "row", m) for m in range(1, 4)]
+    quarter, grad_bias = call(
+        near_terms_kernel,
+        (shape((middle, width), BF16), shape((1, width), F32)),
         [VMEM] * 4,
-        (adjacency, send, swap(send, "rep", 1), keep),
-    )
-    got = [swap(msg, "row", m + 1) for m, msg in enumerate(near_msgs)]
-    keep, *far_msgs = call(
+        near_terms,
+    )
+    keep_block, *far_msgs = call(
         near_sum_kernel,
-        (shape((BLK + terms, width), F32),) + (shape((BLK + terms, width), BF16),) * (far - 1),
+        (shape((BLK, width), F32),) + (shape((BLK, width), BF16),) * (far - 1),
         [VMEM] * 4,
-        (keep, *got),
+        (keep_blocks, *got),
     )
     got = [swap(msg, "row", 4 * (h + 1)) for h, msg in enumerate(far_msgs)]
-    d_features, quarter, grad_bias = call(
+    d_features = call(
         finish_kernel,
-        (shape((rows, width), F32), shape((middle, width), BF16), shape((1, width), F32)),
+        shape((rows, width), F32),
         [VMEM] * (2 + len(got)),
-        (self_term, keep, *got),
+        (self_term, keep_block, *got),
     )
     grads = lax.all_gather(quarter, "rep", axis=0, tiled=True).astype(F32)
     return (out, d_features, grads[:width], grads[width:], grad_bias[0])

time: 58.4 us -> 52.8 us (0.904)
  waiting for transfers between devices: 25.9 us -> 14.1 us
  starting transfers between devices: 14.6 us -> 20.3 us
    ppermute x12 -> x16, waiting for transfers between devices: 25.9 us -> 14.1 us  [swap(): lax.ppermute(value, axis, [(i, i ^ bits) for i in range(lax.axis_size(axi...]
    ppermute x12 -> x16, starting transfers between devices: 14.6 us -> 20.3 us  [swap(): lax.ppermute(value, axis, [(i, i ^ bits) for i in range(lax.axis_size(axi...]
    pallas_call x8 -> x11, Pallas kernels: 10.4 us -> 10.9 us  [call(): pl.pallas_call(kernel, out_shape=out_shape, in_specs=specs, out_specs=[VM...]
  transfers between devices with their start and end apart: 12 -> 16, of which waited for: 9 -> 8; matrix products, arithmetic and copies ran while one was open for 0% -> 2% of each run, Pallas kernels for 13% -> 15%
where the time goes in v5:
time: 52.8 us; the launch traced here: 52.6 us
  starting transfers between devices  20.3 us (38%)
  waiting for transfers between devices  14.1 us (27%)
  Pallas kernels  10.9 us (21%)
  blocking collectives  5.77 us (11%)
  local copies, waits for them, and re-layouts  0.84 us (2%)
  between operations  0.72 us (1%)
    ppermute x16, starting transfers between devices, swap(): lax.ppermute(value, axis, [(i, i ^ bits) for i in range(lax.axis_size(axi...  20.3 us
    ppermute x16, waiting for transfers between devices, swap(): lax.ppermute(value, axis, [(i, i ^ bits) for i in range(lax.axis_size(axi...  14.1 us
    pallas_call x11, Pallas kernels, call(): pl.pallas_call(kernel, out_shape=out_shape, in_specs=specs, out_specs=[VM...  10.9 us
    all_gather x1, blocking collectives, on_device(): grads = lax.all_gather(quarter, 'rep', axis=0, tiled=True).astype(F32)  5.77 us
  transfers between devices with their start and end apart: 16, of which 8 were waited for; matrix products, arithmetic and copies ran while one was open for 2% of the time, Pallas kernels for 15%

profile of v5, /device:TPU:0, one launch (start us, length us, event | category | flops | bytes accessed | tf_op | source)
XLA Modules:
  0.0 52.6 jit_solution(9597134853850194698)
XLA Ops:
  0.6 4.1 %collective-permute-start = (bf16[128,256]{1,0:T(8,128)(2,1)}, bf16[128,256]{1,0:T(8,128)(2,1)S(1)}, u32[]{:S(2)}, u32[]{:S(2)}) collective-permute-start(bf16[128,256]{1,0:T(8,128)(2,1)} %features_ref.1), channel_id=1, source_target_pairs={{0,16},{4,20},{8,24},{12,28},{16,0},{20,4},{24,8},{28,12},{1,17},{... | collective-permute-start | bytes 196616 | tf_op jit(solution)/shard_map/ppermute | solution.py:294
  4.7 3.7 %shard_map.137 = (f32[4,8,128,128]{3,2,1,0:T(8,128)S(1)}, bf16[256,256]{1,0:T(8,128)(2,1)S(1)}, bf16[256,256]{1,0:T(8,128)(2,1)S(1)}, s32[128,256]{1,0:T(8,128)S(1)}, s32[128,256]{1,0:T(8,128)S(1)}) custom-call(s32[256]{0:T(256)} %row_ref.3, s32[256]{0:T(256)} %col_ref.3, s32[256]{0:T(256)} %count_ref.3, s32[256,256]{1,0:T(8,128)} %src_ref.1, ...), custom_call_target="tpu_custom_call" | custom-call | tf_op jit(solution)/shard_map/pallas_call | solution.py:273
  8.4 1.6 %collective-permute-start.1 = (bf16[256,256]{1,0:T(8,128)(2,1)S(1)}, bf16[256,256]{1,0:T(8,128)(2,1)S(1)}, u32[]{:S(2)}, u32[]{:S(2)}) collective-permute-start(bf16[256,256]{1,0:T(8,128)(2,1)S(1)} %get-tuple-element.38.own_ref), channel_id=1, source_target_pairs={{0,2},{1,3},{2,0},{3,1},{4,6},{5,7},{6,4},{7,5},{8,10},{9,11},{10,... | collective-permute-start | bytes 393224 | tf_op jit(solution)/shard_map/ppermute | solution.py:294
  10.0 0.0 collective-permute-done
  10.0 2.6 %collective-permute-start.4 = (bf16[256,256]{1,0:T(8,128)(2,1)S(1)}, bf16[256,256]{1,0:T(8,128)(2,1)S(1)}, u32[]{:S(2)}, u32[]{:S(2)}) collective-permute-start(bf16[256,256]{1,0:T(8,128)(2,1)S(1)} %constant_dynamic-update-slice_fusion.refs_0_), channel_id=1, source_target_pairs={{0,12},{4,8},{8,4},{12,0},{16,28},{20,24},{24,20},{28,16},{1,13},{... | collective-permute-start | bytes 393224 | tf_op jit(solution)/shard_map/ppermute | solution.py:294
  12.6 0.4 collective-permute-start.3
  13.0 0.5 collective-permute-start.2
  13.6 0.0 copy-start
  13.6 0.0 copy-start.1
  13.6 0.0 copy-start.2
  13.6 3.6 %shard_map.138.adj_ref = bf16[512,1024]{1,0:T(8,128)(2,1)S(1)} custom-call(s32[256]{0:T(256)} %row_ref.3, s32[256]{0:T(256)} %col_ref.3, s32[256]{0:T(256)} %count_ref.3, s32[128,256]{1,0:T(8,128)S(1)} %get-tuple-element.33.src_ref, s32[128,256]{1,0:T(8,128)S(1)} %get-tuple-element.34.dst_ref, f32[4,8,128,128]{3,2,1,0:T(8,128)S(1)} %get-tuple-element.37.half_ref), custom_call_target="tpu_custom_call" | custom-call | tf_op jit(solution)/shard_map/pallas_call | solution.py:273
  17.2 0.0 collective-permute-done.1.near_ref
  17.2 0.0 collective-permute-done.4.refs_3_
  17.2 1.3 %collective-permute-done.3.refs_2_ = bf16[256,256]{1,0:T(8,128)(2,1)S(1)} collective-permute-done((bf16[256,256]{1,0:T(8,128)(2,1)S(1)}, bf16[256,256]{1,0:T(8,128)(2,1)S(1)}, u32[]{:S(2)}, u32[]{:S(2)}) %collective-permute-start.3) | collective-permute-done | bytes 131104 | tf_op jit(solution)/shard_map/ppermute | solution.py:294
  18.5 0.1 collective-permute-done.2.refs_1_
  18.6 0.7 %shard_map.139 = (f32[272,256]{1,0:T(8,128)S(1)}, bf16[272,256]{1,0:T(8,128)(2,1)S(1)}) custom-call(bf16[512,1024]{1,0:T(8,128)(2,1)S(1)} %shard_map.138.adj_ref, bf16[256,256]{1,0:T(8,128)(2,1)S(1)} %constant_dynamic-update-slice_fusion.refs_0_, bf16[256,256]{1,0:T(8,128)(2,1)S(1)} %collective-permute-done.2.refs_1_, ...), custom_call_target="tpu_custom_call" | custom-call | tf_op jit(solution)/shard_map/pallas_call | solution.py:273
  19.3 0.1 collective-permute-start.5
  19.3 1.3 %collective-permute-done.5.got_ref = bf16[272,256]{1,0:T(8,128)(2,1)S(1)} collective-permute-done((bf16[272,256]{1,0:T(8,128)(2,1)S(1)}, bf16[272,256]{1,0:T(8,128)(2,1)S(1)}, u32[]{:S(2)}, u32[]{:S(2)}) %collective-permute-start.5) | collective-permute-done | bytes 139296 | tf_op jit(solution)/shard_map/ppermute | solution.py:294
  20.7 0.6 %collective-permute-start.6 = (bf16[272,256]{1,0:T(8,128)(2,1)S(1)}, bf16[272,256]{1,0:T(8,128)(2,1)S(1)}, u32[]{:S(2)}, u32[]{:S(2)}) collective-permute-start(bf16[272,256]{1,0:T(8,128)(2,1)S(1)} %shard_map.140.pair_ref), channel_id=1, source_target_pairs={{0,2},{1,3},{2,0},{3,1},{4,6},{5,7},{6,4},{7,5},{8,10},{9,11},{10,... | collective-permute-start | bytes 417800 | tf_op jit(solution)/shard_map/ppermute | solution.py:294
  21.3 5.2 %collective-permute-done.6.got_ref = bf16[272,256]{1,0:T(8,128)(2,1)S(1)} collective-permute-done((bf16[272,256]{1,0:T(8,128)(2,1)S(1)}, bf16[272,256]{1,0:T(8,128)(2,1)S(1)}, u32[]{:S(2)}, u32[]{:S(2)}) %collective-permute-start.6) | collective-permute-done | bytes 139296 | tf_op jit(solution)/shard_map/ppermute | solution.py:294
  26.5 0.0 copy-done
  26.5 0.0 copy-done.1
  26.5 0.0 copy-done.2
  26.5 1.0 %shard_map.141 = (bf16[128,256]{1,0:T(8,128)(2,1)}, f32[128,256]{1,0:T(8,128)S(1)}, f32[144,256]{1,0:T(8,128)S(1)}, bf16[400,256]{1,0:T(8,128)(2,1)S(1)}) custom-call(bf16[272,256]{1,0:T(8,128)(2,1)S(1)} %shard_map.140.pair_ref, bf16[272,256]{1,0:T(8,128)(2,1)S(1)} %collective-permute-done.6.got_ref, bf16[256,256]{1,0:T(8,128)(2,1)S(1)} %get-tuple-element.38.own_ref, ...), custom_call_target="tpu_custom_call" | custom-call | tf_op jit(solution)/shard_map/pallas_call | solution.py:273
  27.5 0.0 collective-permute-start.7
  27.5 1.5 %collective-permute-done.7.got_ref = bf16[400,256]{1,0:T(8,128)(2,1)S(1)} collective-permute-done((bf16[400,256]{1,0:T(8,128)(2,1)S(1)}, bf16[400,256]{1,0:T(8,128)(2,1)S(1)}, u32[]{:S(2)}, u32[]{:S(2)}) %collective-permute-start.7) | collective-permute-done | bytes 204832 | tf_op jit(solution)/shard_map/ppermute | solution.py:294
  29.0 0.5 shard_map.142
  29.5 1.5 %collective-permute-start.8 = (bf16[256,256]{1,0:T(8,128)(2,1)S(1)}, bf16[256,256]{1,0:T(8,128)(2,1)S(1)}, u32[]{:S(2)}, u32[]{:S(2)}) collective-permute-start(bf16[256,256]{1,0:T(8,128)(2,1)S(1)} %get-tuple-element.53), channel_id=1, source_target_pairs={{0,4},{4,0},{8,12},{12,8},{16,20},{20,16},{24,28},{28,24},{1,5},{5... | collective-permute-start | bytes 393224 | tf_op jit(solution)/shard_map/ppermute | solution.py:294
  31.0 0.4 collective-permute-start.12
  31.4 2.5 %collective-permute-start.9 = (bf16[256,256]{1,0:T(8,128)(2,1)S(1)}, bf16[256,256]{1,0:T(8,128)(2,1)S(1)}, u32[]{:S(2)}, u32[]{:S(2)}) collective-permute-start(bf16[256,256]{1,0:T(8,128)(2,1)S(1)} %get-tuple-element.54), channel_id=1, source_target_pairs={{0,8},{4,12},{8,0},{12,4},{16,24},{20,28},{24,16},{28,20},{1,9},{5... | collective-permute-start | bytes 393224 | tf_op jit(solution)/shard_map/ppermute | solution.py:294
  33.9 0.3 collective-permute-start.10
  34.2 3.2 %collective-permute-done.12.refs_1_ = bf16[144,256]{1,0:T(8,128)(2,1)S(1)} collective-permute-done((bf16[144,256]{1,0:T(8,128)(2,1)S(1)}, bf16[144,256]{1,0:T(8,128)(2,1)S(1)}, u32[]{:S(2)}, u32[]{:S(2)}) %collective-permute-start.12) | collective-permute-done | bytes 73760 | tf_op jit(solution)/shard_map/ppermute | solution.py:294
  37.5 1.3 %collective-permute-start.15 = (bf16[144,256]{1,0:T(8,128)(2,1)S(1)}, bf16[144,256]{1,0:T(8,128)(2,1)S(1)}, u32[]{:S(2)}, u32[]{:S(2)}) collective-permute-start(bf16[144,256]{1,0:T(8,128)(2,1)S(1)} %shard_map.146.refs_0_), channel_id=1, source_target_pairs={{0,12},{4,8},{8,4},{12,0},{16,28},{20,24},{24,20},{28,16},{1,13},{... | collective-permute-start | bytes 221192 | tf_op jit(solution)/shard_map/ppermute | solution.py:294
  38.8 0.8 %collective-permute-start.14 = (bf16[144,256]{1,0:T(8,128)(2,1)S(1)}, bf16[144,256]{1,0:T(8,128)(2,1)S(1)}, u32[]{:S(2)}, u32[]{:S(2)}) collective-permute-start(bf16[144,256]{1,0:T(8,128)(2,1)S(1)} %shard_map.146.refs_0_), channel_id=1, source_target_pairs={{0,8},{4,12},{8,0},{12,4},{16,24},{20,28},{24,16},{28,20},{1,9},{5... | collective-permute-start | bytes 221192 | tf_op jit(solution)/shard_map/ppermute | solution.py:294
  39.6 0.0 collective-permute-done.8.refs_0_
  39.6 1.4 %collective-permute-start.13 = (bf16[144,256]{1,0:T(8,128)(2,1)S(1)}, bf16[144,256]{1,0:T(8,128)(2,1)S(1)}, u32[]{:S(2)}, u32[]{:S(2)}) collective-permute-start(bf16[144,256]{1,0:T(8,128)(2,1)S(1)} %shard_map.146.refs_0_), channel_id=1, source_target_pairs={{0,4},{4,0},{8,12},{12,8},{16,20},{20,16},{24,28},{28,24},{1,5},{5... | collective-permute-start | bytes 221192 | tf_op jit(solution)/shard_map/ppermute | solution.py:294
  41.1 0.0 collective-permute-done.9.refs_1_
  41.1 1.2 %collective-permute-done.10.refs_2_ = bf16[256,256]{1,0:T(8,128)(2,1)S(1)} collective-permute-done((bf16[256,256]{1,0:T(8,128)(2,1)S(1)}, bf16[256,256]{1,0:T(8,128)(2,1)S(1)}, u32[]{:S(2)}, u32[]{:S(2)}) %collective-permute-start.10) | collective-permute-done | bytes 131104 | tf_op jit(solution)/shard_map/ppermute | solution.py:294
  42.3 0.1 shard_map.143
  42.4 2.1 %collective-permute-start.11 = (bf16[128,256]{1,0:T(8,128)(2,1)S(1)}, bf16[128,256]{1,0:T(8,128)(2,1)S(1)}, u32[]{:S(2)}, u32[]{:S(2)}) collective-permute-start(bf16[128,256]{1,0:T(8,128)(2,1)S(1)} %get-tuple-element.57), channel_id=1, source_target_pairs={{0,16},{4,20},{8,24},{12,28},{16,0},{20,4},{24,8},{28,12},{1,17},{... | collective-permute-start | bytes 196616 | tf_op jit(solution)/shard_map/ppermute | solution.py:294
  44.5 0.0 collective-permute-done.15.refs_3_
  44.5 0.3 collective-permute-done.14.refs_2_
  44.8 0.0 collective-permute-done.13.refs_1_
  44.8 0.6 %shard_map.147 = (bf16[128,256]{1,0:T(8,128)(2,1)S(1)}, f32[1,256]{1,0:T(1,128)}) custom-call(bf16[144,256]{1,0:T(8,128)(2,1)S(1)} %shard_map.146.refs_0_, bf16[144,256]{1,0:T(8,128)(2,1)S(1)} %collective-permute-done.13.refs_1_, bf16[144,256]{1,0:T(8,128)(2,1)S(1)} %collective-permute-done.14.refs_2_, bf16[144,256]{1,0:T(8,128)(2,1)S(1)} %collective-permute-done.15.refs_3_), custom_call_target="tpu_custom_call" | custom-call | tf_op jit(solution)/shard_map/pallas_call | solution.py:273
  45.4 5.8 %all_gather.3 = bf16[512,256]{1,0:T(8,128)(2,1)S(1)} all-gather(bf16[128,256]{1,0:T(8,128)(2,1)S(1)} %get-tuple-element.59), channel_id=1, replica_groups=mesh['row'=8,'rep'=4] {'rep'}, dimensions={0}, use_global_device_ids=true | all-gather | bytes 327680 | tf_op jit(solution)/shard_map/all_gather | solution.py:391
  51.1 0.8 %fusion = (f32[256,256]{1,0:T(8,128)}, f32[256,256]{1,0:T(8,128)}) fusion(bf16[512,256]{1,0:T(8,128)(2,1)S(1)} %all_gather.3), kind=kLoop, calls=%fused_computation.1 | loop fusion | bytes 1048576 | tf_op jit(solution)/shard_map/slice | solution.py:392
  52.0 0.0 collective-permute-done.11.refs_1_
  52.0 0.7 %shard_map.144 = f32[128,256]{1,0:T(8,128)} custom-call(f32[128,256]{1,0:T(8,128)S(1)} %get-tuple-element.50.self_ref, f32[128,256]{1,0:T(8,128)S(1)} %get-tuple-element.56.refs_0_, bf16[128,256]{1,0:T(8,128)(2,1)S(1)} %collective-permute-done.11.refs_1_), custom_call_target="tpu_custom_call" | custom-call | tf_op jit(solution)/shard_map/pallas_call | solution.py:273
  (4 shorter events, 0.1 us)
Async XLA Ops:
  0.6 9.4 %collective-permute-start = (bf16[128,256]{1,0:T(8,128)(2,1)}, bf16[128,256]{1,0:T(8,128)(2,1)S(1)}, u32[]{:S(2)}, u32[]{:S(2)}) collective-permute-start(bf16[128,256]{1,0:T(8,128)(2,1)} %features_ref.1), channel_id=1, source_target_pairs={{0,16},{4,20},{8,24},{12,28},{16,0},{20,4},{24,8},{28,12},{1,17},{... | collective-permute-start | bytes 196616 | tf_op jit(solution)/shard_map/ppermute | solution.py:294
  8.4 8.8 %collective-permute-start.1 = (bf16[256,256]{1,0:T(8,128)(2,1)S(1)}, bf16[256,256]{1,0:T(8,128)(2,1)S(1)}, u32[]{:S(2)}, u32[]{:S(2)}) collective-permute-start(bf16[256,256]{1,0:T(8,128)(2,1)S(1)} %get-tuple-element.38.own_ref), channel_id=1, source_target_pairs={{0,2},{1,3},{2,0},{3,1},{4,6},{5,7},{6,4},{7,5},{8,10},{9,11},{10,... | collective-permute-start | bytes 393224 | tf_op jit(solution)/shard_map/ppermute | solution.py:294
  10.0 7.2 %collective-permute-start.4 = (bf16[256,256]{1,0:T(8,128)(2,1)S(1)}, bf16[256,256]{1,0:T(8,128)(2,1)S(1)}, u32[]{:S(2)}, u32[]{:S(2)}) collective-permute-start(bf16[256,256]{1,0:T(8,128)(2,1)S(1)} %constant_dynamic-update-slice_fusion.refs_0_), channel_id=1, source_target_pairs={{0,12},{4,8},{8,4},{12,0},{16,28},{20,24},{24,20},{28,16},{1,13},{... | collective-permute-start | bytes 393224 | tf_op jit(solution)/shard_map/ppermute | solution.py:294
  12.6 5.9 %collective-permute-start.3 = (bf16[256,256]{1,0:T(8,128)(2,1)S(1)}, bf16[256,256]{1,0:T(8,128)(2,1)S(1)}, u32[]{:S(2)}, u32[]{:S(2)}) collective-permute-start(bf16[256,256]{1,0:T(8,128)(2,1)S(1)} %constant_dynamic-update-slice_fusion.refs_0_), channel_id=1, source_target_pairs={{0,8},{4,12},{8,0},{12,4},{16,24},{20,28},{24,16},{28,20},{1,9},{5... | collective-permute-start | bytes 393224 | tf_op jit(solution)/shard_map/ppermute | solution.py:294
  13.0 5.5 %collective-permute-start.2 = (bf16[256,256]{1,0:T(8,128)(2,1)S(1)}, bf16[256,256]{1,0:T(8,128)(2,1)S(1)}, u32[]{:S(2)}, u32[]{:S(2)}) collective-permute-start(bf16[256,256]{1,0:T(8,128)(2,1)S(1)} %constant_dynamic-update-slice_fusion.refs_0_), channel_id=1, source_target_pairs={{0,4},{4,0},{8,12},{12,8},{16,20},{20,16},{24,28},{28,24},{1,5},{5... | collective-permute-start | bytes 393224 | tf_op jit(solution)/shard_map/ppermute | solution.py:294
  13.6 13.0 %copy-start = (bf16[256,256]{1,0:T(8,128)(2,1)S(1)}, bf16[256,256]{1,0:T(8,128)(2,1)}, u32[]{:S(2)}) copy-start(bf16[256,256]{1,0:T(8,128)(2,1)} %w_self_ref.1) | copy-start | bytes 393220
  13.6 13.0 %copy-start.1 = (bf16[256,256]{1,0:T(8,128)(2,1)S(1)}, bf16[256,256]{1,0:T(8,128)(2,1)}, u32[]{:S(2)}) copy-start(bf16[256,256]{1,0:T(8,128)(2,1)} %w_neigh_ref.1) | copy-start | bytes 393220
  13.6 13.0 %copy-start.2 = (f32[256]{0:T(256)S(1)}, f32[256]{0:T(256)}, u32[]{:S(2)}) copy-start(f32[256]{0:T(256)} %param.13) | copy-start | bytes 3076
  19.3 1.4 %collective-permute-start.5 = (bf16[272,256]{1,0:T(8,128)(2,1)S(1)}, bf16[272,256]{1,0:T(8,128)(2,1)S(1)}, u32[]{:S(2)}, u32[]{:S(2)}) collective-permute-start(bf16[272,256]{1,0:T(8,128)(2,1)S(1)} %get-tuple-element.47), channel_id=1, source_target_pairs={{0,1},{1,0},{2,3},{3,2},{4,5},{5,4},{6,7},{7,6},{8,9},{9,8},{10,11... | collective-permute-start | bytes 417800 | tf_op jit(solution)/shard_map/ppermute | solution.py:294
  20.7 5.8 %collective-permute-start.6 = (bf16[272,256]{1,0:T(8,128)(2,1)S(1)}, bf16[272,256]{1,0:T(8,128)(2,1)S(1)}, u32[]{:S(2)}, u32[]{:S(2)}) collective-permute-start(bf16[272,256]{1,0:T(8,128)(2,1)S(1)} %shard_map.140.pair_ref), channel_id=1, source_target_pairs={{0,2},{1,3},{2,0},{3,1},{4,6},{5,7},{6,4},{7,5},{8,10},{9,11},{10,... | collective-permute-start | bytes 417800 | tf_op jit(solution)/shard_map/ppermute | solution.py:294
  27.5 1.5 %collective-permute-start.7 = (bf16[400,256]{1,0:T(8,128)(2,1)S(1)}, bf16[400,256]{1,0:T(8,128)(2,1)S(1)}, u32[]{:S(2)}, u32[]{:S(2)}) collective-permute-start(bf16[400,256]{1,0:T(8,128)(2,1)S(1)} %get-tuple-element.51.sent_ref), channel_id=1, source_target_pairs={{0,1},{1,0},{2,3},{3,2},{4,5},{5,4},{6,7},{7,6},{8,9},{9,8},{10,11... | collective-permute-start | bytes 614408 | tf_op jit(solution)/shard_map/ppermute | solution.py:294
  29.5 10.1 %collective-permute-start.8 = (bf16[256,256]{1,0:T(8,128)(2,1)S(1)}, bf16[256,256]{1,0:T(8,128)(2,1)S(1)}, u32[]{:S(2)}, u32[]{:S(2)}) collective-permute-start(bf16[256,256]{1,0:T(8,128)(2,1)S(1)} %get-tuple-element.53), channel_id=1, source_target_pairs={{0,4},{4,0},{8,12},{12,8},{16,20},{20,16},{24,28},{28,24},{1,5},{5... | collective-permute-start | bytes 393224 | tf_op jit(solution)/shard_map/ppermute | solution.py:294
  31.0 6.5 %collective-permute-start.12 = (bf16[144,256]{1,0:T(8,128)(2,1)S(1)}, bf16[144,256]{1,0:T(8,128)(2,1)S(1)}, u32[]{:S(2)}, u32[]{:S(2)}) collective-permute-start(bf16[144,256]{1,0:T(8,128)(2,1)S(1)} %shard_map.145.refs_0_), channel_id=1, source_target_pairs={{0,16},{4,20},{8,24},{12,28},{16,0},{20,4},{24,8},{28,12},{1,17},{... | collective-permute-start | bytes 221192 | tf_op jit(solution)/shard_map/ppermute | solution.py:294
  31.4 9.6 %collective-permute-start.9 = (bf16[256,256]{1,0:T(8,128)(2,1)S(1)}, bf16[256,256]{1,0:T(8,128)(2,1)S(1)}, u32[]{:S(2)}, u32[]{:S(2)}) collective-permute-start(bf16[256,256]{1,0:T(8,128)(2,1)S(1)} %get-tuple-element.54), channel_id=1, source_target_pairs={{0,8},{4,12},{8,0},{12,4},{16,24},{20,28},{24,16},{28,20},{1,9},{5... | collective-permute-start | bytes 393224 | tf_op jit(solution)/shard_map/ppermute | solution.py:294
  33.9 8.4 %collective-permute-start.10 = (bf16[256,256]{1,0:T(8,128)(2,1)S(1)}, bf16[256,256]{1,0:T(8,128)(2,1)S(1)}, u32[]{:S(2)}, u32[]{:S(2)}) collective-permute-start(bf16[256,256]{1,0:T(8,128)(2,1)S(1)} %get-tuple-element.55), channel_id=1, source_target_pairs={{0,12},{4,8},{8,4},{12,0},{16,28},{20,24},{24,20},{28,16},{1,13},{... | collective-permute-start | bytes 393224 | tf_op jit(solution)/shard_map/ppermute | solution.py:294
  37.5 7.0 %collective-permute-start.15 = (bf16[144,256]{1,0:T(8,128)(2,1)S(1)}, bf16[144,256]{1,0:T(8,128)(2,1)S(1)}, u32[]{:S(2)}, u32[]{:S(2)}) collective-permute-start(bf16[144,256]{1,0:T(8,128)(2,1)S(1)} %shard_map.146.refs_0_), channel_id=1, source_target_pairs={{0,12},{4,8},{8,4},{12,0},{16,28},{20,24},{24,20},{28,16},{1,13},{... | collective-permute-start | bytes 221192 | tf_op jit(solution)/shard_map/ppermute | solution.py:294
  38.8 5.9 %collective-permute-start.14 = (bf16[144,256]{1,0:T(8,128)(2,1)S(1)}, bf16[144,256]{1,0:T(8,128)(2,1)S(1)}, u32[]{:S(2)}, u32[]{:S(2)}) collective-permute-start(bf16[144,256]{1,0:T(8,128)(2,1)S(1)} %shard_map.146.refs_0_), channel_id=1, source_target_pairs={{0,8},{4,12},{8,0},{12,4},{16,24},{20,28},{24,16},{28,20},{1,9},{5... | collective-permute-start | bytes 221192 | tf_op jit(solution)/shard_map/ppermute | solution.py:294
  39.6 5.1 %collective-permute-start.13 = (bf16[144,256]{1,0:T(8,128)(2,1)S(1)}, bf16[144,256]{1,0:T(8,128)(2,1)S(1)}, u32[]{:S(2)}, u32[]{:S(2)}) collective-permute-start(bf16[144,256]{1,0:T(8,128)(2,1)S(1)} %shard_map.146.refs_0_), channel_id=1, source_target_pairs={{0,4},{4,0},{8,12},{12,8},{16,20},{20,16},{24,28},{28,24},{1,5},{5... | collective-permute-start | bytes 221192 | tf_op jit(solution)/shard_map/ppermute | solution.py:294
  42.4 9.6 %collective-permute-start.11 = (bf16[128,256]{1,0:T(8,128)(2,1)S(1)}, bf16[128,256]{1,0:T(8,128)(2,1)S(1)}, u32[]{:S(2)}, u32[]{:S(2)}) collective-permute-start(bf16[128,256]{1,0:T(8,128)(2,1)S(1)} %get-tuple-element.57), channel_id=1, source_target_pairs={{0,16},{4,20},{8,24},{12,28},{16,0},{20,4},{24,8},{28,12},{1,17},{... | collective-permute-start | bytes 196616 | tf_op jit(solution)/shard_map/ppermute | solution.py:294

commit v6 on v5

--- a/solution.py
+++ b/solution.py
@@ -74,8 +74,8 @@
 
 
 def first_build_kernel(
-    row_ref, col_ref, count_ref, src_ref, dst_ref, features_ref, d_out_ref,
-    acc_ref, own_ref, line_ref, late_src_ref, late_dst_ref,
+    row_ref, col_ref, count_ref, src_ref, dst_ref, features_ref,
+    acc_ref, line_ref, late_src_ref, late_dst_ref,
     row_buf, col_buf, count_buf, src_buf, dst_buf, sems, src_sems, dst_sems,
 ):
     half, rows = src_buf.shape[0], features_ref.shape[0]
@@ -94,9 +94,7 @@
     late = [
         pltpu.make_async_copy(src_ref.at[pl.ds(half, half)], late_src_ref, sems.at[3]),
         pltpu.make_async_copy(dst_ref.at[pl.ds(half, half)], late_dst_ref, sems.at[4]),
-        pltpu.make_async_copy(features_ref, own_ref.at[pl.ds(0, rows)], sems.at[5]),
-        pltpu.make_async_copy(d_out_ref, own_ref.at[pl.ds(rows, rows)], sems.at[6]),
-        pltpu.make_async_copy(features_ref, line_ref.at[pl.ds(0, rows)], sems.at[7]),
+        pltpu.make_async_copy(features_ref, line_ref.at[pl.ds(0, rows)], sems.at[5]),
     ]
     for copy in copies:
         copy.start()
@@ -165,7 +163,8 @@
 
 
 def node_kernel(
-    pair_ref, got_ref, own_ref, near_ref, w_self_ref, w_neigh_ref, bias_ref,
+    pair_ref, got_ref, features_ref, near_features_ref, d_out_ref, near_d_out_ref,
+    w_self_ref, w_neigh_ref, bias_ref,
     out_ref, self_ref, keep_ref, send_ref,
 ):
     rows, width = out_ref.shape
@@ -180,8 +179,8 @@
     )
     inverse = jnp.sum(jnp.where(diagonal, inverse_row, 0.0), axis=1, keepdims=True)
     agg = (sums * inverse).astype(BF16)
-    features = jnp.concatenate([own_ref[:rows], near_ref[:rows]], axis=0)
-    d_out = jnp.concatenate([own_ref[rows:], near_ref[rows:]], axis=0).astype(F32)
+    features = jnp.concatenate([features_ref[...], near_features_ref[...]], axis=0)
+    d_out = jnp.concatenate([d_out_ref[...], near_d_out_ref[...]], axis=0).astype(F32)
     pre = (
         jnp.dot(features, w_self_ref[...], preferred_element_type=F32)
         + jnp.dot(agg, w_neigh_ref[...], preferred_element_type=F32)
@@ -235,8 +234,15 @@
 
 
 def finish_kernel(self_ref, *refs):
-    *terms, d_features_ref = refs
+    *terms, d_features_ref, grad_self_ref, grad_neigh_ref = refs
+    quarters, terms = terms[:4], terms[4:]
     d_features_ref[...] = self_ref[...] + tree([ref[...].astype(F32) for ref in terms])
+    me = lax.axis_index("rep")
+    low = me >> 1 == 0
+    for h in range(2):
+        same, other = quarters[h][...].astype(F32), quarters[2 + h][...].astype(F32)
+        grad_self_ref[(me & 1) ^ h] = jnp.where(low, same, other)
+        grad_neigh_ref[(me & 1) ^ h] = jnp.where(low, other, same)
 
 
 def core_terms_kernel(keep_ref, got_ref, terms_ref):
@@ -294,36 +300,35 @@
         return lax.ppermute(value, axis, [(i, i ^ bits) for i in range(lax.axis_size(axis))])
 
     far_pieces = [swap(features, "row", 4 * h) for h in range(1, far)]
+    near = [swap(features, "rep", 2), swap(d_out, "rep", 2)]
     tiles, slots = edge_src.shape
     early = tiles // 2
-    tile_row, tile_col, tile_count, edge_src, edge_dst, held_features, d_out = (
+    tile_row, tile_col, tile_count, edge_src, edge_dst, held_features = (
         pltpu.with_memory_space_constraint(v, pltpu.HBM)
-        for v in (tile_row, tile_col, tile_count, edge_src, edge_dst, features, d_out)
+        for v in (tile_row, tile_col, tile_count, edge_src, edge_dst, features)
     )
     scalars = (tile_row, tile_col, tile_count)
     buffers = [pltpu.SMEM((tiles,), jnp.int32)] * 3
     acc_shape = (rep_count, row_count, BLK, BLK)
     chunk_sems = [pltpu.SemaphoreType.DMA((early // UNROLL,))] * 2
-    acc, own, line, late_src, late_dst = call(
+    acc, line, late_src, late_dst = call(
         first_build_kernel,
         (
             shape(acc_shape, F32),
-            shape((2 * rows, width), BF16),
             shape((far * rows, width), BF16),
             shape((early, slots), jnp.int32),
             shape((early, slots), jnp.int32),
         ),
-        [HBM] * 7,
-        (*scalars, edge_src, edge_dst, held_features, d_out),
+        [HBM] * 6,
+        (*scalars, edge_src, edge_dst, held_features),
         buffers
         + [pltpu.VMEM((early, slots), jnp.int32)] * 2
-        + [pltpu.SemaphoreType.DMA((8,))]
+        + [pltpu.SemaphoreType.DMA((6,))]
         + chunk_sems,
     )
-    acc, line, far_pieces = lax.optimization_barrier((acc, line, far_pieces))
+    acc, line, near, far_pieces = lax.optimization_barrier((acc, line, near, far_pieces))
     for h, piece in enumerate(far_pieces):
         line = lax.dynamic_update_slice(line, piece, ((h + 1) * rows, 0))
-    near = swap(own, "rep", 2)
     pieces = [line] + [swap(line, "row", m) for m in range(1, 4)]
     adjacency = call(
         last_build_kernel,
@@ -332,7 +337,6 @@
         (*scalars, late_src, late_dst, acc),
         [pltpu.VMEM(acc_shape, F32)] + buffers + [pltpu.SemaphoreType.DMA((3,))],
     )
-    adjacency, near, pieces = lax.optimization_barrier((adjacency, near, pieces))
     keep, send = call(
         gather_kernel,
         (shape((half + PAD, width), F32), shape((half + PAD, width), BF16)),
@@ -353,10 +357,24 @@
             shape((middle + PAD, width), F32),
             shape((half + middle + PAD, width), BF16),
         ),
-        [VMEM] * 7,
-        (pair_sum, swap(pair_sum, "rep", 2), own, near, w_self, w_neigh, bias[None, :]),
+        [VMEM] * 9,
+        (
+            pair_sum,
+            swap(pair_sum, "rep", 2),
+            features,
+            near[0],
+            d_out,
+            near[1],
+            w_self,
+            w_neigh,
+            bias[None, :],
+        ),
     )
     back = swap(send, "rep", 1)
+    terms_shape = shape((middle + PAD, width), BF16)
+    terms = call(core_terms_kernel, terms_shape, [VMEM] * 2, (keep, back))
+    terms, back = lax.optimization_barrier((terms, back))
+    far_terms = [terms] + [swap(terms, "row", 4 * h) for h in range(1, far)]
     keep_blocks, *near_msgs = call(
         spread_kernel,
         (shape((far * BLK, width), F32),) + (shape((far * BLK, width), BF16),) * 3,
@@ -364,9 +382,6 @@
         (adjacency, send, back),
     )
     got = [swap(msg, "row", m + 1) for m, msg in enumerate(near_msgs)]
-    terms_shape = shape((middle + PAD, width), BF16)
-    terms = call(core_terms_kernel, terms_shape, [VMEM] * 2, (keep, back))
-    far_terms = [terms] + [swap(terms, "row", 4 * h) for h in range(1, far)]
     terms = call(far_terms_kernel, terms_shape, [VMEM] * far, far_terms)
     near_terms = [terms] + [swap(terms, "row", m) for m in range(1, 4)]
     quarter, grad_bias = call(
@@ -382,14 +397,15 @@
         (keep_blocks, *got),
     )
     got = [swap(msg, "row", 4 * (h + 1)) for h, msg in enumerate(far_msgs)]
-    d_features = call(
+    quarters = [quarter] + [swap(quarter, "rep", m) for m in range(1, 4)]
+    d_features, grad_self, grad_neigh = call(
         finish_kernel,
-        shape((rows, width), F32),
-        [VMEM] * (2 + len(got)),
-        (self_term, keep_block, *got),
-    )
-    grads = lax.all_gather(quarter, "rep", axis=0, tiled=True).astype(F32)
-    return (out, d_features, grads[:width], grads[width:], grad_bias[0])
+        (shape((rows, width), F32),) + (shape((2, middle, width), F32),) * 2,
+        [VMEM] * (6 + len(got)),
+        (self_term, *quarters, keep_block, *got),
+    )
+    grad_self, grad_neigh = (v.reshape(width, width) for v in (grad_self, grad_neigh))
+    return (out, d_features, grad_self, grad_neigh, grad_bias[0])
 
 
 def solution(mesh):

time: 52.8 us -> 52.9 us (level)
  blocking collectives: 5.77 us -> 0 us
  starting transfers between devices: 20.3 us -> 23.6 us
  waiting for transfers between devices: 14.1 us -> 17.3 us
  local copies, waits for them, and re-layouts: 0.84 us -> 0.03 us
    all_gather x1 -> x0, blocking collectives: 5.77 us -> none  [on_device(): grads = lax.all_gather(quarter, 'rep', axis=0, tiled=True).astype(F32)]
    ppermute x16 -> x20, starting transfers between devices: 20.3 us -> 23.6 us  [swap(): lax.ppermute(value, axis, [(i, i ^ bits) for i in range(lax.axis_size(axi...]
    ppermute x16 -> x20, waiting for transfers between devices: 14.1 us -> 17.3 us  [swap(): lax.ppermute(value, axis, [(i, i ^ bits) for i in range(lax.axis_size(axi...]
    slice x1 -> x0, local copies, waits for them, and re-layouts: 0.82 us -> none  [on_device(): return (out, d_features, grads[:width], grads[width:], grad_bias[0])]
  transfers between devices with their start and end apart: 16 -> 20, of which waited for: 8 -> 11; matrix products, arithmetic and copies ran while one was open for 2% -> 0% of each run, Pallas kernels for 15% -> 15%
where the time goes in v6:
time: 52.9 us; the launch traced here: 52.7 us
  starting transfers between devices  23.6 us (45%)
  waiting for transfers between devices  17.3 us (33%)
  Pallas kernels  11 us (21%)
  between operations  0.77 us (1%)
    ppermute x20, starting transfers between devices, swap(): lax.ppermute(value, axis, [(i, i ^ bits) for i in range(lax.axis_size(axi...  23.6 us
    ppermute x20, waiting for transfers between devices, swap(): lax.ppermute(value, axis, [(i, i ^ bits) for i in range(lax.axis_size(axi...  17.3 us
    pallas_call x11, Pallas kernels, call(): pl.pallas_call(kernel, out_shape=out_shape, in_specs=specs, out_specs=[VM...  11 us
  transfers between devices with their start and end apart: 20, of which 11 were waited for; matrix products, arithmetic and copies ran while one was open for 0% of the time, Pallas kernels for 15%

profile of v6, /device:TPU:0, one launch (start us, length us, event | category | flops | bytes accessed | tf_op | source)
XLA Modules:
  0.0 52.7 jit_solution(13974026258653872783)
XLA Ops:
  0.6 3.0 %collective-permute-start.1 = (bf16[128,256]{1,0:T(8,128)(2,1)}, bf16[128,256]{1,0:T(8,128)(2,1)S(1)}, u32[]{:S(2)}, u32[]{:S(2)}) collective-permute-start(bf16[128,256]{1,0:T(8,128)(2,1)} %d_out_ref.1), channel_id=1, source_target_pairs={{0,2},{1,3},{2,0},{3,1},{4,6},{5,7},{6,4},{7,5},{8,10},{9,11},{10,... | collective-permute-start | bytes 196616 | tf_op jit(solution)/shard_map/ppermute | solution.py:300
  3.6 0.1 collective-permute-start
  3.7 3.0 %collective-permute-start.2 = (bf16[128,256]{1,0:T(8,128)(2,1)}, bf16[128,256]{1,0:T(8,128)(2,1)S(1)}, u32[]{:S(2)}, u32[]{:S(2)}) collective-permute-start(bf16[128,256]{1,0:T(8,128)(2,1)} %features_ref.3), channel_id=1, source_target_pairs={{0,16},{4,20},{8,24},{12,28},{16,0},{20,4},{24,8},{28,12},{1,17},{... | collective-permute-start | bytes 196616 | tf_op jit(solution)/shard_map/ppermute | solution.py:300
  6.8 3.6 %shard_map.137 = (f32[4,8,128,128]{3,2,1,0:T(8,128)S(1)}, bf16[256,256]{1,0:T(8,128)(2,1)S(1)}, s32[128,256]{1,0:T(8,128)S(1)}, s32[128,256]{1,0:T(8,128)S(1)}) custom-call(s32[256]{0:T(256)} %row_ref.3, s32[256]{0:T(256)} %col_ref.3, s32[256]{0:T(256)} %count_ref.3, s32[256,256]{1,0:T(8,128)} %src_ref.1, s32[256,256]{1,0:T(8,128)} %dst_ref.1, ...), custom_call_target="tpu_custom_call" | custom-call | tf_op jit(solution)/shard_map/pallas_call | solution.py:279
  10.3 0.0 collective-permute-done.1.near_d_out_ref
  10.3 0.0 collective-permute-done.near_features_ref
  10.4 0.0 collective-permute-done.2
  10.4 2.6 %collective-permute-start.5 = (bf16[256,256]{1,0:T(8,128)(2,1)S(1)}, bf16[256,256]{1,0:T(8,128)(2,1)S(1)}, u32[]{:S(2)}, u32[]{:S(2)}) collective-permute-start(bf16[256,256]{1,0:T(8,128)(2,1)S(1)} %constant_dynamic-update-slice_fusion.refs_0_), channel_id=1, source_target_pairs={{0,12},{4,8},{8,4},{12,0},{16,28},{20,24},{24,20},{28,16},{1,13},{... | collective-permute-start | bytes 393224 | tf_op jit(solution)/shard_map/ppermute | solution.py:300
  13.0 0.5 collective-permute-start.4
  13.4 0.5 collective-permute-start.3
  13.9 0.0 copy-start
  13.9 0.0 copy-start.1
  13.9 0.0 copy-start.2
  13.9 0.0 copy-start.3
  13.9 0.0 copy-start.4
  14.0 3.6 %shard_map.138.adj_ref = bf16[512,1024]{1,0:T(8,128)(2,1)S(1)} custom-call(s32[256]{0:T(256)} %row_ref.3, s32[256]{0:T(256)} %col_ref.3, s32[256]{0:T(256)} %count_ref.3, s32[128,256]{1,0:T(8,128)S(1)} %get-tuple-element.33.src_ref, s32[128,256]{1,0:T(8,128)S(1)} %get-tuple-element.34.dst_ref, f32[4,8,128,128]{3,2,1,0:T(8,128)S(1)} %get-tuple-element.37.half_ref), custom_call_target="tpu_custom_call" | custom-call | tf_op jit(solution)/shard_map/pallas_call | solution.py:279
  17.6 0.0 collective-permute-done.5.refs_3_
  17.6 1.0 %collective-permute-done.4.refs_2_ = bf16[256,256]{1,0:T(8,128)(2,1)S(1)} collective-permute-done((bf16[256,256]{1,0:T(8,128)(2,1)S(1)}, bf16[256,256]{1,0:T(8,128)(2,1)S(1)}, u32[]{:S(2)}, u32[]{:S(2)}) %collective-permute-start.4) | collective-permute-done | bytes 131104 | tf_op jit(solution)/shard_map/ppermute | solution.py:300
  18.6 0.1 collective-permute-done.3.refs_1_
  18.7 0.7 %shard_map.139 = (f32[272,256]{1,0:T(8,128)S(1)}, bf16[272,256]{1,0:T(8,128)(2,1)S(1)}) custom-call(bf16[512,1024]{1,0:T(8,128)(2,1)S(1)} %shard_map.138.adj_ref, bf16[256,256]{1,0:T(8,128)(2,1)S(1)} %constant_dynamic-update-slice_fusion.refs_0_, bf16[256,256]{1,0:T(8,128)(2,1)S(1)} %collective-permute-done.3.refs_1_, ...), custom_call_target="tpu_custom_call" | custom-call | tf_op jit(solution)/shard_map/pallas_call | solution.py:279
  19.4 0.1 collective-permute-start.6
  19.4 1.3 %collective-permute-done.6.got_ref = bf16[272,256]{1,0:T(8,128)(2,1)S(1)} collective-permute-done((bf16[272,256]{1,0:T(8,128)(2,1)S(1)}, bf16[272,256]{1,0:T(8,128)(2,1)S(1)}, u32[]{:S(2)}, u32[]{:S(2)}) %collective-permute-start.6) | collective-permute-done | bytes 139296 | tf_op jit(solution)/shard_map/ppermute | solution.py:300
  20.8 1.6 %collective-permute-start.7 = (bf16[272,256]{1,0:T(8,128)(2,1)S(1)}, bf16[272,256]{1,0:T(8,128)(2,1)S(1)}, u32[]{:S(2)}, u32[]{:S(2)}) collective-permute-start(bf16[272,256]{1,0:T(8,128)(2,1)S(1)} %shard_map.140.pair_ref), channel_id=1, source_target_pairs={{0,2},{1,3},{2,0},{3,1},{4,6},{5,7},{6,4},{7,5},{8,10},{9,11},{10,... | collective-permute-start | bytes 417800 | tf_op jit(solution)/shard_map/ppermute | solution.py:300
  22.4 4.2 %collective-permute-done.7.got_ref = bf16[272,256]{1,0:T(8,128)(2,1)S(1)} collective-permute-done((bf16[272,256]{1,0:T(8,128)(2,1)S(1)}, bf16[272,256]{1,0:T(8,128)(2,1)S(1)}, u32[]{:S(2)}, u32[]{:S(2)}) %collective-permute-start.7) | collective-permute-done | bytes 139296 | tf_op jit(solution)/shard_map/ppermute | solution.py:300
  26.6 0.0 copy-done
  26.6 0.0 copy-done.1
  26.6 0.0 copy-done.2
  26.6 0.0 copy-done.3
  26.6 0.0 copy-done.4
  26.7 1.0 %shard_map.141 = (bf16[128,256]{1,0:T(8,128)(2,1)}, f32[128,256]{1,0:T(8,128)S(1)}, f32[144,256]{1,0:T(8,128)S(1)}, bf16[400,256]{1,0:T(8,128)(2,1)S(1)}) custom-call(bf16[272,256]{1,0:T(8,128)(2,1)S(1)} %shard_map.140.pair_ref, bf16[272,256]{1,0:T(8,128)(2,1)S(1)} %collective-permute-done.7.got_ref, bf16[128,256]{1,0:T(8,128)(2,1)S(1)} %copy-done, ...), custom_call_target="tpu_custom_call" | custom-call | tf_op jit(solution)/shard_map/pallas_call | solution.py:279
  27.7 0.0 collective-permute-start.8
  27.7 1.5 %collective-permute-done.8.got_ref = bf16[400,256]{1,0:T(8,128)(2,1)S(1)} collective-permute-done((bf16[400,256]{1,0:T(8,128)(2,1)S(1)}, bf16[400,256]{1,0:T(8,128)(2,1)S(1)}, u32[]{:S(2)}, u32[]{:S(2)}) %collective-permute-start.8) | collective-permute-done | bytes 204832 | tf_op jit(solution)/shard_map/ppermute | solution.py:300
  29.2 0.5 shard_map.145
  29.7 1.5 %collective-permute-start.16 = (bf16[256,256]{1,0:T(8,128)(2,1)S(1)}, bf16[256,256]{1,0:T(8,128)(2,1)S(1)}, u32[]{:S(2)}, u32[]{:S(2)}) collective-permute-start(bf16[256,256]{1,0:T(8,128)(2,1)S(1)} %get-tuple-element.52), channel_id=1, source_target_pairs={{0,4},{4,0},{8,12},{12,8},{16,20},{20,16},{24,28},{28,24},{1,5},{5... | collective-permute-start | bytes 393224 | tf_op jit(solution)/shard_map/ppermute | solution.py:300
  31.1 1.3 %collective-permute-start.9 = (bf16[144,256]{1,0:T(8,128)(2,1)S(1)}, bf16[144,256]{1,0:T(8,128)(2,1)S(1)}, u32[]{:S(2)}, u32[]{:S(2)}) collective-permute-start(bf16[144,256]{1,0:T(8,128)(2,1)S(1)} %shard_map.142.refs_0_), channel_id=1, source_target_pairs={{0,16},{4,20},{8,24},{12,28},{16,0},{20,4},{24,8},{28,12},{1,17},{... | collective-permute-start | bytes 221192 | tf_op jit(solution)/shard_map/ppermute | solution.py:300
  32.4 1.7 %collective-permute-start.17 = (bf16[256,256]{1,0:T(8,128)(2,1)S(1)}, bf16[256,256]{1,0:T(8,128)(2,1)S(1)}, u32[]{:S(2)}, u32[]{:S(2)}) collective-permute-start(bf16[256,256]{1,0:T(8,128)(2,1)S(1)} %get-tuple-element.53), channel_id=1, source_target_pairs={{0,8},{4,12},{8,0},{12,4},{16,24},{20,28},{24,16},{28,20},{1,9},{5... | collective-permute-start | bytes 393224 | tf_op jit(solution)/shard_map/ppermute | solution.py:300
  34.2 0.6 %collective-permute-start.18 = (bf16[256,256]{1,0:T(8,128)(2,1)S(1)}, bf16[256,256]{1,0:T(8,128)(2,1)S(1)}, u32[]{:S(2)}, u32[]{:S(2)}) collective-permute-start(bf16[256,256]{1,0:T(8,128)(2,1)S(1)} %get-tuple-element.54), channel_id=1, source_target_pairs={{0,12},{4,8},{8,4},{12,0},{16,28},{20,24},{24,20},{28,16},{1,13},{... | collective-permute-start | bytes 393224 | tf_op jit(solution)/shard_map/ppermute | solution.py:300
  34.8 2.8 %collective-permute-done.9.refs_1_ = bf16[144,256]{1,0:T(8,128)(2,1)S(1)} collective-permute-done((bf16[144,256]{1,0:T(8,128)(2,1)S(1)}, bf16[144,256]{1,0:T(8,128)(2,1)S(1)}, u32[]{:S(2)}, u32[]{:S(2)}) %collective-permute-start.9) | collective-permute-done | bytes 73760 | tf_op jit(solution)/shard_map/ppermute | solution.py:300
  37.6 1.4 %collective-permute-start.12 = (bf16[144,256]{1,0:T(8,128)(2,1)S(1)}, bf16[144,256]{1,0:T(8,128)(2,1)S(1)}, u32[]{:S(2)}, u32[]{:S(2)}) collective-permute-start(bf16[144,256]{1,0:T(8,128)(2,1)S(1)} %shard_map.143.refs_0_), channel_id=1, source_target_pairs={{0,12},{4,8},{8,4},{12,0},{16,28},{20,24},{24,20},{28,16},{1,13},{... | collective-permute-start | bytes 221192 | tf_op jit(solution)/shard_map/ppermute | solution.py:300
  38.9 0.8 %collective-permute-start.11 = (bf16[144,256]{1,0:T(8,128)(2,1)S(1)}, bf16[144,256]{1,0:T(8,128)(2,1)S(1)}, u32[]{:S(2)}, u32[]{:S(2)}) collective-permute-start(bf16[144,256]{1,0:T(8,128)(2,1)S(1)} %shard_map.143.refs_0_), channel_id=1, source_target_pairs={{0,8},{4,12},{8,0},{12,4},{16,24},{20,28},{24,16},{28,20},{1,9},{5... | collective-permute-start | bytes 221192 | tf_op jit(solution)/shard_map/ppermute | solution.py:300
  39.7 0.0 collective-permute-done.16.refs_0_
  39.7 1.4 %collective-permute-start.10 = (bf16[144,256]{1,0:T(8,128)(2,1)S(1)}, bf16[144,256]{1,0:T(8,128)(2,1)S(1)}, u32[]{:S(2)}, u32[]{:S(2)}) collective-permute-start(bf16[144,256]{1,0:T(8,128)(2,1)S(1)} %shard_map.143.refs_0_), channel_id=1, source_target_pairs={{0,4},{4,0},{8,12},{12,8},{16,20},{20,16},{24,28},{28,24},{1,5},{5... | collective-permute-start | bytes 221192 | tf_op jit(solution)/shard_map/ppermute | solution.py:300
  41.1 0.0 collective-permute-done.17.refs_1_
  41.1 1.6 %collective-permute-done.18.refs_2_ = bf16[256,256]{1,0:T(8,128)(2,1)S(1)} collective-permute-done((bf16[256,256]{1,0:T(8,128)(2,1)S(1)}, bf16[256,256]{1,0:T(8,128)(2,1)S(1)}, u32[]{:S(2)}, u32[]{:S(2)}) %collective-permute-start.18) | collective-permute-done | bytes 131104 | tf_op jit(solution)/shard_map/ppermute | solution.py:300
  42.7 0.1 shard_map.146
  42.8 1.8 %collective-permute-start.19 = (bf16[128,256]{1,0:T(8,128)(2,1)S(1)}, bf16[128,256]{1,0:T(8,128)(2,1)S(1)}, u32[]{:S(2)}, u32[]{:S(2)}) collective-permute-start(bf16[128,256]{1,0:T(8,128)(2,1)S(1)} %get-tuple-element.56), channel_id=1, source_target_pairs={{0,16},{4,20},{8,24},{12,28},{16,0},{20,4},{24,8},{28,12},{1,17},{... | collective-permute-start | bytes 196616 | tf_op jit(solution)/shard_map/ppermute | solution.py:300
  44.6 0.0 collective-permute-done.12.refs_3_
  44.6 0.9 %collective-permute-done.11.refs_2_ = bf16[144,256]{1,0:T(8,128)(2,1)S(1)} collective-permute-done((bf16[144,256]{1,0:T(8,128)(2,1)S(1)}, bf16[144,256]{1,0:T(8,128)(2,1)S(1)}, u32[]{:S(2)}, u32[]{:S(2)}) %collective-permute-start.11) | collective-permute-done | bytes 73760 | tf_op jit(solution)/shard_map/ppermute | solution.py:300
  45.4 0.0 collective-permute-done.10.refs_1_
  45.4 0.6 %shard_map.144 = (bf16[128,256]{1,0:T(8,128)(2,1)S(1)}, f32[1,256]{1,0:T(1,128)}) custom-call(bf16[144,256]{1,0:T(8,128)(2,1)S(1)} %shard_map.143.refs_0_, bf16[144,256]{1,0:T(8,128)(2,1)S(1)} %collective-permute-done.10.refs_1_, bf16[144,256]{1,0:T(8,128)(2,1)S(1)} %collective-permute-done.11.refs_2_, bf16[144,256]{1,0:T(8,128)(2,1)S(1)} %collective-permute-done.12.refs_3_), custom_call_target="tpu_custom_call" | custom-call | tf_op jit(solution)/shard_map/pallas_call | solution.py:279
  46.0 0.0 collective-permute-start.15
  46.0 1.5 %collective-permute-start.14 = (bf16[128,256]{1,0:T(8,128)(2,1)S(1)}, bf16[128,256]{1,0:T(8,128)(2,1)S(1)}, u32[]{:S(2)}, u32[]{:S(2)}) collective-permute-start(bf16[128,256]{1,0:T(8,128)(2,1)S(1)} %get-tuple-element.49.refs_0_), channel_id=1, source_target_pairs={{0,2},{1,3},{2,0},{3,1},{4,6},{5,7},{6,4},{7,5},{8,10},{9,11},{10,... | collective-permute-start | bytes 196616 | tf_op jit(solution)/shard_map/ppermute | solution.py:300
  47.5 0.4 collective-permute-start.13
  47.9 0.1 collective-permute-done.19.refs_5_
  48.0 2.4 %collective-permute-done.15.refs_3_ = bf16[128,256]{1,0:T(8,128)(2,1)S(1)} collective-permute-done((bf16[128,256]{1,0:T(8,128)(2,1)S(1)}, bf16[128,256]{1,0:T(8,128)(2,1)S(1)}, u32[]{:S(2)}, u32[]{:S(2)}) %collective-permute-start.15) | collective-permute-done | bytes 65568 | tf_op jit(solution)/shard_map/ppermute | solution.py:300
  50.4 1.4 %collective-permute-done.14.refs_2_ = bf16[128,256]{1,0:T(8,128)(2,1)S(1)} collective-permute-done((bf16[128,256]{1,0:T(8,128)(2,1)S(1)}, bf16[128,256]{1,0:T(8,128)(2,1)S(1)}, u32[]{:S(2)}, u32[]{:S(2)}) %collective-permute-start.14) | collective-permute-done | bytes 65568 | tf_op jit(solution)/shard_map/ppermute | solution.py:300
  51.8 0.0 collective-permute-done.13.refs_1_
  51.8 0.9 %shard_map.147 = (f32[128,256]{1,0:T(8,128)}, f32[2,128,256]{2,1,0:T(8,128)}, f32[2,128,256]{2,1,0:T(8,128)}) custom-call(f32[128,256]{1,0:T(8,128)S(1)} %get-tuple-element.45.self_ref, bf16[128,256]{1,0:T(8,128)(2,1)S(1)} %get-tuple-element.49.refs_0_, bf16[128,256]{1,0:T(8,128)(2,1)S(1)} %collective-permute-done.13.refs_1_, ...), custom_call_target="tpu_custom_call" | custom-call | tf_op jit(solution)/shard_map/pallas_call | solution.py:279
  (4 shorter events, 0.1 us)
Async XLA Ops:
  0.6 9.7 %collective-permute-start.1 = (bf16[128,256]{1,0:T(8,128)(2,1)}, bf16[128,256]{1,0:T(8,128)(2,1)S(1)}, u32[]{:S(2)}, u32[]{:S(2)}) collective-permute-start(bf16[128,256]{1,0:T(8,128)(2,1)} %d_out_ref.1), channel_id=1, source_target_pairs={{0,2},{1,3},{2,0},{3,1},{4,6},{5,7},{6,4},{7,5},{8,10},{9,11},{10,... | collective-permute-start | bytes 196616 | tf_op jit(solution)/shard_map/ppermute | solution.py:300
  3.6 6.7 %collective-permute-start = (bf16[128,256]{1,0:T(8,128)(2,1)}, bf16[128,256]{1,0:T(8,128)(2,1)S(1)}, u32[]{:S(2)}, u32[]{:S(2)}) collective-permute-start(bf16[128,256]{1,0:T(8,128)(2,1)} %features_ref.3), channel_id=1, source_target_pairs={{0,2},{1,3},{2,0},{3,1},{4,6},{5,7},{6,4},{7,5},{8,10},{9,11},{10,... | collective-permute-start | bytes 196616 | tf_op jit(solution)/shard_map/ppermute | solution.py:300
  3.7 6.6 %collective-permute-start.2 = (bf16[128,256]{1,0:T(8,128)(2,1)}, bf16[128,256]{1,0:T(8,128)(2,1)S(1)}, u32[]{:S(2)}, u32[]{:S(2)}) collective-permute-start(bf16[128,256]{1,0:T(8,128)(2,1)} %features_ref.3), channel_id=1, source_target_pairs={{0,16},{4,20},{8,24},{12,28},{16,0},{20,4},{24,8},{28,12},{1,17},{... | collective-permute-start | bytes 196616 | tf_op jit(solution)/shard_map/ppermute | solution.py:300
  10.4 7.2 %collective-permute-start.5 = (bf16[256,256]{1,0:T(8,128)(2,1)S(1)}, bf16[256,256]{1,0:T(8,128)(2,1)S(1)}, u32[]{:S(2)}, u32[]{:S(2)}) collective-permute-start(bf16[256,256]{1,0:T(8,128)(2,1)S(1)} %constant_dynamic-update-slice_fusion.refs_0_), channel_id=1, source_target_pairs={{0,12},{4,8},{8,4},{12,0},{16,28},{20,24},{24,20},{28,16},{1,13},{... | collective-permute-start | bytes 393224 | tf_op jit(solution)/shard_map/ppermute | solution.py:300
  13.0 5.6 %collective-permute-start.4 = (bf16[256,256]{1,0:T(8,128)(2,1)S(1)}, bf16[256,256]{1,0:T(8,128)(2,1)S(1)}, u32[]{:S(2)}, u32[]{:S(2)}) collective-permute-start(bf16[256,256]{1,0:T(8,128)(2,1)S(1)} %constant_dynamic-update-slice_fusion.refs_0_), channel_id=1, source_target_pairs={{0,8},{4,12},{8,0},{12,4},{16,24},{20,28},{24,16},{28,20},{1,9},{5... | collective-permute-start | bytes 393224 | tf_op jit(solution)/shard_map/ppermute | solution.py:300
  13.4 5.2 %collective-permute-start.3 = (bf16[256,256]{1,0:T(8,128)(2,1)S(1)}, bf16[256,256]{1,0:T(8,128)(2,1)S(1)}, u32[]{:S(2)}, u32[]{:S(2)}) collective-permute-start(bf16[256,256]{1,0:T(8,128)(2,1)S(1)} %constant_dynamic-update-slice_fusion.refs_0_), channel_id=1, source_target_pairs={{0,4},{4,0},{8,12},{12,8},{16,20},{20,16},{24,28},{28,24},{1,5},{5... | collective-permute-start | bytes 393224 | tf_op jit(solution)/shard_map/ppermute | solution.py:300
  13.9 12.7 %copy-start = (bf16[128,256]{1,0:T(8,128)(2,1)S(1)}, bf16[128,256]{1,0:T(8,128)(2,1)}, u32[]{:S(2)}) copy-start(bf16[128,256]{1,0:T(8,128)(2,1)} %features_ref.3) | copy-start | bytes 196612
  13.9 12.7 %copy-start.1 = (bf16[256,256]{1,0:T(8,128)(2,1)S(1)}, bf16[256,256]{1,0:T(8,128)(2,1)}, u32[]{:S(2)}) copy-start(bf16[256,256]{1,0:T(8,128)(2,1)} %w_self_ref.1) | copy-start | bytes 393220
  13.9 12.7 %copy-start.2 = (bf16[256,256]{1,0:T(8,128)(2,1)S(1)}, bf16[256,256]{1,0:T(8,128)(2,1)}, u32[]{:S(2)}) copy-start(bf16[256,256]{1,0:T(8,128)(2,1)} %w_neigh_ref.1) | copy-start | bytes 393220
  13.9 12.7 %copy-start.3 = (bf16[128,256]{1,0:T(8,128)(2,1)S(1)}, bf16[128,256]{1,0:T(8,128)(2,1)}, u32[]{:S(2)}) copy-start(bf16[128,256]{1,0:T(8,128)(2,1)} %d_out_ref.1) | copy-start | bytes 196612
  13.9 12.7 %copy-start.4 = (f32[256]{0:T(256)S(1)}, f32[256]{0:T(256)}, u32[]{:S(2)}) copy-start(f32[256]{0:T(256)} %param.13) | copy-start | bytes 3076
  19.4 1.4 %collective-permute-start.6 = (bf16[272,256]{1,0:T(8,128)(2,1)S(1)}, bf16[272,256]{1,0:T(8,128)(2,1)S(1)}, u32[]{:S(2)}, u32[]{:S(2)}) collective-permute-start(bf16[272,256]{1,0:T(8,128)(2,1)S(1)} %get-tuple-element.41), channel_id=1, source_target_pairs={{0,1},{1,0},{2,3},{3,2},{4,5},{5,4},{6,7},{7,6},{8,9},{9,8},{10,11... | collective-permute-start | bytes 417800 | tf_op jit(solution)/shard_map/ppermute | solution.py:300
  20.8 5.8 %collective-permute-start.7 = (bf16[272,256]{1,0:T(8,128)(2,1)S(1)}, bf16[272,256]{1,0:T(8,128)(2,1)S(1)}, u32[]{:S(2)}, u32[]{:S(2)}) collective-permute-start(bf16[272,256]{1,0:T(8,128)(2,1)S(1)} %shard_map.140.pair_ref), channel_id=1, source_target_pairs={{0,2},{1,3},{2,0},{3,1},{4,6},{5,7},{6,4},{7,5},{8,10},{9,11},{10,... | collective-permute-start | bytes 417800 | tf_op jit(solution)/shard_map/ppermute | solution.py:300
  27.7 1.5 %collective-permute-start.8 = (bf16[400,256]{1,0:T(8,128)(2,1)S(1)}, bf16[400,256]{1,0:T(8,128)(2,1)S(1)}, u32[]{:S(2)}, u32[]{:S(2)}) collective-permute-start(bf16[400,256]{1,0:T(8,128)(2,1)S(1)} %get-tuple-element.47.sent_ref), channel_id=1, source_target_pairs={{0,1},{1,0},{2,3},{3,2},{4,5},{5,4},{6,7},{7,6},{8,9},{9,8},{10,11... | collective-permute-start | bytes 614408 | tf_op jit(solution)/shard_map/ppermute | solution.py:300
  29.7 10.0 %collective-permute-start.16 = (bf16[256,256]{1,0:T(8,128)(2,1)S(1)}, bf16[256,256]{1,0:T(8,128)(2,1)S(1)}, u32[]{:S(2)}, u32[]{:S(2)}) collective-permute-start(bf16[256,256]{1,0:T(8,128)(2,1)S(1)} %get-tuple-element.52), channel_id=1, source_target_pairs={{0,4},{4,0},{8,12},{12,8},{16,20},{20,16},{24,28},{28,24},{1,5},{5... | collective-permute-start | bytes 393224 | tf_op jit(solution)/shard_map/ppermute | solution.py:300
  31.1 6.4 %collective-permute-start.9 = (bf16[144,256]{1,0:T(8,128)(2,1)S(1)}, bf16[144,256]{1,0:T(8,128)(2,1)S(1)}, u32[]{:S(2)}, u32[]{:S(2)}) collective-permute-start(bf16[144,256]{1,0:T(8,128)(2,1)S(1)} %shard_map.142.refs_0_), channel_id=1, source_target_pairs={{0,16},{4,20},{8,24},{12,28},{16,0},{20,4},{24,8},{28,12},{1,17},{... | collective-permute-start | bytes 221192 | tf_op jit(solution)/shard_map/ppermute | solution.py:300
  32.4 8.7 %collective-permute-start.17 = (bf16[256,256]{1,0:T(8,128)(2,1)S(1)}, bf16[256,256]{1,0:T(8,128)(2,1)S(1)}, u32[]{:S(2)}, u32[]{:S(2)}) collective-permute-start(bf16[256,256]{1,0:T(8,128)(2,1)S(1)} %get-tuple-element.53), channel_id=1, source_target_pairs={{0,8},{4,12},{8,0},{12,4},{16,24},{20,28},{24,16},{28,20},{1,9},{5... | collective-permute-start | bytes 393224 | tf_op jit(solution)/shard_map/ppermute | solution.py:300
  34.2 8.6 %collective-permute-start.18 = (bf16[256,256]{1,0:T(8,128)(2,1)S(1)}, bf16[256,256]{1,0:T(8,128)(2,1)S(1)}, u32[]{:S(2)}, u32[]{:S(2)}) collective-permute-start(bf16[256,256]{1,0:T(8,128)(2,1)S(1)} %get-tuple-element.54), channel_id=1, source_target_pairs={{0,12},{4,8},{8,4},{12,0},{16,28},{20,24},{24,20},{28,16},{1,13},{... | collective-permute-start | bytes 393224 | tf_op jit(solution)/shard_map/ppermute | solution.py:300
  37.6 7.0 %collective-permute-start.12 = (bf16[144,256]{1,0:T(8,128)(2,1)S(1)}, bf16[144,256]{1,0:T(8,128)(2,1)S(1)}, u32[]{:S(2)}, u32[]{:S(2)}) collective-permute-start(bf16[144,256]{1,0:T(8,128)(2,1)S(1)} %shard_map.143.refs_0_), channel_id=1, source_target_pairs={{0,12},{4,8},{8,4},{12,0},{16,28},{20,24},{24,20},{28,16},{1,13},{... | collective-permute-start | bytes 221192 | tf_op jit(solution)/shard_map/ppermute | solution.py:300
  38.9 6.5 %collective-permute-start.11 = (bf16[144,256]{1,0:T(8,128)(2,1)S(1)}, bf16[144,256]{1,0:T(8,128)(2,1)S(1)}, u32[]{:S(2)}, u32[]{:S(2)}) collective-permute-start(bf16[144,256]{1,0:T(8,128)(2,1)S(1)} %shard_map.143.refs_0_), channel_id=1, source_target_pairs={{0,8},{4,12},{8,0},{12,4},{16,24},{20,28},{24,16},{28,20},{1,9},{5... | collective-permute-start | bytes 221192 | tf_op jit(solution)/shard_map/ppermute | solution.py:300
  39.7 5.7 %collective-permute-start.10 = (bf16[144,256]{1,0:T(8,128)(2,1)S(1)}, bf16[144,256]{1,0:T(8,128)(2,1)S(1)}, u32[]{:S(2)}, u32[]{:S(2)}) collective-permute-start(bf16[144,256]{1,0:T(8,128)(2,1)S(1)} %shard_map.143.refs_0_), channel_id=1, source_target_pairs={{0,4},{4,0},{8,12},{12,8},{16,20},{20,16},{24,28},{28,24},{1,5},{5... | collective-permute-start | bytes 221192 | tf_op jit(solution)/shard_map/ppermute | solution.py:300
  42.8 5.2 %collective-permute-start.19 = (bf16[128,256]{1,0:T(8,128)(2,1)S(1)}, bf16[128,256]{1,0:T(8,128)(2,1)S(1)}, u32[]{:S(2)}, u32[]{:S(2)}) collective-permute-start(bf16[128,256]{1,0:T(8,128)(2,1)S(1)} %get-tuple-element.56), channel_id=1, source_target_pairs={{0,16},{4,20},{8,24},{12,28},{16,0},{20,4},{24,8},{28,12},{1,17},{... | collective-permute-start | bytes 196616 | tf_op jit(solution)/shard_map/ppermute | solution.py:300
  46.0 4.4 %collective-permute-start.15 = (bf16[128,256]{1,0:T(8,128)(2,1)S(1)}, bf16[128,256]{1,0:T(8,128)(2,1)S(1)}, u32[]{:S(2)}, u32[]{:S(2)}) collective-permute-start(bf16[128,256]{1,0:T(8,128)(2,1)S(1)} %get-tuple-element.49.refs_0_), channel_id=1, source_target_pairs={{0,3},{1,2},{2,1},{3,0},{4,7},{5,6},{6,5},{7,4},{8,11},{9,10},{10,... | collective-permute-start | bytes 196616 | tf_op jit(solution)/shard_map/ppermute | solution.py:300
  46.0 5.8 %collective-permute-start.14 = (bf16[128,256]{1,0:T(8,128)(2,1)S(1)}, bf16[128,256]{1,0:T(8,128)(2,1)S(1)}, u32[]{:S(2)}, u32[]{:S(2)}) collective-permute-start(bf16[128,256]{1,0:T(8,128)(2,1)S(1)} %get-tuple-element.49.refs_0_), channel_id=1, source_target_pairs={{0,2},{1,3},{2,0},{3,1},{4,6},{5,7},{6,4},{7,5},{8,10},{9,11},{10,... | collective-permute-start | bytes 196616 | tf_op jit(solution)/shard_map/ppermute | solution.py:300
  47.5 4.3 %collective-permute-start.13 = (bf16[128,256]{1,0:T(8,128)(2,1)S(1)}, bf16[128,256]{1,0:T(8,128)(2,1)S(1)}, u32[]{:S(2)}, u32[]{:S(2)}) collective-permute-start(bf16[128,256]{1,0:T(8,128)(2,1)S(1)} %get-tuple-element.49.refs_0_), channel_id=1, source_target_pairs={{0,1},{1,0},{2,3},{3,2},{4,5},{5,4},{6,7},{7,6},{8,9},{9,8},{10,11... | collective-permute-start | bytes 196616 | tf_op jit(solution)/shard_map/ppermute | solution.py:300

commit v7 on v6

--- a/solution.py
+++ b/solution.py
@@ -11,6 +11,7 @@
 PAD = 16
 BF16 = jnp.bfloat16
 F32 = jnp.float32
+HOT = jnp.float8_e4m3fn
 UNROLL = 64
 VMEM = pl.BlockSpec(memory_space=pltpu.VMEM)
 HBM = pl.BlockSpec(memory_space=pltpu.HBM)
@@ -62,8 +63,8 @@
         for u in range(UNROLL):
             tile = first + base + u
             live = jnp.where(slot < count_ref[tile], dst[u : u + 1], -1)
-            dst_hot = jnp.where(line == live.astype(BF16), one, zero)
-            src_hot = jnp.where(line == src[u : u + 1].astype(BF16), one, zero)
+            dst_hot = jnp.where(line == live.astype(BF16), one, zero).astype(HOT)
+            src_hot = jnp.where(line == src[u : u + 1].astype(BF16), one, zero).astype(HOT)
             part = lax.dot_general(
                 dst_hot, src_hot, (((1,), (1,)), ((), ())), preferred_element_type=F32
             )
@@ -381,7 +382,7 @@
         [VMEM] * 3,
         (adjacency, send, back),
     )
-    got = [swap(msg, "row", m + 1) for m, msg in enumerate(near_msgs)]
+    got = [swap(msg, "row", m + 1) for m, msg in enumerate(near_msgs)][::-1]
     terms = call(far_terms_kernel, terms_shape, [VMEM] * far, far_terms)
     near_terms = [terms] + [swap(terms, "row", m) for m in range(1, 4)]
     quarter, grad_bias = call(

time: 52.9 us -> 52.4 us (level)
  starting transfers between devices: 23.6 us -> 25 us
  waiting for transfers between devices: 17.3 us -> 16 us
  Pallas kernels: 11 us -> 10.4 us
    ppermute x20, starting transfers between devices: 23.6 us -> 25 us  [swap(): lax.ppermute(value, axis, [(i, i ^ bits) for i in range(lax.axis_size(axi...]
    ppermute x20, waiting for transfers between devices: 17.3 us -> 16 us  [swap(): lax.ppermute(value, axis, [(i, i ^ bits) for i in range(lax.axis_size(axi...]
    pallas_call x11, Pallas kernels: 11 us -> 10.4 us  [call(): pl.pallas_call(kernel, out_shape=out_shape, in_specs=specs, out_specs=[VM...]
  transfers between devices with their start and end apart: 20 -> 20, of which waited for: 11 -> 9; matrix products, arithmetic and copies ran while one was open for 0% -> 0% of each run, Pallas kernels for 15% -> 14%
where the time goes in v7:
time: 52.4 us; the launch traced here: 52.2 us
  starting transfers between devices  25 us (48%)
  waiting for transfers between devices  16 us (31%)
  Pallas kernels  10.4 us (20%)
  between operations  0.77 us (1%)
    ppermute x20, starting transfers between devices, swap(): lax.ppermute(value, axis, [(i, i ^ bits) for i in range(lax.axis_size(axi...  25 us
    ppermute x20, waiting for transfers between devices, swap(): lax.ppermute(value, axis, [(i, i ^ bits) for i in range(lax.axis_size(axi...  16 us
    pallas_call x11, Pallas kernels, call(): pl.pallas_call(kernel, out_shape=out_shape, in_specs=specs, out_specs=[VM...  10.4 us
  transfers between devices with their start and end apart: 20, of which 9 were waited for; matrix products, arithmetic and copies ran while one was open for 0% of the time, Pallas kernels for 14%

profile of v7, /device:TPU:0, one launch (start us, length us, event | category | flops | bytes accessed | tf_op | source)
XLA Modules:
  0.0 52.2 jit_solution(334223575780965773)
XLA Ops:
  0.6 3.0 %collective-permute-start.1 = (bf16[128,256]{1,0:T(8,128)(2,1)}, bf16[128,256]{1,0:T(8,128)(2,1)S(1)}, u32[]{:S(2)}, u32[]{:S(2)}) collective-permute-start(bf16[128,256]{1,0:T(8,128)(2,1)} %d_out_ref.1), channel_id=1, source_target_pairs={{0,2},{1,3},{2,0},{3,1},{4,6},{5,7},{6,4},{7,5},{8,10},{9,11},{10,... | collective-permute-start | bytes 196616 | tf_op jit(solution)/shard_map/ppermute | solution.py:301
  3.6 0.1 collective-permute-start
  3.7 3.0 %collective-permute-start.2 = (bf16[128,256]{1,0:T(8,128)(2,1)}, bf16[128,256]{1,0:T(8,128)(2,1)S(1)}, u32[]{:S(2)}, u32[]{:S(2)}) collective-permute-start(bf16[128,256]{1,0:T(8,128)(2,1)} %features_ref.3), channel_id=1, source_target_pairs={{0,16},{4,20},{8,24},{12,28},{16,0},{20,4},{24,8},{28,12},{1,17},{... | collective-permute-start | bytes 196616 | tf_op jit(solution)/shard_map/ppermute | solution.py:301
  6.8 3.3 %shard_map.137 = (f32[4,8,128,128]{3,2,1,0:T(8,128)S(1)}, bf16[256,256]{1,0:T(8,128)(2,1)S(1)}, s32[128,256]{1,0:T(8,128)S(1)}, s32[128,256]{1,0:T(8,128)S(1)}) custom-call(s32[256]{0:T(256)} %row_ref.3, s32[256]{0:T(256)} %col_ref.3, s32[256]{0:T(256)} %count_ref.3, s32[256,256]{1,0:T(8,128)} %src_ref.1, s32[256,256]{1,0:T(8,128)} %dst_ref.1, ...), custom_call_target="tpu_custom_call" | custom-call | tf_op jit(solution)/shard_map/pallas_call | solution.py:280
  10.0 0.0 collective-permute-done.1.near_d_out_ref
  10.0 0.0 collective-permute-done.near_features_ref
  10.1 0.0 collective-permute-done.2
  10.1 2.6 %collective-permute-start.5 = (bf16[256,256]{1,0:T(8,128)(2,1)S(1)}, bf16[256,256]{1,0:T(8,128)(2,1)S(1)}, u32[]{:S(2)}, u32[]{:S(2)}) collective-permute-start(bf16[256,256]{1,0:T(8,128)(2,1)S(1)} %constant_dynamic-update-slice_fusion.refs_0_), channel_id=1, source_target_pairs={{0,12},{4,8},{8,4},{12,0},{16,28},{20,24},{24,20},{28,16},{1,13},{... | collective-permute-start | bytes 393224 | tf_op jit(solution)/shard_map/ppermute | solution.py:301
  12.7 0.4 collective-permute-start.4
  13.1 0.5 collective-permute-start.3
  13.6 0.0 copy-start
  13.6 0.0 copy-start.1
  13.6 0.0 copy-start.2
  13.6 0.0 copy-start.3
  13.6 0.0 copy-start.4
  13.7 3.3 %shard_map.138.adj_ref = bf16[512,1024]{1,0:T(8,128)(2,1)S(1)} custom-call(s32[256]{0:T(256)} %row_ref.3, s32[256]{0:T(256)} %col_ref.3, s32[256]{0:T(256)} %count_ref.3, s32[128,256]{1,0:T(8,128)S(1)} %get-tuple-element.33.src_ref, s32[128,256]{1,0:T(8,128)S(1)} %get-tuple-element.34.dst_ref, f32[4,8,128,128]{3,2,1,0:T(8,128)S(1)} %get-tuple-element.37.half_ref), custom_call_target="tpu_custom_call" | custom-call | tf_op jit(solution)/shard_map/pallas_call | solution.py:280
  17.0 0.0 collective-permute-done.5.refs_3_
  17.0 1.3 %collective-permute-done.4.refs_2_ = bf16[256,256]{1,0:T(8,128)(2,1)S(1)} collective-permute-done((bf16[256,256]{1,0:T(8,128)(2,1)S(1)}, bf16[256,256]{1,0:T(8,128)(2,1)S(1)}, u32[]{:S(2)}, u32[]{:S(2)}) %collective-permute-start.4) | collective-permute-done | bytes 131104 | tf_op jit(solution)/shard_map/ppermute | solution.py:301
  18.3 0.1 collective-permute-done.3.refs_1_
  18.4 0.7 %shard_map.139 = (f32[272,256]{1,0:T(8,128)S(1)}, bf16[272,256]{1,0:T(8,128)(2,1)S(1)}) custom-call(bf16[512,1024]{1,0:T(8,128)(2,1)S(1)} %shard_map.138.adj_ref, bf16[256,256]{1,0:T(8,128)(2,1)S(1)} %constant_dynamic-update-slice_fusion.refs_0_, bf16[256,256]{1,0:T(8,128)(2,1)S(1)} %collective-permute-done.3.refs_1_, ...), custom_call_target="tpu_custom_call" | custom-call | tf_op jit(solution)/shard_map/pallas_call | solution.py:280
  19.1 0.1 collective-permute-start.6
  19.1 1.3 %collective-permute-done.6.got_ref = bf16[272,256]{1,0:T(8,128)(2,1)S(1)} collective-permute-done((bf16[272,256]{1,0:T(8,128)(2,1)S(1)}, bf16[272,256]{1,0:T(8,128)(2,1)S(1)}, u32[]{:S(2)}, u32[]{:S(2)}) %collective-permute-start.6) | collective-permute-done | bytes 139296 | tf_op jit(solution)/shard_map/ppermute | solution.py:301
  20.5 1.6 %collective-permute-start.7 = (bf16[272,256]{1,0:T(8,128)(2,1)S(1)}, bf16[272,256]{1,0:T(8,128)(2,1)S(1)}, u32[]{:S(2)}, u32[]{:S(2)}) collective-permute-start(bf16[272,256]{1,0:T(8,128)(2,1)S(1)} %shard_map.140.pair_ref), channel_id=1, source_target_pairs={{0,2},{1,3},{2,0},{3,1},{4,6},{5,7},{6,4},{7,5},{8,10},{9,11},{10,... | collective-permute-start | bytes 417800 | tf_op jit(solution)/shard_map/ppermute | solution.py:301
  22.1 4.2 %collective-permute-done.7.got_ref = bf16[272,256]{1,0:T(8,128)(2,1)S(1)} collective-permute-done((bf16[272,256]{1,0:T(8,128)(2,1)S(1)}, bf16[272,256]{1,0:T(8,128)(2,1)S(1)}, u32[]{:S(2)}, u32[]{:S(2)}) %collective-permute-start.7) | collective-permute-done | bytes 139296 | tf_op jit(solution)/shard_map/ppermute | solution.py:301
  26.3 0.0 copy-done
  26.3 0.0 copy-done.1
  26.3 0.0 copy-done.2
  26.3 0.0 copy-done.3
  26.3 0.0 copy-done.4
  26.4 1.0 %shard_map.141 = (bf16[128,256]{1,0:T(8,128)(2,1)}, f32[128,256]{1,0:T(8,128)S(1)}, f32[144,256]{1,0:T(8,128)S(1)}, bf16[400,256]{1,0:T(8,128)(2,1)S(1)}) custom-call(bf16[272,256]{1,0:T(8,128)(2,1)S(1)} %shard_map.140.pair_ref, bf16[272,256]{1,0:T(8,128)(2,1)S(1)} %collective-permute-done.7.got_ref, bf16[128,256]{1,0:T(8,128)(2,1)S(1)} %copy-done, ...), custom_call_target="tpu_custom_call" | custom-call | tf_op jit(solution)/shard_map/pallas_call | solution.py:280
  27.4 0.0 collective-permute-start.8
  27.4 1.5 %collective-permute-done.8.got_ref = bf16[400,256]{1,0:T(8,128)(2,1)S(1)} collective-permute-done((bf16[400,256]{1,0:T(8,128)(2,1)S(1)}, bf16[400,256]{1,0:T(8,128)(2,1)S(1)}, u32[]{:S(2)}, u32[]{:S(2)}) %collective-permute-start.8) | collective-permute-done | bytes 204832 | tf_op jit(solution)/shard_map/ppermute | solution.py:301
  28.9 0.5 shard_map.145
  29.4 2.5 %collective-permute-start.16 = (bf16[256,256]{1,0:T(8,128)(2,1)S(1)}, bf16[256,256]{1,0:T(8,128)(2,1)S(1)}, u32[]{:S(2)}, u32[]{:S(2)}) collective-permute-start(bf16[256,256]{1,0:T(8,128)(2,1)S(1)} %get-tuple-element.52), channel_id=1, source_target_pairs={{0,12},{4,8},{8,4},{12,0},{16,28},{20,24},{24,20},{28,16},{1,13},{... | collective-permute-start | bytes 393224 | tf_op jit(solution)/shard_map/ppermute | solution.py:301
  31.8 1.8 %collective-permute-start.9 = (bf16[144,256]{1,0:T(8,128)(2,1)S(1)}, bf16[144,256]{1,0:T(8,128)(2,1)S(1)}, u32[]{:S(2)}, u32[]{:S(2)}) collective-permute-start(bf16[144,256]{1,0:T(8,128)(2,1)S(1)} %shard_map.142.refs_0_), channel_id=1, source_target_pairs={{0,16},{4,20},{8,24},{12,28},{16,0},{20,4},{24,8},{28,12},{1,17},{... | collective-permute-start | bytes 221192 | tf_op jit(solution)/shard_map/ppermute | solution.py:301
  33.6 0.3 collective-permute-start.17
  33.9 0.9 %collective-permute-start.18 = (bf16[256,256]{1,0:T(8,128)(2,1)S(1)}, bf16[256,256]{1,0:T(8,128)(2,1)S(1)}, u32[]{:S(2)}, u32[]{:S(2)}) collective-permute-start(bf16[256,256]{1,0:T(8,128)(2,1)S(1)} %get-tuple-element.54), channel_id=1, source_target_pairs={{0,4},{4,0},{8,12},{12,8},{16,20},{20,16},{24,28},{28,24},{1,5},{5... | collective-permute-start | bytes 393224 | tf_op jit(solution)/shard_map/ppermute | solution.py:301
  34.8 3.1 %collective-permute-done.9.refs_1_ = bf16[144,256]{1,0:T(8,128)(2,1)S(1)} collective-permute-done((bf16[144,256]{1,0:T(8,128)(2,1)S(1)}, bf16[144,256]{1,0:T(8,128)(2,1)S(1)}, u32[]{:S(2)}, u32[]{:S(2)}) %collective-permute-start.9) | collective-permute-done | bytes 73760 | tf_op jit(solution)/shard_map/ppermute | solution.py:301
  37.9 2.3 %collective-permute-start.12 = (bf16[144,256]{1,0:T(8,128)(2,1)S(1)}, bf16[144,256]{1,0:T(8,128)(2,1)S(1)}, u32[]{:S(2)}, u32[]{:S(2)}) collective-permute-start(bf16[144,256]{1,0:T(8,128)(2,1)S(1)} %shard_map.143.refs_0_), channel_id=1, source_target_pairs={{0,12},{4,8},{8,4},{12,0},{16,28},{20,24},{24,20},{28,16},{1,13},{... | collective-permute-start | bytes 221192 | tf_op jit(solution)/shard_map/ppermute | solution.py:301
  40.2 0.0 collective-permute-start.11
  40.2 0.0 collective-permute-done.16.refs_0_
  40.2 1.2 %collective-permute-start.10 = (bf16[144,256]{1,0:T(8,128)(2,1)S(1)}, bf16[144,256]{1,0:T(8,128)(2,1)S(1)}, u32[]{:S(2)}, u32[]{:S(2)}) collective-permute-start(bf16[144,256]{1,0:T(8,128)(2,1)S(1)} %shard_map.143.refs_0_), channel_id=1, source_target_pairs={{0,4},{4,0},{8,12},{12,8},{16,20},{20,16},{24,28},{28,24},{1,5},{5... | collective-permute-start | bytes 221192 | tf_op jit(solution)/shard_map/ppermute | solution.py:301
  41.4 0.0 collective-permute-done.17.refs_1_
  41.4 0.0 collective-permute-done.18.refs_2_
  41.4 0.1 shard_map.146
  41.5 2.9 %collective-permute-start.19 = (bf16[128,256]{1,0:T(8,128)(2,1)S(1)}, bf16[128,256]{1,0:T(8,128)(2,1)S(1)}, u32[]{:S(2)}, u32[]{:S(2)}) collective-permute-start(bf16[128,256]{1,0:T(8,128)(2,1)S(1)} %get-tuple-element.56), channel_id=1, source_target_pairs={{0,16},{4,20},{8,24},{12,28},{16,0},{20,4},{24,8},{28,12},{1,17},{... | collective-permute-start | bytes 196616 | tf_op jit(solution)/shard_map/ppermute | solution.py:301
  44.4 0.0 collective-permute-done.12.refs_3_
  44.4 0.6 %collective-permute-done.11.refs_2_ = bf16[144,256]{1,0:T(8,128)(2,1)S(1)} collective-permute-done((bf16[144,256]{1,0:T(8,128)(2,1)S(1)}, bf16[144,256]{1,0:T(8,128)(2,1)S(1)}, u32[]{:S(2)}, u32[]{:S(2)}) %collective-permute-start.11) | collective-permute-done | bytes 73760 | tf_op jit(solution)/shard_map/ppermute | solution.py:301
  45.0 0.0 collective-permute-done.10.refs_1_
  45.0 0.6 %shard_map.144 = (bf16[128,256]{1,0:T(8,128)(2,1)S(1)}, f32[1,256]{1,0:T(1,128)}) custom-call(bf16[144,256]{1,0:T(8,128)(2,1)S(1)} %shard_map.143.refs_0_, bf16[144,256]{1,0:T(8,128)(2,1)S(1)} %collective-permute-done.10.refs_1_, bf16[144,256]{1,0:T(8,128)(2,1)S(1)} %collective-permute-done.11.refs_2_, bf16[144,256]{1,0:T(8,128)(2,1)S(1)} %collective-permute-done.12.refs_3_), custom_call_target="tpu_custom_call" | custom-call | tf_op jit(solution)/shard_map/pallas_call | solution.py:280
  45.6 0.0 collective-permute-start.15
  45.6 1.5 %collective-permute-start.14 = (bf16[128,256]{1,0:T(8,128)(2,1)S(1)}, bf16[128,256]{1,0:T(8,128)(2,1)S(1)}, u32[]{:S(2)}, u32[]{:S(2)}) collective-permute-start(bf16[128,256]{1,0:T(8,128)(2,1)S(1)} %get-tuple-element.49.refs_0_), channel_id=1, source_target_pairs={{0,2},{1,3},{2,0},{3,1},{4,6},{5,7},{6,4},{7,5},{8,10},{9,11},{10,... | collective-permute-start | bytes 196616 | tf_op jit(solution)/shard_map/ppermute | solution.py:301
  47.1 0.3 collective-permute-start.13
  47.4 0.0 collective-permute-done.19.refs_5_
  47.4 2.5 %collective-permute-done.15.refs_3_ = bf16[128,256]{1,0:T(8,128)(2,1)S(1)} collective-permute-done((bf16[128,256]{1,0:T(8,128)(2,1)S(1)}, bf16[128,256]{1,0:T(8,128)(2,1)S(1)}, u32[]{:S(2)}, u32[]{:S(2)}) %collective-permute-start.15) | collective-permute-done | bytes 65568 | tf_op jit(solution)/shard_map/ppermute | solution.py:301
  49.9 1.5 %collective-permute-done.14.refs_2_ = bf16[128,256]{1,0:T(8,128)(2,1)S(1)} collective-permute-done((bf16[128,256]{1,0:T(8,128)(2,1)S(1)}, bf16[128,256]{1,0:T(8,128)(2,1)S(1)}, u32[]{:S(2)}, u32[]{:S(2)}) %collective-permute-start.14) | collective-permute-done | bytes 65568 | tf_op jit(solution)/shard_map/ppermute | solution.py:301
  51.4 0.0 collective-permute-done.13.refs_1_
  51.4 0.9 %shard_map.147 = (f32[128,256]{1,0:T(8,128)}, f32[2,128,256]{2,1,0:T(8,128)}, f32[2,128,256]{2,1,0:T(8,128)}) custom-call(f32[128,256]{1,0:T(8,128)S(1)} %get-tuple-element.45.self_ref, bf16[128,256]{1,0:T(8,128)(2,1)S(1)} %get-tuple-element.49.refs_0_, bf16[128,256]{1,0:T(8,128)(2,1)S(1)} %collective-permute-done.13.refs_1_, ...), custom_call_target="tpu_custom_call" | custom-call | tf_op jit(solution)/shard_map/pallas_call | solution.py:280
  (4 shorter events, 0.1 us)
Async XLA Ops:
  0.6 9.4 %collective-permute-start.1 = (bf16[128,256]{1,0:T(8,128)(2,1)}, bf16[128,256]{1,0:T(8,128)(2,1)S(1)}, u32[]{:S(2)}, u32[]{:S(2)}) collective-permute-start(bf16[128,256]{1,0:T(8,128)(2,1)} %d_out_ref.1), channel_id=1, source_target_pairs={{0,2},{1,3},{2,0},{3,1},{4,6},{5,7},{6,4},{7,5},{8,10},{9,11},{10,... | collective-permute-start | bytes 196616 | tf_op jit(solution)/shard_map/ppermute | solution.py:301
  3.6 6.4 %collective-permute-start = (bf16[128,256]{1,0:T(8,128)(2,1)}, bf16[128,256]{1,0:T(8,128)(2,1)S(1)}, u32[]{:S(2)}, u32[]{:S(2)}) collective-permute-start(bf16[128,256]{1,0:T(8,128)(2,1)} %features_ref.3), channel_id=1, source_target_pairs={{0,2},{1,3},{2,0},{3,1},{4,6},{5,7},{6,4},{7,5},{8,10},{9,11},{10,... | collective-permute-start | bytes 196616 | tf_op jit(solution)/shard_map/ppermute | solution.py:301
  3.7 6.3 %collective-permute-start.2 = (bf16[128,256]{1,0:T(8,128)(2,1)}, bf16[128,256]{1,0:T(8,128)(2,1)S(1)}, u32[]{:S(2)}, u32[]{:S(2)}) collective-permute-start(bf16[128,256]{1,0:T(8,128)(2,1)} %features_ref.3), channel_id=1, source_target_pairs={{0,16},{4,20},{8,24},{12,28},{16,0},{20,4},{24,8},{28,12},{1,17},{... | collective-permute-start | bytes 196616 | tf_op jit(solution)/shard_map/ppermute | solution.py:301
  10.1 6.9 %collective-permute-start.5 = (bf16[256,256]{1,0:T(8,128)(2,1)S(1)}, bf16[256,256]{1,0:T(8,128)(2,1)S(1)}, u32[]{:S(2)}, u32[]{:S(2)}) collective-permute-start(bf16[256,256]{1,0:T(8,128)(2,1)S(1)} %constant_dynamic-update-slice_fusion.refs_0_), channel_id=1, source_target_pairs={{0,12},{4,8},{8,4},{12,0},{16,28},{20,24},{24,20},{28,16},{1,13},{... | collective-permute-start | bytes 393224 | tf_op jit(solution)/shard_map/ppermute | solution.py:301
  12.7 5.6 %collective-permute-start.4 = (bf16[256,256]{1,0:T(8,128)(2,1)S(1)}, bf16[256,256]{1,0:T(8,128)(2,1)S(1)}, u32[]{:S(2)}, u32[]{:S(2)}) collective-permute-start(bf16[256,256]{1,0:T(8,128)(2,1)S(1)} %constant_dynamic-update-slice_fusion.refs_0_), channel_id=1, source_target_pairs={{0,8},{4,12},{8,0},{12,4},{16,24},{20,28},{24,16},{28,20},{1,9},{5... | collective-permute-start | bytes 393224 | tf_op jit(solution)/shard_map/ppermute | solution.py:301
  13.1 5.2 %collective-permute-start.3 = (bf16[256,256]{1,0:T(8,128)(2,1)S(1)}, bf16[256,256]{1,0:T(8,128)(2,1)S(1)}, u32[]{:S(2)}, u32[]{:S(2)}) collective-permute-start(bf16[256,256]{1,0:T(8,128)(2,1)S(1)} %constant_dynamic-update-slice_fusion.refs_0_), channel_id=1, source_target_pairs={{0,4},{4,0},{8,12},{12,8},{16,20},{20,16},{24,28},{28,24},{1,5},{5... | collective-permute-start | bytes 393224 | tf_op jit(solution)/shard_map/ppermute | solution.py:301
  13.6 12.7 %copy-start = (bf16[128,256]{1,0:T(8,128)(2,1)S(1)}, bf16[128,256]{1,0:T(8,128)(2,1)}, u32[]{:S(2)}) copy-start(bf16[128,256]{1,0:T(8,128)(2,1)} %features_ref.3) | copy-start | bytes 196612
  13.6 12.7 %copy-start.1 = (bf16[256,256]{1,0:T(8,128)(2,1)S(1)}, bf16[256,256]{1,0:T(8,128)(2,1)}, u32[]{:S(2)}) copy-start(bf16[256,256]{1,0:T(8,128)(2,1)} %w_self_ref.1) | copy-start | bytes 393220
  13.6 12.7 %copy-start.2 = (bf16[256,256]{1,0:T(8,128)(2,1)S(1)}, bf16[256,256]{1,0:T(8,128)(2,1)}, u32[]{:S(2)}) copy-start(bf16[256,256]{1,0:T(8,128)(2,1)} %w_neigh_ref.1) | copy-start | bytes 393220
  13.6 12.7 %copy-start.3 = (bf16[128,256]{1,0:T(8,128)(2,1)S(1)}, bf16[128,256]{1,0:T(8,128)(2,1)}, u32[]{:S(2)}) copy-start(bf16[128,256]{1,0:T(8,128)(2,1)} %d_out_ref.1) | copy-start | bytes 196612
  13.6 12.7 %copy-start.4 = (f32[256]{0:T(256)S(1)}, f32[256]{0:T(256)}, u32[]{:S(2)}) copy-start(f32[256]{0:T(256)} %param.13) | copy-start | bytes 3076
  19.1 1.4 %collective-permute-start.6 = (bf16[272,256]{1,0:T(8,128)(2,1)S(1)}, bf16[272,256]{1,0:T(8,128)(2,1)S(1)}, u32[]{:S(2)}, u32[]{:S(2)}) collective-permute-start(bf16[272,256]{1,0:T(8,128)(2,1)S(1)} %get-tuple-element.41), channel_id=1, source_target_pairs={{0,1},{1,0},{2,3},{3,2},{4,5},{5,4},{6,7},{7,6},{8,9},{9,8},{10,11... | collective-permute-start | bytes 417800 | tf_op jit(solution)/shard_map/ppermute | solution.py:301
  20.5 5.8 %collective-permute-start.7 = (bf16[272,256]{1,0:T(8,128)(2,1)S(1)}, bf16[272,256]{1,0:T(8,128)(2,1)S(1)}, u32[]{:S(2)}, u32[]{:S(2)}) collective-permute-start(bf16[272,256]{1,0:T(8,128)(2,1)S(1)} %shard_map.140.pair_ref), channel_id=1, source_target_pairs={{0,2},{1,3},{2,0},{3,1},{4,6},{5,7},{6,4},{7,5},{8,10},{9,11},{10,... | collective-permute-start | bytes 417800 | tf_op jit(solution)/shard_map/ppermute | solution.py:301
  27.4 1.5 %collective-permute-start.8 = (bf16[400,256]{1,0:T(8,128)(2,1)S(1)}, bf16[400,256]{1,0:T(8,128)(2,1)S(1)}, u32[]{:S(2)}, u32[]{:S(2)}) collective-permute-start(bf16[400,256]{1,0:T(8,128)(2,1)S(1)} %get-tuple-element.47.sent_ref), channel_id=1, source_target_pairs={{0,1},{1,0},{2,3},{3,2},{4,5},{5,4},{6,7},{7,6},{8,9},{9,8},{10,11... | collective-permute-start | bytes 614408 | tf_op jit(solution)/shard_map/ppermute | solution.py:301
  29.4 10.9 %collective-permute-start.16 = (bf16[256,256]{1,0:T(8,128)(2,1)S(1)}, bf16[256,256]{1,0:T(8,128)(2,1)S(1)}, u32[]{:S(2)}, u32[]{:S(2)}) collective-permute-start(bf16[256,256]{1,0:T(8,128)(2,1)S(1)} %get-tuple-element.52), channel_id=1, source_target_pairs={{0,12},{4,8},{8,4},{12,0},{16,28},{20,24},{24,20},{28,16},{1,13},{... | collective-permute-start | bytes 393224 | tf_op jit(solution)/shard_map/ppermute | solution.py:301
  31.8 6.0 %collective-permute-start.9 = (bf16[144,256]{1,0:T(8,128)(2,1)S(1)}, bf16[144,256]{1,0:T(8,128)(2,1)S(1)}, u32[]{:S(2)}, u32[]{:S(2)}) collective-permute-start(bf16[144,256]{1,0:T(8,128)(2,1)S(1)} %shard_map.142.refs_0_), channel_id=1, source_target_pairs={{0,16},{4,20},{8,24},{12,28},{16,0},{20,4},{24,8},{28,12},{1,17},{... | collective-permute-start | bytes 221192 | tf_op jit(solution)/shard_map/ppermute | solution.py:301
  33.6 7.8 %collective-permute-start.17 = (bf16[256,256]{1,0:T(8,128)(2,1)S(1)}, bf16[256,256]{1,0:T(8,128)(2,1)S(1)}, u32[]{:S(2)}, u32[]{:S(2)}) collective-permute-start(bf16[256,256]{1,0:T(8,128)(2,1)S(1)} %get-tuple-element.53), channel_id=1, source_target_pairs={{0,8},{4,12},{8,0},{12,4},{16,24},{20,28},{24,16},{28,20},{1,9},{5... | collective-permute-start | bytes 393224 | tf_op jit(solution)/shard_map/ppermute | solution.py:301
  33.9 7.5 %collective-permute-start.18 = (bf16[256,256]{1,0:T(8,128)(2,1)S(1)}, bf16[256,256]{1,0:T(8,128)(2,1)S(1)}, u32[]{:S(2)}, u32[]{:S(2)}) collective-permute-start(bf16[256,256]{1,0:T(8,128)(2,1)S(1)} %get-tuple-element.54), channel_id=1, source_target_pairs={{0,4},{4,0},{8,12},{12,8},{16,20},{20,16},{24,28},{28,24},{1,5},{5... | collective-permute-start | bytes 393224 | tf_op jit(solution)/shard_map/ppermute | solution.py:301
  37.9 6.5 %collective-permute-start.12 = (bf16[144,256]{1,0:T(8,128)(2,1)S(1)}, bf16[144,256]{1,0:T(8,128)(2,1)S(1)}, u32[]{:S(2)}, u32[]{:S(2)}) collective-permute-start(bf16[144,256]{1,0:T(8,128)(2,1)S(1)} %shard_map.143.refs_0_), channel_id=1, source_target_pairs={{0,12},{4,8},{8,4},{12,0},{16,28},{20,24},{24,20},{28,16},{1,13},{... | collective-permute-start | bytes 221192 | tf_op jit(solution)/shard_map/ppermute | solution.py:301
  40.2 4.8 %collective-permute-start.11 = (bf16[144,256]{1,0:T(8,128)(2,1)S(1)}, bf16[144,256]{1,0:T(8,128)(2,1)S(1)}, u32[]{:S(2)}, u32[]{:S(2)}) collective-permute-start(bf16[144,256]{1,0:T(8,128)(2,1)S(1)} %shard_map.143.refs_0_), channel_id=1, source_target_pairs={{0,8},{4,12},{8,0},{12,4},{16,24},{20,28},{24,16},{28,20},{1,9},{5... | collective-permute-start | bytes 221192 | tf_op jit(solution)/shard_map/ppermute | solution.py:301
  40.2 4.8 %collective-permute-start.10 = (bf16[144,256]{1,0:T(8,128)(2,1)S(1)}, bf16[144,256]{1,0:T(8,128)(2,1)S(1)}, u32[]{:S(2)}, u32[]{:S(2)}) collective-permute-start(bf16[144,256]{1,0:T(8,128)(2,1)S(1)} %shard_map.143.refs_0_), channel_id=1, source_target_pairs={{0,4},{4,0},{8,12},{12,8},{16,20},{20,16},{24,28},{28,24},{1,5},{5... | collective-permute-start | bytes 221192 | tf_op jit(solution)/shard_map/ppermute | solution.py:301
  41.5 5.9 %collective-permute-start.19 = (bf16[128,256]{1,0:T(8,128)(2,1)S(1)}, bf16[128,256]{1,0:T(8,128)(2,1)S(1)}, u32[]{:S(2)}, u32[]{:S(2)}) collective-permute-start(bf16[128,256]{1,0:T(8,128)(2,1)S(1)} %get-tuple-element.56), channel_id=1, source_target_pairs={{0,16},{4,20},{8,24},{12,28},{16,0},{20,4},{24,8},{28,12},{1,17},{... | collective-permute-start | bytes 196616 | tf_op jit(solution)/shard_map/ppermute | solution.py:301
  45.6 4.3 %collective-permute-start.15 = (bf16[128,256]{1,0:T(8,128)(2,1)S(1)}, bf16[128,256]{1,0:T(8,128)(2,1)S(1)}, u32[]{:S(2)}, u32[]{:S(2)}) collective-permute-start(bf16[128,256]{1,0:T(8,128)(2,1)S(1)} %get-tuple-element.49.refs_0_), channel_id=1, source_target_pairs={{0,3},{1,2},{2,1},{3,0},{4,7},{5,6},{6,5},{7,4},{8,11},{9,10},{10,... | collective-permute-start | bytes 196616 | tf_op jit(solution)/shard_map/ppermute | solution.py:301
  45.6 5.8 %collective-permute-start.14 = (bf16[128,256]{1,0:T(8,128)(2,1)S(1)}, bf16[128,256]{1,0:T(8,128)(2,1)S(1)}, u32[]{:S(2)}, u32[]{:S(2)}) collective-permute-start(bf16[128,256]{1,0:T(8,128)(2,1)S(1)} %get-tuple-element.49.refs_0_), channel_id=1, source_target_pairs={{0,2},{1,3},{2,0},{3,1},{4,6},{5,7},{6,4},{7,5},{8,10},{9,11},{10,... | collective-permute-start | bytes 196616 | tf_op jit(solution)/shard_map/ppermute | solution.py:301
  47.1 4.3 %collective-permute-start.13 = (bf16[128,256]{1,0:T(8,128)(2,1)S(1)}, bf16[128,256]{1,0:T(8,128)(2,1)S(1)}, u32[]{:S(2)}, u32[]{:S(2)}) collective-permute-start(bf16[128,256]{1,0:T(8,128)(2,1)S(1)} %get-tuple-element.49.refs_0_), channel_id=1, source_target_pairs={{0,1},{1,0},{2,3},{3,2},{4,5},{5,4},{6,7},{7,6},{8,9},{9,8},{10,11... | collective-permute-start | bytes 196616 | tf_op jit(solution)/shard_map/ppermute | solution.py:301

commit v8 on v7

--- a/solution.py
+++ b/solution.py
@@ -301,7 +301,6 @@
         return lax.ppermute(value, axis, [(i, i ^ bits) for i in range(lax.axis_size(axis))])
 
     far_pieces = [swap(features, "row", 4 * h) for h in range(1, far)]
-    near = [swap(features, "rep", 2), swap(d_out, "rep", 2)]
     tiles, slots = edge_src.shape
     early = tiles // 2
     tile_row, tile_col, tile_count, edge_src, edge_dst, held_features = (
@@ -327,10 +326,12 @@
         + [pltpu.SemaphoreType.DMA((6,))]
         + chunk_sems,
     )
-    acc, line, near, far_pieces = lax.optimization_barrier((acc, line, near, far_pieces))
+    acc, line, far_pieces = lax.optimization_barrier((acc, line, far_pieces))
     for h, piece in enumerate(far_pieces):
         line = lax.dynamic_update_slice(line, piece, ((h + 1) * rows, 0))
     pieces = [line] + [swap(line, "row", m) for m in range(1, 4)]
+    near_features, near_d_out, acc = lax.optimization_barrier((features, d_out, acc))
+    near = [swap(near_features, "rep", 2), swap(near_d_out, "rep", 2)]
     adjacency = call(
         last_build_kernel,
         shape((group, columns), BF16),
@@ -338,6 +339,7 @@
         (*scalars, late_src, late_dst, acc),
         [pltpu.VMEM(acc_shape, F32)] + buffers + [pltpu.SemaphoreType.DMA((3,))],
     )
+    adjacency, near, pieces = lax.optimization_barrier((adjacency, near, pieces))
     keep, send = call(
         gather_kernel,
         (shape((half + PAD, width), F32), shape((half + PAD, width), BF16)),

time: 52.4 us -> 51.2 us (0.977)
  waiting for transfers between devices: 16 us -> 14.9 us
    ppermute x20, waiting for transfers between devices: 16 us -> 14.9 us  [swap(): lax.ppermute(value, axis, [(i, i ^ bits) for i in range(lax.axis_size(axi...]
where the time goes in v8:
time: 51.2 us; the launch traced here: 51 us
  starting transfers between devices  25 us (49%)
  waiting for transfers between devices  14.9 us (29%)
  Pallas kernels  10.4 us (20%)
  between operations  0.74 us (1%)
    ppermute x20, starting transfers between devices, swap(): lax.ppermute(value, axis, [(i, i ^ bits) for i in range(lax.axis_size(axi...  25 us
    ppermute x20, waiting for transfers between devices, swap(): lax.ppermute(value, axis, [(i, i ^ bits) for i in range(lax.axis_size(axi...  14.9 us
    pallas_call x11, Pallas kernels, call(): pl.pallas_call(kernel, out_shape=out_shape, in_specs=specs, out_specs=[VM...  10.4 us
  transfers between devices with their start and end apart: 20, of which 9 were waited for; matrix products, arithmetic and copies ran while one was open for 0% of the time, Pallas kernels for 14%

profile of v8, /device:TPU:0, one launch (start us, length us, event | category | flops | bytes accessed | tf_op | source)
XLA Modules:
  0.0 51.0 jit_solution(16229258295776400486)
XLA Ops:
  0.6 4.1 %collective-permute-start = (bf16[128,256]{1,0:T(8,128)(2,1)}, bf16[128,256]{1,0:T(8,128)(2,1)S(1)}, u32[]{:S(2)}, u32[]{:S(2)}) collective-permute-start(bf16[128,256]{1,0:T(8,128)(2,1)} %features_ref.3), channel_id=1, source_target_pairs={{0,16},{4,20},{8,24},{12,28},{16,0},{20,4},{24,8},{28,12},{1,17},{... | collective-permute-start | bytes 196616 | tf_op jit(solution)/shard_map/ppermute | solution.py:301
  4.7 3.3 %shard_map.137 = (f32[4,8,128,128]{3,2,1,0:T(8,128)S(1)}, bf16[256,256]{1,0:T(8,128)(2,1)S(1)}, s32[128,256]{1,0:T(8,128)S(1)}, s32[128,256]{1,0:T(8,128)S(1)}) custom-call(s32[256]{0:T(256)} %row_ref.3, s32[256]{0:T(256)} %col_ref.3, s32[256]{0:T(256)} %count_ref.3, s32[256,256]{1,0:T(8,128)} %src_ref.1, s32[256,256]{1,0:T(8,128)} %dst_ref.1, ...), custom_call_target="tpu_custom_call" | custom-call | tf_op jit(solution)/shard_map/pallas_call | solution.py:280
  8.0 0.6 %collective-permute-done = bf16[128,256]{1,0:T(8,128)(2,1)S(1)} collective-permute-done((bf16[128,256]{1,0:T(8,128)(2,1)}, bf16[128,256]{1,0:T(8,128)(2,1)S(1)}, u32[]{:S(2)}, u32[]{:S(2)}) %collective-permute-start) | collective-permute-done | bytes 65568 | tf_op jit(solution)/shard_map/ppermute | solution.py:301
  8.6 2.0 %collective-permute-start.5 = (bf16[256,256]{1,0:T(8,128)(2,1)S(1)}, bf16[256,256]{1,0:T(8,128)(2,1)S(1)}, u32[]{:S(2)}, u32[]{:S(2)}) collective-permute-start(bf16[256,256]{1,0:T(8,128)(2,1)S(1)} %constant_dynamic-update-slice_fusion.refs_0_), channel_id=1, source_target_pairs={{0,12},{4,8},{8,4},{12,0},{16,28},{20,24},{24,20},{28,16},{1,13},{... | collective-permute-start | bytes 393224 | tf_op jit(solution)/shard_map/ppermute | solution.py:301
  10.6 1.2 %collective-permute-start.4 = (bf16[256,256]{1,0:T(8,128)(2,1)S(1)}, bf16[256,256]{1,0:T(8,128)(2,1)S(1)}, u32[]{:S(2)}, u32[]{:S(2)}) collective-permute-start(bf16[256,256]{1,0:T(8,128)(2,1)S(1)} %constant_dynamic-update-slice_fusion.refs_0_), channel_id=1, source_target_pairs={{0,8},{4,12},{8,0},{12,4},{16,24},{20,28},{24,16},{28,20},{1,9},{5... | collective-permute-start | bytes 393224 | tf_op jit(solution)/shard_map/ppermute | solution.py:301
  11.8 0.3 collective-permute-start.3
  12.1 1.7 %collective-permute-start.1 = (bf16[128,256]{1,0:T(8,128)(2,1)}, bf16[128,256]{1,0:T(8,128)(2,1)S(1)}, u32[]{:S(2)}, u32[]{:S(2)}) collective-permute-start(bf16[128,256]{1,0:T(8,128)(2,1)} %features_ref.3), channel_id=1, source_target_pairs={{0,2},{1,3},{2,0},{3,1},{4,6},{5,7},{6,4},{7,5},{8,10},{9,11},{10,... | collective-permute-start | bytes 196616 | tf_op jit(solution)/shard_map/ppermute | solution.py:301
  13.8 0.3 collective-permute-start.2
  14.1 0.0 copy-start
  14.1 0.0 copy-start.1
  14.1 0.0 copy-start.2
  14.1 0.0 copy-start.3
  14.1 0.0 copy-start.4
  14.1 3.3 %shard_map.138.adj_ref = bf16[512,1024]{1,0:T(8,128)(2,1)S(1)} custom-call(s32[256]{0:T(256)} %row_ref.3, s32[256]{0:T(256)} %col_ref.3, s32[256]{0:T(256)} %count_ref.3, s32[128,256]{1,0:T(8,128)S(1)} %get-tuple-element.41.src_ref, s32[128,256]{1,0:T(8,128)S(1)} %get-tuple-element.42.dst_ref, f32[4,8,128,128]{3,2,1,0:T(8,128)S(1)} %get-tuple-element.46.half_ref), custom_call_target="tpu_custom_call" | custom-call | tf_op jit(solution)/shard_map/pallas_call | solution.py:280
  17.5 0.0 collective-permute-done.1.near_features_ref
  17.5 0.8 %collective-permute-done.2.near_d_out_ref = bf16[128,256]{1,0:T(8,128)(2,1)S(1)} collective-permute-done((bf16[128,256]{1,0:T(8,128)(2,1)}, bf16[128,256]{1,0:T(8,128)(2,1)S(1)}, u32[]{:S(2)}, u32[]{:S(2)}) %collective-permute-start.2) | collective-permute-done | bytes 65568 | tf_op jit(solution)/shard_map/ppermute | solution.py:301
  18.3 0.0 collective-permute-done.5.refs_3_
  18.3 0.0 collective-permute-done.4.refs_2_
  18.3 0.0 collective-permute-done.3.refs_1_
  18.3 0.7 %shard_map.139 = (f32[272,256]{1,0:T(8,128)S(1)}, bf16[272,256]{1,0:T(8,128)(2,1)S(1)}) custom-call(bf16[512,1024]{1,0:T(8,128)(2,1)S(1)} %shard_map.138.adj_ref, bf16[256,256]{1,0:T(8,128)(2,1)S(1)} %constant_dynamic-update-slice_fusion.refs_0_, bf16[256,256]{1,0:T(8,128)(2,1)S(1)} %collective-permute-done.3.refs_1_, ...), custom_call_target="tpu_custom_call" | custom-call | tf_op jit(solution)/shard_map/pallas_call | solution.py:280
  19.0 0.1 collective-permute-start.6
  19.1 1.3 %collective-permute-done.6.got_ref = bf16[272,256]{1,0:T(8,128)(2,1)S(1)} collective-permute-done((bf16[272,256]{1,0:T(8,128)(2,1)S(1)}, bf16[272,256]{1,0:T(8,128)(2,1)S(1)}, u32[]{:S(2)}, u32[]{:S(2)}) %collective-permute-start.6) | collective-permute-done | bytes 139296 | tf_op jit(solution)/shard_map/ppermute | solution.py:301
  20.4 1.0 %collective-permute-start.7 = (bf16[272,256]{1,0:T(8,128)(2,1)S(1)}, bf16[272,256]{1,0:T(8,128)(2,1)S(1)}, u32[]{:S(2)}, u32[]{:S(2)}) collective-permute-start(bf16[272,256]{1,0:T(8,128)(2,1)S(1)} %shard_map.140.pair_ref), channel_id=1, source_target_pairs={{0,2},{1,3},{2,0},{3,1},{4,6},{5,7},{6,4},{7,5},{8,10},{9,11},{10,... | collective-permute-start | bytes 417800 | tf_op jit(solution)/shard_map/ppermute | solution.py:301
  21.5 4.8 %collective-permute-done.7.got_ref = bf16[272,256]{1,0:T(8,128)(2,1)S(1)} collective-permute-done((bf16[272,256]{1,0:T(8,128)(2,1)S(1)}, bf16[272,256]{1,0:T(8,128)(2,1)S(1)}, u32[]{:S(2)}, u32[]{:S(2)}) %collective-permute-start.7) | collective-permute-done | bytes 139296 | tf_op jit(solution)/shard_map/ppermute | solution.py:301
  26.2 0.0 copy-done
  26.2 0.0 copy-done.1
  26.2 0.0 copy-done.2
  26.2 0.0 copy-done.3
  26.2 0.0 copy-done.4
  26.3 1.0 %shard_map.141 = (bf16[128,256]{1,0:T(8,128)(2,1)}, f32[128,256]{1,0:T(8,128)S(1)}, f32[144,256]{1,0:T(8,128)S(1)}, bf16[400,256]{1,0:T(8,128)(2,1)S(1)}) custom-call(bf16[272,256]{1,0:T(8,128)(2,1)S(1)} %shard_map.140.pair_ref, bf16[272,256]{1,0:T(8,128)(2,1)S(1)} %collective-permute-done.7.got_ref, bf16[128,256]{1,0:T(8,128)(2,1)S(1)} %copy-done, ...), custom_call_target="tpu_custom_call" | custom-call | tf_op jit(solution)/shard_map/pallas_call | solution.py:280
  27.3 0.0 collective-permute-start.8
  27.3 1.5 %collective-permute-done.8.got_ref = bf16[400,256]{1,0:T(8,128)(2,1)S(1)} collective-permute-done((bf16[400,256]{1,0:T(8,128)(2,1)S(1)}, bf16[400,256]{1,0:T(8,128)(2,1)S(1)}, u32[]{:S(2)}, u32[]{:S(2)}) %collective-permute-start.8) | collective-permute-done | bytes 204832 | tf_op jit(solution)/shard_map/ppermute | solution.py:301
  28.8 0.5 shard_map.145
  29.3 1.9 %collective-permute-start.16 = (bf16[256,256]{1,0:T(8,128)(2,1)S(1)}, bf16[256,256]{1,0:T(8,128)(2,1)S(1)}, u32[]{:S(2)}, u32[]{:S(2)}) collective-permute-start(bf16[256,256]{1,0:T(8,128)(2,1)S(1)} %get-tuple-element.68), channel_id=1, source_target_pairs={{0,12},{4,8},{8,4},{12,0},{16,28},{20,24},{24,20},{28,16},{1,13},{... | collective-permute-start | bytes 393224 | tf_op jit(solution)/shard_map/ppermute | solution.py:301
  31.2 2.9 %collective-permute-start.9 = (bf16[144,256]{1,0:T(8,128)(2,1)S(1)}, bf16[144,256]{1,0:T(8,128)(2,1)S(1)}, u32[]{:S(2)}, u32[]{:S(2)}) collective-permute-start(bf16[144,256]{1,0:T(8,128)(2,1)S(1)} %shard_map.142.refs_0_), channel_id=1, source_target_pairs={{0,16},{4,20},{8,24},{12,28},{16,0},{20,4},{24,8},{28,12},{1,17},{... | collective-permute-start | bytes 221192 | tf_op jit(solution)/shard_map/ppermute | solution.py:301
  34.0 0.0 collective-permute-start.17
  34.0 0.6 %collective-permute-start.18 = (bf16[256,256]{1,0:T(8,128)(2,1)S(1)}, bf16[256,256]{1,0:T(8,128)(2,1)S(1)}, u32[]{:S(2)}, u32[]{:S(2)}) collective-permute-start(bf16[256,256]{1,0:T(8,128)(2,1)S(1)} %get-tuple-element.70), channel_id=1, source_target_pairs={{0,4},{4,0},{8,12},{12,8},{16,20},{20,16},{24,28},{28,24},{1,5},{5... | collective-permute-start | bytes 393224 | tf_op jit(solution)/shard_map/ppermute | solution.py:301
  34.7 2.0 %collective-permute-done.9.refs_1_ = bf16[144,256]{1,0:T(8,128)(2,1)S(1)} collective-permute-done((bf16[144,256]{1,0:T(8,128)(2,1)S(1)}, bf16[144,256]{1,0:T(8,128)(2,1)S(1)}, u32[]{:S(2)}, u32[]{:S(2)}) %collective-permute-start.9) | collective-permute-done | bytes 73760 | tf_op jit(solution)/shard_map/ppermute | solution.py:301
  36.7 3.3 %collective-permute-start.12 = (bf16[144,256]{1,0:T(8,128)(2,1)S(1)}, bf16[144,256]{1,0:T(8,128)(2,1)S(1)}, u32[]{:S(2)}, u32[]{:S(2)}) collective-permute-start(bf16[144,256]{1,0:T(8,128)(2,1)S(1)} %shard_map.143.refs_0_), channel_id=1, source_target_pairs={{0,12},{4,8},{8,4},{12,0},{16,28},{20,24},{24,20},{28,16},{1,13},{... | collective-permute-start | bytes 221192 | tf_op jit(solution)/shard_map/ppermute | solution.py:301
  40.1 0.0 collective-permute-start.11
  40.1 0.0 collective-permute-done.16.refs_0_
  40.1 1.4 %collective-permute-start.10 = (bf16[144,256]{1,0:T(8,128)(2,1)S(1)}, bf16[144,256]{1,0:T(8,128)(2,1)S(1)}, u32[]{:S(2)}, u32[]{:S(2)}) collective-permute-start(bf16[144,256]{1,0:T(8,128)(2,1)S(1)} %shard_map.143.refs_0_), channel_id=1, source_target_pairs={{0,4},{4,0},{8,12},{12,8},{16,20},{20,16},{24,28},{28,24},{1,5},{5... | collective-permute-start | bytes 221192 | tf_op jit(solution)/shard_map/ppermute | solution.py:301
  41.5 0.0 collective-permute-done.17.refs_1_
  41.5 0.0 collective-permute-done.18.refs_2_
  41.5 0.1 shard_map.146
  41.6 2.2 %collective-permute-start.19 = (bf16[128,256]{1,0:T(8,128)(2,1)S(1)}, bf16[128,256]{1,0:T(8,128)(2,1)S(1)}, u32[]{:S(2)}, u32[]{:S(2)}) collective-permute-start(bf16[128,256]{1,0:T(8,128)(2,1)S(1)} %get-tuple-element.72), channel_id=1, source_target_pairs={{0,16},{4,20},{8,24},{12,28},{16,0},{20,4},{24,8},{28,12},{1,17},{... | collective-permute-start | bytes 196616 | tf_op jit(solution)/shard_map/ppermute | solution.py:301
  43.8 0.0 collective-permute-done.12.refs_3_
  43.8 0.8 %collective-permute-done.11.refs_2_ = bf16[144,256]{1,0:T(8,128)(2,1)S(1)} collective-permute-done((bf16[144,256]{1,0:T(8,128)(2,1)S(1)}, bf16[144,256]{1,0:T(8,128)(2,1)S(1)}, u32[]{:S(2)}, u32[]{:S(2)}) %collective-permute-start.11) | collective-permute-done | bytes 73760 | tf_op jit(solution)/shard_map/ppermute | solution.py:301
  44.6 0.0 collective-permute-done.10.refs_1_
  44.6 0.6 %shard_map.144 = (bf16[128,256]{1,0:T(8,128)(2,1)S(1)}, f32[1,256]{1,0:T(1,128)}) custom-call(bf16[144,256]{1,0:T(8,128)(2,1)S(1)} %shard_map.143.refs_0_, bf16[144,256]{1,0:T(8,128)(2,1)S(1)} %collective-permute-done.10.refs_1_, bf16[144,256]{1,0:T(8,128)(2,1)S(1)} %collective-permute-done.11.refs_2_, bf16[144,256]{1,0:T(8,128)(2,1)S(1)} %collective-permute-done.12.refs_3_), custom_call_target="tpu_custom_call" | custom-call | tf_op jit(solution)/shard_map/pallas_call | solution.py:280
  45.2 0.0 collective-permute-start.15
  45.2 1.0 %collective-permute-start.14 = (bf16[128,256]{1,0:T(8,128)(2,1)S(1)}, bf16[128,256]{1,0:T(8,128)(2,1)S(1)}, u32[]{:S(2)}, u32[]{:S(2)}) collective-permute-start(bf16[128,256]{1,0:T(8,128)(2,1)S(1)} %get-tuple-element.65.refs_0_), channel_id=1, source_target_pairs={{0,2},{1,3},{2,0},{3,1},{4,6},{5,7},{6,4},{7,5},{8,10},{9,11},{10,... | collective-permute-start | bytes 196616 | tf_op jit(solution)/shard_map/ppermute | solution.py:301
  46.2 0.9 %collective-permute-start.13 = (bf16[128,256]{1,0:T(8,128)(2,1)S(1)}, bf16[128,256]{1,0:T(8,128)(2,1)S(1)}, u32[]{:S(2)}, u32[]{:S(2)}) collective-permute-start(bf16[128,256]{1,0:T(8,128)(2,1)S(1)} %get-tuple-element.65.refs_0_), channel_id=1, source_target_pairs={{0,1},{1,0},{2,3},{3,2},{4,5},{5,4},{6,7},{7,6},{8,9},{9,8},{10,11... | collective-permute-start | bytes 196616 | tf_op jit(solution)/shard_map/ppermute | solution.py:301
  47.1 0.0 collective-permute-done.19.refs_5_
  47.1 2.4 %collective-permute-done.15.refs_3_ = bf16[128,256]{1,0:T(8,128)(2,1)S(1)} collective-permute-done((bf16[128,256]{1,0:T(8,128)(2,1)S(1)}, bf16[128,256]{1,0:T(8,128)(2,1)S(1)}, u32[]{:S(2)}, u32[]{:S(2)}) %collective-permute-start.15) | collective-permute-done | bytes 65568 | tf_op jit(solution)/shard_map/ppermute | solution.py:301
  49.5 0.7 %collective-permute-done.14.refs_2_ = bf16[128,256]{1,0:T(8,128)(2,1)S(1)} collective-permute-done((bf16[128,256]{1,0:T(8,128)(2,1)S(1)}, bf16[128,256]{1,0:T(8,128)(2,1)S(1)}, u32[]{:S(2)}, u32[]{:S(2)}) %collective-permute-start.14) | collective-permute-done | bytes 65568 | tf_op jit(solution)/shard_map/ppermute | solution.py:301
  50.2 0.0 collective-permute-done.13.refs_1_
  50.2 0.9 %shard_map.147 = (f32[128,256]{1,0:T(8,128)}, f32[2,128,256]{2,1,0:T(8,128)}, f32[2,128,256]{2,1,0:T(8,128)}) custom-call(f32[128,256]{1,0:T(8,128)S(1)} %get-tuple-element.61.self_ref, bf16[128,256]{1,0:T(8,128)(2,1)S(1)} %get-tuple-element.65.refs_0_, bf16[128,256]{1,0:T(8,128)(2,1)S(1)} %collective-permute-done.13.refs_1_, ...), custom_call_target="tpu_custom_call" | custom-call | tf_op jit(solution)/shard_map/pallas_call | solution.py:280
  (4 shorter events, 0.1 us)
Async XLA Ops:
  0.6 8.0 %collective-permute-start = (bf16[128,256]{1,0:T(8,128)(2,1)}, bf16[128,256]{1,0:T(8,128)(2,1)S(1)}, u32[]{:S(2)}, u32[]{:S(2)}) collective-permute-start(bf16[128,256]{1,0:T(8,128)(2,1)} %features_ref.3), channel_id=1, source_target_pairs={{0,16},{4,20},{8,24},{12,28},{16,0},{20,4},{24,8},{28,12},{1,17},{... | collective-permute-start | bytes 196616 | tf_op jit(solution)/shard_map/ppermute | solution.py:301
  8.6 9.7 %collective-permute-start.5 = (bf16[256,256]{1,0:T(8,128)(2,1)S(1)}, bf16[256,256]{1,0:T(8,128)(2,1)S(1)}, u32[]{:S(2)}, u32[]{:S(2)}) collective-permute-start(bf16[256,256]{1,0:T(8,128)(2,1)S(1)} %constant_dynamic-update-slice_fusion.refs_0_), channel_id=1, source_target_pairs={{0,12},{4,8},{8,4},{12,0},{16,28},{20,24},{24,20},{28,16},{1,13},{... | collective-permute-start | bytes 393224 | tf_op jit(solution)/shard_map/ppermute | solution.py:301
  10.6 7.6 %collective-permute-start.4 = (bf16[256,256]{1,0:T(8,128)(2,1)S(1)}, bf16[256,256]{1,0:T(8,128)(2,1)S(1)}, u32[]{:S(2)}, u32[]{:S(2)}) collective-permute-start(bf16[256,256]{1,0:T(8,128)(2,1)S(1)} %constant_dynamic-update-slice_fusion.refs_0_), channel_id=1, source_target_pairs={{0,8},{4,12},{8,0},{12,4},{16,24},{20,28},{24,16},{28,20},{1,9},{5... | collective-permute-start | bytes 393224 | tf_op jit(solution)/shard_map/ppermute | solution.py:301
  11.8 6.5 %collective-permute-start.3 = (bf16[256,256]{1,0:T(8,128)(2,1)S(1)}, bf16[256,256]{1,0:T(8,128)(2,1)S(1)}, u32[]{:S(2)}, u32[]{:S(2)}) collective-permute-start(bf16[256,256]{1,0:T(8,128)(2,1)S(1)} %constant_dynamic-update-slice_fusion.refs_0_), channel_id=1, source_target_pairs={{0,4},{4,0},{8,12},{12,8},{16,20},{20,16},{24,28},{28,24},{1,5},{5... | collective-permute-start | bytes 393224 | tf_op jit(solution)/shard_map/ppermute | solution.py:301
  12.1 5.4 %collective-permute-start.1 = (bf16[128,256]{1,0:T(8,128)(2,1)}, bf16[128,256]{1,0:T(8,128)(2,1)S(1)}, u32[]{:S(2)}, u32[]{:S(2)}) collective-permute-start(bf16[128,256]{1,0:T(8,128)(2,1)} %features_ref.3), channel_id=1, source_target_pairs={{0,2},{1,3},{2,0},{3,1},{4,6},{5,7},{6,4},{7,5},{8,10},{9,11},{10,... | collective-permute-start | bytes 196616 | tf_op jit(solution)/shard_map/ppermute | solution.py:301
  13.8 4.5 %collective-permute-start.2 = (bf16[128,256]{1,0:T(8,128)(2,1)}, bf16[128,256]{1,0:T(8,128)(2,1)S(1)}, u32[]{:S(2)}, u32[]{:S(2)}) collective-permute-start(bf16[128,256]{1,0:T(8,128)(2,1)} %d_out_ref.1), channel_id=1, source_target_pairs={{0,2},{1,3},{2,0},{3,1},{4,6},{5,7},{6,4},{7,5},{8,10},{9,11},{10,... | collective-permute-start | bytes 196616 | tf_op jit(solution)/shard_map/ppermute | solution.py:301
  14.1 12.1 %copy-start = (bf16[128,256]{1,0:T(8,128)(2,1)S(1)}, bf16[128,256]{1,0:T(8,128)(2,1)}, u32[]{:S(2)}) copy-start(bf16[128,256]{1,0:T(8,128)(2,1)} %features_ref.3) | copy-start | bytes 196612
  14.1 12.1 %copy-start.1 = (bf16[256,256]{1,0:T(8,128)(2,1)S(1)}, bf16[256,256]{1,0:T(8,128)(2,1)}, u32[]{:S(2)}) copy-start(bf16[256,256]{1,0:T(8,128)(2,1)} %w_self_ref.1) | copy-start | bytes 393220
  14.1 12.1 %copy-start.2 = (bf16[256,256]{1,0:T(8,128)(2,1)S(1)}, bf16[256,256]{1,0:T(8,128)(2,1)}, u32[]{:S(2)}) copy-start(bf16[256,256]{1,0:T(8,128)(2,1)} %w_neigh_ref.1) | copy-start | bytes 393220
  14.1 12.1 %copy-start.3 = (bf16[128,256]{1,0:T(8,128)(2,1)S(1)}, bf16[128,256]{1,0:T(8,128)(2,1)}, u32[]{:S(2)}) copy-start(bf16[128,256]{1,0:T(8,128)(2,1)} %d_out_ref.1) | copy-start | bytes 196612
  14.1 12.1 %copy-start.4 = (f32[256]{0:T(256)S(1)}, f32[256]{0:T(256)}, u32[]{:S(2)}) copy-start(f32[256]{0:T(256)} %param.13) | copy-start | bytes 3076
  19.0 1.4 %collective-permute-start.6 = (bf16[272,256]{1,0:T(8,128)(2,1)S(1)}, bf16[272,256]{1,0:T(8,128)(2,1)S(1)}, u32[]{:S(2)}, u32[]{:S(2)}) collective-permute-start(bf16[272,256]{1,0:T(8,128)(2,1)S(1)} %get-tuple-element.57), channel_id=1, source_target_pairs={{0,1},{1,0},{2,3},{3,2},{4,5},{5,4},{6,7},{7,6},{8,9},{9,8},{10,11... | collective-permute-start | bytes 417800 | tf_op jit(solution)/shard_map/ppermute | solution.py:301
  20.4 5.8 %collective-permute-start.7 = (bf16[272,256]{1,0:T(8,128)(2,1)S(1)}, bf16[272,256]{1,0:T(8,128)(2,1)S(1)}, u32[]{:S(2)}, u32[]{:S(2)}) collective-permute-start(bf16[272,256]{1,0:T(8,128)(2,1)S(1)} %shard_map.140.pair_ref), channel_id=1, source_target_pairs={{0,2},{1,3},{2,0},{3,1},{4,6},{5,7},{6,4},{7,5},{8,10},{9,11},{10,... | collective-permute-start | bytes 417800 | tf_op jit(solution)/shard_map/ppermute | solution.py:301
  27.3 1.5 %collective-permute-start.8 = (bf16[400,256]{1,0:T(8,128)(2,1)S(1)}, bf16[400,256]{1,0:T(8,128)(2,1)S(1)}, u32[]{:S(2)}, u32[]{:S(2)}) collective-permute-start(bf16[400,256]{1,0:T(8,128)(2,1)S(1)} %get-tuple-element.63.sent_ref), channel_id=1, source_target_pairs={{0,1},{1,0},{2,3},{3,2},{4,5},{5,4},{6,7},{7,6},{8,9},{9,8},{10,11... | collective-permute-start | bytes 614408 | tf_op jit(solution)/shard_map/ppermute | solution.py:301
  29.3 10.8 %collective-permute-start.16 = (bf16[256,256]{1,0:T(8,128)(2,1)S(1)}, bf16[256,256]{1,0:T(8,128)(2,1)S(1)}, u32[]{:S(2)}, u32[]{:S(2)}) collective-permute-start(bf16[256,256]{1,0:T(8,128)(2,1)S(1)} %get-tuple-element.68), channel_id=1, source_target_pairs={{0,12},{4,8},{8,4},{12,0},{16,28},{20,24},{24,20},{28,16},{1,13},{... | collective-permute-start | bytes 393224 | tf_op jit(solution)/shard_map/ppermute | solution.py:301
  31.2 5.6 %collective-permute-start.9 = (bf16[144,256]{1,0:T(8,128)(2,1)S(1)}, bf16[144,256]{1,0:T(8,128)(2,1)S(1)}, u32[]{:S(2)}, u32[]{:S(2)}) collective-permute-start(bf16[144,256]{1,0:T(8,128)(2,1)S(1)} %shard_map.142.refs_0_), channel_id=1, source_target_pairs={{0,16},{4,20},{8,24},{12,28},{16,0},{20,4},{24,8},{28,12},{1,17},{... | collective-permute-start | bytes 221192 | tf_op jit(solution)/shard_map/ppermute | solution.py:301
  34.0 7.5 %collective-permute-start.17 = (bf16[256,256]{1,0:T(8,128)(2,1)S(1)}, bf16[256,256]{1,0:T(8,128)(2,1)S(1)}, u32[]{:S(2)}, u32[]{:S(2)}) collective-permute-start(bf16[256,256]{1,0:T(8,128)(2,1)S(1)} %get-tuple-element.69), channel_id=1, source_target_pairs={{0,8},{4,12},{8,0},{12,4},{16,24},{20,28},{24,16},{28,20},{1,9},{5... | collective-permute-start | bytes 393224 | tf_op jit(solution)/shard_map/ppermute | solution.py:301
  34.0 7.5 %collective-permute-start.18 = (bf16[256,256]{1,0:T(8,128)(2,1)S(1)}, bf16[256,256]{1,0:T(8,128)(2,1)S(1)}, u32[]{:S(2)}, u32[]{:S(2)}) collective-permute-start(bf16[256,256]{1,0:T(8,128)(2,1)S(1)} %get-tuple-element.70), channel_id=1, source_target_pairs={{0,4},{4,0},{8,12},{12,8},{16,20},{20,16},{24,28},{28,24},{1,5},{5... | collective-permute-start | bytes 393224 | tf_op jit(solution)/shard_map/ppermute | solution.py:301
  36.7 7.1 %collective-permute-start.12 = (bf16[144,256]{1,0:T(8,128)(2,1)S(1)}, bf16[144,256]{1,0:T(8,128)(2,1)S(1)}, u32[]{:S(2)}, u32[]{:S(2)}) collective-permute-start(bf16[144,256]{1,0:T(8,128)(2,1)S(1)} %shard_map.143.refs_0_), channel_id=1, source_target_pairs={{0,12},{4,8},{8,4},{12,0},{16,28},{20,24},{24,20},{28,16},{1,13},{... | collective-permute-start | bytes 221192 | tf_op jit(solution)/shard_map/ppermute | solution.py:301
  40.1 4.6 %collective-permute-start.11 = (bf16[144,256]{1,0:T(8,128)(2,1)S(1)}, bf16[144,256]{1,0:T(8,128)(2,1)S(1)}, u32[]{:S(2)}, u32[]{:S(2)}) collective-permute-start(bf16[144,256]{1,0:T(8,128)(2,1)S(1)} %shard_map.143.refs_0_), channel_id=1, source_target_pairs={{0,8},{4,12},{8,0},{12,4},{16,24},{20,28},{24,16},{28,20},{1,9},{5... | collective-permute-start | bytes 221192 | tf_op jit(solution)/shard_map/ppermute | solution.py:301
  40.1 4.5 %collective-permute-start.10 = (bf16[144,256]{1,0:T(8,128)(2,1)S(1)}, bf16[144,256]{1,0:T(8,128)(2,1)S(1)}, u32[]{:S(2)}, u32[]{:S(2)}) collective-permute-start(bf16[144,256]{1,0:T(8,128)(2,1)S(1)} %shard_map.143.refs_0_), channel_id=1, source_target_pairs={{0,4},{4,0},{8,12},{12,8},{16,20},{20,16},{24,28},{28,24},{1,5},{5... | collective-permute-start | bytes 221192 | tf_op jit(solution)/shard_map/ppermute | solution.py:301
  41.6 5.5 %collective-permute-start.19 = (bf16[128,256]{1,0:T(8,128)(2,1)S(1)}, bf16[128,256]{1,0:T(8,128)(2,1)S(1)}, u32[]{:S(2)}, u32[]{:S(2)}) collective-permute-start(bf16[128,256]{1,0:T(8,128)(2,1)S(1)} %get-tuple-element.72), channel_id=1, source_target_pairs={{0,16},{4,20},{8,24},{12,28},{16,0},{20,4},{24,8},{28,12},{1,17},{... | collective-permute-start | bytes 196616 | tf_op jit(solution)/shard_map/ppermute | solution.py:301
  45.2 4.3 %collective-permute-start.15 = (bf16[128,256]{1,0:T(8,128)(2,1)S(1)}, bf16[128,256]{1,0:T(8,128)(2,1)S(1)}, u32[]{:S(2)}, u32[]{:S(2)}) collective-permute-start(bf16[128,256]{1,0:T(8,128)(2,1)S(1)} %get-tuple-element.65.refs_0_), channel_id=1, source_target_pairs={{0,3},{1,2},{2,1},{3,0},{4,7},{5,6},{6,5},{7,4},{8,11},{9,10},{10,... | collective-permute-start | bytes 196616 | tf_op jit(solution)/shard_map/ppermute | solution.py:301
  45.2 4.9 %collective-permute-start.14 = (bf16[128,256]{1,0:T(8,128)(2,1)S(1)}, bf16[128,256]{1,0:T(8,128)(2,1)S(1)}, u32[]{:S(2)}, u32[]{:S(2)}) collective-permute-start(bf16[128,256]{1,0:T(8,128)(2,1)S(1)} %get-tuple-element.65.refs_0_), channel_id=1, source_target_pairs={{0,2},{1,3},{2,0},{3,1},{4,6},{5,7},{6,4},{7,5},{8,10},{9,11},{10,... | collective-permute-start | bytes 196616 | tf_op jit(solution)/shard_map/ppermute | solution.py:301
  46.2 4.0 %collective-permute-start.13 = (bf16[128,256]{1,0:T(8,128)(2,1)S(1)}, bf16[128,256]{1,0:T(8,128)(2,1)S(1)}, u32[]{:S(2)}, u32[]{:S(2)}) collective-permute-start(bf16[128,256]{1,0:T(8,128)(2,1)S(1)} %get-tuple-element.65.refs_0_), channel_id=1, source_target_pairs={{0,1},{1,0},{2,3},{3,2},{4,5},{5,4},{6,7},{7,6},{8,9},{9,8},{10,11... | collective-permute-start | bytes 196616 | tf_op jit(solution)/shard_map/ppermute | solution.py:301

commit v9 on v8

--- a/solution.py
+++ b/solution.py
@@ -229,15 +229,18 @@
 
 
 def near_sum_kernel(keep_ref, *refs):
+    *sums, out_ref = refs[4:]
     blocks = tree([ref[...].astype(F32) for ref in (keep_ref, *refs[:3])])
-    for h, ref in enumerate(refs[3:]):
+    for h, ref in enumerate(sums):
         ref[...] = blocks[h * BLK : (h + 1) * BLK].astype(ref.dtype)
-
-
-def finish_kernel(self_ref, *refs):
-    *terms, d_features_ref, grad_self_ref, grad_neigh_ref = refs
+    out_ref[...] = refs[3][...]
+
+
+def finish_kernel(self_ref, bias_term_ref, *refs):
+    *terms, d_features_ref, grad_self_ref, grad_neigh_ref, bias_ref = refs
     quarters, terms = terms[:4], terms[4:]
     d_features_ref[...] = self_ref[...] + tree([ref[...].astype(F32) for ref in terms])
+    bias_ref[...] = bias_term_ref[...]
     me = lax.axis_index("rep")
     low = me >> 1 == 0
     for h in range(2):
@@ -260,7 +263,7 @@
     return grads, tree([joined(ref[middle:]) for ref in refs])
 
 
-def far_terms_kernel(*refs):
+def part_terms_kernel(*refs):
     *terms, sum_ref = refs
     middle = sum_ref.shape[0] - PAD
     grads, bias_term = add_terms(terms)
@@ -268,7 +271,7 @@
     sum_ref[middle:] = split(bias_term)
 
 
-def near_terms_kernel(*refs):
+def all_terms_kernel(*refs):
     *terms, quarter_ref, bias_ref = refs
     quarter_ref[...], bias_ref[...] = add_terms(terms)
 
@@ -377,35 +380,39 @@
     terms_shape = shape((middle + PAD, width), BF16)
     terms = call(core_terms_kernel, terms_shape, [VMEM] * 2, (keep, back))
     terms, back = lax.optimization_barrier((terms, back))
-    far_terms = [terms] + [swap(terms, "row", 4 * h) for h in range(1, far)]
     keep_blocks, *near_msgs = call(
         spread_kernel,
         (shape((far * BLK, width), F32),) + (shape((far * BLK, width), BF16),) * 3,
         [VMEM] * 3,
         (adjacency, send, back),
     )
-    got = [swap(msg, "row", m + 1) for m, msg in enumerate(near_msgs)][::-1]
-    terms = call(far_terms_kernel, terms_shape, [VMEM] * far, far_terms)
     near_terms = [terms] + [swap(terms, "row", m) for m in range(1, 4)]
-    quarter, grad_bias = call(
-        near_terms_kernel,
+    got = [swap(msg, "row", m + 1) for m, msg in enumerate(near_msgs)]
+    terms = call(part_terms_kernel, terms_shape, [VMEM] * 4, near_terms)
+    far_terms = [terms] + [swap(terms, "row", 4 * h) for h in range(1, far)]
+    quarter, bias_term = call(
+        all_terms_kernel,
         (shape((middle, width), BF16), shape((1, width), F32)),
-        [VMEM] * 4,
-        near_terms,
-    )
-    keep_block, *far_msgs = call(
+        [VMEM] * far,
+        far_terms,
+    )
+    keep_block, *far_msgs, out = call(
         near_sum_kernel,
-        (shape((BLK, width), F32),) + (shape((BLK, width), BF16),) * (far - 1),
-        [VMEM] * 4,
-        (keep_blocks, *got),
+        (shape((BLK, width), F32),)
+        + (shape((BLK, width), BF16),) * (far - 1)
+        + (shape((rows, width), BF16),),
+        [VMEM] * 5,
+        (keep_blocks, *got, out),
     )
     got = [swap(msg, "row", 4 * (h + 1)) for h, msg in enumerate(far_msgs)]
     quarters = [quarter] + [swap(quarter, "rep", m) for m in range(1, 4)]
-    d_features, grad_self, grad_neigh = call(
+    d_features, grad_self, grad_neigh, grad_bias = call(
         finish_kernel,
-        (shape((rows, width), F32),) + (shape((2, middle, width), F32),) * 2,
-        [VMEM] * (6 + len(got)),
-        (self_term, *quarters, keep_block, *got),
+        (shape((rows, width), F32),)
+        + (shape((2, middle, width), F32),) * 2
+        + (shape((1, width), F32),),
+        [VMEM] * (7 + len(got)),
+        (self_term, bias_term, *quarters, keep_block, *got),
     )
     grad_self, grad_neigh = (v.reshape(width, width) for v in (grad_self, grad_neigh))
     return (out, d_features, grad_self, grad_neigh, grad_bias[0])

time: 51.2 us -> 51.3 us (level)
  waiting for transfers between devices: 14.9 us -> 15.8 us
  starting transfers between devices: 25 us -> 24.4 us
    ppermute x20, waiting for transfers between devices: 14.9 us -> 15.8 us  [swap(): lax.ppermute(value, axis, [(i, i ^ bits) for i in range(lax.axis_size(axi...]
    ppermute x20, starting transfers between devices: 25 us -> 24.4 us  [swap(): lax.ppermute(value, axis, [(i, i ^ bits) for i in range(lax.axis_size(axi...]
  transfers between devices with their start and end apart: 20 -> 20, of which waited for: 9 -> 12; matrix products, arithmetic and copies ran while one was open for 0% -> 0% of each run, Pallas kernels for 14% -> 15%
where the time goes in v9:
time: 51.3 us; the launch traced here: 51.1 us
  starting transfers between devices  24.4 us (48%)
  waiting for transfers between devices  15.8 us (31%)
  Pallas kernels  10.1 us (20%)
  between operations  0.76 us (1%)
    ppermute x20, starting transfers between devices, swap(): lax.ppermute(value, axis, [(i, i ^ bits) for i in range(lax.axis_size(axi...  24.4 us
    ppermute x20, waiting for transfers between devices, swap(): lax.ppermute(value, axis, [(i, i ^ bits) for i in range(lax.axis_size(axi...  15.8 us
    pallas_call x11, Pallas kernels, call(): pl.pallas_call(kernel, out_shape=out_shape, in_specs=specs, out_specs=[VM...  10.1 us
  transfers between devices with their start and end apart: 20, of which 12 were waited for; matrix products, arithmetic and copies ran while one was open for 0% of the time, Pallas kernels for 15%

profile of v9, /device:TPU:0, one launch (start us, length us, event | category | flops | bytes accessed | tf_op | source)
XLA Modules:
  0.0 51.1 jit_solution(2454225497863370404)
XLA Ops:
  0.6 4.1 %collective-permute-start = (bf16[128,256]{1,0:T(8,128)(2,1)}, bf16[128,256]{1,0:T(8,128)(2,1)S(1)}, u32[]{:S(2)}, u32[]{:S(2)}) collective-permute-start(bf16[128,256]{1,0:T(8,128)(2,1)} %features_ref.3), channel_id=1, source_target_pairs={{0,16},{4,20},{8,24},{12,28},{16,0},{20,4},{24,8},{28,12},{1,17},{... | collective-permute-start | bytes 196616 | tf_op jit(solution)/shard_map/ppermute | solution.py:304
  4.7 3.3 %shard_map.137 = (f32[4,8,128,128]{3,2,1,0:T(8,128)S(1)}, bf16[256,256]{1,0:T(8,128)(2,1)S(1)}, s32[128,256]{1,0:T(8,128)S(1)}, s32[128,256]{1,0:T(8,128)S(1)}) custom-call(s32[256]{0:T(256)} %row_ref.3, s32[256]{0:T(256)} %col_ref.3, s32[256]{0:T(256)} %count_ref.3, s32[256,256]{1,0:T(8,128)} %src_ref.1, s32[256,256]{1,0:T(8,128)} %dst_ref.1, ...), custom_call_target="tpu_custom_call" | custom-call | tf_op jit(solution)/shard_map/pallas_call | solution.py:283
  8.0 0.6 %collective-permute-done = bf16[128,256]{1,0:T(8,128)(2,1)S(1)} collective-permute-done((bf16[128,256]{1,0:T(8,128)(2,1)}, bf16[128,256]{1,0:T(8,128)(2,1)S(1)}, u32[]{:S(2)}, u32[]{:S(2)}) %collective-permute-start) | collective-permute-done | bytes 65568 | tf_op jit(solution)/shard_map/ppermute | solution.py:304
  8.6 2.0 %collective-permute-start.5 = (bf16[256,256]{1,0:T(8,128)(2,1)S(1)}, bf16[256,256]{1,0:T(8,128)(2,1)S(1)}, u32[]{:S(2)}, u32[]{:S(2)}) collective-permute-start(bf16[256,256]{1,0:T(8,128)(2,1)S(1)} %constant_dynamic-update-slice_fusion.refs_0_), channel_id=1, source_target_pairs={{0,12},{4,8},{8,4},{12,0},{16,28},{20,24},{24,20},{28,16},{1,13},{... | collective-permute-start | bytes 393224 | tf_op jit(solution)/shard_map/ppermute | solution.py:304
  10.6 1.2 %collective-permute-start.4 = (bf16[256,256]{1,0:T(8,128)(2,1)S(1)}, bf16[256,256]{1,0:T(8,128)(2,1)S(1)}, u32[]{:S(2)}, u32[]{:S(2)}) collective-permute-start(bf16[256,256]{1,0:T(8,128)(2,1)S(1)} %constant_dynamic-update-slice_fusion.refs_0_), channel_id=1, source_target_pairs={{0,8},{4,12},{8,0},{12,4},{16,24},{20,28},{24,16},{28,20},{1,9},{5... | collective-permute-start | bytes 393224 | tf_op jit(solution)/shard_map/ppermute | solution.py:304
  11.8 0.3 collective-permute-start.3
  12.1 1.7 %collective-permute-start.1 = (bf16[128,256]{1,0:T(8,128)(2,1)}, bf16[128,256]{1,0:T(8,128)(2,1)S(1)}, u32[]{:S(2)}, u32[]{:S(2)}) collective-permute-start(bf16[128,256]{1,0:T(8,128)(2,1)} %features_ref.3), channel_id=1, source_target_pairs={{0,2},{1,3},{2,0},{3,1},{4,6},{5,7},{6,4},{7,5},{8,10},{9,11},{10,... | collective-permute-start | bytes 196616 | tf_op jit(solution)/shard_map/ppermute | solution.py:304
  13.8 0.3 collective-permute-start.2
  14.1 0.0 copy-start
  14.1 0.0 copy-start.1
  14.1 0.0 copy-start.2
  14.1 0.0 copy-start.3
  14.1 0.0 copy-start.4
  14.1 3.3 %shard_map.138.adj_ref = bf16[512,1024]{1,0:T(8,128)(2,1)S(1)} custom-call(s32[256]{0:T(256)} %row_ref.3, s32[256]{0:T(256)} %col_ref.3, s32[256]{0:T(256)} %count_ref.3, s32[128,256]{1,0:T(8,128)S(1)} %get-tuple-element.43.src_ref, s32[128,256]{1,0:T(8,128)S(1)} %get-tuple-element.44.dst_ref, f32[4,8,128,128]{3,2,1,0:T(8,128)S(1)} %get-tuple-element.48.half_ref), custom_call_target="tpu_custom_call" | custom-call | tf_op jit(solution)/shard_map/pallas_call | solution.py:283
  17.5 0.0 collective-permute-done.1.near_features_ref
  17.5 0.8 %collective-permute-done.2.near_d_out_ref = bf16[128,256]{1,0:T(8,128)(2,1)S(1)} collective-permute-done((bf16[128,256]{1,0:T(8,128)(2,1)}, bf16[128,256]{1,0:T(8,128)(2,1)S(1)}, u32[]{:S(2)}, u32[]{:S(2)}) %collective-permute-start.2) | collective-permute-done | bytes 65568 | tf_op jit(solution)/shard_map/ppermute | solution.py:304
  18.3 0.0 collective-permute-done.5.refs_3_
  18.3 0.0 collective-permute-done.4.refs_2_
  18.3 0.0 collective-permute-done.3.refs_1_
  18.3 0.7 %shard_map.139 = (f32[272,256]{1,0:T(8,128)S(1)}, bf16[272,256]{1,0:T(8,128)(2,1)S(1)}) custom-call(bf16[512,1024]{1,0:T(8,128)(2,1)S(1)} %shard_map.138.adj_ref, bf16[256,256]{1,0:T(8,128)(2,1)S(1)} %constant_dynamic-update-slice_fusion.refs_0_, bf16[256,256]{1,0:T(8,128)(2,1)S(1)} %collective-permute-done.3.refs_1_, ...), custom_call_target="tpu_custom_call" | custom-call | tf_op jit(solution)/shard_map/pallas_call | solution.py:283
  19.0 0.1 collective-permute-start.6
  19.1 1.3 %collective-permute-done.6.got_ref = bf16[272,256]{1,0:T(8,128)(2,1)S(1)} collective-permute-done((bf16[272,256]{1,0:T(8,128)(2,1)S(1)}, bf16[272,256]{1,0:T(8,128)(2,1)S(1)}, u32[]{:S(2)}, u32[]{:S(2)}) %collective-permute-start.6) | collective-permute-done | bytes 139296 | tf_op jit(solution)/shard_map/ppermute | solution.py:304
  20.4 1.0 %collective-permute-start.7 = (bf16[272,256]{1,0:T(8,128)(2,1)S(1)}, bf16[272,256]{1,0:T(8,128)(2,1)S(1)}, u32[]{:S(2)}, u32[]{:S(2)}) collective-permute-start(bf16[272,256]{1,0:T(8,128)(2,1)S(1)} %shard_map.140.pair_ref), channel_id=1, source_target_pairs={{0,2},{1,3},{2,0},{3,1},{4,6},{5,7},{6,4},{7,5},{8,10},{9,11},{10,... | collective-permute-start | bytes 417800 | tf_op jit(solution)/shard_map/ppermute | solution.py:304
  21.5 4.8 %collective-permute-done.7.got_ref = bf16[272,256]{1,0:T(8,128)(2,1)S(1)} collective-permute-done((bf16[272,256]{1,0:T(8,128)(2,1)S(1)}, bf16[272,256]{1,0:T(8,128)(2,1)S(1)}, u32[]{:S(2)}, u32[]{:S(2)}) %collective-permute-start.7) | collective-permute-done | bytes 139296 | tf_op jit(solution)/shard_map/ppermute | solution.py:304
  26.2 0.0 copy-done
  26.2 0.0 copy-done.1
  26.2 0.0 copy-done.2
  26.2 0.0 copy-done.3
  26.2 0.0 copy-done.4
  26.3 0.7 %shard_map.141 = (bf16[128,256]{1,0:T(8,128)(2,1)S(1)}, f32[128,256]{1,0:T(8,128)S(1)}, f32[144,256]{1,0:T(8,128)S(1)}, bf16[400,256]{1,0:T(8,128)(2,1)S(1)}) custom-call(bf16[272,256]{1,0:T(8,128)(2,1)S(1)} %shard_map.140.pair_ref, bf16[272,256]{1,0:T(8,128)(2,1)S(1)} %collective-permute-done.7.got_ref, bf16[128,256]{1,0:T(8,128)(2,1)S(1)} %copy-done, ...), custom_call_target="tpu_custom_call" | custom-call | tf_op jit(solution)/shard_map/pallas_call | solution.py:283
  26.9 0.1 collective-permute-start.8
  27.0 1.4 %collective-permute-done.8.got_ref = bf16[400,256]{1,0:T(8,128)(2,1)S(1)} collective-permute-done((bf16[400,256]{1,0:T(8,128)(2,1)S(1)}, bf16[400,256]{1,0:T(8,128)(2,1)S(1)}, u32[]{:S(2)}, u32[]{:S(2)}) %collective-permute-start.8) | collective-permute-done | bytes 204832 | tf_op jit(solution)/shard_map/ppermute | solution.py:304
  28.5 1.9 %collective-permute-start.14 = (bf16[144,256]{1,0:T(8,128)(2,1)S(1)}, bf16[144,256]{1,0:T(8,128)(2,1)S(1)}, u32[]{:S(2)}, u32[]{:S(2)}) collective-permute-start(bf16[144,256]{1,0:T(8,128)(2,1)S(1)} %shard_map.142.refs_0_), channel_id=1, source_target_pairs={{0,12},{4,8},{8,4},{12,0},{16,28},{20,24},{24,20},{28,16},{1,13},{... | collective-permute-start | bytes 221192 | tf_op jit(solution)/shard_map/ppermute | solution.py:304
  30.4 1.2 %collective-permute-start.13 = (bf16[144,256]{1,0:T(8,128)(2,1)S(1)}, bf16[144,256]{1,0:T(8,128)(2,1)S(1)}, u32[]{:S(2)}, u32[]{:S(2)}) collective-permute-start(bf16[144,256]{1,0:T(8,128)(2,1)S(1)} %shard_map.142.refs_0_), channel_id=1, source_target_pairs={{0,8},{4,12},{8,0},{12,4},{16,24},{20,28},{24,16},{28,20},{1,9},{5... | collective-permute-start | bytes 221192 | tf_op jit(solution)/shard_map/ppermute | solution.py:304
  31.5 0.5 collective-permute-start.12
  32.0 0.5 shard_map.143
  32.5 1.6 %collective-permute-start.9 = (bf16[256,256]{1,0:T(8,128)(2,1)S(1)}, bf16[256,256]{1,0:T(8,128)(2,1)S(1)}, u32[]{:S(2)}, u32[]{:S(2)}) collective-permute-start(bf16[256,256]{1,0:T(8,128)(2,1)S(1)} %get-tuple-element.66), channel_id=1, source_target_pairs={{0,4},{4,0},{8,12},{12,8},{16,20},{20,16},{24,28},{28,24},{1,5},{5... | collective-permute-start | bytes 393224 | tf_op jit(solution)/shard_map/ppermute | solution.py:304
  34.1 0.9 %collective-permute-start.10 = (bf16[256,256]{1,0:T(8,128)(2,1)S(1)}, bf16[256,256]{1,0:T(8,128)(2,1)S(1)}, u32[]{:S(2)}, u32[]{:S(2)}) collective-permute-start(bf16[256,256]{1,0:T(8,128)(2,1)S(1)} %get-tuple-element.67), channel_id=1, source_target_pairs={{0,8},{4,12},{8,0},{12,4},{16,24},{20,28},{24,16},{28,20},{1,9},{5... | collective-permute-start | bytes 393224 | tf_op jit(solution)/shard_map/ppermute | solution.py:304
  35.0 0.0 collective-permute-done.14.refs_3_
  35.0 1.3 %collective-permute-start.11 = (bf16[256,256]{1,0:T(8,128)(2,1)S(1)}, bf16[256,256]{1,0:T(8,128)(2,1)S(1)}, u32[]{:S(2)}, u32[]{:S(2)}) collective-permute-start(bf16[256,256]{1,0:T(8,128)(2,1)S(1)} %get-tuple-element.68), channel_id=1, source_target_pairs={{0,12},{4,8},{8,4},{12,0},{16,28},{20,24},{24,20},{28,16},{1,13},{... | collective-permute-start | bytes 393224 | tf_op jit(solution)/shard_map/ppermute | solution.py:304
  36.3 0.0 collective-permute-done.13.refs_2_
  36.4 0.4 collective-permute-done.12.refs_1_
  36.8 2.6 %collective-permute-start.15 = (bf16[144,256]{1,0:T(8,128)(2,1)S(1)}, bf16[144,256]{1,0:T(8,128)(2,1)S(1)}, u32[]{:S(2)}, u32[]{:S(2)}) collective-permute-start(bf16[144,256]{1,0:T(8,128)(2,1)S(1)} %shard_map.145.refs_0_), channel_id=1, source_target_pairs={{0,16},{4,20},{8,24},{12,28},{16,0},{20,4},{24,8},{28,12},{1,17},{... | collective-permute-start | bytes 221192 | tf_op jit(solution)/shard_map/ppermute | solution.py:304
  39.4 0.4 collective-permute-done.9.refs_0_
  39.8 0.9 %collective-permute-done.10.refs_1_ = bf16[256,256]{1,0:T(8,128)(2,1)S(1)} collective-permute-done((bf16[256,256]{1,0:T(8,128)(2,1)S(1)}, bf16[256,256]{1,0:T(8,128)(2,1)S(1)}, u32[]{:S(2)}, u32[]{:S(2)}) %collective-permute-start.10) | collective-permute-done | bytes 131104 | tf_op jit(solution)/shard_map/ppermute | solution.py:304
  40.7 2.0 %collective-permute-done.11.refs_2_ = bf16[256,256]{1,0:T(8,128)(2,1)S(1)} collective-permute-done((bf16[256,256]{1,0:T(8,128)(2,1)S(1)}, bf16[256,256]{1,0:T(8,128)(2,1)S(1)}, u32[]{:S(2)}, u32[]{:S(2)}) %collective-permute-start.11) | collective-permute-done | bytes 131104 | tf_op jit(solution)/shard_map/ppermute | solution.py:304
  42.7 0.7 %shard_map.144 = (f32[128,256]{1,0:T(8,128)S(1)}, bf16[128,256]{1,0:T(8,128)(2,1)S(1)}, bf16[128,256]{1,0:T(8,128)(2,1)}) custom-call(f32[256,256]{1,0:T(8,128)S(1)} %get-tuple-element.65.keep_ref, bf16[256,256]{1,0:T(8,128)(2,1)S(1)} %collective-permute-done.9.refs_0_, bf16[256,256]{1,0:T(8,128)(2,1)S(1)} %collective-permute-done.10.refs_1_, ...), custom_call_target="tpu_custom_call" | custom-call | tf_op jit(solution)/shard_map/pallas_call | solution.py:283
  43.4 1.7 %collective-permute-start.19 = (bf16[128,256]{1,0:T(8,128)(2,1)S(1)}, bf16[128,256]{1,0:T(8,128)(2,1)S(1)}, u32[]{:S(2)}, u32[]{:S(2)}) collective-permute-start(bf16[128,256]{1,0:T(8,128)(2,1)S(1)} %get-tuple-element.76), channel_id=1, source_target_pairs={{0,16},{4,20},{8,24},{12,28},{16,0},{20,4},{24,8},{28,12},{1,17},{... | collective-permute-start | bytes 196616 | tf_op jit(solution)/shard_map/ppermute | solution.py:304
  45.1 0.0 collective-permute-done.15.refs_1_
  45.2 0.1 collective-permute-start.18
  45.3 1.1 %collective-permute-start.17 = (bf16[128,256]{1,0:T(8,128)(2,1)S(1)}, bf16[128,256]{1,0:T(8,128)(2,1)S(1)}, u32[]{:S(2)}, u32[]{:S(2)}) collective-permute-start(bf16[128,256]{1,0:T(8,128)(2,1)S(1)} %get-tuple-element.74.refs_0_), channel_id=1, source_target_pairs={{0,2},{1,3},{2,0},{3,1},{4,6},{5,7},{6,4},{7,5},{8,10},{9,11},{10,... | collective-permute-start | bytes 196616 | tf_op jit(solution)/shard_map/ppermute | solution.py:304
  46.3 0.8 %collective-permute-start.16 = (bf16[128,256]{1,0:T(8,128)(2,1)S(1)}, bf16[128,256]{1,0:T(8,128)(2,1)S(1)}, u32[]{:S(2)}, u32[]{:S(2)}) collective-permute-start(bf16[128,256]{1,0:T(8,128)(2,1)S(1)} %get-tuple-element.74.refs_0_), channel_id=1, source_target_pairs={{0,1},{1,0},{2,3},{3,2},{4,5},{5,4},{6,7},{7,6},{8,9},{9,8},{10,11... | collective-permute-start | bytes 196616 | tf_op jit(solution)/shard_map/ppermute | solution.py:304
  47.1 2.2 %collective-permute-done.19.refs_5_ = bf16[128,256]{1,0:T(8,128)(2,1)S(1)} collective-permute-done((bf16[128,256]{1,0:T(8,128)(2,1)S(1)}, bf16[128,256]{1,0:T(8,128)(2,1)S(1)}, u32[]{:S(2)}, u32[]{:S(2)}) %collective-permute-start.19) | collective-permute-done | bytes 65568 | tf_op jit(solution)/shard_map/ppermute | solution.py:304
  49.3 0.2 collective-permute-done.18.refs_3_
  49.5 0.7 %collective-permute-done.17.refs_2_ = bf16[128,256]{1,0:T(8,128)(2,1)S(1)} collective-permute-done((bf16[128,256]{1,0:T(8,128)(2,1)S(1)}, bf16[128,256]{1,0:T(8,128)(2,1)S(1)}, u32[]{:S(2)}, u32[]{:S(2)}) %collective-permute-start.17) | collective-permute-done | bytes 65568 | tf_op jit(solution)/shard_map/ppermute | solution.py:304
  50.2 0.0 collective-permute-done.16.refs_1_
  50.2 0.9 %shard_map.147 = (f32[128,256]{1,0:T(8,128)}, f32[2,128,256]{2,1,0:T(8,128)}, f32[2,128,256]{2,1,0:T(8,128)}, f32[1,256]{1,0:T(1,128)}) custom-call(f32[128,256]{1,0:T(8,128)S(1)} %get-tuple-element.71.self_ref, f32[1,256]{1,0:T(1,128)S(1)} %get-tuple-element.73.bias_term_ref, bf16[128,256]{1,0:T(8,128)(2,1)S(1)} %get-tuple-element.74.refs_0_, ...), custom_call_target="tpu_custom_call" | custom-call | tf_op jit(solution)/shard_map/pallas_call | solution.py:283
  (5 shorter events, 0.1 us)
Async XLA Ops:
  0.6 8.0 %collective-permute-start = (bf16[128,256]{1,0:T(8,128)(2,1)}, bf16[128,256]{1,0:T(8,128)(2,1)S(1)}, u32[]{:S(2)}, u32[]{:S(2)}) collective-permute-start(bf16[128,256]{1,0:T(8,128)(2,1)} %features_ref.3), channel_id=1, source_target_pairs={{0,16},{4,20},{8,24},{12,28},{16,0},{20,4},{24,8},{28,12},{1,17},{... | collective-permute-start | bytes 196616 | tf_op jit(solution)/shard_map/ppermute | solution.py:304
  8.6 9.7 %collective-permute-start.5 = (bf16[256,256]{1,0:T(8,128)(2,1)S(1)}, bf16[256,256]{1,0:T(8,128)(2,1)S(1)}, u32[]{:S(2)}, u32[]{:S(2)}) collective-permute-start(bf16[256,256]{1,0:T(8,128)(2,1)S(1)} %constant_dynamic-update-slice_fusion.refs_0_), channel_id=1, source_target_pairs={{0,12},{4,8},{8,4},{12,0},{16,28},{20,24},{24,20},{28,16},{1,13},{... | collective-permute-start | bytes 393224 | tf_op jit(solution)/shard_map/ppermute | solution.py:304
  10.6 7.6 %collective-permute-start.4 = (bf16[256,256]{1,0:T(8,128)(2,1)S(1)}, bf16[256,256]{1,0:T(8,128)(2,1)S(1)}, u32[]{:S(2)}, u32[]{:S(2)}) collective-permute-start(bf16[256,256]{1,0:T(8,128)(2,1)S(1)} %constant_dynamic-update-slice_fusion.refs_0_), channel_id=1, source_target_pairs={{0,8},{4,12},{8,0},{12,4},{16,24},{20,28},{24,16},{28,20},{1,9},{5... | collective-permute-start | bytes 393224 | tf_op jit(solution)/shard_map/ppermute | solution.py:304
  11.8 6.5 %collective-permute-start.3 = (bf16[256,256]{1,0:T(8,128)(2,1)S(1)}, bf16[256,256]{1,0:T(8,128)(2,1)S(1)}, u32[]{:S(2)}, u32[]{:S(2)}) collective-permute-start(bf16[256,256]{1,0:T(8,128)(2,1)S(1)} %constant_dynamic-update-slice_fusion.refs_0_), channel_id=1, source_target_pairs={{0,4},{4,0},{8,12},{12,8},{16,20},{20,16},{24,28},{28,24},{1,5},{5... | collective-permute-start | bytes 393224 | tf_op jit(solution)/shard_map/ppermute | solution.py:304
  12.1 5.4 %collective-permute-start.1 = (bf16[128,256]{1,0:T(8,128)(2,1)}, bf16[128,256]{1,0:T(8,128)(2,1)S(1)}, u32[]{:S(2)}, u32[]{:S(2)}) collective-permute-start(bf16[128,256]{1,0:T(8,128)(2,1)} %features_ref.3), channel_id=1, source_target_pairs={{0,2},{1,3},{2,0},{3,1},{4,6},{5,7},{6,4},{7,5},{8,10},{9,11},{10,... | collective-permute-start | bytes 196616 | tf_op jit(solution)/shard_map/ppermute | solution.py:304
  13.8 4.5 %collective-permute-start.2 = (bf16[128,256]{1,0:T(8,128)(2,1)}, bf16[128,256]{1,0:T(8,128)(2,1)S(1)}, u32[]{:S(2)}, u32[]{:S(2)}) collective-permute-start(bf16[128,256]{1,0:T(8,128)(2,1)} %d_out_ref.1), channel_id=1, source_target_pairs={{0,2},{1,3},{2,0},{3,1},{4,6},{5,7},{6,4},{7,5},{8,10},{9,11},{10,... | collective-permute-start | bytes 196616 | tf_op jit(solution)/shard_map/ppermute | solution.py:304
  14.1 12.1 %copy-start = (bf16[128,256]{1,0:T(8,128)(2,1)S(1)}, bf16[128,256]{1,0:T(8,128)(2,1)}, u32[]{:S(2)}) copy-start(bf16[128,256]{1,0:T(8,128)(2,1)} %features_ref.3) | copy-start | bytes 196612
  14.1 12.1 %copy-start.1 = (bf16[256,256]{1,0:T(8,128)(2,1)S(1)}, bf16[256,256]{1,0:T(8,128)(2,1)}, u32[]{:S(2)}) copy-start(bf16[256,256]{1,0:T(8,128)(2,1)} %w_self_ref.1) | copy-start | bytes 393220
  14.1 12.1 %copy-start.2 = (bf16[256,256]{1,0:T(8,128)(2,1)S(1)}, bf16[256,256]{1,0:T(8,128)(2,1)}, u32[]{:S(2)}) copy-start(bf16[256,256]{1,0:T(8,128)(2,1)} %w_neigh_ref.1) | copy-start | bytes 393220
  14.1 12.1 %copy-start.3 = (bf16[128,256]{1,0:T(8,128)(2,1)S(1)}, bf16[128,256]{1,0:T(8,128)(2,1)}, u32[]{:S(2)}) copy-start(bf16[128,256]{1,0:T(8,128)(2,1)} %d_out_ref.1) | copy-start | bytes 196612
  14.1 12.1 %copy-start.4 = (f32[256]{0:T(256)S(1)}, f32[256]{0:T(256)}, u32[]{:S(2)}) copy-start(f32[256]{0:T(256)} %param.13) | copy-start | bytes 3076
  19.0 1.4 %collective-permute-start.6 = (bf16[272,256]{1,0:T(8,128)(2,1)S(1)}, bf16[272,256]{1,0:T(8,128)(2,1)S(1)}, u32[]{:S(2)}, u32[]{:S(2)}) collective-permute-start(bf16[272,256]{1,0:T(8,128)(2,1)S(1)} %get-tuple-element.59), channel_id=1, source_target_pairs={{0,1},{1,0},{2,3},{3,2},{4,5},{5,4},{6,7},{7,6},{8,9},{9,8},{10,11... | collective-permute-start | bytes 417800 | tf_op jit(solution)/shard_map/ppermute | solution.py:304
  20.4 5.8 %collective-permute-start.7 = (bf16[272,256]{1,0:T(8,128)(2,1)S(1)}, bf16[272,256]{1,0:T(8,128)(2,1)S(1)}, u32[]{:S(2)}, u32[]{:S(2)}) collective-permute-start(bf16[272,256]{1,0:T(8,128)(2,1)S(1)} %shard_map.140.pair_ref), channel_id=1, source_target_pairs={{0,2},{1,3},{2,0},{3,1},{4,6},{5,7},{6,4},{7,5},{8,10},{9,11},{10,... | collective-permute-start | bytes 417800 | tf_op jit(solution)/shard_map/ppermute | solution.py:304
  26.9 1.5 %collective-permute-start.8 = (bf16[400,256]{1,0:T(8,128)(2,1)S(1)}, bf16[400,256]{1,0:T(8,128)(2,1)S(1)}, u32[]{:S(2)}, u32[]{:S(2)}) collective-permute-start(bf16[400,256]{1,0:T(8,128)(2,1)S(1)} %get-tuple-element.62.sent_ref), channel_id=1, source_target_pairs={{0,1},{1,0},{2,3},{3,2},{4,5},{5,4},{6,7},{7,6},{8,9},{9,8},{10,11... | collective-permute-start | bytes 614408 | tf_op jit(solution)/shard_map/ppermute | solution.py:304
  28.5 6.5 %collective-permute-start.14 = (bf16[144,256]{1,0:T(8,128)(2,1)S(1)}, bf16[144,256]{1,0:T(8,128)(2,1)S(1)}, u32[]{:S(2)}, u32[]{:S(2)}) collective-permute-start(bf16[144,256]{1,0:T(8,128)(2,1)S(1)} %shard_map.142.refs_0_), channel_id=1, source_target_pairs={{0,12},{4,8},{8,4},{12,0},{16,28},{20,24},{24,20},{28,16},{1,13},{... | collective-permute-start | bytes 221192 | tf_op jit(solution)/shard_map/ppermute | solution.py:304
  30.4 6.0 %collective-permute-start.13 = (bf16[144,256]{1,0:T(8,128)(2,1)S(1)}, bf16[144,256]{1,0:T(8,128)(2,1)S(1)}, u32[]{:S(2)}, u32[]{:S(2)}) collective-permute-start(bf16[144,256]{1,0:T(8,128)(2,1)S(1)} %shard_map.142.refs_0_), channel_id=1, source_target_pairs={{0,8},{4,12},{8,0},{12,4},{16,24},{20,28},{24,16},{28,20},{1,9},{5... | collective-permute-start | bytes 221192 | tf_op jit(solution)/shard_map/ppermute | solution.py:304
  31.5 5.2 %collective-permute-start.12 = (bf16[144,256]{1,0:T(8,128)(2,1)S(1)}, bf16[144,256]{1,0:T(8,128)(2,1)S(1)}, u32[]{:S(2)}, u32[]{:S(2)}) collective-permute-start(bf16[144,256]{1,0:T(8,128)(2,1)S(1)} %shard_map.142.refs_0_), channel_id=1, source_target_pairs={{0,4},{4,0},{8,12},{12,8},{16,20},{20,16},{24,28},{28,24},{1,5},{5... | collective-permute-start | bytes 221192 | tf_op jit(solution)/shard_map/ppermute | solution.py:304
  32.5 7.3 %collective-permute-start.9 = (bf16[256,256]{1,0:T(8,128)(2,1)S(1)}, bf16[256,256]{1,0:T(8,128)(2,1)S(1)}, u32[]{:S(2)}, u32[]{:S(2)}) collective-permute-start(bf16[256,256]{1,0:T(8,128)(2,1)S(1)} %get-tuple-element.66), channel_id=1, source_target_pairs={{0,4},{4,0},{8,12},{12,8},{16,20},{20,16},{24,28},{28,24},{1,5},{5... | collective-permute-start | bytes 393224 | tf_op jit(solution)/shard_map/ppermute | solution.py:304
  34.1 6.6 %collective-permute-start.10 = (bf16[256,256]{1,0:T(8,128)(2,1)S(1)}, bf16[256,256]{1,0:T(8,128)(2,1)S(1)}, u32[]{:S(2)}, u32[]{:S(2)}) collective-permute-start(bf16[256,256]{1,0:T(8,128)(2,1)S(1)} %get-tuple-element.67), channel_id=1, source_target_pairs={{0,8},{4,12},{8,0},{12,4},{16,24},{20,28},{24,16},{28,20},{1,9},{5... | collective-permute-start | bytes 393224 | tf_op jit(solution)/shard_map/ppermute | solution.py:304
  35.0 7.7 %collective-permute-start.11 = (bf16[256,256]{1,0:T(8,128)(2,1)S(1)}, bf16[256,256]{1,0:T(8,128)(2,1)S(1)}, u32[]{:S(2)}, u32[]{:S(2)}) collective-permute-start(bf16[256,256]{1,0:T(8,128)(2,1)S(1)} %get-tuple-element.68), channel_id=1, source_target_pairs={{0,12},{4,8},{8,4},{12,0},{16,28},{20,24},{24,20},{28,16},{1,13},{... | collective-permute-start | bytes 393224 | tf_op jit(solution)/shard_map/ppermute | solution.py:304
  36.8 8.4 %collective-permute-start.15 = (bf16[144,256]{1,0:T(8,128)(2,1)S(1)}, bf16[144,256]{1,0:T(8,128)(2,1)S(1)}, u32[]{:S(2)}, u32[]{:S(2)}) collective-permute-start(bf16[144,256]{1,0:T(8,128)(2,1)S(1)} %shard_map.145.refs_0_), channel_id=1, source_target_pairs={{0,16},{4,20},{8,24},{12,28},{16,0},{20,4},{24,8},{28,12},{1,17},{... | collective-permute-start | bytes 221192 | tf_op jit(solution)/shard_map/ppermute | solution.py:304
  43.4 5.9 %collective-permute-start.19 = (bf16[128,256]{1,0:T(8,128)(2,1)S(1)}, bf16[128,256]{1,0:T(8,128)(2,1)S(1)}, u32[]{:S(2)}, u32[]{:S(2)}) collective-permute-start(bf16[128,256]{1,0:T(8,128)(2,1)S(1)} %get-tuple-element.76), channel_id=1, source_target_pairs={{0,16},{4,20},{8,24},{12,28},{16,0},{20,4},{24,8},{28,12},{1,17},{... | collective-permute-start | bytes 196616 | tf_op jit(solution)/shard_map/ppermute | solution.py:304
  45.2 4.4 %collective-permute-start.18 = (bf16[128,256]{1,0:T(8,128)(2,1)S(1)}, bf16[128,256]{1,0:T(8,128)(2,1)S(1)}, u32[]{:S(2)}, u32[]{:S(2)}) collective-permute-start(bf16[128,256]{1,0:T(8,128)(2,1)S(1)} %get-tuple-element.74.refs_0_), channel_id=1, source_target_pairs={{0,3},{1,2},{2,1},{3,0},{4,7},{5,6},{6,5},{7,4},{8,11},{9,10},{10,... | collective-permute-start | bytes 196616 | tf_op jit(solution)/shard_map/ppermute | solution.py:304
  45.3 5.0 %collective-permute-start.17 = (bf16[128,256]{1,0:T(8,128)(2,1)S(1)}, bf16[128,256]{1,0:T(8,128)(2,1)S(1)}, u32[]{:S(2)}, u32[]{:S(2)}) collective-permute-start(bf16[128,256]{1,0:T(8,128)(2,1)S(1)} %get-tuple-element.74.refs_0_), channel_id=1, source_target_pairs={{0,2},{1,3},{2,0},{3,1},{4,6},{5,7},{6,4},{7,5},{8,10},{9,11},{10,... | collective-permute-start | bytes 196616 | tf_op jit(solution)/shard_map/ppermute | solution.py:304
  46.3 3.9 %collective-permute-start.16 = (bf16[128,256]{1,0:T(8,128)(2,1)S(1)}, bf16[128,256]{1,0:T(8,128)(2,1)S(1)}, u32[]{:S(2)}, u32[]{:S(2)}) collective-permute-start(bf16[128,256]{1,0:T(8,128)(2,1)S(1)} %get-tuple-element.74.refs_0_), channel_id=1, source_target_pairs={{0,1},{1,0},{2,3},{3,2},{4,5},{5,4},{6,7},{7,6},{8,9},{9,8},{10,11... | collective-permute-start | bytes 196616 | tf_op jit(solution)/shard_map/ppermute | solution.py:304

commit v10 on v9

--- a/solution.py
+++ b/solution.py
@@ -387,7 +387,7 @@
         (adjacency, send, back),
     )
     near_terms = [terms] + [swap(terms, "row", m) for m in range(1, 4)]
-    got = [swap(msg, "row", m + 1) for m, msg in enumerate(near_msgs)]
+    got = [swap(msg, "row", m + 1) for m, msg in enumerate(near_msgs)][::-1]
     terms = call(part_terms_kernel, terms_shape, [VMEM] * 4, near_terms)
     far_terms = [terms] + [swap(terms, "row", 4 * h) for h in range(1, far)]
     quarter, bias_term = call(

time: 51.3 us -> 50.8 us (level)
  starting transfers between devices: 24.4 us -> 22 us
  waiting for transfers between devices: 15.8 us -> 17.7 us
    ppermute x20, starting transfers between devices: 24.4 us -> 22 us  [swap(): lax.ppermute(value, axis, [(i, i ^ bits) for i in range(lax.axis_size(axi...]
    ppermute x20, waiting for transfers between devices: 15.8 us -> 17.7 us  [swap(): lax.ppermute(value, axis, [(i, i ^ bits) for i in range(lax.axis_size(axi...]
  transfers between devices with their start and end apart: 20 -> 20, of which waited for: 12 -> 11; matrix products, arithmetic and copies ran while one was open for 0% -> 0% of each run, Pallas kernels for 15% -> 16%
where the time goes in v10:
time: 50.8 us; the launch traced here: 50.6 us
  starting transfers between devices  22 us (43%)
  waiting for transfers between devices  17.7 us (35%)
  Pallas kernels  10.1 us (20%)
  between operations  0.77 us (2%)
    ppermute x20, starting transfers between devices, swap(): lax.ppermute(value, axis, [(i, i ^ bits) for i in range(lax.axis_size(axi...  22 us
    ppermute x20, waiting for transfers between devices, swap(): lax.ppermute(value, axis, [(i, i ^ bits) for i in range(lax.axis_size(axi...  17.7 us
    pallas_call x11, Pallas kernels, call(): pl.pallas_call(kernel, out_shape=out_shape, in_specs=specs, out_specs=[VM...  10.1 us
  transfers between devices with their start and end apart: 20, of which 11 were waited for; matrix products, arithmetic and copies ran while one was open for 0% of the time, Pallas kernels for 16%

profile of v10, /device:TPU:0, one launch (start us, length us, event | category | flops | bytes accessed | tf_op | source)
XLA Modules:
  0.0 50.6 jit_solution(5160878107341784193)
XLA Ops:
  0.6 4.1 %collective-permute-start = (bf16[128,256]{1,0:T(8,128)(2,1)}, bf16[128,256]{1,0:T(8,128)(2,1)S(1)}, u32[]{:S(2)}, u32[]{:S(2)}) collective-permute-start(bf16[128,256]{1,0:T(8,128)(2,1)} %features_ref.3), channel_id=1, source_target_pairs={{0,16},{4,20},{8,24},{12,28},{16,0},{20,4},{24,8},{28,12},{1,17},{... | collective-permute-start | bytes 196616 | tf_op jit(solution)/shard_map/ppermute | solution.py:304
  4.7 3.3 %shard_map.137 = (f32[4,8,128,128]{3,2,1,0:T(8,128)S(1)}, bf16[256,256]{1,0:T(8,128)(2,1)S(1)}, s32[128,256]{1,0:T(8,128)S(1)}, s32[128,256]{1,0:T(8,128)S(1)}) custom-call(s32[256]{0:T(256)} %row_ref.3, s32[256]{0:T(256)} %col_ref.3, s32[256]{0:T(256)} %count_ref.3, s32[256,256]{1,0:T(8,128)} %src_ref.1, s32[256,256]{1,0:T(8,128)} %dst_ref.1, ...), custom_call_target="tpu_custom_call" | custom-call | tf_op jit(solution)/shard_map/pallas_call | solution.py:283
  8.0 0.6 %collective-permute-done = bf16[128,256]{1,0:T(8,128)(2,1)S(1)} collective-permute-done((bf16[128,256]{1,0:T(8,128)(2,1)}, bf16[128,256]{1,0:T(8,128)(2,1)S(1)}, u32[]{:S(2)}, u32[]{:S(2)}) %collective-permute-start) | collective-permute-done | bytes 65568 | tf_op jit(solution)/shard_map/ppermute | solution.py:304
  8.6 2.0 %collective-permute-start.5 = (bf16[256,256]{1,0:T(8,128)(2,1)S(1)}, bf16[256,256]{1,0:T(8,128)(2,1)S(1)}, u32[]{:S(2)}, u32[]{:S(2)}) collective-permute-start(bf16[256,256]{1,0:T(8,128)(2,1)S(1)} %constant_dynamic-update-slice_fusion.refs_0_), channel_id=1, source_target_pairs={{0,12},{4,8},{8,4},{12,0},{16,28},{20,24},{24,20},{28,16},{1,13},{... | collective-permute-start | bytes 393224 | tf_op jit(solution)/shard_map/ppermute | solution.py:304
  10.6 1.2 %collective-permute-start.4 = (bf16[256,256]{1,0:T(8,128)(2,1)S(1)}, bf16[256,256]{1,0:T(8,128)(2,1)S(1)}, u32[]{:S(2)}, u32[]{:S(2)}) collective-permute-start(bf16[256,256]{1,0:T(8,128)(2,1)S(1)} %constant_dynamic-update-slice_fusion.refs_0_), channel_id=1, source_target_pairs={{0,8},{4,12},{8,0},{12,4},{16,24},{20,28},{24,16},{28,20},{1,9},{5... | collective-permute-start | bytes 393224 | tf_op jit(solution)/shard_map/ppermute | solution.py:304
  11.8 0.3 collective-permute-start.3
  12.1 1.7 %collective-permute-start.1 = (bf16[128,256]{1,0:T(8,128)(2,1)}, bf16[128,256]{1,0:T(8,128)(2,1)S(1)}, u32[]{:S(2)}, u32[]{:S(2)}) collective-permute-start(bf16[128,256]{1,0:T(8,128)(2,1)} %features_ref.3), channel_id=1, source_target_pairs={{0,2},{1,3},{2,0},{3,1},{4,6},{5,7},{6,4},{7,5},{8,10},{9,11},{10,... | collective-permute-start | bytes 196616 | tf_op jit(solution)/shard_map/ppermute | solution.py:304
  13.8 0.3 collective-permute-start.2
  14.1 0.0 copy-start
  14.1 0.0 copy-start.1
  14.1 0.0 copy-start.2
  14.1 0.0 copy-start.3
  14.1 0.0 copy-start.4
  14.1 3.3 %shard_map.138.adj_ref = bf16[512,1024]{1,0:T(8,128)(2,1)S(1)} custom-call(s32[256]{0:T(256)} %row_ref.3, s32[256]{0:T(256)} %col_ref.3, s32[256]{0:T(256)} %count_ref.3, s32[128,256]{1,0:T(8,128)S(1)} %get-tuple-element.43.src_ref, s32[128,256]{1,0:T(8,128)S(1)} %get-tuple-element.44.dst_ref, f32[4,8,128,128]{3,2,1,0:T(8,128)S(1)} %get-tuple-element.48.half_ref), custom_call_target="tpu_custom_call" | custom-call | tf_op jit(solution)/shard_map/pallas_call | solution.py:283
  17.5 0.0 collective-permute-done.1.near_features_ref
  17.5 0.8 %collective-permute-done.2.near_d_out_ref = bf16[128,256]{1,0:T(8,128)(2,1)S(1)} collective-permute-done((bf16[128,256]{1,0:T(8,128)(2,1)}, bf16[128,256]{1,0:T(8,128)(2,1)S(1)}, u32[]{:S(2)}, u32[]{:S(2)}) %collective-permute-start.2) | collective-permute-done | bytes 65568 | tf_op jit(solution)/shard_map/ppermute | solution.py:304
  18.3 0.0 collective-permute-done.5.refs_3_
  18.3 0.0 collective-permute-done.4.refs_2_
  18.3 0.0 collective-permute-done.3.refs_1_
  18.3 0.7 %shard_map.139 = (f32[272,256]{1,0:T(8,128)S(1)}, bf16[272,256]{1,0:T(8,128)(2,1)S(1)}) custom-call(bf16[512,1024]{1,0:T(8,128)(2,1)S(1)} %shard_map.138.adj_ref, bf16[256,256]{1,0:T(8,128)(2,1)S(1)} %constant_dynamic-update-slice_fusion.refs_0_, bf16[256,256]{1,0:T(8,128)(2,1)S(1)} %collective-permute-done.3.refs_1_, ...), custom_call_target="tpu_custom_call" | custom-call | tf_op jit(solution)/shard_map/pallas_call | solution.py:283
  19.0 0.1 collective-permute-start.6
  19.1 1.3 %collective-permute-done.6.got_ref = bf16[272,256]{1,0:T(8,128)(2,1)S(1)} collective-permute-done((bf16[272,256]{1,0:T(8,128)(2,1)S(1)}, bf16[272,256]{1,0:T(8,128)(2,1)S(1)}, u32[]{:S(2)}, u32[]{:S(2)}) %collective-permute-start.6) | collective-permute-done | bytes 139296 | tf_op jit(solution)/shard_map/ppermute | solution.py:304
  20.4 1.0 %collective-permute-start.7 = (bf16[272,256]{1,0:T(8,128)(2,1)S(1)}, bf16[272,256]{1,0:T(8,128)(2,1)S(1)}, u32[]{:S(2)}, u32[]{:S(2)}) collective-permute-start(bf16[272,256]{1,0:T(8,128)(2,1)S(1)} %shard_map.140.pair_ref), channel_id=1, source_target_pairs={{0,2},{1,3},{2,0},{3,1},{4,6},{5,7},{6,4},{7,5},{8,10},{9,11},{10,... | collective-permute-start | bytes 417800 | tf_op jit(solution)/shard_map/ppermute | solution.py:304
  21.5 4.8 %collective-permute-done.7.got_ref = bf16[272,256]{1,0:T(8,128)(2,1)S(1)} collective-permute-done((bf16[272,256]{1,0:T(8,128)(2,1)S(1)}, bf16[272,256]{1,0:T(8,128)(2,1)S(1)}, u32[]{:S(2)}, u32[]{:S(2)}) %collective-permute-start.7) | collective-permute-done | bytes 139296 | tf_op jit(solution)/shard_map/ppermute | solution.py:304
  26.2 0.0 copy-done
  26.2 0.0 copy-done.1
  26.2 0.0 copy-done.2
  26.2 0.0 copy-done.3
  26.2 0.0 copy-done.4
  26.3 0.7 %shard_map.141 = (bf16[128,256]{1,0:T(8,128)(2,1)S(1)}, f32[128,256]{1,0:T(8,128)S(1)}, f32[144,256]{1,0:T(8,128)S(1)}, bf16[400,256]{1,0:T(8,128)(2,1)S(1)}) custom-call(bf16[272,256]{1,0:T(8,128)(2,1)S(1)} %shard_map.140.pair_ref, bf16[272,256]{1,0:T(8,128)(2,1)S(1)} %collective-permute-done.7.got_ref, bf16[128,256]{1,0:T(8,128)(2,1)S(1)} %copy-done, ...), custom_call_target="tpu_custom_call" | custom-call | tf_op jit(solution)/shard_map/pallas_call | solution.py:283
  26.9 0.1 collective-permute-start.8
  27.0 1.4 %collective-permute-done.8.got_ref = bf16[400,256]{1,0:T(8,128)(2,1)S(1)} collective-permute-done((bf16[400,256]{1,0:T(8,128)(2,1)S(1)}, bf16[400,256]{1,0:T(8,128)(2,1)S(1)}, u32[]{:S(2)}, u32[]{:S(2)}) %collective-permute-start.8) | collective-permute-done | bytes 204832 | tf_op jit(solution)/shard_map/ppermute | solution.py:304
  28.5 1.9 %collective-permute-start.14 = (bf16[144,256]{1,0:T(8,128)(2,1)S(1)}, bf16[144,256]{1,0:T(8,128)(2,1)S(1)}, u32[]{:S(2)}, u32[]{:S(2)}) collective-permute-start(bf16[144,256]{1,0:T(8,128)(2,1)S(1)} %shard_map.142.refs_0_), channel_id=1, source_target_pairs={{0,12},{4,8},{8,4},{12,0},{16,28},{20,24},{24,20},{28,16},{1,13},{... | collective-permute-start | bytes 221192 | tf_op jit(solution)/shard_map/ppermute | solution.py:304
  30.4 1.2 %collective-permute-start.13 = (bf16[144,256]{1,0:T(8,128)(2,1)S(1)}, bf16[144,256]{1,0:T(8,128)(2,1)S(1)}, u32[]{:S(2)}, u32[]{:S(2)}) collective-permute-start(bf16[144,256]{1,0:T(8,128)(2,1)S(1)} %shard_map.142.refs_0_), channel_id=1, source_target_pairs={{0,8},{4,12},{8,0},{12,4},{16,24},{20,28},{24,16},{28,20},{1,9},{5... | collective-permute-start | bytes 221192 | tf_op jit(solution)/shard_map/ppermute | solution.py:304
  31.5 0.5 collective-permute-start.12
  32.0 0.5 shard_map.143
  32.5 1.9 %collective-permute-start.9 = (bf16[256,256]{1,0:T(8,128)(2,1)S(1)}, bf16[256,256]{1,0:T(8,128)(2,1)S(1)}, u32[]{:S(2)}, u32[]{:S(2)}) collective-permute-start(bf16[256,256]{1,0:T(8,128)(2,1)S(1)} %get-tuple-element.66), channel_id=1, source_target_pairs={{0,12},{4,8},{8,4},{12,0},{16,28},{20,24},{24,20},{28,16},{1,13},{... | collective-permute-start | bytes 393224 | tf_op jit(solution)/shard_map/ppermute | solution.py:304
  34.4 1.2 %collective-permute-start.10 = (bf16[256,256]{1,0:T(8,128)(2,1)S(1)}, bf16[256,256]{1,0:T(8,128)(2,1)S(1)}, u32[]{:S(2)}, u32[]{:S(2)}) collective-permute-start(bf16[256,256]{1,0:T(8,128)(2,1)S(1)} %get-tuple-element.67), channel_id=1, source_target_pairs={{0,8},{4,12},{8,0},{12,4},{16,24},{20,28},{24,16},{28,20},{1,9},{5... | collective-permute-start | bytes 393224 | tf_op jit(solution)/shard_map/ppermute | solution.py:304
  35.6 0.0 collective-permute-done.14.refs_3_
  35.6 0.5 collective-permute-start.11
  36.1 0.0 collective-permute-done.13.refs_2_
  36.1 1.9 %collective-permute-done.12.refs_1_ = bf16[144,256]{1,0:T(8,128)(2,1)S(1)} collective-permute-done((bf16[144,256]{1,0:T(8,128)(2,1)S(1)}, bf16[144,256]{1,0:T(8,128)(2,1)S(1)}, u32[]{:S(2)}, u32[]{:S(2)}) %collective-permute-start.12) | collective-permute-done | bytes 73760 | tf_op jit(solution)/shard_map/ppermute | solution.py:304
  38.1 0.1 collective-permute-start.15
  38.1 2.4 %collective-permute-done.9.refs_0_ = bf16[256,256]{1,0:T(8,128)(2,1)S(1)} collective-permute-done((bf16[256,256]{1,0:T(8,128)(2,1)S(1)}, bf16[256,256]{1,0:T(8,128)(2,1)S(1)}, u32[]{:S(2)}, u32[]{:S(2)}) %collective-permute-start.9) | collective-permute-done | bytes 131104 | tf_op jit(solution)/shard_map/ppermute | solution.py:304
  40.5 1.3 %collective-permute-done.10.refs_1_ = bf16[256,256]{1,0:T(8,128)(2,1)S(1)} collective-permute-done((bf16[256,256]{1,0:T(8,128)(2,1)S(1)}, bf16[256,256]{1,0:T(8,128)(2,1)S(1)}, u32[]{:S(2)}, u32[]{:S(2)}) %collective-permute-start.10) | collective-permute-done | bytes 131104 | tf_op jit(solution)/shard_map/ppermute | solution.py:304
  41.9 0.0 collective-permute-done.11.refs_2_
  41.9 0.7 %shard_map.144 = (f32[128,256]{1,0:T(8,128)S(1)}, bf16[128,256]{1,0:T(8,128)(2,1)S(1)}, bf16[128,256]{1,0:T(8,128)(2,1)}) custom-call(f32[256,256]{1,0:T(8,128)S(1)} %get-tuple-element.65.keep_ref, bf16[256,256]{1,0:T(8,128)(2,1)S(1)} %collective-permute-done.9.refs_0_, bf16[256,256]{1,0:T(8,128)(2,1)S(1)} %collective-permute-done.10.refs_1_, ...), custom_call_target="tpu_custom_call" | custom-call | tf_op jit(solution)/shard_map/pallas_call | solution.py:283
  42.5 2.1 %collective-permute-start.19 = (bf16[128,256]{1,0:T(8,128)(2,1)S(1)}, bf16[128,256]{1,0:T(8,128)(2,1)S(1)}, u32[]{:S(2)}, u32[]{:S(2)}) collective-permute-start(bf16[128,256]{1,0:T(8,128)(2,1)S(1)} %get-tuple-element.76), channel_id=1, source_target_pairs={{0,16},{4,20},{8,24},{12,28},{16,0},{20,4},{24,8},{28,12},{1,17},{... | collective-permute-start | bytes 196616 | tf_op jit(solution)/shard_map/ppermute | solution.py:304
  44.7 0.0 collective-permute-done.15.refs_1_
  44.7 0.1 collective-permute-start.18
  44.8 1.0 %collective-permute-start.17 = (bf16[128,256]{1,0:T(8,128)(2,1)S(1)}, bf16[128,256]{1,0:T(8,128)(2,1)S(1)}, u32[]{:S(2)}, u32[]{:S(2)}) collective-permute-start(bf16[128,256]{1,0:T(8,128)(2,1)S(1)} %get-tuple-element.74.refs_0_), channel_id=1, source_target_pairs={{0,2},{1,3},{2,0},{3,1},{4,6},{5,7},{6,4},{7,5},{8,10},{9,11},{10,... | collective-permute-start | bytes 196616 | tf_op jit(solution)/shard_map/ppermute | solution.py:304
  45.8 0.8 %collective-permute-start.16 = (bf16[128,256]{1,0:T(8,128)(2,1)S(1)}, bf16[128,256]{1,0:T(8,128)(2,1)S(1)}, u32[]{:S(2)}, u32[]{:S(2)}) collective-permute-start(bf16[128,256]{1,0:T(8,128)(2,1)S(1)} %get-tuple-element.74.refs_0_), channel_id=1, source_target_pairs={{0,1},{1,0},{2,3},{3,2},{4,5},{5,4},{6,7},{7,6},{8,9},{9,8},{10,11... | collective-permute-start | bytes 196616 | tf_op jit(solution)/shard_map/ppermute | solution.py:304
  46.6 1.8 %collective-permute-done.19.refs_5_ = bf16[128,256]{1,0:T(8,128)(2,1)S(1)} collective-permute-done((bf16[128,256]{1,0:T(8,128)(2,1)S(1)}, bf16[128,256]{1,0:T(8,128)(2,1)S(1)}, u32[]{:S(2)}, u32[]{:S(2)}) %collective-permute-start.19) | collective-permute-done | bytes 65568 | tf_op jit(solution)/shard_map/ppermute | solution.py:304
  48.4 0.6 %collective-permute-done.18.refs_3_ = bf16[128,256]{1,0:T(8,128)(2,1)S(1)} collective-permute-done((bf16[128,256]{1,0:T(8,128)(2,1)S(1)}, bf16[128,256]{1,0:T(8,128)(2,1)S(1)}, u32[]{:S(2)}, u32[]{:S(2)}) %collective-permute-start.18) | collective-permute-done | bytes 65568 | tf_op jit(solution)/shard_map/ppermute | solution.py:304
  49.0 0.8 %collective-permute-done.17.refs_2_ = bf16[128,256]{1,0:T(8,128)(2,1)S(1)} collective-permute-done((bf16[128,256]{1,0:T(8,128)(2,1)S(1)}, bf16[128,256]{1,0:T(8,128)(2,1)S(1)}, u32[]{:S(2)}, u32[]{:S(2)}) %collective-permute-start.17) | collective-permute-done | bytes 65568 | tf_op jit(solution)/shard_map/ppermute | solution.py:304
  49.8 0.0 collective-permute-done.16.refs_1_
  49.8 0.9 %shard_map.147 = (f32[128,256]{1,0:T(8,128)}, f32[2,128,256]{2,1,0:T(8,128)}, f32[2,128,256]{2,1,0:T(8,128)}, f32[1,256]{1,0:T(1,128)}) custom-call(f32[128,256]{1,0:T(8,128)S(1)} %get-tuple-element.71.self_ref, f32[1,256]{1,0:T(1,128)S(1)} %get-tuple-element.73.bias_term_ref, bf16[128,256]{1,0:T(8,128)(2,1)S(1)} %get-tuple-element.74.refs_0_, ...), custom_call_target="tpu_custom_call" | custom-call | tf_op jit(solution)/shard_map/pallas_call | solution.py:283
  (5 shorter events, 0.1 us)
Async XLA Ops:
  0.6 8.0 %collective-permute-start = (bf16[128,256]{1,0:T(8,128)(2,1)}, bf16[128,256]{1,0:T(8,128)(2,1)S(1)}, u32[]{:S(2)}, u32[]{:S(2)}) collective-permute-start(bf16[128,256]{1,0:T(8,128)(2,1)} %features_ref.3), channel_id=1, source_target_pairs={{0,16},{4,20},{8,24},{12,28},{16,0},{20,4},{24,8},{28,12},{1,17},{... | collective-permute-start | bytes 196616 | tf_op jit(solution)/shard_map/ppermute | solution.py:304
  8.6 9.7 %collective-permute-start.5 = (bf16[256,256]{1,0:T(8,128)(2,1)S(1)}, bf16[256,256]{1,0:T(8,128)(2,1)S(1)}, u32[]{:S(2)}, u32[]{:S(2)}) collective-permute-start(bf16[256,256]{1,0:T(8,128)(2,1)S(1)} %constant_dynamic-update-slice_fusion.refs_0_), channel_id=1, source_target_pairs={{0,12},{4,8},{8,4},{12,0},{16,28},{20,24},{24,20},{28,16},{1,13},{... | collective-permute-start | bytes 393224 | tf_op jit(solution)/shard_map/ppermute | solution.py:304
  10.6 7.6 %collective-permute-start.4 = (bf16[256,256]{1,0:T(8,128)(2,1)S(1)}, bf16[256,256]{1,0:T(8,128)(2,1)S(1)}, u32[]{:S(2)}, u32[]{:S(2)}) collective-permute-start(bf16[256,256]{1,0:T(8,128)(2,1)S(1)} %constant_dynamic-update-slice_fusion.refs_0_), channel_id=1, source_target_pairs={{0,8},{4,12},{8,0},{12,4},{16,24},{20,28},{24,16},{28,20},{1,9},{5... | collective-permute-start | bytes 393224 | tf_op jit(solution)/shard_map/ppermute | solution.py:304
  11.8 6.5 %collective-permute-start.3 = (bf16[256,256]{1,0:T(8,128)(2,1)S(1)}, bf16[256,256]{1,0:T(8,128)(2,1)S(1)}, u32[]{:S(2)}, u32[]{:S(2)}) collective-permute-start(bf16[256,256]{1,0:T(8,128)(2,1)S(1)} %constant_dynamic-update-slice_fusion.refs_0_), channel_id=1, source_target_pairs={{0,4},{4,0},{8,12},{12,8},{16,20},{20,16},{24,28},{28,24},{1,5},{5... | collective-permute-start | bytes 393224 | tf_op jit(solution)/shard_map/ppermute | solution.py:304
  12.1 5.4 %collective-permute-start.1 = (bf16[128,256]{1,0:T(8,128)(2,1)}, bf16[128,256]{1,0:T(8,128)(2,1)S(1)}, u32[]{:S(2)}, u32[]{:S(2)}) collective-permute-start(bf16[128,256]{1,0:T(8,128)(2,1)} %features_ref.3), channel_id=1, source_target_pairs={{0,2},{1,3},{2,0},{3,1},{4,6},{5,7},{6,4},{7,5},{8,10},{9,11},{10,... | collective-permute-start | bytes 196616 | tf_op jit(solution)/shard_map/ppermute | solution.py:304
  13.8 4.5 %collective-permute-start.2 = (bf16[128,256]{1,0:T(8,128)(2,1)}, bf16[128,256]{1,0:T(8,128)(2,1)S(1)}, u32[]{:S(2)}, u32[]{:S(2)}) collective-permute-start(bf16[128,256]{1,0:T(8,128)(2,1)} %d_out_ref.1), channel_id=1, source_target_pairs={{0,2},{1,3},{2,0},{3,1},{4,6},{5,7},{6,4},{7,5},{8,10},{9,11},{10,... | collective-permute-start | bytes 196616 | tf_op jit(solution)/shard_map/ppermute | solution.py:304
  14.1 12.1 %copy-start = (bf16[128,256]{1,0:T(8,128)(2,1)S(1)}, bf16[128,256]{1,0:T(8,128)(2,1)}, u32[]{:S(2)}) copy-start(bf16[128,256]{1,0:T(8,128)(2,1)} %features_ref.3) | copy-start | bytes 196612
  14.1 12.1 %copy-start.1 = (bf16[256,256]{1,0:T(8,128)(2,1)S(1)}, bf16[256,256]{1,0:T(8,128)(2,1)}, u32[]{:S(2)}) copy-start(bf16[256,256]{1,0:T(8,128)(2,1)} %w_self_ref.1) | copy-start | bytes 393220
  14.1 12.1 %copy-start.2 = (bf16[256,256]{1,0:T(8,128)(2,1)S(1)}, bf16[256,256]{1,0:T(8,128)(2,1)}, u32[]{:S(2)}) copy-start(bf16[256,256]{1,0:T(8,128)(2,1)} %w_neigh_ref.1) | copy-start | bytes 393220
  14.1 12.1 %copy-start.3 = (bf16[128,256]{1,0:T(8,128)(2,1)S(1)}, bf16[128,256]{1,0:T(8,128)(2,1)}, u32[]{:S(2)}) copy-start(bf16[128,256]{1,0:T(8,128)(2,1)} %d_out_ref.1) | copy-start | bytes 196612
  14.1 12.1 %copy-start.4 = (f32[256]{0:T(256)S(1)}, f32[256]{0:T(256)}, u32[]{:S(2)}) copy-start(f32[256]{0:T(256)} %param.13) | copy-start | bytes 3076
  19.0 1.4 %collective-permute-start.6 = (bf16[272,256]{1,0:T(8,128)(2,1)S(1)}, bf16[272,256]{1,0:T(8,128)(2,1)S(1)}, u32[]{:S(2)}, u32[]{:S(2)}) collective-permute-start(bf16[272,256]{1,0:T(8,128)(2,1)S(1)} %get-tuple-element.59), channel_id=1, source_target_pairs={{0,1},{1,0},{2,3},{3,2},{4,5},{5,4},{6,7},{7,6},{8,9},{9,8},{10,11... | collective-permute-start | bytes 417800 | tf_op jit(solution)/shard_map/ppermute | solution.py:304
  20.4 5.8 %collective-permute-start.7 = (bf16[272,256]{1,0:T(8,128)(2,1)S(1)}, bf16[272,256]{1,0:T(8,128)(2,1)S(1)}, u32[]{:S(2)}, u32[]{:S(2)}) collective-permute-start(bf16[272,256]{1,0:T(8,128)(2,1)S(1)} %shard_map.140.pair_ref), channel_id=1, source_target_pairs={{0,2},{1,3},{2,0},{3,1},{4,6},{5,7},{6,4},{7,5},{8,10},{9,11},{10,... | collective-permute-start | bytes 417800 | tf_op jit(solution)/shard_map/ppermute | solution.py:304
  26.9 1.5 %collective-permute-start.8 = (bf16[400,256]{1,0:T(8,128)(2,1)S(1)}, bf16[400,256]{1,0:T(8,128)(2,1)S(1)}, u32[]{:S(2)}, u32[]{:S(2)}) collective-permute-start(bf16[400,256]{1,0:T(8,128)(2,1)S(1)} %get-tuple-element.62.sent_ref), channel_id=1, source_target_pairs={{0,1},{1,0},{2,3},{3,2},{4,5},{5,4},{6,7},{7,6},{8,9},{9,8},{10,11... | collective-permute-start | bytes 614408 | tf_op jit(solution)/shard_map/ppermute | solution.py:304
  28.5 7.1 %collective-permute-start.14 = (bf16[144,256]{1,0:T(8,128)(2,1)S(1)}, bf16[144,256]{1,0:T(8,128)(2,1)S(1)}, u32[]{:S(2)}, u32[]{:S(2)}) collective-permute-start(bf16[144,256]{1,0:T(8,128)(2,1)S(1)} %shard_map.142.refs_0_), channel_id=1, source_target_pairs={{0,12},{4,8},{8,4},{12,0},{16,28},{20,24},{24,20},{28,16},{1,13},{... | collective-permute-start | bytes 221192 | tf_op jit(solution)/shard_map/ppermute | solution.py:304
  30.4 5.7 %collective-permute-start.13 = (bf16[144,256]{1,0:T(8,128)(2,1)S(1)}, bf16[144,256]{1,0:T(8,128)(2,1)S(1)}, u32[]{:S(2)}, u32[]{:S(2)}) collective-permute-start(bf16[144,256]{1,0:T(8,128)(2,1)S(1)} %shard_map.142.refs_0_), channel_id=1, source_target_pairs={{0,8},{4,12},{8,0},{12,4},{16,24},{20,28},{24,16},{28,20},{1,9},{5... | collective-permute-start | bytes 221192 | tf_op jit(solution)/shard_map/ppermute | solution.py:304
  31.5 6.5 %collective-permute-start.12 = (bf16[144,256]{1,0:T(8,128)(2,1)S(1)}, bf16[144,256]{1,0:T(8,128)(2,1)S(1)}, u32[]{:S(2)}, u32[]{:S(2)}) collective-permute-start(bf16[144,256]{1,0:T(8,128)(2,1)S(1)} %shard_map.142.refs_0_), channel_id=1, source_target_pairs={{0,4},{4,0},{8,12},{12,8},{16,20},{20,16},{24,28},{28,24},{1,5},{5... | collective-permute-start | bytes 221192 | tf_op jit(solution)/shard_map/ppermute | solution.py:304
  32.5 8.0 %collective-permute-start.9 = (bf16[256,256]{1,0:T(8,128)(2,1)S(1)}, bf16[256,256]{1,0:T(8,128)(2,1)S(1)}, u32[]{:S(2)}, u32[]{:S(2)}) collective-permute-start(bf16[256,256]{1,0:T(8,128)(2,1)S(1)} %get-tuple-element.66), channel_id=1, source_target_pairs={{0,12},{4,8},{8,4},{12,0},{16,28},{20,24},{24,20},{28,16},{1,13},{... | collective-permute-start | bytes 393224 | tf_op jit(solution)/shard_map/ppermute | solution.py:304
  34.4 7.4 %collective-permute-start.10 = (bf16[256,256]{1,0:T(8,128)(2,1)S(1)}, bf16[256,256]{1,0:T(8,128)(2,1)S(1)}, u32[]{:S(2)}, u32[]{:S(2)}) collective-permute-start(bf16[256,256]{1,0:T(8,128)(2,1)S(1)} %get-tuple-element.67), channel_id=1, source_target_pairs={{0,8},{4,12},{8,0},{12,4},{16,24},{20,28},{24,16},{28,20},{1,9},{5... | collective-permute-start | bytes 393224 | tf_op jit(solution)/shard_map/ppermute | solution.py:304
  35.6 6.3 %collective-permute-start.11 = (bf16[256,256]{1,0:T(8,128)(2,1)S(1)}, bf16[256,256]{1,0:T(8,128)(2,1)S(1)}, u32[]{:S(2)}, u32[]{:S(2)}) collective-permute-start(bf16[256,256]{1,0:T(8,128)(2,1)S(1)} %get-tuple-element.68), channel_id=1, source_target_pairs={{0,4},{4,0},{8,12},{12,8},{16,20},{20,16},{24,28},{28,24},{1,5},{5... | collective-permute-start | bytes 393224 | tf_op jit(solution)/shard_map/ppermute | solution.py:304
  38.1 6.6 %collective-permute-start.15 = (bf16[144,256]{1,0:T(8,128)(2,1)S(1)}, bf16[144,256]{1,0:T(8,128)(2,1)S(1)}, u32[]{:S(2)}, u32[]{:S(2)}) collective-permute-start(bf16[144,256]{1,0:T(8,128)(2,1)S(1)} %shard_map.145.refs_0_), channel_id=1, source_target_pairs={{0,16},{4,20},{8,24},{12,28},{16,0},{20,4},{24,8},{28,12},{1,17},{... | collective-permute-start | bytes 221192 | tf_op jit(solution)/shard_map/ppermute | solution.py:304
  42.5 5.9 %collective-permute-start.19 = (bf16[128,256]{1,0:T(8,128)(2,1)S(1)}, bf16[128,256]{1,0:T(8,128)(2,1)S(1)}, u32[]{:S(2)}, u32[]{:S(2)}) collective-permute-start(bf16[128,256]{1,0:T(8,128)(2,1)S(1)} %get-tuple-element.76), channel_id=1, source_target_pairs={{0,16},{4,20},{8,24},{12,28},{16,0},{20,4},{24,8},{28,12},{1,17},{... | collective-permute-start | bytes 196616 | tf_op jit(solution)/shard_map/ppermute | solution.py:304
  44.7 4.3 %collective-permute-start.18 = (bf16[128,256]{1,0:T(8,128)(2,1)S(1)}, bf16[128,256]{1,0:T(8,128)(2,1)S(1)}, u32[]{:S(2)}, u32[]{:S(2)}) collective-permute-start(bf16[128,256]{1,0:T(8,128)(2,1)S(1)} %get-tuple-element.74.refs_0_), channel_id=1, source_target_pairs={{0,3},{1,2},{2,1},{3,0},{4,7},{5,6},{6,5},{7,4},{8,11},{9,10},{10,... | collective-permute-start | bytes 196616 | tf_op jit(solution)/shard_map/ppermute | solution.py:304
  44.8 5.0 %collective-permute-start.17 = (bf16[128,256]{1,0:T(8,128)(2,1)S(1)}, bf16[128,256]{1,0:T(8,128)(2,1)S(1)}, u32[]{:S(2)}, u32[]{:S(2)}) collective-permute-start(bf16[128,256]{1,0:T(8,128)(2,1)S(1)} %get-tuple-element.74.refs_0_), channel_id=1, source_target_pairs={{0,2},{1,3},{2,0},{3,1},{4,6},{5,7},{6,4},{7,5},{8,10},{9,11},{10,... | collective-permute-start | bytes 196616 | tf_op jit(solution)/shard_map/ppermute | solution.py:304
  45.8 4.0 %collective-permute-start.16 = (bf16[128,256]{1,0:T(8,128)(2,1)S(1)}, bf16[128,256]{1,0:T(8,128)(2,1)S(1)}, u32[]{:S(2)}, u32[]{:S(2)}) collective-permute-start(bf16[128,256]{1,0:T(8,128)(2,1)S(1)} %get-tuple-element.74.refs_0_), channel_id=1, source_target_pairs={{0,1},{1,0},{2,3},{3,2},{4,5},{5,4},{6,7},{7,6},{8,9},{9,8},{10,11... | collective-permute-start | bytes 196616 | tf_op jit(solution)/shard_map/ppermute | solution.py:304

commit v11 on v10

--- a/solution.py
+++ b/solution.py
@@ -12,7 +12,6 @@
 BF16 = jnp.bfloat16
 F32 = jnp.float32
 HOT = jnp.float8_e4m3fn
-UNROLL = 64
 VMEM = pl.BlockSpec(memory_space=pltpu.VMEM)
 HBM = pl.BlockSpec(memory_space=pltpu.HBM)
 
@@ -51,16 +50,17 @@
 def add_tiles(first, scalars, src_ref, dst_ref, acc_ref, ready):
     row_ref, col_ref, count_ref = scalars
     tiles, slots = src_ref.shape
+    unroll = tiles // 2
     col_blocks = acc_ref.shape[1]
     line = lax.broadcasted_iota(jnp.int32, (BLK, slots), 0).astype(BF16)
     slot = lax.broadcasted_iota(jnp.int32, (1, slots), 1)
     one, zero = jnp.ones((), BF16), jnp.zeros((), BF16)
 
     def step(i, carry):
-        base = pl.multiple_of(i * UNROLL, UNROLL)
-        ready(i, pl.ds(base, UNROLL))
-        dst, src = dst_ref[pl.ds(base, UNROLL), :], src_ref[pl.ds(base, UNROLL), :]
-        for u in range(UNROLL):
+        base = pl.multiple_of(i * unroll, unroll)
+        ready(i, pl.ds(base, unroll))
+        dst, src = dst_ref[pl.ds(base, unroll), :], src_ref[pl.ds(base, unroll), :]
+        for u in range(unroll):
             tile = first + base + u
             live = jnp.where(slot < count_ref[tile], dst[u : u + 1], -1)
             dst_hot = jnp.where(line == live.astype(BF16), one, zero).astype(HOT)
@@ -71,7 +71,7 @@
             acc_ref[row_place(row_ref[tile]), col_place(col_ref[tile], col_blocks)] += part
         return carry
 
-    lax.fori_loop(0, tiles // UNROLL, step, 0)
+    lax.fori_loop(0, tiles // unroll, step, 0)
 
 
 def first_build_kernel(
@@ -79,7 +79,9 @@
     acc_ref, line_ref, late_src_ref, late_dst_ref,
     row_buf, col_buf, count_buf, src_buf, dst_buf, sems, src_sems, dst_sems,
 ):
-    half, rows = src_buf.shape[0], features_ref.shape[0]
+    early, late_tiles = src_buf.shape[0], late_src_ref.shape[0]
+    rows = features_ref.shape[0]
+    unroll = early // 2
     scalars = [row_buf, col_buf, count_buf]
     copies = [
         pltpu.make_async_copy(ref, buf, sems.at[i])
@@ -93,14 +95,14 @@
         )
 
     late = [
-        pltpu.make_async_copy(src_ref.at[pl.ds(half, half)], late_src_ref, sems.at[3]),
-        pltpu.make_async_copy(dst_ref.at[pl.ds(half, half)], late_dst_ref, sems.at[4]),
+        pltpu.make_async_copy(src_ref.at[pl.ds(early, late_tiles)], late_src_ref, sems.at[3]),
+        pltpu.make_async_copy(dst_ref.at[pl.ds(early, late_tiles)], late_dst_ref, sems.at[4]),
         pltpu.make_async_copy(features_ref, line_ref.at[pl.ds(0, rows)], sems.at[5]),
     ]
     for copy in copies:
         copy.start()
-    for i in range(half // UNROLL):
-        for copy in edges(i, pl.ds(i * UNROLL, UNROLL)):
+    for i in range(2):
+        for copy in edges(i, pl.ds(i * unroll, unroll)):
             copy.start()
     for copy in late:
         copy.start()
@@ -131,7 +133,8 @@
     acc_ref[...] = half_ref[...]
     for copy in copies:
         copy.wait()
-    add_tiles(src_ref.shape[0], scalars, src_ref, dst_ref, acc_ref, lambda i, at: None)
+    first = row_ref.shape[0] - src_ref.shape[0]
+    add_tiles(first, scalars, src_ref, dst_ref, acc_ref, lambda i, at: None)
     row_blocks, col_blocks = acc_ref.shape[:2]
     for g in range(row_blocks):
         for c in range(col_blocks):
@@ -229,17 +232,16 @@
 
 
 def near_sum_kernel(keep_ref, *refs):
-    *sums, out_ref = refs[4:]
     blocks = tree([ref[...].astype(F32) for ref in (keep_ref, *refs[:3])])
-    for h, ref in enumerate(sums):
+    for h, ref in enumerate(refs[3:]):
         ref[...] = blocks[h * BLK : (h + 1) * BLK].astype(ref.dtype)
-    out_ref[...] = refs[3][...]
-
-
-def finish_kernel(self_ref, bias_term_ref, *refs):
-    *terms, d_features_ref, grad_self_ref, grad_neigh_ref, bias_ref = refs
+
+
+def finish_kernel(own_out_ref, self_ref, bias_term_ref, *refs):
+    *terms, out_ref, d_features_ref, grad_self_ref, grad_neigh_ref, bias_ref = refs
     quarters, terms = terms[:4], terms[4:]
     d_features_ref[...] = self_ref[...] + tree([ref[...].astype(F32) for ref in terms])
+    out_ref[...] = own_out_ref[...]
     bias_ref[...] = bias_term_ref[...]
     me = lax.axis_index("rep")
     low = me >> 1 == 0
@@ -305,7 +307,8 @@
 
     far_pieces = [swap(features, "row", 4 * h) for h in range(1, far)]
     tiles, slots = edge_src.shape
-    early = tiles // 2
+    early = tiles * 7 // 16
+    late = tiles - early
     tile_row, tile_col, tile_count, edge_src, edge_dst, held_features = (
         pltpu.with_memory_space_constraint(v, pltpu.HBM)
         for v in (tile_row, tile_col, tile_count, edge_src, edge_dst, features)
@@ -313,14 +316,14 @@
     scalars = (tile_row, tile_col, tile_count)
     buffers = [pltpu.SMEM((tiles,), jnp.int32)] * 3
     acc_shape = (rep_count, row_count, BLK, BLK)
-    chunk_sems = [pltpu.SemaphoreType.DMA((early // UNROLL,))] * 2
+    chunk_sems = [pltpu.SemaphoreType.DMA((2,))] * 2
     acc, line, late_src, late_dst = call(
         first_build_kernel,
         (
             shape(acc_shape, F32),
             shape((far * rows, width), BF16),
-            shape((early, slots), jnp.int32),
-            shape((early, slots), jnp.int32),
+            shape((late, slots), jnp.int32),
+            shape((late, slots), jnp.int32),
         ),
         [HBM] * 6,
         (*scalars, edge_src, edge_dst, held_features),
@@ -396,23 +399,21 @@
         [VMEM] * far,
         far_terms,
     )
-    keep_block, *far_msgs, out = call(
+    keep_block, *far_msgs = call(
         near_sum_kernel,
-        (shape((BLK, width), F32),)
-        + (shape((BLK, width), BF16),) * (far - 1)
-        + (shape((rows, width), BF16),),
-        [VMEM] * 5,
-        (keep_blocks, *got, out),
+        (shape((BLK, width), F32),) + (shape((BLK, width), BF16),) * (far - 1),
+        [VMEM] * 4,
+        (keep_blocks, *got),
     )
     got = [swap(msg, "row", 4 * (h + 1)) for h, msg in enumerate(far_msgs)]
     quarters = [quarter] + [swap(quarter, "rep", m) for m in range(1, 4)]
-    d_features, grad_self, grad_neigh, grad_bias = call(
+    out, d_features, grad_self, grad_neigh, grad_bias = call(
         finish_kernel,
-        (shape((rows, width), F32),)
+        (shape((rows, width), BF16), shape((rows, width), F32))
         + (shape((2, middle, width), F32),) * 2
         + (shape((1, width), F32),),
-        [VMEM] * (7 + len(got)),
-        (self_term, bias_term, *quarters, keep_block, *got),
+        [VMEM] * (8 + len(got)),
+        (out, self_term, bias_term, *quarters, keep_block, *got),
     )
     grad_self, grad_neigh = (v.reshape(width, width) for v in (grad_self, grad_neigh))
     return (out, d_features, grad_self, grad_neigh, grad_bias[0])

time: 50.8 us -> 50.8 us (level)
  Pallas kernels: 10.1 us -> 9.53 us
    pallas_call x11, Pallas kernels: 10.1 us -> 9.53 us  [call(): pl.pallas_call(kernel, out_shape=out_shape, in_specs=specs, out_specs=[VM...]
  transfers between devices with their start and end apart: 20 -> 20, of which waited for: 11 -> 12; matrix products, arithmetic and copies ran while one was open for 0% -> 0% of each run, Pallas kernels for 16% -> 14%
where the time goes in v11:
time: 50.8 us; the launch traced here: 50.6 us
  starting transfers between devices  22.3 us (44%)
  waiting for transfers between devices  18 us (35%)
  Pallas kernels  9.53 us (19%)
  between operations  0.77 us (2%)
    ppermute x20, starting transfers between devices, swap(): lax.ppermute(value, axis, [(i, i ^ bits) for i in range(lax.axis_size(axi...  22.3 us
    ppermute x20, waiting for transfers between devices, swap(): lax.ppermute(value, axis, [(i, i ^ bits) for i in range(lax.axis_size(axi...  18 us
    pallas_call x11, Pallas kernels, call(): pl.pallas_call(kernel, out_shape=out_shape, in_specs=specs, out_specs=[VM...  9.53 us
  transfers between devices with their start and end apart: 20, of which 12 were waited for; matrix products, arithmetic and copies ran while one was open for 0% of the time, Pallas kernels for 14%

profile of v11, /device:TPU:0, one launch (start us, length us, event | category | flops | bytes accessed | tf_op | source)
XLA Modules:
  0.0 50.6 jit_solution(1868801423880022708)
XLA Ops:
  0.6 4.1 %collective-permute-start = (bf16[128,256]{1,0:T(8,128)(2,1)}, bf16[128,256]{1,0:T(8,128)(2,1)S(1)}, u32[]{:S(2)}, u32[]{:S(2)}) collective-permute-start(bf16[128,256]{1,0:T(8,128)(2,1)} %features_ref.3), channel_id=1, source_target_pairs={{0,16},{4,20},{8,24},{12,28},{16,0},{20,4},{24,8},{28,12},{1,17},{... | collective-permute-start | bytes 196616 | tf_op jit(solution)/shard_map/ppermute | solution.py:306
  4.7 3.0 %shard_map.137 = (f32[4,8,128,128]{3,2,1,0:T(8,128)S(1)}, bf16[256,256]{1,0:T(8,128)(2,1)S(1)}, s32[144,256]{1,0:T(8,128)S(1)}, s32[144,256]{1,0:T(8,128)S(1)}) custom-call(s32[256]{0:T(256)} %row_ref.3, s32[256]{0:T(256)} %col_ref.3, s32[256]{0:T(256)} %count_ref.3, s32[256,256]{1,0:T(8,128)} %src_ref.1, s32[256,256]{1,0:T(8,128)} %dst_ref.1, ...), custom_call_target="tpu_custom_call" | custom-call | tf_op jit(solution)/shard_map/pallas_call | solution.py:285
  7.7 0.9 %collective-permute-done = bf16[128,256]{1,0:T(8,128)(2,1)S(1)} collective-permute-done((bf16[128,256]{1,0:T(8,128)(2,1)}, bf16[128,256]{1,0:T(8,128)(2,1)S(1)}, u32[]{:S(2)}, u32[]{:S(2)}) %collective-permute-start) | collective-permute-done | bytes 65568 | tf_op jit(solution)/shard_map/ppermute | solution.py:306
  8.6 1.8 %collective-permute-start.5 = (bf16[256,256]{1,0:T(8,128)(2,1)S(1)}, bf16[256,256]{1,0:T(8,128)(2,1)S(1)}, u32[]{:S(2)}, u32[]{:S(2)}) collective-permute-start(bf16[256,256]{1,0:T(8,128)(2,1)S(1)} %constant_dynamic-update-slice_fusion.refs_0_), channel_id=1, source_target_pairs={{0,12},{4,8},{8,4},{12,0},{16,28},{20,24},{24,20},{28,16},{1,13},{... | collective-permute-start | bytes 393224 | tf_op jit(solution)/shard_map/ppermute | solution.py:306
  10.4 1.4 %collective-permute-start.4 = (bf16[256,256]{1,0:T(8,128)(2,1)S(1)}, bf16[256,256]{1,0:T(8,128)(2,1)S(1)}, u32[]{:S(2)}, u32[]{:S(2)}) collective-permute-start(bf16[256,256]{1,0:T(8,128)(2,1)S(1)} %constant_dynamic-update-slice_fusion.refs_0_), channel_id=1, source_target_pairs={{0,8},{4,12},{8,0},{12,4},{16,24},{20,28},{24,16},{28,20},{1,9},{5... | collective-permute-start | bytes 393224 | tf_op jit(solution)/shard_map/ppermute | solution.py:306
  11.8 0.3 collective-permute-start.3
  12.1 1.7 %collective-permute-start.1 = (bf16[128,256]{1,0:T(8,128)(2,1)}, bf16[128,256]{1,0:T(8,128)(2,1)S(1)}, u32[]{:S(2)}, u32[]{:S(2)}) collective-permute-start(bf16[128,256]{1,0:T(8,128)(2,1)} %features_ref.3), channel_id=1, source_target_pairs={{0,2},{1,3},{2,0},{3,1},{4,6},{5,7},{6,4},{7,5},{8,10},{9,11},{10,... | collective-permute-start | bytes 196616 | tf_op jit(solution)/shard_map/ppermute | solution.py:306
  13.8 0.3 collective-permute-start.2
  14.1 0.0 copy-start
  14.1 0.0 copy-start.1
  14.1 0.0 copy-start.2
  14.1 0.0 copy-start.3
  14.1 0.0 copy-start.4
  14.1 3.6 %shard_map.138.adj_ref = bf16[512,1024]{1,0:T(8,128)(2,1)S(1)} custom-call(s32[256]{0:T(256)} %row_ref.3, s32[256]{0:T(256)} %col_ref.3, s32[256]{0:T(256)} %count_ref.3, s32[144,256]{1,0:T(8,128)S(1)} %get-tuple-element.43.src_ref, s32[144,256]{1,0:T(8,128)S(1)} %get-tuple-element.44.dst_ref, f32[4,8,128,128]{3,2,1,0:T(8,128)S(1)} %get-tuple-element.48.half_ref), custom_call_target="tpu_custom_call" | custom-call | tf_op jit(solution)/shard_map/pallas_call | solution.py:285
  17.7 0.0 collective-permute-done.1.near_features_ref
  17.8 0.5 %collective-permute-done.2.near_d_out_ref = bf16[128,256]{1,0:T(8,128)(2,1)S(1)} collective-permute-done((bf16[128,256]{1,0:T(8,128)(2,1)}, bf16[128,256]{1,0:T(8,128)(2,1)S(1)}, u32[]{:S(2)}, u32[]{:S(2)}) %collective-permute-start.2) | collective-permute-done | bytes 65568 | tf_op jit(solution)/shard_map/ppermute | solution.py:306
  18.3 0.0 collective-permute-done.5.refs_3_
  18.3 0.0 collective-permute-done.4.refs_2_
  18.3 0.0 collective-permute-done.3.refs_1_
  18.3 0.7 %shard_map.139 = (f32[272,256]{1,0:T(8,128)S(1)}, bf16[272,256]{1,0:T(8,128)(2,1)S(1)}) custom-call(bf16[512,1024]{1,0:T(8,128)(2,1)S(1)} %shard_map.138.adj_ref, bf16[256,256]{1,0:T(8,128)(2,1)S(1)} %constant_dynamic-update-slice_fusion.refs_0_, bf16[256,256]{1,0:T(8,128)(2,1)S(1)} %collective-permute-done.3.refs_1_, ...), custom_call_target="tpu_custom_call" | custom-call | tf_op jit(solution)/shard_map/pallas_call | solution.py:285
  19.0 0.1 collective-permute-start.6
  19.1 1.3 %collective-permute-done.6.got_ref = bf16[272,256]{1,0:T(8,128)(2,1)S(1)} collective-permute-done((bf16[272,256]{1,0:T(8,128)(2,1)S(1)}, bf16[272,256]{1,0:T(8,128)(2,1)S(1)}, u32[]{:S(2)}, u32[]{:S(2)}) %collective-permute-start.6) | collective-permute-done | bytes 139296 | tf_op jit(solution)/shard_map/ppermute | solution.py:306
  20.4 1.3 %collective-permute-start.7 = (bf16[272,256]{1,0:T(8,128)(2,1)S(1)}, bf16[272,256]{1,0:T(8,128)(2,1)S(1)}, u32[]{:S(2)}, u32[]{:S(2)}) collective-permute-start(bf16[272,256]{1,0:T(8,128)(2,1)S(1)} %shard_map.140.pair_ref), channel_id=1, source_target_pairs={{0,2},{1,3},{2,0},{3,1},{4,6},{5,7},{6,4},{7,5},{8,10},{9,11},{10,... | collective-permute-start | bytes 417800 | tf_op jit(solution)/shard_map/ppermute | solution.py:306
  21.7 4.5 %collective-permute-done.7.got_ref = bf16[272,256]{1,0:T(8,128)(2,1)S(1)} collective-permute-done((bf16[272,256]{1,0:T(8,128)(2,1)S(1)}, bf16[272,256]{1,0:T(8,128)(2,1)S(1)}, u32[]{:S(2)}, u32[]{:S(2)}) %collective-permute-start.7) | collective-permute-done | bytes 139296 | tf_op jit(solution)/shard_map/ppermute | solution.py:306
  26.2 0.0 copy-done
  26.2 0.0 copy-done.1
  26.2 0.0 copy-done.2
  26.2 0.0 copy-done.3
  26.2 0.0 copy-done.4
  26.3 0.7 %shard_map.141 = (bf16[128,256]{1,0:T(8,128)(2,1)S(1)}, f32[128,256]{1,0:T(8,128)S(1)}, f32[144,256]{1,0:T(8,128)S(1)}, bf16[400,256]{1,0:T(8,128)(2,1)S(1)}) custom-call(bf16[272,256]{1,0:T(8,128)(2,1)S(1)} %shard_map.140.pair_ref, bf16[272,256]{1,0:T(8,128)(2,1)S(1)} %collective-permute-done.7.got_ref, bf16[128,256]{1,0:T(8,128)(2,1)S(1)} %copy-done, ...), custom_call_target="tpu_custom_call" | custom-call | tf_op jit(solution)/shard_map/pallas_call | solution.py:285
  26.9 0.1 collective-permute-start.8
  27.0 1.4 %collective-permute-done.8.got_ref = bf16[400,256]{1,0:T(8,128)(2,1)S(1)} collective-permute-done((bf16[400,256]{1,0:T(8,128)(2,1)S(1)}, bf16[400,256]{1,0:T(8,128)(2,1)S(1)}, u32[]{:S(2)}, u32[]{:S(2)}) %collective-permute-start.8) | collective-permute-done | bytes 204832 | tf_op jit(solution)/shard_map/ppermute | solution.py:306
  28.5 1.6 %collective-permute-start.11 = (bf16[144,256]{1,0:T(8,128)(2,1)S(1)}, bf16[144,256]{1,0:T(8,128)(2,1)S(1)}, u32[]{:S(2)}, u32[]{:S(2)}) collective-permute-start(bf16[144,256]{1,0:T(8,128)(2,1)S(1)} %shard_map.142.refs_0_), channel_id=1, source_target_pairs={{0,12},{4,8},{8,4},{12,0},{16,28},{20,24},{24,20},{28,16},{1,13},{... | collective-permute-start | bytes 221192 | tf_op jit(solution)/shard_map/ppermute | solution.py:306
  30.1 1.4 %collective-permute-start.10 = (bf16[144,256]{1,0:T(8,128)(2,1)S(1)}, bf16[144,256]{1,0:T(8,128)(2,1)S(1)}, u32[]{:S(2)}, u32[]{:S(2)}) collective-permute-start(bf16[144,256]{1,0:T(8,128)(2,1)S(1)} %shard_map.142.refs_0_), channel_id=1, source_target_pairs={{0,8},{4,12},{8,0},{12,4},{16,24},{20,28},{24,16},{28,20},{1,9},{5... | collective-permute-start | bytes 221192 | tf_op jit(solution)/shard_map/ppermute | solution.py:306
  31.5 0.5 collective-permute-start.9
  32.0 0.5 shard_map.145
  32.5 1.6 %collective-permute-start.16 = (bf16[256,256]{1,0:T(8,128)(2,1)S(1)}, bf16[256,256]{1,0:T(8,128)(2,1)S(1)}, u32[]{:S(2)}, u32[]{:S(2)}) collective-permute-start(bf16[256,256]{1,0:T(8,128)(2,1)S(1)} %get-tuple-element.71), channel_id=1, source_target_pairs={{0,12},{4,8},{8,4},{12,0},{16,28},{20,24},{24,20},{28,16},{1,13},{... | collective-permute-start | bytes 393224 | tf_op jit(solution)/shard_map/ppermute | solution.py:306
  34.1 1.4 %collective-permute-start.17 = (bf16[256,256]{1,0:T(8,128)(2,1)S(1)}, bf16[256,256]{1,0:T(8,128)(2,1)S(1)}, u32[]{:S(2)}, u32[]{:S(2)}) collective-permute-start(bf16[256,256]{1,0:T(8,128)(2,1)S(1)} %get-tuple-element.72), channel_id=1, source_target_pairs={{0,8},{4,12},{8,0},{12,4},{16,24},{20,28},{24,16},{28,20},{1,9},{5... | collective-permute-start | bytes 393224 | tf_op jit(solution)/shard_map/ppermute | solution.py:306
  35.6 0.0 collective-permute-done.11.refs_3_
  35.6 0.5 collective-permute-start.18
  36.1 0.0 collective-permute-done.10.refs_2_
  36.1 1.9 %collective-permute-done.9.refs_1_ = bf16[144,256]{1,0:T(8,128)(2,1)S(1)} collective-permute-done((bf16[144,256]{1,0:T(8,128)(2,1)S(1)}, bf16[144,256]{1,0:T(8,128)(2,1)S(1)}, u32[]{:S(2)}, u32[]{:S(2)}) %collective-permute-start.9) | collective-permute-done | bytes 73760 | tf_op jit(solution)/shard_map/ppermute | solution.py:306
  38.1 0.1 collective-permute-start.12
  38.1 2.4 %collective-permute-done.16.refs_0_ = bf16[256,256]{1,0:T(8,128)(2,1)S(1)} collective-permute-done((bf16[256,256]{1,0:T(8,128)(2,1)S(1)}, bf16[256,256]{1,0:T(8,128)(2,1)S(1)}, u32[]{:S(2)}, u32[]{:S(2)}) %collective-permute-start.16) | collective-permute-done | bytes 131104 | tf_op jit(solution)/shard_map/ppermute | solution.py:306
  40.5 1.3 %collective-permute-done.17.refs_1_ = bf16[256,256]{1,0:T(8,128)(2,1)S(1)} collective-permute-done((bf16[256,256]{1,0:T(8,128)(2,1)S(1)}, bf16[256,256]{1,0:T(8,128)(2,1)S(1)}, u32[]{:S(2)}, u32[]{:S(2)}) %collective-permute-start.17) | collective-permute-done | bytes 131104 | tf_op jit(solution)/shard_map/ppermute | solution.py:306
  41.9 0.0 collective-permute-done.18.refs_2_
  41.9 0.1 shard_map.146
  41.9 2.2 %collective-permute-start.19 = (bf16[128,256]{1,0:T(8,128)(2,1)S(1)}, bf16[128,256]{1,0:T(8,128)(2,1)S(1)}, u32[]{:S(2)}, u32[]{:S(2)}) collective-permute-start(bf16[128,256]{1,0:T(8,128)(2,1)S(1)} %get-tuple-element.75), channel_id=1, source_target_pairs={{0,16},{4,20},{8,24},{12,28},{16,0},{20,4},{24,8},{28,12},{1,17},{... | collective-permute-start | bytes 196616 | tf_op jit(solution)/shard_map/ppermute | solution.py:306
  44.1 0.2 collective-permute-done.12.refs_1_
  44.4 0.1 collective-permute-start.15
  44.4 1.3 %collective-permute-start.14 = (bf16[128,256]{1,0:T(8,128)(2,1)S(1)}, bf16[128,256]{1,0:T(8,128)(2,1)S(1)}, u32[]{:S(2)}, u32[]{:S(2)}) collective-permute-start(bf16[128,256]{1,0:T(8,128)(2,1)S(1)} %get-tuple-element.68.refs_0_), channel_id=1, source_target_pairs={{0,2},{1,3},{2,0},{3,1},{4,6},{5,7},{6,4},{7,5},{8,10},{9,11},{10,... | collective-permute-start | bytes 196616 | tf_op jit(solution)/shard_map/ppermute | solution.py:306
  45.7 0.6 %collective-permute-start.13 = (bf16[128,256]{1,0:T(8,128)(2,1)S(1)}, bf16[128,256]{1,0:T(8,128)(2,1)S(1)}, u32[]{:S(2)}, u32[]{:S(2)}) collective-permute-start(bf16[128,256]{1,0:T(8,128)(2,1)S(1)} %get-tuple-element.68.refs_0_), channel_id=1, source_target_pairs={{0,1},{1,0},{2,3},{3,2},{4,5},{5,4},{6,7},{7,6},{8,9},{9,8},{10,11... | collective-permute-start | bytes 196616 | tf_op jit(solution)/shard_map/ppermute | solution.py:306
  46.3 1.6 %collective-permute-done.19.refs_5_ = bf16[128,256]{1,0:T(8,128)(2,1)S(1)} collective-permute-done((bf16[128,256]{1,0:T(8,128)(2,1)S(1)}, bf16[128,256]{1,0:T(8,128)(2,1)S(1)}, u32[]{:S(2)}, u32[]{:S(2)}) %collective-permute-start.19) | collective-permute-done | bytes 65568 | tf_op jit(solution)/shard_map/ppermute | solution.py:306
  47.9 1.0 %collective-permute-done.15.refs_3_ = bf16[128,256]{1,0:T(8,128)(2,1)S(1)} collective-permute-done((bf16[128,256]{1,0:T(8,128)(2,1)S(1)}, bf16[128,256]{1,0:T(8,128)(2,1)S(1)}, u32[]{:S(2)}, u32[]{:S(2)}) %collective-permute-start.15) | collective-permute-done | bytes 65568 | tf_op jit(solution)/shard_map/ppermute | solution.py:306
  48.8 0.9 %collective-permute-done.14.refs_2_ = bf16[128,256]{1,0:T(8,128)(2,1)S(1)} collective-permute-done((bf16[128,256]{1,0:T(8,128)(2,1)S(1)}, bf16[128,256]{1,0:T(8,128)(2,1)S(1)}, u32[]{:S(2)}, u32[]{:S(2)}) %collective-permute-start.14) | collective-permute-done | bytes 65568 | tf_op jit(solution)/shard_map/ppermute | solution.py:306
  49.7 0.0 collective-permute-done.13.refs_1_
  49.7 0.9 %shard_map.147 = (bf16[128,256]{1,0:T(8,128)(2,1)}, f32[128,256]{1,0:T(8,128)}, f32[2,128,256]{2,1,0:T(8,128)}, f32[2,128,256]{2,1,0:T(8,128)}, f32[1,256]{1,0:T(1,128)}) custom-call(bf16[128,256]{1,0:T(8,128)(2,1)S(1)} %get-tuple-element.62.own_out_ref, f32[128,256]{1,0:T(8,128)S(1)} %get-tuple-element.63.self_ref, ...), custom_call_target="tpu_custom_call" | custom-call | tf_op jit(solution)/shard_map/pallas_call | solution.py:285
  (5 shorter events, 0.1 us)
Async XLA Ops:
  0.6 8.0 %collective-permute-start = (bf16[128,256]{1,0:T(8,128)(2,1)}, bf16[128,256]{1,0:T(8,128)(2,1)S(1)}, u32[]{:S(2)}, u32[]{:S(2)}) collective-permute-start(bf16[128,256]{1,0:T(8,128)(2,1)} %features_ref.3), channel_id=1, source_target_pairs={{0,16},{4,20},{8,24},{12,28},{16,0},{20,4},{24,8},{28,12},{1,17},{... | collective-permute-start | bytes 196616 | tf_op jit(solution)/shard_map/ppermute | solution.py:306
  8.6 9.7 %collective-permute-start.5 = (bf16[256,256]{1,0:T(8,128)(2,1)S(1)}, bf16[256,256]{1,0:T(8,128)(2,1)S(1)}, u32[]{:S(2)}, u32[]{:S(2)}) collective-permute-start(bf16[256,256]{1,0:T(8,128)(2,1)S(1)} %constant_dynamic-update-slice_fusion.refs_0_), channel_id=1, source_target_pairs={{0,12},{4,8},{8,4},{12,0},{16,28},{20,24},{24,20},{28,16},{1,13},{... | collective-permute-start | bytes 393224 | tf_op jit(solution)/shard_map/ppermute | solution.py:306
  10.4 7.9 %collective-permute-start.4 = (bf16[256,256]{1,0:T(8,128)(2,1)S(1)}, bf16[256,256]{1,0:T(8,128)(2,1)S(1)}, u32[]{:S(2)}, u32[]{:S(2)}) collective-permute-start(bf16[256,256]{1,0:T(8,128)(2,1)S(1)} %constant_dynamic-update-slice_fusion.refs_0_), channel_id=1, source_target_pairs={{0,8},{4,12},{8,0},{12,4},{16,24},{20,28},{24,16},{28,20},{1,9},{5... | collective-permute-start | bytes 393224 | tf_op jit(solution)/shard_map/ppermute | solution.py:306
  11.8 6.5 %collective-permute-start.3 = (bf16[256,256]{1,0:T(8,128)(2,1)S(1)}, bf16[256,256]{1,0:T(8,128)(2,1)S(1)}, u32[]{:S(2)}, u32[]{:S(2)}) collective-permute-start(bf16[256,256]{1,0:T(8,128)(2,1)S(1)} %constant_dynamic-update-slice_fusion.refs_0_), channel_id=1, source_target_pairs={{0,4},{4,0},{8,12},{12,8},{16,20},{20,16},{24,28},{28,24},{1,5},{5... | collective-permute-start | bytes 393224 | tf_op jit(solution)/shard_map/ppermute | solution.py:306
  12.1 5.7 %collective-permute-start.1 = (bf16[128,256]{1,0:T(8,128)(2,1)}, bf16[128,256]{1,0:T(8,128)(2,1)S(1)}, u32[]{:S(2)}, u32[]{:S(2)}) collective-permute-start(bf16[128,256]{1,0:T(8,128)(2,1)} %features_ref.3), channel_id=1, source_target_pairs={{0,2},{1,3},{2,0},{3,1},{4,6},{5,7},{6,4},{7,5},{8,10},{9,11},{10,... | collective-permute-start | bytes 196616 | tf_op jit(solution)/shard_map/ppermute | solution.py:306
  13.8 4.5 %collective-permute-start.2 = (bf16[128,256]{1,0:T(8,128)(2,1)}, bf16[128,256]{1,0:T(8,128)(2,1)S(1)}, u32[]{:S(2)}, u32[]{:S(2)}) collective-permute-start(bf16[128,256]{1,0:T(8,128)(2,1)} %d_out_ref.1), channel_id=1, source_target_pairs={{0,2},{1,3},{2,0},{3,1},{4,6},{5,7},{6,4},{7,5},{8,10},{9,11},{10,... | collective-permute-start | bytes 196616 | tf_op jit(solution)/shard_map/ppermute | solution.py:306
  14.1 12.1 %copy-start = (bf16[128,256]{1,0:T(8,128)(2,1)S(1)}, bf16[128,256]{1,0:T(8,128)(2,1)}, u32[]{:S(2)}) copy-start(bf16[128,256]{1,0:T(8,128)(2,1)} %features_ref.3) | copy-start | bytes 196612
  14.1 12.1 %copy-start.1 = (bf16[256,256]{1,0:T(8,128)(2,1)S(1)}, bf16[256,256]{1,0:T(8,128)(2,1)}, u32[]{:S(2)}) copy-start(bf16[256,256]{1,0:T(8,128)(2,1)} %w_self_ref.1) | copy-start | bytes 393220
  14.1 12.1 %copy-start.2 = (bf16[256,256]{1,0:T(8,128)(2,1)S(1)}, bf16[256,256]{1,0:T(8,128)(2,1)}, u32[]{:S(2)}) copy-start(bf16[256,256]{1,0:T(8,128)(2,1)} %w_neigh_ref.1) | copy-start | bytes 393220
  14.1 12.1 %copy-start.3 = (bf16[128,256]{1,0:T(8,128)(2,1)S(1)}, bf16[128,256]{1,0:T(8,128)(2,1)}, u32[]{:S(2)}) copy-start(bf16[128,256]{1,0:T(8,128)(2,1)} %d_out_ref.1) | copy-start | bytes 196612
  14.1 12.1 %copy-start.4 = (f32[256]{0:T(256)S(1)}, f32[256]{0:T(256)}, u32[]{:S(2)}) copy-start(f32[256]{0:T(256)} %param.13) | copy-start | bytes 3076
  19.0 1.4 %collective-permute-start.6 = (bf16[272,256]{1,0:T(8,128)(2,1)S(1)}, bf16[272,256]{1,0:T(8,128)(2,1)S(1)}, u32[]{:S(2)}, u32[]{:S(2)}) collective-permute-start(bf16[272,256]{1,0:T(8,128)(2,1)S(1)} %get-tuple-element.59), channel_id=1, source_target_pairs={{0,1},{1,0},{2,3},{3,2},{4,5},{5,4},{6,7},{7,6},{8,9},{9,8},{10,11... | collective-permute-start | bytes 417800 | tf_op jit(solution)/shard_map/ppermute | solution.py:306
  20.4 5.8 %collective-permute-start.7 = (bf16[272,256]{1,0:T(8,128)(2,1)S(1)}, bf16[272,256]{1,0:T(8,128)(2,1)S(1)}, u32[]{:S(2)}, u32[]{:S(2)}) collective-permute-start(bf16[272,256]{1,0:T(8,128)(2,1)S(1)} %shard_map.140.pair_ref), channel_id=1, source_target_pairs={{0,2},{1,3},{2,0},{3,1},{4,6},{5,7},{6,4},{7,5},{8,10},{9,11},{10,... | collective-permute-start | bytes 417800 | tf_op jit(solution)/shard_map/ppermute | solution.py:306
  26.9 1.5 %collective-permute-start.8 = (bf16[400,256]{1,0:T(8,128)(2,1)S(1)}, bf16[400,256]{1,0:T(8,128)(2,1)S(1)}, u32[]{:S(2)}, u32[]{:S(2)}) collective-permute-start(bf16[400,256]{1,0:T(8,128)(2,1)S(1)} %get-tuple-element.65.sent_ref), channel_id=1, source_target_pairs={{0,1},{1,0},{2,3},{3,2},{4,5},{5,4},{6,7},{7,6},{8,9},{9,8},{10,11... | collective-permute-start | bytes 614408 | tf_op jit(solution)/shard_map/ppermute | solution.py:306
  28.5 7.1 %collective-permute-start.11 = (bf16[144,256]{1,0:T(8,128)(2,1)S(1)}, bf16[144,256]{1,0:T(8,128)(2,1)S(1)}, u32[]{:S(2)}, u32[]{:S(2)}) collective-permute-start(bf16[144,256]{1,0:T(8,128)(2,1)S(1)} %shard_map.142.refs_0_), channel_id=1, source_target_pairs={{0,12},{4,8},{8,4},{12,0},{16,28},{20,24},{24,20},{28,16},{1,13},{... | collective-permute-start | bytes 221192 | tf_op jit(solution)/shard_map/ppermute | solution.py:306
  30.1 6.0 %collective-permute-start.10 = (bf16[144,256]{1,0:T(8,128)(2,1)S(1)}, bf16[144,256]{1,0:T(8,128)(2,1)S(1)}, u32[]{:S(2)}, u32[]{:S(2)}) collective-permute-start(bf16[144,256]{1,0:T(8,128)(2,1)S(1)} %shard_map.142.refs_0_), channel_id=1, source_target_pairs={{0,8},{4,12},{8,0},{12,4},{16,24},{20,28},{24,16},{28,20},{1,9},{5... | collective-permute-start | bytes 221192 | tf_op jit(solution)/shard_map/ppermute | solution.py:306
  31.5 6.5 %collective-permute-start.9 = (bf16[144,256]{1,0:T(8,128)(2,1)S(1)}, bf16[144,256]{1,0:T(8,128)(2,1)S(1)}, u32[]{:S(2)}, u32[]{:S(2)}) collective-permute-start(bf16[144,256]{1,0:T(8,128)(2,1)S(1)} %shard_map.142.refs_0_), channel_id=1, source_target_pairs={{0,4},{4,0},{8,12},{12,8},{16,20},{20,16},{24,28},{28,24},{1,5},{5... | collective-permute-start | bytes 221192 | tf_op jit(solution)/shard_map/ppermute | solution.py:306
  32.5 8.0 %collective-permute-start.16 = (bf16[256,256]{1,0:T(8,128)(2,1)S(1)}, bf16[256,256]{1,0:T(8,128)(2,1)S(1)}, u32[]{:S(2)}, u32[]{:S(2)}) collective-permute-start(bf16[256,256]{1,0:T(8,128)(2,1)S(1)} %get-tuple-element.71), channel_id=1, source_target_pairs={{0,12},{4,8},{8,4},{12,0},{16,28},{20,24},{24,20},{28,16},{1,13},{... | collective-permute-start | bytes 393224 | tf_op jit(solution)/shard_map/ppermute | solution.py:306
  34.1 7.7 %collective-permute-start.17 = (bf16[256,256]{1,0:T(8,128)(2,1)S(1)}, bf16[256,256]{1,0:T(8,128)(2,1)S(1)}, u32[]{:S(2)}, u32[]{:S(2)}) collective-permute-start(bf16[256,256]{1,0:T(8,128)(2,1)S(1)} %get-tuple-element.72), channel_id=1, source_target_pairs={{0,8},{4,12},{8,0},{12,4},{16,24},{20,28},{24,16},{28,20},{1,9},{5... | collective-permute-start | bytes 393224 | tf_op jit(solution)/shard_map/ppermute | solution.py:306
  35.6 6.3 %collective-permute-start.18 = (bf16[256,256]{1,0:T(8,128)(2,1)S(1)}, bf16[256,256]{1,0:T(8,128)(2,1)S(1)}, u32[]{:S(2)}, u32[]{:S(2)}) collective-permute-start(bf16[256,256]{1,0:T(8,128)(2,1)S(1)} %get-tuple-element.73), channel_id=1, source_target_pairs={{0,4},{4,0},{8,12},{12,8},{16,20},{20,16},{24,28},{28,24},{1,5},{5... | collective-permute-start | bytes 393224 | tf_op jit(solution)/shard_map/ppermute | solution.py:306
  38.1 6.3 %collective-permute-start.12 = (bf16[144,256]{1,0:T(8,128)(2,1)S(1)}, bf16[144,256]{1,0:T(8,128)(2,1)S(1)}, u32[]{:S(2)}, u32[]{:S(2)}) collective-permute-start(bf16[144,256]{1,0:T(8,128)(2,1)S(1)} %shard_map.143.refs_0_), channel_id=1, source_target_pairs={{0,16},{4,20},{8,24},{12,28},{16,0},{20,4},{24,8},{28,12},{1,17},{... | collective-permute-start | bytes 221192 | tf_op jit(solution)/shard_map/ppermute | solution.py:306
  41.9 5.9 %collective-permute-start.19 = (bf16[128,256]{1,0:T(8,128)(2,1)S(1)}, bf16[128,256]{1,0:T(8,128)(2,1)S(1)}, u32[]{:S(2)}, u32[]{:S(2)}) collective-permute-start(bf16[128,256]{1,0:T(8,128)(2,1)S(1)} %get-tuple-element.75), channel_id=1, source_target_pairs={{0,16},{4,20},{8,24},{12,28},{16,0},{20,4},{24,8},{28,12},{1,17},{... | collective-permute-start | bytes 196616 | tf_op jit(solution)/shard_map/ppermute | solution.py:306
  44.4 4.5 %collective-permute-start.15 = (bf16[128,256]{1,0:T(8,128)(2,1)S(1)}, bf16[128,256]{1,0:T(8,128)(2,1)S(1)}, u32[]{:S(2)}, u32[]{:S(2)}) collective-permute-start(bf16[128,256]{1,0:T(8,128)(2,1)S(1)} %get-tuple-element.68.refs_0_), channel_id=1, source_target_pairs={{0,3},{1,2},{2,1},{3,0},{4,7},{5,6},{6,5},{7,4},{8,11},{9,10},{10,... | collective-permute-start | bytes 196616 | tf_op jit(solution)/shard_map/ppermute | solution.py:306
  44.4 5.3 %collective-permute-start.14 = (bf16[128,256]{1,0:T(8,128)(2,1)S(1)}, bf16[128,256]{1,0:T(8,128)(2,1)S(1)}, u32[]{:S(2)}, u32[]{:S(2)}) collective-permute-start(bf16[128,256]{1,0:T(8,128)(2,1)S(1)} %get-tuple-element.68.refs_0_), channel_id=1, source_target_pairs={{0,2},{1,3},{2,0},{3,1},{4,6},{5,7},{6,4},{7,5},{8,10},{9,11},{10,... | collective-permute-start | bytes 196616 | tf_op jit(solution)/shard_map/ppermute | solution.py:306
  45.7 4.0 %collective-permute-start.13 = (bf16[128,256]{1,0:T(8,128)(2,1)S(1)}, bf16[128,256]{1,0:T(8,128)(2,1)S(1)}, u32[]{:S(2)}, u32[]{:S(2)}) collective-permute-start(bf16[128,256]{1,0:T(8,128)(2,1)S(1)} %get-tuple-element.68.refs_0_), channel_id=1, source_target_pairs={{0,1},{1,0},{2,3},{3,2},{4,5},{5,4},{6,7},{7,6},{8,9},{9,8},{10,11... | collective-permute-start | bytes 196616 | tf_op jit(solution)/shard_map/ppermute | solution.py:306

commit v12 on v11

--- a/solution.py
+++ b/solution.py
@@ -1,3 +1,4 @@
+import functools
 import math
 
 import jax
@@ -141,23 +142,22 @@
             adj_ref[g * BLK : (g + 1) * BLK, c * BLK : (c + 1) * BLK] = acc_ref[g, c].astype(BF16)
 
 
-def gather_kernel(adj_ref, *refs):
-    *feature_refs, keep_ref, send_ref = refs
-    half = keep_ref.shape[0] - PAD
+def gather_kernel(keep, adj_ref, *refs):
+    *feature_refs, sum_ref = refs
+    half = sum_ref.shape[0] - PAD
+    rows = slice(0, half) if keep else slice(half, 2 * half)
     total, at = None, 0
     for ref in feature_refs:
         size = ref.shape[0]
-        part = jnp.dot(adj_ref[:, at : at + size], ref[...], preferred_element_type=F32)
+        part = jnp.dot(adj_ref[rows, at : at + size], ref[...], preferred_element_type=F32)
         total = part if total is None else total + part
         at += size
     ones = jnp.ones((PAD, adj_ref.shape[1]), BF16)
     degree = lax.dot_general(
-        ones, adj_ref[...], (((1,), (1,)), ((), ())), preferred_element_type=F32
-    )
-    keep_ref[:half] = total[:half]
-    keep_ref[half:] = degree[:, :half]
-    send_ref[:half] = total[half:].astype(BF16)
-    send_ref[half:] = split(degree[:1, half:])
+        ones, adj_ref[rows, :], (((1,), (1,)), ((), ())), preferred_element_type=F32
+    )
+    sum_ref[:half] = total.astype(sum_ref.dtype)
+    sum_ref[half:] = degree if keep else split(degree[:1])
 
 
 def pair_kernel(keep_ref, got_ref, pair_ref):
@@ -238,11 +238,14 @@
 
 
 def finish_kernel(own_out_ref, self_ref, bias_term_ref, *refs):
-    *terms, out_ref, d_features_ref, grad_self_ref, grad_neigh_ref, bias_ref = refs
-    quarters, terms = terms[:4], terms[4:]
+    *terms, out_ref, d_features_ref, bias_ref = refs
     d_features_ref[...] = self_ref[...] + tree([ref[...].astype(F32) for ref in terms])
     out_ref[...] = own_out_ref[...]
     bias_ref[...] = bias_term_ref[...]
+
+
+def grads_kernel(*refs):
+    *quarters, grad_self_ref, grad_neigh_ref = refs
     me = lax.axis_index("rep")
     low = me >> 1 == 0
     for h in range(2):
@@ -346,11 +349,14 @@
         [pltpu.VMEM(acc_shape, F32)] + buffers + [pltpu.SemaphoreType.DMA((3,))],
     )
     adjacency, near, pieces = lax.optimization_barrier((adjacency, near, pieces))
-    keep, send = call(
-        gather_kernel,
-        (shape((half + PAD, width), F32), shape((half + PAD, width), BF16)),
-        [VMEM] * (1 + len(pieces)),
-        (adjacency, *pieces),
+    send, keep = (
+        call(
+            functools.partial(gather_kernel, stays),
+            shape((half + PAD, width), F32 if stays else BF16),
+            [VMEM] * (1 + len(pieces)),
+            (adjacency, *pieces),
+        )
+        for stays in (False, True)
     )
     pair_sum = call(
         pair_kernel,
@@ -407,13 +413,14 @@
     )
     got = [swap(msg, "row", 4 * (h + 1)) for h, msg in enumerate(far_msgs)]
     quarters = [quarter] + [swap(quarter, "rep", m) for m in range(1, 4)]
-    out, d_features, grad_self, grad_neigh, grad_bias = call(
+    out, d_features, grad_bias = call(
         finish_kernel,
-        (shape((rows, width), BF16), shape((rows, width), F32))
-        + (shape((2, middle, width), F32),) * 2
-        + (shape((1, width), F32),),
-        [VMEM] * (8 + len(got)),
-        (out, self_term, bias_term, *quarters, keep_block, *got),
+        (shape((rows, width), BF16), shape((rows, width), F32), shape((1, width), F32)),
+        [VMEM] * (4 + len(got)),
+        (out, self_term, bias_term, keep_block, *got),
+    )
+    grad_self, grad_neigh = call(
+        grads_kernel, (shape((2, middle, width), F32),) * 2, [VMEM] * 4, quarters
     )
     grad_self, grad_neigh = (v.reshape(width, width) for v in (grad_self, grad_neigh))
     return (out, d_features, grad_self, grad_neigh, grad_bias[0])

time: 50.8 us -> 50.3 us (level)
  waiting for transfers between devices: 18 us -> 16.9 us
  Pallas kernels: 9.53 us -> 10.2 us
    ppermute x20, waiting for transfers between devices: 18 us -> 16.9 us  [swap(): lax.ppermute(value, axis, [(i, i ^ bits) for i in range(lax.axis_size(axi...]
    pallas_call x11 -> x13, Pallas kernels: 9.53 us -> 10.2 us  [call(): pl.pallas_call(kernel, out_shape=out_shape, in_specs=specs, out_specs=[VM...]
  transfers between devices with their start and end apart: 20 -> 20, of which waited for: 12 -> 12; matrix products, arithmetic and copies ran while one was open for 0% -> 0% of each run, Pallas kernels for 14% -> 16%
where the time goes in v12:
time: 50.3 us; the launch traced here: 50.1 us
  starting transfers between devices  22.2 us (44%)
  waiting for transfers between devices  16.9 us (34%)
  Pallas kernels  10.2 us (20%)
  between operations  0.8 us (2%)
    ppermute x20, starting transfers between devices, swap(): lax.ppermute(value, axis, [(i, i ^ bits) for i in range(lax.axis_size(axi...  22.2 us
    ppermute x20, waiting for transfers between devices, swap(): lax.ppermute(value, axis, [(i, i ^ bits) for i in range(lax.axis_size(axi...  16.9 us
    pallas_call x13, Pallas kernels, call(): pl.pallas_call(kernel, out_shape=out_shape, in_specs=specs, out_specs=[VM...  10.2 us
  transfers between devices with their start and end apart: 20, of which 12 were waited for; matrix products, arithmetic and copies ran while one was open for 0% of the time, Pallas kernels for 16%

profile of v12, /device:TPU:0, one launch (start us, length us, event | category | flops | bytes accessed | tf_op | source)
XLA Modules:
  0.0 50.1 jit_solution(9173556191487380808)
XLA Ops:
  0.6 4.1 %collective-permute-start = (bf16[128,256]{1,0:T(8,128)(2,1)}, bf16[128,256]{1,0:T(8,128)(2,1)S(1)}, u32[]{:S(2)}, u32[]{:S(2)}) collective-permute-start(bf16[128,256]{1,0:T(8,128)(2,1)} %features_ref.3), channel_id=1, source_target_pairs={{0,16},{4,20},{8,24},{12,28},{16,0},{20,4},{24,8},{28,12},{1,17},{... | collective-permute-start | bytes 196616 | tf_op jit(solution)/shard_map/ppermute | solution.py:309
  4.7 3.0 %shard_map.137 = (f32[4,8,128,128]{3,2,1,0:T(8,128)S(1)}, bf16[256,256]{1,0:T(8,128)(2,1)S(1)}, s32[144,256]{1,0:T(8,128)S(1)}, s32[144,256]{1,0:T(8,128)S(1)}) custom-call(s32[256]{0:T(256)} %row_ref.3, s32[256]{0:T(256)} %col_ref.3, s32[256]{0:T(256)} %count_ref.3, s32[256,256]{1,0:T(8,128)} %src_ref.1, s32[256,256]{1,0:T(8,128)} %dst_ref.1, ...), custom_call_target="tpu_custom_call" | custom-call | tf_op jit(solution)/shard_map/pallas_call | solution.py:288
  7.7 0.9 %collective-permute-done = bf16[128,256]{1,0:T(8,128)(2,1)S(1)} collective-permute-done((bf16[128,256]{1,0:T(8,128)(2,1)}, bf16[128,256]{1,0:T(8,128)(2,1)S(1)}, u32[]{:S(2)}, u32[]{:S(2)}) %collective-permute-start) | collective-permute-done | bytes 65568 | tf_op jit(solution)/shard_map/ppermute | solution.py:309
  8.6 1.8 %collective-permute-start.5 = (bf16[256,256]{1,0:T(8,128)(2,1)S(1)}, bf16[256,256]{1,0:T(8,128)(2,1)S(1)}, u32[]{:S(2)}, u32[]{:S(2)}) collective-permute-start(bf16[256,256]{1,0:T(8,128)(2,1)S(1)} %constant_dynamic-update-slice_fusion.refs_0_), channel_id=1, source_target_pairs={{0,12},{4,8},{8,4},{12,0},{16,28},{20,24},{24,20},{28,16},{1,13},{... | collective-permute-start | bytes 393224 | tf_op jit(solution)/shard_map/ppermute | solution.py:309
  10.4 1.4 %collective-permute-start.4 = (bf16[256,256]{1,0:T(8,128)(2,1)S(1)}, bf16[256,256]{1,0:T(8,128)(2,1)S(1)}, u32[]{:S(2)}, u32[]{:S(2)}) collective-permute-start(bf16[256,256]{1,0:T(8,128)(2,1)S(1)} %constant_dynamic-update-slice_fusion.refs_0_), channel_id=1, source_target_pairs={{0,8},{4,12},{8,0},{12,4},{16,24},{20,28},{24,16},{28,20},{1,9},{5... | collective-permute-start | bytes 393224 | tf_op jit(solution)/shard_map/ppermute | solution.py:309
  11.8 0.3 collective-permute-start.3
  12.1 1.7 %collective-permute-start.1 = (bf16[128,256]{1,0:T(8,128)(2,1)}, bf16[128,256]{1,0:T(8,128)(2,1)S(1)}, u32[]{:S(2)}, u32[]{:S(2)}) collective-permute-start(bf16[128,256]{1,0:T(8,128)(2,1)} %features_ref.3), channel_id=1, source_target_pairs={{0,2},{1,3},{2,0},{3,1},{4,6},{5,7},{6,4},{7,5},{8,10},{9,11},{10,... | collective-permute-start | bytes 196616 | tf_op jit(solution)/shard_map/ppermute | solution.py:309
  13.8 0.3 collective-permute-start.2
  14.1 3.5 %shard_map.138.adj_ref = bf16[512,1024]{1,0:T(8,128)(2,1)S(1)} custom-call(s32[256]{0:T(256)} %row_ref.3, s32[256]{0:T(256)} %col_ref.3, s32[256]{0:T(256)} %count_ref.3, s32[144,256]{1,0:T(8,128)S(1)} %get-tuple-element.41.src_ref, s32[144,256]{1,0:T(8,128)S(1)} %get-tuple-element.42.dst_ref, f32[4,8,128,128]{3,2,1,0:T(8,128)S(1)} %get-tuple-element.46.half_ref), custom_call_target="tpu_custom_call" | custom-call | tf_op jit(solution)/shard_map/pallas_call | solution.py:288
  17.6 0.0 copy-start
  17.6 0.0 copy-start.1
  17.6 0.0 copy-start.2
  17.6 0.0 copy-start.3
  17.6 0.0 copy-start.4
  17.6 0.0 collective-permute-done.1.near_features_ref
  17.7 0.6 %collective-permute-done.2.near_d_out_ref = bf16[128,256]{1,0:T(8,128)(2,1)S(1)} collective-permute-done((bf16[128,256]{1,0:T(8,128)(2,1)}, bf16[128,256]{1,0:T(8,128)(2,1)S(1)}, u32[]{:S(2)}, u32[]{:S(2)}) %collective-permute-start.2) | collective-permute-done | bytes 65568 | tf_op jit(solution)/shard_map/ppermute | solution.py:309
  18.3 0.0 collective-permute-done.5.refs_3_
  18.3 0.0 collective-permute-done.4.refs_2_
  18.3 0.0 collective-permute-done.3.refs_1_
  18.3 0.4 shard_map.140
  18.7 0.1 collective-permute-start.6
  18.8 0.4 shard_map.139.keep_ref
  19.2 0.9 %collective-permute-done.6.got_ref = bf16[272,256]{1,0:T(8,128)(2,1)S(1)} collective-permute-done((bf16[272,256]{1,0:T(8,128)(2,1)S(1)}, bf16[272,256]{1,0:T(8,128)(2,1)S(1)}, u32[]{:S(2)}, u32[]{:S(2)}) %collective-permute-start.6) | collective-permute-done | bytes 139296 | tf_op jit(solution)/shard_map/ppermute | solution.py:309
  20.1 0.1 shard_map.141.pair_ref
  20.2 1.2 %collective-permute-start.7 = (bf16[272,256]{1,0:T(8,128)(2,1)S(1)}, bf16[272,256]{1,0:T(8,128)(2,1)S(1)}, u32[]{:S(2)}, u32[]{:S(2)}) collective-permute-start(bf16[272,256]{1,0:T(8,128)(2,1)S(1)} %shard_map.141.pair_ref), channel_id=1, source_target_pairs={{0,2},{1,3},{2,0},{3,1},{4,6},{5,7},{6,4},{7,5},{8,10},{9,11},{10,... | collective-permute-start | bytes 417800 | tf_op jit(solution)/shard_map/ppermute | solution.py:309
  21.4 4.6 %collective-permute-done.7.got_ref = bf16[272,256]{1,0:T(8,128)(2,1)S(1)} collective-permute-done((bf16[272,256]{1,0:T(8,128)(2,1)S(1)}, bf16[272,256]{1,0:T(8,128)(2,1)S(1)}, u32[]{:S(2)}, u32[]{:S(2)}) %collective-permute-start.7) | collective-permute-done | bytes 139296 | tf_op jit(solution)/shard_map/ppermute | solution.py:309
  26.0 0.0 copy-done
  26.0 0.0 copy-done.1
  26.0 0.0 copy-done.2
  26.0 0.0 copy-done.3
  26.0 0.0 copy-done.4
  26.0 0.7 %shard_map.142 = (bf16[128,256]{1,0:T(8,128)(2,1)S(1)}, f32[128,256]{1,0:T(8,128)S(1)}, f32[144,256]{1,0:T(8,128)S(1)}, bf16[400,256]{1,0:T(8,128)(2,1)S(1)}) custom-call(bf16[272,256]{1,0:T(8,128)(2,1)S(1)} %shard_map.141.pair_ref, bf16[272,256]{1,0:T(8,128)(2,1)S(1)} %collective-permute-done.7.got_ref, bf16[128,256]{1,0:T(8,128)(2,1)S(1)} %copy-done, ...), custom_call_target="tpu_custom_call" | custom-call | tf_op jit(solution)/shard_map/pallas_call | solution.py:288
  26.7 0.1 collective-permute-start.8
  26.7 1.4 %collective-permute-done.8.got_ref = bf16[400,256]{1,0:T(8,128)(2,1)S(1)} collective-permute-done((bf16[400,256]{1,0:T(8,128)(2,1)S(1)}, bf16[400,256]{1,0:T(8,128)(2,1)S(1)}, u32[]{:S(2)}, u32[]{:S(2)}) %collective-permute-start.8) | collective-permute-done | bytes 204832 | tf_op jit(solution)/shard_map/ppermute | solution.py:309
  28.2 1.6 %collective-permute-start.11 = (bf16[144,256]{1,0:T(8,128)(2,1)S(1)}, bf16[144,256]{1,0:T(8,128)(2,1)S(1)}, u32[]{:S(2)}, u32[]{:S(2)}) collective-permute-start(bf16[144,256]{1,0:T(8,128)(2,1)S(1)} %shard_map.143.refs_0_), channel_id=1, source_target_pairs={{0,12},{4,8},{8,4},{12,0},{16,28},{20,24},{24,20},{28,16},{1,13},{... | collective-permute-start | bytes 221192 | tf_op jit(solution)/shard_map/ppermute | solution.py:309
  29.8 1.4 %collective-permute-start.10 = (bf16[144,256]{1,0:T(8,128)(2,1)S(1)}, bf16[144,256]{1,0:T(8,128)(2,1)S(1)}, u32[]{:S(2)}, u32[]{:S(2)}) collective-permute-start(bf16[144,256]{1,0:T(8,128)(2,1)S(1)} %shard_map.143.refs_0_), channel_id=1, source_target_pairs={{0,8},{4,12},{8,0},{12,4},{16,24},{20,28},{24,16},{28,20},{1,9},{5... | collective-permute-start | bytes 221192 | tf_op jit(solution)/shard_map/ppermute | solution.py:309
  31.3 0.5 %collective-permute-start.9 = (bf16[144,256]{1,0:T(8,128)(2,1)S(1)}, bf16[144,256]{1,0:T(8,128)(2,1)S(1)}, u32[]{:S(2)}, u32[]{:S(2)}) collective-permute-start(bf16[144,256]{1,0:T(8,128)(2,1)S(1)} %shard_map.143.refs_0_), channel_id=1, source_target_pairs={{0,4},{4,0},{8,12},{12,8},{16,20},{20,16},{24,28},{28,24},{1,5},{5... | collective-permute-start | bytes 221192 | tf_op jit(solution)/shard_map/ppermute | solution.py:309
  31.8 0.5 shard_map.146
  32.3 1.6 %collective-permute-start.13 = (bf16[256,256]{1,0:T(8,128)(2,1)S(1)}, bf16[256,256]{1,0:T(8,128)(2,1)S(1)}, u32[]{:S(2)}, u32[]{:S(2)}) collective-permute-start(bf16[256,256]{1,0:T(8,128)(2,1)S(1)} %get-tuple-element.66), channel_id=1, source_target_pairs={{0,12},{4,8},{8,4},{12,0},{16,28},{20,24},{24,20},{28,16},{1,13},{... | collective-permute-start | bytes 393224 | tf_op jit(solution)/shard_map/ppermute | solution.py:309
  33.9 1.4 %collective-permute-start.14 = (bf16[256,256]{1,0:T(8,128)(2,1)S(1)}, bf16[256,256]{1,0:T(8,128)(2,1)S(1)}, u32[]{:S(2)}, u32[]{:S(2)}) collective-permute-start(bf16[256,256]{1,0:T(8,128)(2,1)S(1)} %get-tuple-element.67), channel_id=1, source_target_pairs={{0,8},{4,12},{8,0},{12,4},{16,24},{20,28},{24,16},{28,20},{1,9},{5... | collective-permute-start | bytes 393224 | tf_op jit(solution)/shard_map/ppermute | solution.py:309
  35.3 0.0 collective-permute-done.11.refs_3_
  35.3 0.5 collective-permute-start.15
  35.8 0.0 collective-permute-done.10.refs_2_
  35.8 1.9 %collective-permute-done.9.refs_1_ = bf16[144,256]{1,0:T(8,128)(2,1)S(1)} collective-permute-done((bf16[144,256]{1,0:T(8,128)(2,1)S(1)}, bf16[144,256]{1,0:T(8,128)(2,1)S(1)}, u32[]{:S(2)}, u32[]{:S(2)}) %collective-permute-start.9) | collective-permute-done | bytes 73760 | tf_op jit(solution)/shard_map/ppermute | solution.py:309
  37.8 0.1 collective-permute-start.12
  37.9 2.4 %collective-permute-done.13.refs_0_ = bf16[256,256]{1,0:T(8,128)(2,1)S(1)} collective-permute-done((bf16[256,256]{1,0:T(8,128)(2,1)S(1)}, bf16[256,256]{1,0:T(8,128)(2,1)S(1)}, u32[]{:S(2)}, u32[]{:S(2)}) %collective-permute-start.13) | collective-permute-done | bytes 131104 | tf_op jit(solution)/shard_map/ppermute | solution.py:309
  40.3 1.3 %collective-permute-done.14.refs_1_ = bf16[256,256]{1,0:T(8,128)(2,1)S(1)} collective-permute-done((bf16[256,256]{1,0:T(8,128)(2,1)S(1)}, bf16[256,256]{1,0:T(8,128)(2,1)S(1)}, u32[]{:S(2)}, u32[]{:S(2)}) %collective-permute-start.14) | collective-permute-done | bytes 131104 | tf_op jit(solution)/shard_map/ppermute | solution.py:309
  41.6 0.0 collective-permute-done.15.refs_2_
  41.6 0.1 shard_map.147
  41.7 2.2 %collective-permute-start.16 = (bf16[128,256]{1,0:T(8,128)(2,1)S(1)}, bf16[128,256]{1,0:T(8,128)(2,1)S(1)}, u32[]{:S(2)}, u32[]{:S(2)}) collective-permute-start(bf16[128,256]{1,0:T(8,128)(2,1)S(1)} %get-tuple-element.70), channel_id=1, source_target_pairs={{0,16},{4,20},{8,24},{12,28},{16,0},{20,4},{24,8},{28,12},{1,17},{... | collective-permute-start | bytes 196616 | tf_op jit(solution)/shard_map/ppermute | solution.py:309
  43.9 0.2 collective-permute-done.12.refs_1_
  44.1 0.1 collective-permute-start.19
  44.2 1.2 %collective-permute-start.18 = (bf16[128,256]{1,0:T(8,128)(2,1)S(1)}, bf16[128,256]{1,0:T(8,128)(2,1)S(1)}, u32[]{:S(2)}, u32[]{:S(2)}) collective-permute-start(bf16[128,256]{1,0:T(8,128)(2,1)S(1)} %get-tuple-element.73.refs_0_), channel_id=1, source_target_pairs={{0,2},{1,3},{2,0},{3,1},{4,6},{5,7},{6,4},{7,5},{8,10},{9,11},{10,... | collective-permute-start | bytes 196616 | tf_op jit(solution)/shard_map/ppermute | solution.py:309
  45.4 0.7 %collective-permute-start.17 = (bf16[128,256]{1,0:T(8,128)(2,1)S(1)}, bf16[128,256]{1,0:T(8,128)(2,1)S(1)}, u32[]{:S(2)}, u32[]{:S(2)}) collective-permute-start(bf16[128,256]{1,0:T(8,128)(2,1)S(1)} %get-tuple-element.73.refs_0_), channel_id=1, source_target_pairs={{0,1},{1,0},{2,3},{3,2},{4,5},{5,4},{6,7},{7,6},{8,9},{9,8},{10,11... | collective-permute-start | bytes 196616 | tf_op jit(solution)/shard_map/ppermute | solution.py:309
  46.0 1.6 %collective-permute-done.16.refs_1_ = bf16[128,256]{1,0:T(8,128)(2,1)S(1)} collective-permute-done((bf16[128,256]{1,0:T(8,128)(2,1)S(1)}, bf16[128,256]{1,0:T(8,128)(2,1)S(1)}, u32[]{:S(2)}, u32[]{:S(2)}) %collective-permute-start.16) | collective-permute-done | bytes 65568 | tf_op jit(solution)/shard_map/ppermute | solution.py:309
  47.6 0.7 %shard_map.148 = (bf16[128,256]{1,0:T(8,128)(2,1)}, f32[128,256]{1,0:T(8,128)}, f32[1,256]{1,0:T(1,128)}) custom-call(bf16[128,256]{1,0:T(8,128)(2,1)S(1)} %get-tuple-element.58.own_out_ref, f32[128,256]{1,0:T(8,128)S(1)} %get-tuple-element.59.self_ref, f32[1,256]{1,0:T(1,128)S(1)} %get-tuple-element.63.bias_term_ref, ...), custom_call_target="tpu_custom_call" | custom-call | tf_op jit(solution)/shard_map/pallas_call | solution.py:288
  48.3 0.3 collective-permute-done.19.refs_3_
  48.6 0.7 %collective-permute-done.18.refs_2_ = bf16[128,256]{1,0:T(8,128)(2,1)S(1)} collective-permute-done((bf16[128,256]{1,0:T(8,128)(2,1)S(1)}, bf16[128,256]{1,0:T(8,128)(2,1)S(1)}, u32[]{:S(2)}, u32[]{:S(2)}) %collective-permute-start.18) | collective-permute-done | bytes 65568 | tf_op jit(solution)/shard_map/ppermute | solution.py:309
  49.3 0.0 collective-permute-done.17.refs_1_
  49.3 0.8 %shard_map.149 = (f32[2,128,256]{2,1,0:T(8,128)}, f32[2,128,256]{2,1,0:T(8,128)}) custom-call(bf16[128,256]{1,0:T(8,128)(2,1)S(1)} %get-tuple-element.73.refs_0_, bf16[128,256]{1,0:T(8,128)(2,1)S(1)} %collective-permute-done.17.refs_1_, bf16[128,256]{1,0:T(8,128)(2,1)S(1)} %collective-permute-done.18.refs_2_, ...), custom_call_target="tpu_custom_call" | custom-call | tf_op jit(solution)/shard_map/pallas_call | solution.py:288
  (4 shorter events, 0.1 us)
Async XLA Ops:
  0.6 8.0 %collective-permute-start = (bf16[128,256]{1,0:T(8,128)(2,1)}, bf16[128,256]{1,0:T(8,128)(2,1)S(1)}, u32[]{:S(2)}, u32[]{:S(2)}) collective-permute-start(bf16[128,256]{1,0:T(8,128)(2,1)} %features_ref.3), channel_id=1, source_target_pairs={{0,16},{4,20},{8,24},{12,28},{16,0},{20,4},{24,8},{28,12},{1,17},{... | collective-permute-start | bytes 196616 | tf_op jit(solution)/shard_map/ppermute | solution.py:309
  8.6 9.7 %collective-permute-start.5 = (bf16[256,256]{1,0:T(8,128)(2,1)S(1)}, bf16[256,256]{1,0:T(8,128)(2,1)S(1)}, u32[]{:S(2)}, u32[]{:S(2)}) collective-permute-start(bf16[256,256]{1,0:T(8,128)(2,1)S(1)} %constant_dynamic-update-slice_fusion.refs_0_), channel_id=1, source_target_pairs={{0,12},{4,8},{8,4},{12,0},{16,28},{20,24},{24,20},{28,16},{1,13},{... | collective-permute-start | bytes 393224 | tf_op jit(solution)/shard_map/ppermute | solution.py:309
  10.4 7.9 %collective-permute-start.4 = (bf16[256,256]{1,0:T(8,128)(2,1)S(1)}, bf16[256,256]{1,0:T(8,128)(2,1)S(1)}, u32[]{:S(2)}, u32[]{:S(2)}) collective-permute-start(bf16[256,256]{1,0:T(8,128)(2,1)S(1)} %constant_dynamic-update-slice_fusion.refs_0_), channel_id=1, source_target_pairs={{0,8},{4,12},{8,0},{12,4},{16,24},{20,28},{24,16},{28,20},{1,9},{5... | collective-permute-start | bytes 393224 | tf_op jit(solution)/shard_map/ppermute | solution.py:309
  11.8 6.5 %collective-permute-start.3 = (bf16[256,256]{1,0:T(8,128)(2,1)S(1)}, bf16[256,256]{1,0:T(8,128)(2,1)S(1)}, u32[]{:S(2)}, u32[]{:S(2)}) collective-permute-start(bf16[256,256]{1,0:T(8,128)(2,1)S(1)} %constant_dynamic-update-slice_fusion.refs_0_), channel_id=1, source_target_pairs={{0,4},{4,0},{8,12},{12,8},{16,20},{20,16},{24,28},{28,24},{1,5},{5... | collective-permute-start | bytes 393224 | tf_op jit(solution)/shard_map/ppermute | solution.py:309
  12.1 5.6 %collective-permute-start.1 = (bf16[128,256]{1,0:T(8,128)(2,1)}, bf16[128,256]{1,0:T(8,128)(2,1)S(1)}, u32[]{:S(2)}, u32[]{:S(2)}) collective-permute-start(bf16[128,256]{1,0:T(8,128)(2,1)} %features_ref.3), channel_id=1, source_target_pairs={{0,2},{1,3},{2,0},{3,1},{4,6},{5,7},{6,4},{7,5},{8,10},{9,11},{10,... | collective-permute-start | bytes 196616 | tf_op jit(solution)/shard_map/ppermute | solution.py:309
  13.8 4.5 %collective-permute-start.2 = (bf16[128,256]{1,0:T(8,128)(2,1)}, bf16[128,256]{1,0:T(8,128)(2,1)S(1)}, u32[]{:S(2)}, u32[]{:S(2)}) collective-permute-start(bf16[128,256]{1,0:T(8,128)(2,1)} %d_out_ref.1), channel_id=1, source_target_pairs={{0,2},{1,3},{2,0},{3,1},{4,6},{5,7},{6,4},{7,5},{8,10},{9,11},{10,... | collective-permute-start | bytes 196616 | tf_op jit(solution)/shard_map/ppermute | solution.py:309
  17.6 8.4 %copy-start = (bf16[128,256]{1,0:T(8,128)(2,1)S(1)}, bf16[128,256]{1,0:T(8,128)(2,1)}, u32[]{:S(2)}) copy-start(bf16[128,256]{1,0:T(8,128)(2,1)} %features_ref.3) | copy-start | bytes 196612
  17.6 8.4 %copy-start.1 = (bf16[256,256]{1,0:T(8,128)(2,1)S(1)}, bf16[256,256]{1,0:T(8,128)(2,1)}, u32[]{:S(2)}) copy-start(bf16[256,256]{1,0:T(8,128)(2,1)} %w_self_ref.1) | copy-start | bytes 393220
  17.6 8.4 %copy-start.2 = (bf16[256,256]{1,0:T(8,128)(2,1)S(1)}, bf16[256,256]{1,0:T(8,128)(2,1)}, u32[]{:S(2)}) copy-start(bf16[256,256]{1,0:T(8,128)(2,1)} %w_neigh_ref.1) | copy-start | bytes 393220
  17.6 8.4 %copy-start.3 = (bf16[128,256]{1,0:T(8,128)(2,1)S(1)}, bf16[128,256]{1,0:T(8,128)(2,1)}, u32[]{:S(2)}) copy-start(bf16[128,256]{1,0:T(8,128)(2,1)} %d_out_ref.1) | copy-start | bytes 196612
  17.6 8.4 %copy-start.4 = (f32[256]{0:T(256)S(1)}, f32[256]{0:T(256)}, u32[]{:S(2)}) copy-start(f32[256]{0:T(256)} %param.13) | copy-start | bytes 3076
  18.7 1.4 %collective-permute-start.6 = (bf16[272,256]{1,0:T(8,128)(2,1)S(1)}, bf16[272,256]{1,0:T(8,128)(2,1)S(1)}, u32[]{:S(2)}, u32[]{:S(2)}) collective-permute-start(bf16[272,256]{1,0:T(8,128)(2,1)S(1)} %shard_map.140), channel_id=1, source_target_pairs={{0,1},{1,0},{2,3},{3,2},{4,5},{5,4},{6,7},{7,6},{8,9},{9,8},{10,11... | collective-permute-start | bytes 417800 | tf_op jit(solution)/shard_map/ppermute | solution.py:309
  20.2 5.8 %collective-permute-start.7 = (bf16[272,256]{1,0:T(8,128)(2,1)S(1)}, bf16[272,256]{1,0:T(8,128)(2,1)S(1)}, u32[]{:S(2)}, u32[]{:S(2)}) collective-permute-start(bf16[272,256]{1,0:T(8,128)(2,1)S(1)} %shard_map.141.pair_ref), channel_id=1, source_target_pairs={{0,2},{1,3},{2,0},{3,1},{4,6},{5,7},{6,4},{7,5},{8,10},{9,11},{10,... | collective-permute-start | bytes 417800 | tf_op jit(solution)/shard_map/ppermute | solution.py:309
  26.7 1.5 %collective-permute-start.8 = (bf16[400,256]{1,0:T(8,128)(2,1)S(1)}, bf16[400,256]{1,0:T(8,128)(2,1)S(1)}, u32[]{:S(2)}, u32[]{:S(2)}) collective-permute-start(bf16[400,256]{1,0:T(8,128)(2,1)S(1)} %get-tuple-element.61.sent_ref), channel_id=1, source_target_pairs={{0,1},{1,0},{2,3},{3,2},{4,5},{5,4},{6,7},{7,6},{8,9},{9,8},{10,11... | collective-permute-start | bytes 614408 | tf_op jit(solution)/shard_map/ppermute | solution.py:309
  28.2 7.1 %collective-permute-start.11 = (bf16[144,256]{1,0:T(8,128)(2,1)S(1)}, bf16[144,256]{1,0:T(8,128)(2,1)S(1)}, u32[]{:S(2)}, u32[]{:S(2)}) collective-permute-start(bf16[144,256]{1,0:T(8,128)(2,1)S(1)} %shard_map.143.refs_0_), channel_id=1, source_target_pairs={{0,12},{4,8},{8,4},{12,0},{16,28},{20,24},{24,20},{28,16},{1,13},{... | collective-permute-start | bytes 221192 | tf_op jit(solution)/shard_map/ppermute | solution.py:309
  29.8 6.0 %collective-permute-start.10 = (bf16[144,256]{1,0:T(8,128)(2,1)S(1)}, bf16[144,256]{1,0:T(8,128)(2,1)S(1)}, u32[]{:S(2)}, u32[]{:S(2)}) collective-permute-start(bf16[144,256]{1,0:T(8,128)(2,1)S(1)} %shard_map.143.refs_0_), channel_id=1, source_target_pairs={{0,8},{4,12},{8,0},{12,4},{16,24},{20,28},{24,16},{28,20},{1,9},{5... | collective-permute-start | bytes 221192 | tf_op jit(solution)/shard_map/ppermute | solution.py:309
  31.3 6.5 %collective-permute-start.9 = (bf16[144,256]{1,0:T(8,128)(2,1)S(1)}, bf16[144,256]{1,0:T(8,128)(2,1)S(1)}, u32[]{:S(2)}, u32[]{:S(2)}) collective-permute-start(bf16[144,256]{1,0:T(8,128)(2,1)S(1)} %shard_map.143.refs_0_), channel_id=1, source_target_pairs={{0,4},{4,0},{8,12},{12,8},{16,20},{20,16},{24,28},{28,24},{1,5},{5... | collective-permute-start | bytes 221192 | tf_op jit(solution)/shard_map/ppermute | solution.py:309
  32.3 8.0 %collective-permute-start.13 = (bf16[256,256]{1,0:T(8,128)(2,1)S(1)}, bf16[256,256]{1,0:T(8,128)(2,1)S(1)}, u32[]{:S(2)}, u32[]{:S(2)}) collective-permute-start(bf16[256,256]{1,0:T(8,128)(2,1)S(1)} %get-tuple-element.66), channel_id=1, source_target_pairs={{0,12},{4,8},{8,4},{12,0},{16,28},{20,24},{24,20},{28,16},{1,13},{... | collective-permute-start | bytes 393224 | tf_op jit(solution)/shard_map/ppermute | solution.py:309
  33.9 7.7 %collective-permute-start.14 = (bf16[256,256]{1,0:T(8,128)(2,1)S(1)}, bf16[256,256]{1,0:T(8,128)(2,1)S(1)}, u32[]{:S(2)}, u32[]{:S(2)}) collective-permute-start(bf16[256,256]{1,0:T(8,128)(2,1)S(1)} %get-tuple-element.67), channel_id=1, source_target_pairs={{0,8},{4,12},{8,0},{12,4},{16,24},{20,28},{24,16},{28,20},{1,9},{5... | collective-permute-start | bytes 393224 | tf_op jit(solution)/shard_map/ppermute | solution.py:309
  35.3 6.3 %collective-permute-start.15 = (bf16[256,256]{1,0:T(8,128)(2,1)S(1)}, bf16[256,256]{1,0:T(8,128)(2,1)S(1)}, u32[]{:S(2)}, u32[]{:S(2)}) collective-permute-start(bf16[256,256]{1,0:T(8,128)(2,1)S(1)} %get-tuple-element.68), channel_id=1, source_target_pairs={{0,4},{4,0},{8,12},{12,8},{16,20},{20,16},{24,28},{28,24},{1,5},{5... | collective-permute-start | bytes 393224 | tf_op jit(solution)/shard_map/ppermute | solution.py:309
  37.8 6.3 %collective-permute-start.12 = (bf16[144,256]{1,0:T(8,128)(2,1)S(1)}, bf16[144,256]{1,0:T(8,128)(2,1)S(1)}, u32[]{:S(2)}, u32[]{:S(2)}) collective-permute-start(bf16[144,256]{1,0:T(8,128)(2,1)S(1)} %shard_map.144.refs_0_), channel_id=1, source_target_pairs={{0,16},{4,20},{8,24},{12,28},{16,0},{20,4},{24,8},{28,12},{1,17},{... | collective-permute-start | bytes 221192 | tf_op jit(solution)/shard_map/ppermute | solution.py:309
  41.7 5.9 %collective-permute-start.16 = (bf16[128,256]{1,0:T(8,128)(2,1)S(1)}, bf16[128,256]{1,0:T(8,128)(2,1)S(1)}, u32[]{:S(2)}, u32[]{:S(2)}) collective-permute-start(bf16[128,256]{1,0:T(8,128)(2,1)S(1)} %get-tuple-element.70), channel_id=1, source_target_pairs={{0,16},{4,20},{8,24},{12,28},{16,0},{20,4},{24,8},{28,12},{1,17},{... | collective-permute-start | bytes 196616 | tf_op jit(solution)/shard_map/ppermute | solution.py:309
  44.1 4.5 %collective-permute-start.19 = (bf16[128,256]{1,0:T(8,128)(2,1)S(1)}, bf16[128,256]{1,0:T(8,128)(2,1)S(1)}, u32[]{:S(2)}, u32[]{:S(2)}) collective-permute-start(bf16[128,256]{1,0:T(8,128)(2,1)S(1)} %get-tuple-element.73.refs_0_), channel_id=1, source_target_pairs={{0,3},{1,2},{2,1},{3,0},{4,7},{5,6},{6,5},{7,4},{8,11},{9,10},{10,... | collective-permute-start | bytes 196616 | tf_op jit(solution)/shard_map/ppermute | solution.py:309
  44.2 5.1 %collective-permute-start.18 = (bf16[128,256]{1,0:T(8,128)(2,1)S(1)}, bf16[128,256]{1,0:T(8,128)(2,1)S(1)}, u32[]{:S(2)}, u32[]{:S(2)}) collective-permute-start(bf16[128,256]{1,0:T(8,128)(2,1)S(1)} %get-tuple-element.73.refs_0_), channel_id=1, source_target_pairs={{0,2},{1,3},{2,0},{3,1},{4,6},{5,7},{6,4},{7,5},{8,10},{9,11},{10,... | collective-permute-start | bytes 196616 | tf_op jit(solution)/shard_map/ppermute | solution.py:309
  45.4 3.9 %collective-permute-start.17 = (bf16[128,256]{1,0:T(8,128)(2,1)S(1)}, bf16[128,256]{1,0:T(8,128)(2,1)S(1)}, u32[]{:S(2)}, u32[]{:S(2)}) collective-permute-start(bf16[128,256]{1,0:T(8,128)(2,1)S(1)} %get-tuple-element.73.refs_0_), channel_id=1, source_target_pairs={{0,1},{1,0},{2,3},{3,2},{4,5},{5,4},{6,7},{7,6},{8,9},{9,8},{10,11... | collective-permute-start | bytes 196616 | tf_op jit(solution)/shard_map/ppermute | solution.py:309

commit v13 on v12

--- a/solution.py
+++ b/solution.py
@@ -9,7 +9,7 @@
 from jax.sharding import PartitionSpec as P
 
 BLK = 128
-PAD = 16
+PAD = 8
 BF16 = jnp.bfloat16
 F32 = jnp.float32
 HOT = jnp.float8_e4m3fn

time: 50.3 us -> 49.9 us (level)
  transfers between devices with their start and end apart: 20 -> 20, of which waited for: 12 -> 10; matrix products, arithmetic and copies ran while one was open for 0% -> 0% of each run, Pallas kernels for 16% -> 16%
where the time goes in v13:
time: 49.9 us; the launch traced here: 49.8 us
  starting transfers between devices  22.3 us (45%)
  waiting for transfers between devices  16.4 us (33%)
  Pallas kernels  10.2 us (20%)
  between operations  0.8 us (2%)
    ppermute x20, starting transfers between devices, swap(): lax.ppermute(value, axis, [(i, i ^ bits) for i in range(lax.axis_size(axi...  22.3 us
    ppermute x20, waiting for transfers between devices, swap(): lax.ppermute(value, axis, [(i, i ^ bits) for i in range(lax.axis_size(axi...  16.4 us
    pallas_call x13, Pallas kernels, call(): pl.pallas_call(kernel, out_shape=out_shape, in_specs=specs, out_specs=[VM...  10.2 us
  transfers between devices with their start and end apart: 20, of which 10 were waited for; matrix products, arithmetic and copies ran while one was open for 0% of the time, Pallas kernels for 16%

profile of v13, /device:TPU:0, one launch (start us, length us, event | category | flops | bytes accessed | tf_op | source)
XLA Modules:
  0.0 49.8 jit_solution(4754685804534205835)
XLA Ops:
  0.6 4.1 %collective-permute-start = (bf16[128,256]{1,0:T(8,128)(2,1)}, bf16[128,256]{1,0:T(8,128)(2,1)S(1)}, u32[]{:S(2)}, u32[]{:S(2)}) collective-permute-start(bf16[128,256]{1,0:T(8,128)(2,1)} %features_ref.3), channel_id=1, source_target_pairs={{0,16},{4,20},{8,24},{12,28},{16,0},{20,4},{24,8},{28,12},{1,17},{... | collective-permute-start | bytes 196616 | tf_op jit(solution)/shard_map/ppermute | solution.py:309
  4.7 3.0 %shard_map.137 = (f32[4,8,128,128]{3,2,1,0:T(8,128)S(1)}, bf16[256,256]{1,0:T(8,128)(2,1)S(1)}, s32[144,256]{1,0:T(8,128)S(1)}, s32[144,256]{1,0:T(8,128)S(1)}) custom-call(s32[256]{0:T(256)} %row_ref.3, s32[256]{0:T(256)} %col_ref.3, s32[256]{0:T(256)} %count_ref.3, s32[256,256]{1,0:T(8,128)} %src_ref.1, s32[256,256]{1,0:T(8,128)} %dst_ref.1, ...), custom_call_target="tpu_custom_call" | custom-call | tf_op jit(solution)/shard_map/pallas_call | solution.py:288
  7.7 0.9 %collective-permute-done = bf16[128,256]{1,0:T(8,128)(2,1)S(1)} collective-permute-done((bf16[128,256]{1,0:T(8,128)(2,1)}, bf16[128,256]{1,0:T(8,128)(2,1)S(1)}, u32[]{:S(2)}, u32[]{:S(2)}) %collective-permute-start) | collective-permute-done | bytes 65568 | tf_op jit(solution)/shard_map/ppermute | solution.py:309
  8.6 1.8 %collective-permute-start.5 = (bf16[256,256]{1,0:T(8,128)(2,1)S(1)}, bf16[256,256]{1,0:T(8,128)(2,1)S(1)}, u32[]{:S(2)}, u32[]{:S(2)}) collective-permute-start(bf16[256,256]{1,0:T(8,128)(2,1)S(1)} %constant_dynamic-update-slice_fusion.refs_0_), channel_id=1, source_target_pairs={{0,12},{4,8},{8,4},{12,0},{16,28},{20,24},{24,20},{28,16},{1,13},{... | collective-permute-start | bytes 393224 | tf_op jit(solution)/shard_map/ppermute | solution.py:309
  10.4 1.4 %collective-permute-start.4 = (bf16[256,256]{1,0:T(8,128)(2,1)S(1)}, bf16[256,256]{1,0:T(8,128)(2,1)S(1)}, u32[]{:S(2)}, u32[]{:S(2)}) collective-permute-start(bf16[256,256]{1,0:T(8,128)(2,1)S(1)} %constant_dynamic-update-slice_fusion.refs_0_), channel_id=1, source_target_pairs={{0,8},{4,12},{8,0},{12,4},{16,24},{20,28},{24,16},{28,20},{1,9},{5... | collective-permute-start | bytes 393224 | tf_op jit(solution)/shard_map/ppermute | solution.py:309
  11.8 0.3 collective-permute-start.3
  12.1 1.7 %collective-permute-start.1 = (bf16[128,256]{1,0:T(8,128)(2,1)}, bf16[128,256]{1,0:T(8,128)(2,1)S(1)}, u32[]{:S(2)}, u32[]{:S(2)}) collective-permute-start(bf16[128,256]{1,0:T(8,128)(2,1)} %features_ref.3), channel_id=1, source_target_pairs={{0,2},{1,3},{2,0},{3,1},{4,6},{5,7},{6,4},{7,5},{8,10},{9,11},{10,... | collective-permute-start | bytes 196616 | tf_op jit(solution)/shard_map/ppermute | solution.py:309
  13.8 0.3 collective-permute-start.2
  14.1 3.5 %shard_map.138.adj_ref = bf16[512,1024]{1,0:T(8,128)(2,1)S(1)} custom-call(s32[256]{0:T(256)} %row_ref.3, s32[256]{0:T(256)} %col_ref.3, s32[256]{0:T(256)} %count_ref.3, s32[144,256]{1,0:T(8,128)S(1)} %get-tuple-element.41.src_ref, s32[144,256]{1,0:T(8,128)S(1)} %get-tuple-element.42.dst_ref, f32[4,8,128,128]{3,2,1,0:T(8,128)S(1)} %get-tuple-element.46.half_ref), custom_call_target="tpu_custom_call" | custom-call | tf_op jit(solution)/shard_map/pallas_call | solution.py:288
  17.6 0.0 copy-start
  17.6 0.0 copy-start.1
  17.6 0.0 copy-start.2
  17.6 0.0 copy-start.3
  17.6 0.0 copy-start.4
  17.6 0.0 collective-permute-done.1.near_features_ref
  17.7 0.6 %collective-permute-done.2.near_d_out_ref = bf16[128,256]{1,0:T(8,128)(2,1)S(1)} collective-permute-done((bf16[128,256]{1,0:T(8,128)(2,1)}, bf16[128,256]{1,0:T(8,128)(2,1)S(1)}, u32[]{:S(2)}, u32[]{:S(2)}) %collective-permute-start.2) | collective-permute-done | bytes 65568 | tf_op jit(solution)/shard_map/ppermute | solution.py:309
  18.3 0.0 collective-permute-done.5.refs_3_
  18.3 0.0 collective-permute-done.4.refs_2_
  18.3 0.0 collective-permute-done.3.refs_1_
  18.3 0.4 shard_map.140
  18.7 0.1 collective-permute-start.6
  18.8 0.4 shard_map.139.keep_ref
  19.2 0.9 %collective-permute-done.6.got_ref = bf16[264,256]{1,0:T(8,128)(2,1)S(1)} collective-permute-done((bf16[264,256]{1,0:T(8,128)(2,1)S(1)}, bf16[264,256]{1,0:T(8,128)(2,1)S(1)}, u32[]{:S(2)}, u32[]{:S(2)}) %collective-permute-start.6) | collective-permute-done | bytes 135200 | tf_op jit(solution)/shard_map/ppermute | solution.py:309
  20.2 1.2 %collective-permute-start.7 = (bf16[264,256]{1,0:T(8,128)(2,1)S(1)}, bf16[264,256]{1,0:T(8,128)(2,1)S(1)}, u32[]{:S(2)}, u32[]{:S(2)}) collective-permute-start(bf16[264,256]{1,0:T(8,128)(2,1)S(1)} %shard_map.141.pair_ref), channel_id=1, source_target_pairs={{0,2},{1,3},{2,0},{3,1},{4,6},{5,7},{6,4},{7,5},{8,10},{9,11},{10,... | collective-permute-start | bytes 405512 | tf_op jit(solution)/shard_map/ppermute | solution.py:309
  21.4 4.5 %collective-permute-done.7.got_ref = bf16[264,256]{1,0:T(8,128)(2,1)S(1)} collective-permute-done((bf16[264,256]{1,0:T(8,128)(2,1)S(1)}, bf16[264,256]{1,0:T(8,128)(2,1)S(1)}, u32[]{:S(2)}, u32[]{:S(2)}) %collective-permute-start.7) | collective-permute-done | bytes 135200 | tf_op jit(solution)/shard_map/ppermute | solution.py:309
  25.9 0.0 copy-done
  25.9 0.0 copy-done.1
  25.9 0.0 copy-done.2
  25.9 0.0 copy-done.3
  25.9 0.0 copy-done.4
  25.9 0.7 %shard_map.142 = (bf16[128,256]{1,0:T(8,128)(2,1)S(1)}, f32[128,256]{1,0:T(8,128)S(1)}, f32[136,256]{1,0:T(8,128)S(1)}, bf16[392,256]{1,0:T(8,128)(2,1)S(1)}) custom-call(bf16[264,256]{1,0:T(8,128)(2,1)S(1)} %shard_map.141.pair_ref, bf16[264,256]{1,0:T(8,128)(2,1)S(1)} %collective-permute-done.7.got_ref, bf16[128,256]{1,0:T(8,128)(2,1)S(1)} %copy-done, ...), custom_call_target="tpu_custom_call" | custom-call | tf_op jit(solution)/shard_map/pallas_call | solution.py:288
  26.6 0.1 collective-permute-start.8
  26.6 1.4 %collective-permute-done.8.got_ref = bf16[392,256]{1,0:T(8,128)(2,1)S(1)} collective-permute-done((bf16[392,256]{1,0:T(8,128)(2,1)S(1)}, bf16[392,256]{1,0:T(8,128)(2,1)S(1)}, u32[]{:S(2)}, u32[]{:S(2)}) %collective-permute-start.8) | collective-permute-done | bytes 200736 | tf_op jit(solution)/shard_map/ppermute | solution.py:309
  28.1 1.6 %collective-permute-start.11 = (bf16[136,256]{1,0:T(8,128)(2,1)S(1)}, bf16[136,256]{1,0:T(8,128)(2,1)S(1)}, u32[]{:S(2)}, u32[]{:S(2)}) collective-permute-start(bf16[136,256]{1,0:T(8,128)(2,1)S(1)} %shard_map.143.refs_0_), channel_id=1, source_target_pairs={{0,12},{4,8},{8,4},{12,0},{16,28},{20,24},{24,20},{28,16},{1,13},{... | collective-permute-start | bytes 208904 | tf_op jit(solution)/shard_map/ppermute | solution.py:309
  29.7 1.4 %collective-permute-start.10 = (bf16[136,256]{1,0:T(8,128)(2,1)S(1)}, bf16[136,256]{1,0:T(8,128)(2,1)S(1)}, u32[]{:S(2)}, u32[]{:S(2)}) collective-permute-start(bf16[136,256]{1,0:T(8,128)(2,1)S(1)} %shard_map.143.refs_0_), channel_id=1, source_target_pairs={{0,8},{4,12},{8,0},{12,4},{16,24},{20,28},{24,16},{28,20},{1,9},{5... | collective-permute-start | bytes 208904 | tf_op jit(solution)/shard_map/ppermute | solution.py:309
  31.1 0.5 %collective-permute-start.9 = (bf16[136,256]{1,0:T(8,128)(2,1)S(1)}, bf16[136,256]{1,0:T(8,128)(2,1)S(1)}, u32[]{:S(2)}, u32[]{:S(2)}) collective-permute-start(bf16[136,256]{1,0:T(8,128)(2,1)S(1)} %shard_map.143.refs_0_), channel_id=1, source_target_pairs={{0,4},{4,0},{8,12},{12,8},{16,20},{20,16},{24,28},{28,24},{1,5},{5... | collective-permute-start | bytes 208904 | tf_op jit(solution)/shard_map/ppermute | solution.py:309
  31.7 0.5 shard_map.146
  32.2 1.6 %collective-permute-start.13 = (bf16[256,256]{1,0:T(8,128)(2,1)S(1)}, bf16[256,256]{1,0:T(8,128)(2,1)S(1)}, u32[]{:S(2)}, u32[]{:S(2)}) collective-permute-start(bf16[256,256]{1,0:T(8,128)(2,1)S(1)} %get-tuple-element.66), channel_id=1, source_target_pairs={{0,12},{4,8},{8,4},{12,0},{16,28},{20,24},{24,20},{28,16},{1,13},{... | collective-permute-start | bytes 393224 | tf_op jit(solution)/shard_map/ppermute | solution.py:309
  33.8 1.4 %collective-permute-start.14 = (bf16[256,256]{1,0:T(8,128)(2,1)S(1)}, bf16[256,256]{1,0:T(8,128)(2,1)S(1)}, u32[]{:S(2)}, u32[]{:S(2)}) collective-permute-start(bf16[256,256]{1,0:T(8,128)(2,1)S(1)} %get-tuple-element.67), channel_id=1, source_target_pairs={{0,8},{4,12},{8,0},{12,4},{16,24},{20,28},{24,16},{28,20},{1,9},{5... | collective-permute-start | bytes 393224 | tf_op jit(solution)/shard_map/ppermute | solution.py:309
  35.2 0.0 collective-permute-done.11.refs_3_
  35.2 0.5 %collective-permute-start.15 = (bf16[256,256]{1,0:T(8,128)(2,1)S(1)}, bf16[256,256]{1,0:T(8,128)(2,1)S(1)}, u32[]{:S(2)}, u32[]{:S(2)}) collective-permute-start(bf16[256,256]{1,0:T(8,128)(2,1)S(1)} %get-tuple-element.68), channel_id=1, source_target_pairs={{0,4},{4,0},{8,12},{12,8},{16,20},{20,16},{24,28},{28,24},{1,5},{5... | collective-permute-start | bytes 393224 | tf_op jit(solution)/shard_map/ppermute | solution.py:309
  35.7 0.0 collective-permute-done.10.refs_2_
  35.7 1.8 %collective-permute-done.9.refs_1_ = bf16[136,256]{1,0:T(8,128)(2,1)S(1)} collective-permute-done((bf16[136,256]{1,0:T(8,128)(2,1)S(1)}, bf16[136,256]{1,0:T(8,128)(2,1)S(1)}, u32[]{:S(2)}, u32[]{:S(2)}) %collective-permute-start.9) | collective-permute-done | bytes 69664 | tf_op jit(solution)/shard_map/ppermute | solution.py:309
  37.5 0.2 collective-permute-start.12
  37.7 2.4 %collective-permute-done.13.refs_0_ = bf16[256,256]{1,0:T(8,128)(2,1)S(1)} collective-permute-done((bf16[256,256]{1,0:T(8,128)(2,1)S(1)}, bf16[256,256]{1,0:T(8,128)(2,1)S(1)}, u32[]{:S(2)}, u32[]{:S(2)}) %collective-permute-start.13) | collective-permute-done | bytes 131104 | tf_op jit(solution)/shard_map/ppermute | solution.py:309
  40.1 1.3 %collective-permute-done.14.refs_1_ = bf16[256,256]{1,0:T(8,128)(2,1)S(1)} collective-permute-done((bf16[256,256]{1,0:T(8,128)(2,1)S(1)}, bf16[256,256]{1,0:T(8,128)(2,1)S(1)}, u32[]{:S(2)}, u32[]{:S(2)}) %collective-permute-start.14) | collective-permute-done | bytes 131104 | tf_op jit(solution)/shard_map/ppermute | solution.py:309
  41.4 0.0 collective-permute-done.15.refs_2_
  41.4 0.1 shard_map.147
  41.5 2.2 %collective-permute-start.16 = (bf16[128,256]{1,0:T(8,128)(2,1)S(1)}, bf16[128,256]{1,0:T(8,128)(2,1)S(1)}, u32[]{:S(2)}, u32[]{:S(2)}) collective-permute-start(bf16[128,256]{1,0:T(8,128)(2,1)S(1)} %get-tuple-element.70), channel_id=1, source_target_pairs={{0,16},{4,20},{8,24},{12,28},{16,0},{20,4},{24,8},{28,12},{1,17},{... | collective-permute-start | bytes 196616 | tf_op jit(solution)/shard_map/ppermute | solution.py:309
  43.7 0.0 collective-permute-done.12.refs_1_
  43.7 0.1 collective-permute-start.19
  43.8 1.2 %collective-permute-start.18 = (bf16[128,256]{1,0:T(8,128)(2,1)S(1)}, bf16[128,256]{1,0:T(8,128)(2,1)S(1)}, u32[]{:S(2)}, u32[]{:S(2)}) collective-permute-start(bf16[128,256]{1,0:T(8,128)(2,1)S(1)} %get-tuple-element.73.refs_0_), channel_id=1, source_target_pairs={{0,2},{1,3},{2,0},{3,1},{4,6},{5,7},{6,4},{7,5},{8,10},{9,11},{10,... | collective-permute-start | bytes 196616 | tf_op jit(solution)/shard_map/ppermute | solution.py:309
  45.0 0.7 %collective-permute-start.17 = (bf16[128,256]{1,0:T(8,128)(2,1)S(1)}, bf16[128,256]{1,0:T(8,128)(2,1)S(1)}, u32[]{:S(2)}, u32[]{:S(2)}) collective-permute-start(bf16[128,256]{1,0:T(8,128)(2,1)S(1)} %get-tuple-element.73.refs_0_), channel_id=1, source_target_pairs={{0,1},{1,0},{2,3},{3,2},{4,5},{5,4},{6,7},{7,6},{8,9},{9,8},{10,11... | collective-permute-start | bytes 196616 | tf_op jit(solution)/shard_map/ppermute | solution.py:309
  45.6 1.8 %collective-permute-done.16.refs_1_ = bf16[128,256]{1,0:T(8,128)(2,1)S(1)} collective-permute-done((bf16[128,256]{1,0:T(8,128)(2,1)S(1)}, bf16[128,256]{1,0:T(8,128)(2,1)S(1)}, u32[]{:S(2)}, u32[]{:S(2)}) %collective-permute-start.16) | collective-permute-done | bytes 65568 | tf_op jit(solution)/shard_map/ppermute | solution.py:309
  47.4 0.7 %shard_map.148 = (bf16[128,256]{1,0:T(8,128)(2,1)}, f32[128,256]{1,0:T(8,128)}, f32[1,256]{1,0:T(1,128)}) custom-call(bf16[128,256]{1,0:T(8,128)(2,1)S(1)} %get-tuple-element.58.own_out_ref, f32[128,256]{1,0:T(8,128)S(1)} %get-tuple-element.59.self_ref, f32[1,256]{1,0:T(1,128)S(1)} %get-tuple-element.63.bias_term_ref, ...), custom_call_target="tpu_custom_call" | custom-call | tf_op jit(solution)/shard_map/pallas_call | solution.py:288
  48.1 0.0 collective-permute-done.19.refs_3_
  48.2 0.8 %collective-permute-done.18.refs_2_ = bf16[128,256]{1,0:T(8,128)(2,1)S(1)} collective-permute-done((bf16[128,256]{1,0:T(8,128)(2,1)S(1)}, bf16[128,256]{1,0:T(8,128)(2,1)S(1)}, u32[]{:S(2)}, u32[]{:S(2)}) %collective-permute-start.18) | collective-permute-done | bytes 65568 | tf_op jit(solution)/shard_map/ppermute | solution.py:309
  48.9 0.0 collective-permute-done.17.refs_1_
  48.9 0.8 %shard_map.149 = (f32[2,128,256]{2,1,0:T(8,128)}, f32[2,128,256]{2,1,0:T(8,128)}) custom-call(bf16[128,256]{1,0:T(8,128)(2,1)S(1)} %get-tuple-element.73.refs_0_, bf16[128,256]{1,0:T(8,128)(2,1)S(1)} %collective-permute-done.17.refs_1_, bf16[128,256]{1,0:T(8,128)(2,1)S(1)} %collective-permute-done.18.refs_2_, ...), custom_call_target="tpu_custom_call" | custom-call | tf_op jit(solution)/shard_map/pallas_call | solution.py:288
  (5 shorter events, 0.2 us)
Async XLA Ops:
  0.6 8.0 %collective-permute-start = (bf16[128,256]{1,0:T(8,128)(2,1)}, bf16[128,256]{1,0:T(8,128)(2,1)S(1)}, u32[]{:S(2)}, u32[]{:S(2)}) collective-permute-start(bf16[128,256]{1,0:T(8,128)(2,1)} %features_ref.3), channel_id=1, source_target_pairs={{0,16},{4,20},{8,24},{12,28},{16,0},{20,4},{24,8},{28,12},{1,17},{... | collective-permute-start | bytes 196616 | tf_op jit(solution)/shard_map/ppermute | solution.py:309
  8.6 9.7 %collective-permute-start.5 = (bf16[256,256]{1,0:T(8,128)(2,1)S(1)}, bf16[256,256]{1,0:T(8,128)(2,1)S(1)}, u32[]{:S(2)}, u32[]{:S(2)}) collective-permute-start(bf16[256,256]{1,0:T(8,128)(2,1)S(1)} %constant_dynamic-update-slice_fusion.refs_0_), channel_id=1, source_target_pairs={{0,12},{4,8},{8,4},{12,0},{16,28},{20,24},{24,20},{28,16},{1,13},{... | collective-permute-start | bytes 393224 | tf_op jit(solution)/shard_map/ppermute | solution.py:309
  10.4 7.9 %collective-permute-start.4 = (bf16[256,256]{1,0:T(8,128)(2,1)S(1)}, bf16[256,256]{1,0:T(8,128)(2,1)S(1)}, u32[]{:S(2)}, u32[]{:S(2)}) collective-permute-start(bf16[256,256]{1,0:T(8,128)(2,1)S(1)} %constant_dynamic-update-slice_fusion.refs_0_), channel_id=1, source_target_pairs={{0,8},{4,12},{8,0},{12,4},{16,24},{20,28},{24,16},{28,20},{1,9},{5... | collective-permute-start | bytes 393224 | tf_op jit(solution)/shard_map/ppermute | solution.py:309
  11.8 6.5 %collective-permute-start.3 = (bf16[256,256]{1,0:T(8,128)(2,1)S(1)}, bf16[256,256]{1,0:T(8,128)(2,1)S(1)}, u32[]{:S(2)}, u32[]{:S(2)}) collective-permute-start(bf16[256,256]{1,0:T(8,128)(2,1)S(1)} %constant_dynamic-update-slice_fusion.refs_0_), channel_id=1, source_target_pairs={{0,4},{4,0},{8,12},{12,8},{16,20},{20,16},{24,28},{28,24},{1,5},{5... | collective-permute-start | bytes 393224 | tf_op jit(solution)/shard_map/ppermute | solution.py:309
  12.1 5.6 %collective-permute-start.1 = (bf16[128,256]{1,0:T(8,128)(2,1)}, bf16[128,256]{1,0:T(8,128)(2,1)S(1)}, u32[]{:S(2)}, u32[]{:S(2)}) collective-permute-start(bf16[128,256]{1,0:T(8,128)(2,1)} %features_ref.3), channel_id=1, source_target_pairs={{0,2},{1,3},{2,0},{3,1},{4,6},{5,7},{6,4},{7,5},{8,10},{9,11},{10,... | collective-permute-start | bytes 196616 | tf_op jit(solution)/shard_map/ppermute | solution.py:309
  13.8 4.5 %collective-permute-start.2 = (bf16[128,256]{1,0:T(8,128)(2,1)}, bf16[128,256]{1,0:T(8,128)(2,1)S(1)}, u32[]{:S(2)}, u32[]{:S(2)}) collective-permute-start(bf16[128,256]{1,0:T(8,128)(2,1)} %d_out_ref.1), channel_id=1, source_target_pairs={{0,2},{1,3},{2,0},{3,1},{4,6},{5,7},{6,4},{7,5},{8,10},{9,11},{10,... | collective-permute-start | bytes 196616 | tf_op jit(solution)/shard_map/ppermute | solution.py:309
  17.6 8.3 %copy-start = (bf16[128,256]{1,0:T(8,128)(2,1)S(1)}, bf16[128,256]{1,0:T(8,128)(2,1)}, u32[]{:S(2)}) copy-start(bf16[128,256]{1,0:T(8,128)(2,1)} %features_ref.3) | copy-start | bytes 196612
  17.6 8.3 %copy-start.1 = (bf16[256,256]{1,0:T(8,128)(2,1)S(1)}, bf16[256,256]{1,0:T(8,128)(2,1)}, u32[]{:S(2)}) copy-start(bf16[256,256]{1,0:T(8,128)(2,1)} %w_self_ref.1) | copy-start | bytes 393220
  17.6 8.3 %copy-start.2 = (bf16[256,256]{1,0:T(8,128)(2,1)S(1)}, bf16[256,256]{1,0:T(8,128)(2,1)}, u32[]{:S(2)}) copy-start(bf16[256,256]{1,0:T(8,128)(2,1)} %w_neigh_ref.1) | copy-start | bytes 393220
  17.6 8.3 %copy-start.3 = (bf16[128,256]{1,0:T(8,128)(2,1)S(1)}, bf16[128,256]{1,0:T(8,128)(2,1)}, u32[]{:S(2)}) copy-start(bf16[128,256]{1,0:T(8,128)(2,1)} %d_out_ref.1) | copy-start | bytes 196612
  17.6 8.3 %copy-start.4 = (f32[256]{0:T(256)S(1)}, f32[256]{0:T(256)}, u32[]{:S(2)}) copy-start(f32[256]{0:T(256)} %param.13) | copy-start | bytes 3076
  18.7 1.4 %collective-permute-start.6 = (bf16[264,256]{1,0:T(8,128)(2,1)S(1)}, bf16[264,256]{1,0:T(8,128)(2,1)S(1)}, u32[]{:S(2)}, u32[]{:S(2)}) collective-permute-start(bf16[264,256]{1,0:T(8,128)(2,1)S(1)} %shard_map.140), channel_id=1, source_target_pairs={{0,1},{1,0},{2,3},{3,2},{4,5},{5,4},{6,7},{7,6},{8,9},{9,8},{10,11... | collective-permute-start | bytes 405512 | tf_op jit(solution)/shard_map/ppermute | solution.py:309
  20.2 5.7 %collective-permute-start.7 = (bf16[264,256]{1,0:T(8,128)(2,1)S(1)}, bf16[264,256]{1,0:T(8,128)(2,1)S(1)}, u32[]{:S(2)}, u32[]{:S(2)}) collective-permute-start(bf16[264,256]{1,0:T(8,128)(2,1)S(1)} %shard_map.141.pair_ref), channel_id=1, source_target_pairs={{0,2},{1,3},{2,0},{3,1},{4,6},{5,7},{6,4},{7,5},{8,10},{9,11},{10,... | collective-permute-start | bytes 405512 | tf_op jit(solution)/shard_map/ppermute | solution.py:309
  26.6 1.5 %collective-permute-start.8 = (bf16[392,256]{1,0:T(8,128)(2,1)S(1)}, bf16[392,256]{1,0:T(8,128)(2,1)S(1)}, u32[]{:S(2)}, u32[]{:S(2)}) collective-permute-start(bf16[392,256]{1,0:T(8,128)(2,1)S(1)} %get-tuple-element.61.sent_ref), channel_id=1, source_target_pairs={{0,1},{1,0},{2,3},{3,2},{4,5},{5,4},{6,7},{7,6},{8,9},{9,8},{10,11... | collective-permute-start | bytes 602120 | tf_op jit(solution)/shard_map/ppermute | solution.py:309
  28.1 7.1 %collective-permute-start.11 = (bf16[136,256]{1,0:T(8,128)(2,1)S(1)}, bf16[136,256]{1,0:T(8,128)(2,1)S(1)}, u32[]{:S(2)}, u32[]{:S(2)}) collective-permute-start(bf16[136,256]{1,0:T(8,128)(2,1)S(1)} %shard_map.143.refs_0_), channel_id=1, source_target_pairs={{0,12},{4,8},{8,4},{12,0},{16,28},{20,24},{24,20},{28,16},{1,13},{... | collective-permute-start | bytes 208904 | tf_op jit(solution)/shard_map/ppermute | solution.py:309
  29.7 6.0 %collective-permute-start.10 = (bf16[136,256]{1,0:T(8,128)(2,1)S(1)}, bf16[136,256]{1,0:T(8,128)(2,1)S(1)}, u32[]{:S(2)}, u32[]{:S(2)}) collective-permute-start(bf16[136,256]{1,0:T(8,128)(2,1)S(1)} %shard_map.143.refs_0_), channel_id=1, source_target_pairs={{0,8},{4,12},{8,0},{12,4},{16,24},{20,28},{24,16},{28,20},{1,9},{5... | collective-permute-start | bytes 208904 | tf_op jit(solution)/shard_map/ppermute | solution.py:309
  31.1 6.3 %collective-permute-start.9 = (bf16[136,256]{1,0:T(8,128)(2,1)S(1)}, bf16[136,256]{1,0:T(8,128)(2,1)S(1)}, u32[]{:S(2)}, u32[]{:S(2)}) collective-permute-start(bf16[136,256]{1,0:T(8,128)(2,1)S(1)} %shard_map.143.refs_0_), channel_id=1, source_target_pairs={{0,4},{4,0},{8,12},{12,8},{16,20},{20,16},{24,28},{28,24},{1,5},{5... | collective-permute-start | bytes 208904 | tf_op jit(solution)/shard_map/ppermute | solution.py:309
  32.2 8.0 %collective-permute-start.13 = (bf16[256,256]{1,0:T(8,128)(2,1)S(1)}, bf16[256,256]{1,0:T(8,128)(2,1)S(1)}, u32[]{:S(2)}, u32[]{:S(2)}) collective-permute-start(bf16[256,256]{1,0:T(8,128)(2,1)S(1)} %get-tuple-element.66), channel_id=1, source_target_pairs={{0,12},{4,8},{8,4},{12,0},{16,28},{20,24},{24,20},{28,16},{1,13},{... | collective-permute-start | bytes 393224 | tf_op jit(solution)/shard_map/ppermute | solution.py:309
  33.8 7.7 %collective-permute-start.14 = (bf16[256,256]{1,0:T(8,128)(2,1)S(1)}, bf16[256,256]{1,0:T(8,128)(2,1)S(1)}, u32[]{:S(2)}, u32[]{:S(2)}) collective-permute-start(bf16[256,256]{1,0:T(8,128)(2,1)S(1)} %get-tuple-element.67), channel_id=1, source_target_pairs={{0,8},{4,12},{8,0},{12,4},{16,24},{20,28},{24,16},{28,20},{1,9},{5... | collective-permute-start | bytes 393224 | tf_op jit(solution)/shard_map/ppermute | solution.py:309
  35.2 6.2 %collective-permute-start.15 = (bf16[256,256]{1,0:T(8,128)(2,1)S(1)}, bf16[256,256]{1,0:T(8,128)(2,1)S(1)}, u32[]{:S(2)}, u32[]{:S(2)}) collective-permute-start(bf16[256,256]{1,0:T(8,128)(2,1)S(1)} %get-tuple-element.68), channel_id=1, source_target_pairs={{0,4},{4,0},{8,12},{12,8},{16,20},{20,16},{24,28},{28,24},{1,5},{5... | collective-permute-start | bytes 393224 | tf_op jit(solution)/shard_map/ppermute | solution.py:309
  37.5 6.1 %collective-permute-start.12 = (bf16[136,256]{1,0:T(8,128)(2,1)S(1)}, bf16[136,256]{1,0:T(8,128)(2,1)S(1)}, u32[]{:S(2)}, u32[]{:S(2)}) collective-permute-start(bf16[136,256]{1,0:T(8,128)(2,1)S(1)} %shard_map.144.refs_0_), channel_id=1, source_target_pairs={{0,16},{4,20},{8,24},{12,28},{16,0},{20,4},{24,8},{28,12},{1,17},{... | collective-permute-start | bytes 208904 | tf_op jit(solution)/shard_map/ppermute | solution.py:309
  41.5 5.9 %collective-permute-start.16 = (bf16[128,256]{1,0:T(8,128)(2,1)S(1)}, bf16[128,256]{1,0:T(8,128)(2,1)S(1)}, u32[]{:S(2)}, u32[]{:S(2)}) collective-permute-start(bf16[128,256]{1,0:T(8,128)(2,1)S(1)} %get-tuple-element.70), channel_id=1, source_target_pairs={{0,16},{4,20},{8,24},{12,28},{16,0},{20,4},{24,8},{28,12},{1,17},{... | collective-permute-start | bytes 196616 | tf_op jit(solution)/shard_map/ppermute | solution.py:309
  43.7 4.5 %collective-permute-start.19 = (bf16[128,256]{1,0:T(8,128)(2,1)S(1)}, bf16[128,256]{1,0:T(8,128)(2,1)S(1)}, u32[]{:S(2)}, u32[]{:S(2)}) collective-permute-start(bf16[128,256]{1,0:T(8,128)(2,1)S(1)} %get-tuple-element.73.refs_0_), channel_id=1, source_target_pairs={{0,3},{1,2},{2,1},{3,0},{4,7},{5,6},{6,5},{7,4},{8,11},{9,10},{10,... | collective-permute-start | bytes 196616 | tf_op jit(solution)/shard_map/ppermute | solution.py:309
  43.8 5.1 %collective-permute-start.18 = (bf16[128,256]{1,0:T(8,128)(2,1)S(1)}, bf16[128,256]{1,0:T(8,128)(2,1)S(1)}, u32[]{:S(2)}, u32[]{:S(2)}) collective-permute-start(bf16[128,256]{1,0:T(8,128)(2,1)S(1)} %get-tuple-element.73.refs_0_), channel_id=1, source_target_pairs={{0,2},{1,3},{2,0},{3,1},{4,6},{5,7},{6,4},{7,5},{8,10},{9,11},{10,... | collective-permute-start | bytes 196616 | tf_op jit(solution)/shard_map/ppermute | solution.py:309
  45.0 3.9 %collective-permute-start.17 = (bf16[128,256]{1,0:T(8,128)(2,1)S(1)}, bf16[128,256]{1,0:T(8,128)(2,1)S(1)}, u32[]{:S(2)}, u32[]{:S(2)}) collective-permute-start(bf16[128,256]{1,0:T(8,128)(2,1)S(1)} %get-tuple-element.73.refs_0_), channel_id=1, source_target_pairs={{0,1},{1,0},{2,3},{3,2},{4,5},{5,4},{6,7},{7,6},{8,9},{9,8},{10,11... | collective-permute-start | bytes 196616 | tf_op jit(solution)/shard_map/ppermute | solution.py:309
